TPU v7x, 32 devices: a whole 2x2x4 slice. The times are simulated.
32 devices in a mesh: section: 2 (over y), tensor: 2 (over x), dp: 8 (over z, core).
Axes of the slice: x: 2, y: 2, z: 4, core: 2. Of those that a mesh axis runs over, the one named last changes fastest.
Arguments:
- inputs: bfloat16 [32, 512, 1024], P('dp', 'tensor'), may hold values from -6 to 6
- cotangent: bfloat16 [32, 512, 1024], P('dp', 'tensor'), may hold values from -6 to 6
- lengths: int32 [32], P('dp'), may hold values from 256 to 512, as said below
- w_qkv: bfloat16 [2, 1024, 3, 1024], P('section', None, None, 'tensor'), may hold values from -0.1875 to 0.1875
- b_qv: bfloat16 [2, 2, 1024], P('section', None, 'tensor'), may hold values from -4 to 4
- w_out: bfloat16 [2, 1024, 1024], P('section', 'tensor'), may hold values from -0.5 to 0.5
- b_out: bfloat16 [2, 1024], P('section'), may hold values from -3 to 3
- ln_gain: bfloat16 [2, 2, 1024], P('section'), may hold values from 0.5 to 1.5
- ln_bias: bfloat16 [2, 2, 1024], P('section'), may hold values from -3 to 3
- w_up: bfloat16 [2, 2, 1024, 4096], P('section', None, None, 'tensor'), may hold values from -0.1875 to 0.1875
- b_up: bfloat16 [2, 2, 4096], P('section', None, 'tensor'), may hold values from -3 to 3
- w_down: bfloat16 [2, 1024, 4096], P('section', None, 'tensor'), may hold values from -0.125 to 0.125
- b_down: bfloat16 [2, 1024], P('section'), may hold values from -3 to 3
Outputs:
- layer_outputs: bfloat16 [2, 32, 512, 1024], P('section', 'dp', 'tensor')
- input_grads: float32 [2, 32, 512, 1024], P('section', 'dp', 'tensor')
- grad_w_qkv: float32 [2, 1024, 3, 1024], P('section', None, None, 'tensor')
- grad_b_qv: float32 [2, 2, 1024], P('section', None, 'tensor')
- grad_w_out: float32 [2, 1024, 1024], P('section', 'tensor')
- grad_b_out: float32 [2, 1024], P('section')
- grad_ln_gain: float32 [2, 2, 1024], P('section')
- grad_ln_bias: float32 [2, 2, 1024], P('section')
- grad_w_up: float32 [2, 2, 1024, 4096], P('section', None, None, 'tensor')
- grad_b_up: float32 [2, 2, 4096], P('section', None, 'tensor')
- grad_w_down: float32 [2, 1024, 4096], P('section', None, 'tensor')
- grad_b_down: float32 [2, 1024], P('section')
Inputs may be any that keep to these rules, and one draw needn't show every extreme that they name: `lengths`: some sequence in every draw has all 512 positions in use.
All inputs are finite; a program needn't handle non-finite values.
Results may differ from a plain program's by a relative error of at most 0.03.
Values may be sent and summed in bfloat16 or wider, within the bound.
A program may use at most 256 MiB of HBM per device.

v0:
```python
import math

import jax
import jax.numpy as jnp
from jax import lax
from jax.sharding import PartitionSpec as P

H = 16
HD = 64


EPS = 1e-05
MASKED = -1000000000.0


def shifted(value, axis, steps):
    count = lax.axis_size(axis)
    first, last = (max(0, -steps), min(count, count - steps))
    return lax.ppermute(value, axis, [(source, source + steps) for source in range(first, last)])


def layer_norm(values, gain, shift):
    mean = jnp.mean(values, axis=-1, keepdims=True)
    centred = values - mean
    spread = jnp.mean(centred * centred, axis=-1, keepdims=True)
    return centred * lax.rsqrt(spread + EPS) * gain + shift


def alibi_slopes(first, count, heads):
    index = (first + jnp.arange(count)).astype(jnp.float32)
    return jnp.exp2(-8.0 * (index + 1.0) / heads)


def attention_core(projected, qv_bias, slopes, key_ok):
    rows = projected.shape[0]
    width = projected.shape[2]
    count = slopes.shape[0]
    size = width // count
    query = (projected[:, 0] + qv_bias[0]).astype(jnp.bfloat16).reshape(rows, count, size)
    key = projected[:, 1].astype(jnp.bfloat16).reshape(rows, count, size)
    value = (projected[:, 2] + qv_bias[1]).astype(jnp.bfloat16).reshape(rows, count, size)
    place = jnp.arange(rows).astype(jnp.float32)
    distance = jnp.abs(place[:, None] - place[None, :])
    scale = 1.0 / math.sqrt(size)
    scores = (
        jnp.einsum("qhd,khd->hqk", query, key, preferred_element_type=jnp.float32) * scale
        - slopes[:, None, None] * distance[None]
    )
    scores = jnp.where(key_ok[None, None, :], scores, MASKED)
    weights = jax.nn.softmax(scores, axis=-1)
    weights_low = weights.astype(jnp.bfloat16)
    mixed = jnp.einsum("hqk,khd->qhd", weights_low, value, preferred_element_type=jnp.float32)
    mixed = mixed.reshape(rows, width).astype(jnp.bfloat16)
    return (query, key, value, weights, weights_low, mixed)


def attention_back(parts, grad_mixed, key_ok):
    query, key, value, weights, weights_low, mixed = parts
    rows, count, size = query.shape
    scale = 1.0 / math.sqrt(size)
    grad_low = grad_mixed.astype(jnp.bfloat16).reshape(rows, count, size)
    grad_weights = jnp.einsum("qhd,khd->hqk", grad_low, value, preferred_element_type=jnp.float32)
    grad_value = jnp.einsum(
        "hqk,qhd->khd", weights_low, grad_low, preferred_element_type=jnp.float32
    )
    inner = jnp.sum(weights * grad_weights, axis=-1, keepdims=True)
    grad_scores = weights * (grad_weights - inner)
    grad_scores = jnp.where(key_ok[None, None, :], grad_scores, 0.0).astype(jnp.bfloat16)
    grad_query = (
        jnp.einsum("hqk,khd->qhd", grad_scores, key, preferred_element_type=jnp.float32) * scale
    ).astype(jnp.bfloat16)
    grad_key = (
        jnp.einsum("hqk,qhd->khd", grad_scores, query, preferred_element_type=jnp.float32) * scale
    ).astype(jnp.bfloat16)
    grad_value = grad_value.astype(jnp.bfloat16)
    width = count * size
    grad_query = grad_query.reshape(rows, width)
    grad_key = grad_key.reshape(rows, width)
    grad_value = grad_value.reshape(rows, width)
    grad_projected = jnp.stack([grad_query, grad_key, grad_value], axis=1).reshape(rows, 3 * width)
    qv_grad = jnp.stack(
        [
            jnp.sum(grad_query.astype(jnp.float32), axis=0),
            jnp.sum(grad_value.astype(jnp.float32), axis=0),
        ]
    )
    return (grad_projected, qv_grad)


def gelu_product(both):
    return jax.nn.gelu(both[:, 0], approximate=False) * both[:, 1]


def geglu(lifted, up_bias):
    return gelu_product(lifted + up_bias[None])


def ffn_grads(rows_low, grad_low, up_weight, up_bias, down_weight):
    lifted = jnp.einsum("sd,gdf->sgf", rows_low, up_weight, preferred_element_type=jnp.float32)
    hidden, geglu_back = jax.vjp(gelu_product, lifted + up_bias[None])
    grad_hidden = jnp.einsum("sd,df->sf", grad_low, down_weight, preferred_element_type=jnp.float32)
    (grad_both,) = geglu_back(grad_hidden)
    grad_lifted = grad_both.astype(jnp.bfloat16)
    grad_bias = jnp.sum(grad_lifted.astype(jnp.float32), axis=0)
    up_grad = jnp.einsum("sd,sgf->gdf", rows_low, grad_lifted, preferred_element_type=jnp.float32)
    down_grad = jnp.einsum(
        "sd,sf->df", grad_low, hidden.astype(jnp.bfloat16), preferred_element_type=jnp.float32
    )
    return (grad_lifted, grad_bias, up_grad, down_grad)


def on_device(
    inputs,
    cotangent,
    lengths,
    w_qkv,
    b_qv,
    w_out,
    b_out,
    ln_gain,
    ln_bias,
    w_up,
    b_up,
    w_down,
    b_down,
):
    batches, shard_rows, width = inputs.shape
    parts = lax.axis_size("tensor")
    place = lax.axis_index("tensor")
    section = lax.axis_index("section")
    last_section = lax.axis_size("section") - 1
    full_rows = shard_rows * parts
    local_width = w_qkv.shape[3]
    local_heads = local_width // HD
    qkv_flat = w_qkv[0].reshape(width, 3 * local_width)
    out_weight = w_out[0]
    qv_bias = b_qv[0].astype(jnp.float32)
    out_bias = b_out[0].astype(jnp.float32)
    gains = ln_gain[0].astype(jnp.float32)
    shifts = ln_bias[0].astype(jnp.float32)
    down_bias = b_down[0].astype(jnp.float32)
    slopes = alibi_slopes(place * local_heads, local_heads, H)
    row_place = place * shard_rows + jnp.arange(shard_rows)
    kept_rows = 0

    def key_mask(length):
        return jnp.arange(full_rows) < length

    def after_attention(values, attended, bias, gain_rows, shift_rows):
        return layer_norm(values + attended + bias, gain_rows[0], shift_rows[0])

    def after_ffn(normed, lowered, bias, gain_rows, shift_rows):
        return layer_norm(normed + lowered + bias, gain_rows[1], shift_rows[1])

    def gather_inputs(values):
        return lax.all_gather(values.astype(jnp.bfloat16), "tensor", axis=0, tiled=True)

    def project(gathered):
        return jnp.dot(gathered, qkv_flat, preferred_element_type=jnp.float32).reshape(
            full_rows, 3, local_width
        )

    def attention_forward(values, length):
        gathered = gather_inputs(values)
        projected = project(gathered)
        mixed = attention_core(projected, qv_bias, slopes, key_mask(length))[5]

        def term(start, count):
            return jnp.dot(mixed, out_weight, preferred_element_type=jnp.float32)

        return (
            lax.psum_scatter(
                term(jnp.int32(0), shard_rows * lax.axis_size("tensor")).astype(jnp.bfloat16),
                "tensor",
                scatter_dimension=0,
                tiled=True,
            ).astype(jnp.float32),
            gathered,
            projected,
        )

    up_local = w_up[0]
    up_bias_local = b_up[0].astype(jnp.float32)
    down_local = w_down[0]

    def gather_normed(normed):
        return lax.all_gather(normed.astype(jnp.bfloat16), "tensor", axis=0, tiled=True)

    def ffn_forward(normed):
        lifted = jnp.einsum(
            "sd,gdf->sgf", gather_normed(normed), up_local, preferred_element_type=jnp.float32
        )
        hidden = geglu(lifted, up_bias_local).astype(jnp.bfloat16)

        def term(start, count):
            return jnp.einsum("sf,df->sd", hidden, down_local, preferred_element_type=jnp.float32)

        return lax.psum_scatter(
            term(jnp.int32(0), shard_rows * lax.axis_size("tensor")).astype(jnp.bfloat16),
            "tensor",
            scatter_dimension=0,
            tiled=True,
        ).astype(jnp.float32)

    def ffn_backward(normed, grad_lowered):
        gathered = gather_normed(normed)
        grad_whole = lax.all_gather(grad_lowered.astype(jnp.bfloat16), "tensor", axis=0, tiled=True)
        grad_lifted, grad_bias, up_grad, down_grad = ffn_grads(
            gathered, grad_whole, up_local, up_bias_local, down_local
        )

        def term(start, count):
            return jnp.einsum(
                "sgf,gdf->sd", grad_lifted, up_local, preferred_element_type=jnp.float32
            )

        grad_normed = lax.psum_scatter(
            term(jnp.int32(0), shard_rows * lax.axis_size("tensor")).astype(jnp.bfloat16),
            "tensor",
            scatter_dimension=0,
            tiled=True,
        ).astype(jnp.float32)
        return (grad_normed, (up_grad, grad_bias, down_grad))

    ffn_shapes = (up_local.shape, up_bias_local.shape, down_local.shape)

    def layer_forward(values, length):
        attended, gathered, projected = attention_forward(values, length)
        normed = after_attention(values, attended, out_bias, gains, shifts)
        lowered = ffn_forward(normed)
        return (
            after_ffn(normed, lowered, down_bias, gains, shifts),
            attended,
            lowered,
            gathered,
            projected,
        )

    def layer_backward(values, attended, lowered, length, grad_output):
        normed, attention_norm_back = jax.vjp(
            after_attention, values, attended, out_bias, gains, shifts
        )
        outcome, ffn_norm_back = jax.vjp(after_ffn, normed, lowered, down_bias, gains, shifts)
        grad_normed, grad_lowered, grad_down_bias, gain_late, shift_late = ffn_norm_back(
            grad_output
        )
        grad_from_ffn, ffn_terms = ffn_backward(normed, grad_lowered)
        grad_values, grad_attended, grad_out_bias, gain_early, shift_early = attention_norm_back(
            grad_normed + grad_from_ffn
        )
        gathered = gather_inputs(values)
        projected = project(gathered)
        grad_whole = lax.all_gather(
            grad_attended.astype(jnp.bfloat16), "tensor", axis=0, tiled=True
        )
        mask = key_mask(length)
        pieces = attention_core(projected, qv_bias, slopes, mask)
        mixed_low = pieces[5]
        out_grad = jnp.einsum(
            "se,sd->ed", mixed_low, grad_whole, preferred_element_type=jnp.float32
        )
        grad_mixed = jnp.einsum(
            "sd,ed->se", grad_whole, out_weight, preferred_element_type=jnp.float32
        )
        grad_projected, qv_grad = attention_back(pieces, grad_mixed, mask)
        qkv_grad = jnp.einsum(
            "sd,sx->dx", gathered, grad_projected, preferred_element_type=jnp.float32
        )

        def term(start, count):
            return jnp.einsum(
                "sx,dx->sd", grad_projected, qkv_flat, preferred_element_type=jnp.float32
            )

        grad_inputs = grad_values + lax.psum_scatter(
            term(jnp.int32(0), shard_rows * lax.axis_size("tensor")).astype(jnp.bfloat16),
            "tensor",
            scatter_dimension=0,
            tiled=True,
        ).astype(jnp.float32)
        terms = (
            qkv_grad,
            qv_grad,
            out_grad,
            grad_out_bias,
            gain_early + gain_late,
            shift_early + shift_late,
            ffn_terms[0],
            ffn_terms[1],
            ffn_terms[2],
            grad_down_bias,
        )
        return (grad_inputs, terms)

    def keep(store, item, batch, valid):
        old = lax.dynamic_index_in_dim(store, batch, 0, keepdims=False)
        return lax.dynamic_update_index_in_dim(store, jnp.where(valid, item, old), batch, 0)

    def forward_step(step, carry):
        (
            received,
            kept_values,
            kept_attended,
            kept_lowered,
            produced,
            kept_gathered,
            kept_projected,
        ) = carry
        index = step - section
        valid = (index >= 0) & (index < batches)
        batch = jnp.clip(index, 0, batches - 1)
        fresh = lax.dynamic_index_in_dim(
            inputs, jnp.minimum(step, batches - 1), 0, keepdims=False
        ).astype(jnp.float32)
        values = jnp.where(section == 0, fresh, received.astype(jnp.float32))
        output, attended, lowered, gathered, projected = layer_forward(values, lengths[batch])
        sent = output.astype(jnp.bfloat16)
        kept_values = keep(kept_values, values, batch, valid)
        kept_attended = keep(kept_attended, attended, batch, valid)
        kept_lowered = keep(kept_lowered, lowered, batch, valid)
        produced = keep(produced, sent, batch, valid)
        kept_gathered = keep(kept_gathered, gathered[:kept_rows], batch, valid)
        kept_projected = keep(kept_projected, projected[:kept_rows], batch, valid)
        received = shifted(sent, "section", 1)
        return (
            received,
            kept_values,
            kept_attended,
            kept_lowered,
            produced,
            kept_gathered,
            kept_projected,
        )

    store_zeros = jnp.zeros((batches, shard_rows, width), jnp.float32)
    gathered_zeros = jnp.zeros((batches, kept_rows, width), jnp.bfloat16)
    projected_zeros = jnp.zeros((batches, kept_rows, 3, local_width), jnp.float32)
    start_forward = (
        jnp.zeros((shard_rows, width), jnp.bfloat16),
        store_zeros,
        store_zeros,
        store_zeros,
        jnp.zeros((batches, shard_rows, width), jnp.bfloat16),
        gathered_zeros,
        projected_zeros,
    )
    received, kept_values, kept_attended, kept_lowered, produced, kept_gathered, kept_projected = (
        lax.fori_loop(0, batches + last_section, forward_step, start_forward)
    )

    def backward_step(step, carry):
        received, totals, grads_in = carry
        index = step - (last_section - section)
        valid = (index >= 0) & (index < batches)
        batch = jnp.clip(index, 0, batches - 1)
        length = lengths[batch]
        outer = lax.dynamic_index_in_dim(cotangent, batch, 0, keepdims=False).astype(jnp.float32)
        outer = outer * (row_place < length).astype(jnp.float32)[:, None]
        grad_output = jnp.where(section == last_section, outer, received.astype(jnp.float32))
        grad_output = jnp.where(valid, grad_output, 0.0)
        values = lax.dynamic_index_in_dim(kept_values, batch, 0, keepdims=False)
        attended = lax.dynamic_index_in_dim(kept_attended, batch, 0, keepdims=False)
        lowered = lax.dynamic_index_in_dim(kept_lowered, batch, 0, keepdims=False)
        grad_inputs, terms = layer_backward(values, attended, lowered, length, grad_output)
        totals = jax.tree.map(jnp.add, totals, terms)
        grads_in = keep(grads_in, grad_inputs, batch, valid)
        received = shifted(grad_inputs.astype(jnp.bfloat16), "section", -1)
        return (received, totals, grads_in)

    start_totals = (
        jnp.zeros((width, 3 * local_width), jnp.float32),
        jnp.zeros((2, local_width), jnp.float32),
        jnp.zeros((local_width, width), jnp.float32),
        jnp.zeros((width,), jnp.float32),
        jnp.zeros((2, width), jnp.float32),
        jnp.zeros((2, width), jnp.float32),
        jnp.zeros(ffn_shapes[0], jnp.float32),
        jnp.zeros(ffn_shapes[1], jnp.float32),
        jnp.zeros(ffn_shapes[2], jnp.float32),
        jnp.zeros((width,), jnp.float32),
    )
    start_backward = (jnp.zeros((shard_rows, width), jnp.bfloat16), start_totals, store_zeros)
    received, totals, grads_in = lax.fori_loop(
        0, batches + last_section, backward_step, start_backward
    )
    (
        qkv_total,
        qv_total,
        out_total,
        out_bias_total,
        gain_total,
        shift_total,
        up_total,
        up_bias_total,
        down_total,
        down_bias_total,
    ) = totals
    qkv_sum, qv_sum, out_sum, up_sum, up_bias_sum, down_sum = (
        lax.psum(qkv_total.astype(jnp.bfloat16), "dp").astype(jnp.float32),
        lax.psum(qv_total.astype(jnp.bfloat16), "dp").astype(jnp.float32),
        lax.psum(out_total.astype(jnp.bfloat16), "dp").astype(jnp.float32),
        lax.psum(up_total.astype(jnp.bfloat16), "dp").astype(jnp.float32),
        lax.psum(up_bias_total.astype(jnp.bfloat16), "dp").astype(jnp.float32),
        lax.psum(down_total.astype(jnp.bfloat16), "dp").astype(jnp.float32),
    )
    out_bias_sum, gain_sum, shift_sum, down_bias_sum = lax.psum(
        (out_bias_total, gain_total, shift_total, down_bias_total), ("tensor", "dp")
    )
    return (
        produced[None],
        grads_in[None],
        qkv_sum.reshape(1, width, 3, local_width),
        qv_sum[None],
        out_sum[None],
        out_bias_sum[None],
        gain_sum[None],
        shift_sum[None],
        up_sum[None],
        up_bias_sum[None],
        down_sum[None],
        down_bias_sum[None],
    )


def solution(mesh):
    return jax.shard_map(
        on_device,
        mesh=mesh,
        in_specs=(
            P("dp", "tensor", None),
            P("dp", "tensor", None),
            P("dp"),
            P("section", None, None, "tensor"),
            P("section", None, "tensor"),
            P("section", "tensor", None),
            P("section", None),
            P("section", None, None),
            P("section", None, None),
            P("section", None, None, "tensor"),
            P("section", None, "tensor"),
            P("section", None, "tensor"),
            P("section", None),
        ),
        out_specs=(
            P("section", "dp", "tensor", None),
            P("section", "dp", "tensor", None),
            P("section", None, None, "tensor"),
            P("section", None, "tensor"),
            P("section", "tensor", None),
            P("section", None),
            P("section", None, None),
            P("section", None, None),
            P("section", None, None, "tensor"),
            P("section", None, "tensor"),
            P("section", None, "tensor"),
            P("section", None),
        ),
        check_vma=False,
    )
```

profile of v0, /device:TPU:0, one launch (start us, length us, event | category | flops | bytes accessed | tf_op | source)
XLA Modules:
  0.0 2353.0 jit_solution(1913434155665024905)
XLA Ops:
  23.6 750.7 %while.61 = (s32[]{:T(128)}, bf16[256,1024]{1,0:T(8,128)(2,1)S(1)}, f32[4,256,1024]{2,1,0:T(8,128)}, f32[4,256,1024]{2,1,0:T(8,128)}, f32[4,256,1024]{2,1,0:T(8,...) while((s32[]{:T(128)}, bf16[256,1024]{1,0:T(8,128)(2,1)S(1)}, ...), condition=%wide.region_9.10_spmd.clone, body=%wide.region_0.9_spmd.clone.sunk | while | flops 9234024448 | bytes 154839408 | solution.py:348
  27.3 22.7 all-gather.11.cloned.1.call-done
  71.0 20.4 reduce-scatter.5.cloned.1.call-done
  96.5 21.4 all-gather.13.cloned.1.call-done
  125.3 11.7 fusion.288
  178.9 20.8 all-gather.11.cloned.1.call-done
  220.6 20.4 reduce-scatter.5.cloned.1.call-done
  246.1 21.4 all-gather.13.cloned.1.call-done
  274.9 11.7 fusion.288
  295.3 11.8 reduce-scatter.7.cloned.1.call-done
  328.5 21.1 all-gather.11.cloned.1.call-done
  370.5 20.4 reduce-scatter.5.cloned.1.call-done
  396.0 21.4 all-gather.13.cloned.1.call-done
  424.8 11.7 fusion.288
  445.2 11.8 reduce-scatter.7.cloned.1.call-done
  478.5 21.1 all-gather.11.cloned.1.call-done
  520.5 20.4 reduce-scatter.5.cloned.1.call-done
  546.0 21.4 all-gather.13.cloned.1.call-done
  574.8 11.7 fusion.288
  595.2 11.8 reduce-scatter.7.cloned.1.call-done
  628.4 20.8 all-gather.11.cloned.1.call-done
  670.1 20.4 reduce-scatter.5.cloned.1.call-done
  695.6 21.4 all-gather.13.cloned.1.call-done
  724.4 11.7 fusion.288
  744.8 11.8 reduce-scatter.7.cloned.1.call-done
  777.1 1182.9 %while.62 = (s32[]{:T(128)}, bf16[256,1024]{1,0:T(8,128)(2,1)S(1)}, f32[1024,1536]{1,0:T(8,128)}, f32[2,512]{1,0:T(2,128)S(1)}, f32[512,1024]{1,0:T(8,128)}, /*i...) while((s32[]{:T(128)}, bf16[256,1024]{1,0:T(8,128)(2,1)S(1)}, ...), condition=%wide.region_33.34_spmd.clone, body=%wide.region_10.33_spmd.clone.sunk | while | flops 24897421312 | bytes 533102848 | solution.py:383
  807.8 17.2 all-gather.15.cloned.1.call-done
  831.8 16.1 all-gather.17.cloned.1.call-done
  941.1 13.3 fusion.329
  954.5 14.6 convert_reduce_fusion.7
  983.5 12.3 reduce-scatter.11.cloned.1.call-done
  1000.9 11.7 collective-permute-done.1
  1041.2 17.2 all-gather.15.cloned.1.call-done
  1065.2 16.1 all-gather.17.cloned.1.call-done
  1126.6 12.3 bitcast_add_fusion.5
  1149.1 12.4 select_add_fusion.20
  1177.0 13.0 fusion.329
  1190.0 14.6 convert_reduce_fusion.7
  1236.5 11.7 collective-permute-done.1
  1276.8 17.2 all-gather.15.cloned.1.call-done
  1300.8 16.1 all-gather.17.cloned.1.call-done
  1362.5 12.3 bitcast_add_fusion.5
  1384.7 12.5 select_add_fusion.20
  1412.9 13.1 fusion.329
  1425.9 14.6 convert_reduce_fusion.7
  1472.4 11.7 collective-permute-done.1
  1512.7 17.2 all-gather.15.cloned.1.call-done
  1536.7 16.1 all-gather.17.cloned.1.call-done
  1598.4 12.3 bitcast_add_fusion.5
  1620.7 12.5 select_add_fusion.20
  1648.8 13.1 fusion.329
  1661.9 14.6 convert_reduce_fusion.7
  1708.3 11.7 collective-permute-done.1
  1748.9 17.1 all-gather.15.cloned.1.call-done
  1772.8 16.0 all-gather.17.cloned.1.call-done
  1834.0 12.3 bitcast_add_fusion.5
  1856.2 12.5 select_add_fusion.20
  1884.4 13.3 fusion.329
  1897.7 14.6 convert_reduce_fusion.7
  1966.7 13.9 copy.51
  1986.7 29.0 %all-reduce.7 = (bf16[1,2,512]{2,1,0:T(2,128)(2,1)S(1)}, bf16[1,2,2048]{2,1,0:T(2,128)(2,1)S(1)}) all-reduce(bf16[1,2,512]{2,1,0:T(2,128)(2,1)S(1)} %convert_bitcast_fusion.4, bf16[1,2,2048]{2,1,0:T(2,128)(2,1)S(1)} %convert_bitcast_fusion.3), channel_id=1, replica_groups=mesh['section'=2,'tensor'=2,'dp'=8] {'dp'}, use_global_device_ids=true, to_apply=%region_35.36 | all-reduce | flops 5120 | bytes 20480 | tf_op jit(solution)/shard_map/psum | solution.py:400
  2016.9 61.4 %all-reduce.6 = (f32[1,1024]{1,0:T(1,128)}, f32[1,2,1024]{2,1,0:T(2,128)}, f32[1,2,1024]{2,1,0:T(2,128)}, f32[1,1024]{1,0:T(1,128)}) all-reduce(f32[1,1024]{1,0:T(1,128)S(1)} %bitcast.569, f32[1,2,1024]{2,1,0:T(2,128)S(1)} %bitcast.567, ...), channel_id=1, replica_groups=mesh['section'=2,'tensor'=2,'dp'=8] {'tensor','dp'}, use_global_device_ids=true, to_apply=%region_37.38 | all-reduce | flops 6144 | bytes 49152 | tf_op jit(solution)/shard_map/psum | solution.py:406
  2078.2 244.1 %all-reduce.11.cloned.1.call-done = (bf16[1,1024,3,512]{1,3,2,0:T(8,128)(2,1)}, bf16[1,512,1024]{2,1,0:T(8,128)(2,1)}, bf16[1,2,1024,2048]{3,2,1,0:T(8,128)(2,1)}, bf16[1,1024,2048]{2,1,0:T(8,128)(2,1)}) async-done(((bf16[1,1024,3,512]{1,3,2,0:T(8,128)(2,1)}, bf16[1,512,1024]{2,1,0:T(8,128)(2,1)}, bf16[1,2,1024,2048]{3,2,1,0:T(8,128)(2,1)}, bf16[1,1024,2048]{2,1,0:T(8,128)(2,1)}), ...) | async-done | bytes 16777232 | tf_op jit(solution)/shard_map/psum | solution.py:399
  2329.4 11.8 broadcast_in_dim.384
  (903 shorter events, 1083.7 us)
Async XLA Ops:
  23.6 26.4 %all-gather.11.cloned.1.call-start = ((), (), s32[]{:S(2)}) async-start(), calls=%async_computation.5 | async-start | bytes 1572864 | tf_op jit(solution)/shard_map/while/body/eval_jaxpr/all_gather | solution.py:156
  24.7 66.7 %reduce-scatter.5.cloned.1.call-start = ((), (), s32[]{:S(2)}) async-start(), calls=%async_computation.6 | async-start | bytes 1572864 | tf_op jit(solution)/shard_map/while/body/eval_jaxpr/reduce_scatter | solution.py:172
  70.9 47.0 %all-gather.13.cloned.1.call-start = ((), (), s32[]{:S(2)}) async-start(), calls=%async_computation.7 | async-start | bytes 1572864 | tf_op jit(solution)/shard_map/while/body/eval_jaxpr/all_gather | solution.py:187
  96.4 61.0 %reduce-scatter.7.cloned.1.call-start = ((), (), s32[]{:S(2)}) async-start(), calls=%async_computation.8 | async-start | bytes 1572864 | tf_op jit(solution)/shard_map/while/body/eval_jaxpr/reduce_scatter | solution.py:198
  160.7 14.5 collective-permute-start
  175.3 24.4 %all-gather.11.cloned.1.call-start = ((), (), s32[]{:S(2)}) async-start(), calls=%async_computation.5 | async-start | bytes 1572864 | tf_op jit(solution)/shard_map/while/body/eval_jaxpr/all_gather | solution.py:156
  176.3 64.7 %reduce-scatter.5.cloned.1.call-start = ((), (), s32[]{:S(2)}) async-start(), calls=%async_computation.6 | async-start | bytes 1572864 | tf_op jit(solution)/shard_map/while/body/eval_jaxpr/reduce_scatter | solution.py:172
  220.5 47.0 %all-gather.13.cloned.1.call-start = ((), (), s32[]{:S(2)}) async-start(), calls=%async_computation.7 | async-start | bytes 1572864 | tf_op jit(solution)/shard_map/while/body/eval_jaxpr/all_gather | solution.py:187
  246.1 61.0 %reduce-scatter.7.cloned.1.call-start = ((), (), s32[]{:S(2)}) async-start(), calls=%async_computation.8 | async-start | bytes 1572864 | tf_op jit(solution)/shard_map/while/body/eval_jaxpr/reduce_scatter | solution.py:198
  310.4 14.5 collective-permute-start
  324.9 24.7 %all-gather.11.cloned.1.call-start = ((), (), s32[]{:S(2)}) async-start(), calls=%async_computation.5 | async-start | bytes 1572864 | tf_op jit(solution)/shard_map/while/body/eval_jaxpr/all_gather | solution.py:156
  325.9 65.0 %reduce-scatter.5.cloned.1.call-start = ((), (), s32[]{:S(2)}) async-start(), calls=%async_computation.6 | async-start | bytes 1572864 | tf_op jit(solution)/shard_map/while/body/eval_jaxpr/reduce_scatter | solution.py:172
  370.5 47.0 %all-gather.13.cloned.1.call-start = ((), (), s32[]{:S(2)}) async-start(), calls=%async_computation.7 | async-start | bytes 1572864 | tf_op jit(solution)/shard_map/while/body/eval_jaxpr/all_gather | solution.py:187
  396.0 61.0 %reduce-scatter.7.cloned.1.call-start = ((), (), s32[]{:S(2)}) async-start(), calls=%async_computation.8 | async-start | bytes 1572864 | tf_op jit(solution)/shard_map/while/body/eval_jaxpr/reduce_scatter | solution.py:198
  460.3 14.5 collective-permute-start
  474.8 24.7 %all-gather.11.cloned.1.call-start = ((), (), s32[]{:S(2)}) async-start(), calls=%async_computation.5 | async-start | bytes 1572864 | tf_op jit(solution)/shard_map/while/body/eval_jaxpr/all_gather | solution.py:156
  475.8 65.0 %reduce-scatter.5.cloned.1.call-start = ((), (), s32[]{:S(2)}) async-start(), calls=%async_computation.6 | async-start | bytes 1572864 | tf_op jit(solution)/shard_map/while/body/eval_jaxpr/reduce_scatter | solution.py:172
  520.4 47.0 %all-gather.13.cloned.1.call-start = ((), (), s32[]{:S(2)}) async-start(), calls=%async_computation.7 | async-start | bytes 1572864 | tf_op jit(solution)/shard_map/while/body/eval_jaxpr/all_gather | solution.py:187
  545.9 61.0 %reduce-scatter.7.cloned.1.call-start = ((), (), s32[]{:S(2)}) async-start(), calls=%async_computation.8 | async-start | bytes 1572864 | tf_op jit(solution)/shard_map/while/body/eval_jaxpr/reduce_scatter | solution.py:198
  610.2 14.5 collective-permute-start
  624.8 24.4 %all-gather.11.cloned.1.call-start = ((), (), s32[]{:S(2)}) async-start(), calls=%async_computation.5 | async-start | bytes 1572864 | tf_op jit(solution)/shard_map/while/body/eval_jaxpr/all_gather | solution.py:156
  625.8 64.7 %reduce-scatter.5.cloned.1.call-start = ((), (), s32[]{:S(2)}) async-start(), calls=%async_computation.6 | async-start | bytes 1572864 | tf_op jit(solution)/shard_map/while/body/eval_jaxpr/reduce_scatter | solution.py:172
  670.0 47.0 %all-gather.13.cloned.1.call-start = ((), (), s32[]{:S(2)}) async-start(), calls=%async_computation.7 | async-start | bytes 1572864 | tf_op jit(solution)/shard_map/while/body/eval_jaxpr/all_gather | solution.py:187
  695.6 61.0 %reduce-scatter.7.cloned.1.call-start = ((), (), s32[]{:S(2)}) async-start(), calls=%async_computation.8 | async-start | bytes 1572864 | tf_op jit(solution)/shard_map/while/body/eval_jaxpr/reduce_scatter | solution.py:198
  759.9 14.5 collective-permute-start
  777.4 24.7 %all-gather.21.cloned.1.call-start = ((), (), s32[]{:S(2)}) async-start(), calls=%async_computation.13 | async-start | bytes 1572864 | tf_op jit(solution)/shard_map/while/body/eval_jaxpr/all_gather | solution.py:156
  779.6 45.4 %all-gather.15.cloned.1.call-start = ((), (), s32[]{:S(2)}) async-start(), calls=%async_computation.9 | async-start | bytes 1572864 | tf_op jit(solution)/shard_map/while/body/eval_jaxpr/all_gather | solution.py:207
  791.1 56.9 %all-gather.17.cloned.1.call-start = ((), (), s32[]{:S(2)}) async-start(), calls=%async_computation.10 | async-start | bytes 1572864 | tf_op jit(solution)/shard_map/while/body/eval_jaxpr/all_gather | solution.py:187
  791.8 111.2 %reduce-scatter.9.cloned.1.call-start = ((), (), s32[]{:S(2)}) async-start(), calls=%async_computation.11 | async-start | bytes 1572864 | tf_op jit(solution)/shard_map/while/body/eval_jaxpr/reduce_scatter | solution.py:217
  878.1 51.4 %all-gather.19.cloned.1.call-start = ((), (), s32[]{:S(2)}) async-start(), calls=%async_computation.12 | async-start | bytes 1572864 | tf_op jit(solution)/shard_map/while/body/eval_jaxpr/all_gather | solution.py:253
  908.0 87.8 %reduce-scatter.11.cloned.1.call-start = ((), (), s32[]{:S(2)}) async-start(), calls=%async_computation.14 | async-start | bytes 1572864 | tf_op jit(solution)/shard_map/while/body/eval_jaxpr/reduce_scatter | solution.py:275
  997.0 15.6 collective-permute-start.1
  1012.7 22.8 all-gather.21.cloned.1.call-start
  1015.0 43.4 %all-gather.15.cloned.1.call-start = ((), (), s32[]{:S(2)}) async-start(), calls=%async_computation.9 | async-start | bytes 1572864 | tf_op jit(solution)/shard_map/while/body/eval_jaxpr/all_gather | solution.py:207
  1026.4 54.9 %all-gather.17.cloned.1.call-start = ((), (), s32[]{:S(2)}) async-start(), calls=%async_computation.10 | async-start | bytes 1572864 | tf_op jit(solution)/shard_map/while/body/eval_jaxpr/all_gather | solution.py:187
  1027.1 111.8 %reduce-scatter.9.cloned.1.call-start = ((), (), s32[]{:S(2)}) async-start(), calls=%async_computation.11 | async-start | bytes 1572864 | tf_op jit(solution)/shard_map/while/body/eval_jaxpr/reduce_scatter | solution.py:217
  1039.7 72.1 %copy-start.21 = (bf16[512,1,512]{0,2,1:T(8,128)(2,1)}, bf16[512,1,512]{0,2,1:T(8,128)(2,1)S(1)}, u32[]{:S(2)}) copy-start(bf16[512,1,512]{0,2,1:T(8,128)(2,1)S(1)} %slice.300) | copy-start | bytes 1572868 | tf_op jit(solution)/shard_map/while
  1111.5 53.8 %all-gather.19.cloned.1.call-start = ((), (), s32[]{:S(2)}) async-start(), calls=%async_computation.12 | async-start | bytes 1572864 | tf_op jit(solution)/shard_map/while/body/eval_jaxpr/all_gather | solution.py:253
  1143.8 87.5 %reduce-scatter.11.cloned.1.call-start = ((), (), s32[]{:S(2)}) async-start(), calls=%async_computation.14 | async-start | bytes 1572864 | tf_op jit(solution)/shard_map/while/body/eval_jaxpr/reduce_scatter | solution.py:275
  1232.6 15.6 collective-permute-start.1
  1248.4 22.8 all-gather.21.cloned.1.call-start
  1250.6 43.4 %all-gather.15.cloned.1.call-start = ((), (), s32[]{:S(2)}) async-start(), calls=%async_computation.9 | async-start | bytes 1572864 | tf_op jit(solution)/shard_map/while/body/eval_jaxpr/all_gather | solution.py:207
  1262.0 54.9 %all-gather.17.cloned.1.call-start = ((), (), s32[]{:S(2)}) async-start(), calls=%async_computation.10 | async-start | bytes 1572864 | tf_op jit(solution)/shard_map/while/body/eval_jaxpr/all_gather | solution.py:187
  1262.7 112.0 %reduce-scatter.9.cloned.1.call-start = ((), (), s32[]{:S(2)}) async-start(), calls=%async_computation.11 | async-start | bytes 1572864 | tf_op jit(solution)/shard_map/while/body/eval_jaxpr/reduce_scatter | solution.py:217
  1275.3 72.3 %copy-start.21 = (bf16[512,1,512]{0,2,1:T(8,128)(2,1)}, bf16[512,1,512]{0,2,1:T(8,128)(2,1)S(1)}, u32[]{:S(2)}) copy-start(bf16[512,1,512]{0,2,1:T(8,128)(2,1)S(1)} %slice.300) | copy-start | bytes 1572868 | tf_op jit(solution)/shard_map/while
  1347.1 54.0 %all-gather.19.cloned.1.call-start = ((), (), s32[]{:S(2)}) async-start(), calls=%async_computation.12 | async-start | bytes 1572864 | tf_op jit(solution)/shard_map/while/body/eval_jaxpr/all_gather | solution.py:253
  1379.7 87.5 %reduce-scatter.11.cloned.1.call-start = ((), (), s32[]{:S(2)}) async-start(), calls=%async_computation.14 | async-start | bytes 1572864 | tf_op jit(solution)/shard_map/while/body/eval_jaxpr/reduce_scatter | solution.py:275
  1468.5 15.6 collective-permute-start.1
  1484.3 22.8 all-gather.21.cloned.1.call-start
  1486.5 43.4 %all-gather.15.cloned.1.call-start = ((), (), s32[]{:S(2)}) async-start(), calls=%async_computation.9 | async-start | bytes 1572864 | tf_op jit(solution)/shard_map/while/body/eval_jaxpr/all_gather | solution.py:207
  1497.9 54.9 %all-gather.17.cloned.1.call-start = ((), (), s32[]{:S(2)}) async-start(), calls=%async_computation.10 | async-start | bytes 1572864 | tf_op jit(solution)/shard_map/while/body/eval_jaxpr/all_gather | solution.py:187
  1498.7 112.0 %reduce-scatter.9.cloned.1.call-start = ((), (), s32[]{:S(2)}) async-start(), calls=%async_computation.11 | async-start | bytes 1572864 | tf_op jit(solution)/shard_map/while/body/eval_jaxpr/reduce_scatter | solution.py:217
  1511.2 72.4 %copy-start.21 = (bf16[512,1,512]{0,2,1:T(8,128)(2,1)}, bf16[512,1,512]{0,2,1:T(8,128)(2,1)S(1)}, u32[]{:S(2)}) copy-start(bf16[512,1,512]{0,2,1:T(8,128)(2,1)S(1)} %slice.300) | copy-start | bytes 1572868 | tf_op jit(solution)/shard_map/while
  1583.3 53.8 %all-gather.19.cloned.1.call-start = ((), (), s32[]{:S(2)}) async-start(), calls=%async_computation.12 | async-start | bytes 1572864 | tf_op jit(solution)/shard_map/while/body/eval_jaxpr/all_gather | solution.py:253
  1615.6 87.6 %reduce-scatter.11.cloned.1.call-start = ((), (), s32[]{:S(2)}) async-start(), calls=%async_computation.14 | async-start | bytes 1572864 | tf_op jit(solution)/shard_map/while/body/eval_jaxpr/reduce_scatter | solution.py:275
  1704.5 15.6 collective-permute-start.1
  1720.5 22.8 all-gather.21.cloned.1.call-start
  1722.7 43.3 %all-gather.15.cloned.1.call-start = ((), (), s32[]{:S(2)}) async-start(), calls=%async_computation.9 | async-start | bytes 1572864 | tf_op jit(solution)/shard_map/while/body/eval_jaxpr/all_gather | solution.py:207
  1734.1 54.6 %all-gather.17.cloned.1.call-start = ((), (), s32[]{:S(2)}) async-start(), calls=%async_computation.10 | async-start | bytes 1572864 | tf_op jit(solution)/shard_map/while/body/eval_jaxpr/all_gather | solution.py:187
  1734.7 111.6 %reduce-scatter.9.cloned.1.call-start = ((), (), s32[]{:S(2)}) async-start(), calls=%async_computation.11 | async-start | bytes 1572864 | tf_op jit(solution)/shard_map/while/body/eval_jaxpr/reduce_scatter | solution.py:217
  1818.9 53.8 %all-gather.19.cloned.1.call-start = ((), (), s32[]{:S(2)}) async-start(), calls=%async_computation.12 | async-start | bytes 1572864 | tf_op jit(solution)/shard_map/while/body/eval_jaxpr/all_gather | solution.py:253
  1851.2 87.8 %reduce-scatter.11.cloned.1.call-start = ((), (), s32[]{:S(2)}) async-start(), calls=%async_computation.14 | async-start | bytes 1572864 | tf_op jit(solution)/shard_map/while/body/eval_jaxpr/reduce_scatter | solution.py:275
  1940.3 15.6 collective-permute-start.1
  1960.0 362.4 %all-reduce.11.cloned.1.call-start = ((), (), s32[]{:S(2)}) async-start(), calls=%async_computation.4 | async-start | bytes 33554432 | tf_op jit(solution)/shard_map/psum | solution.py:399
  (134 other events, 952.6 us)
Sparse Core Ops, SparseCore 0:
  26.0 23.9 all-gather.10
  71.0 20.3 reduce-scatter.4
  96.6 21.2 all-gather.12
  137.1 20.3 reduce-scatter.6
  177.3 22.3 all-gather.10
  220.7 20.3 reduce-scatter.4
  246.2 21.2 all-gather.12
  286.8 20.3 reduce-scatter.6
  327.3 22.3 all-gather.10
  370.6 20.3 reduce-scatter.4
  396.1 21.2 all-gather.12
  436.7 20.3 reduce-scatter.6
  477.2 22.3 all-gather.10
  520.5 20.3 reduce-scatter.4
  546.1 21.2 all-gather.12
  586.6 20.3 reduce-scatter.6
  626.8 22.3 all-gather.10
  670.2 20.3 reduce-scatter.4
  695.7 21.2 all-gather.12
  736.3 20.3 reduce-scatter.6
  779.8 22.3 all-gather.20
  803.7 21.2 all-gather.14
  826.6 21.2 all-gather.16
  878.2 20.3 reduce-scatter.8
  908.1 21.2 all-gather.18
  975.4 20.3 reduce-scatter.10
  1015.1 20.3 all-gather.20
  1037.0 21.2 all-gather.14
  1059.9 21.2 all-gather.16
  1111.6 20.3 reduce-scatter.8
  1144.0 21.2 all-gather.18
  1211.0 20.3 reduce-scatter.10
  1250.7 20.3 all-gather.20
  1272.7 21.2 all-gather.14
  1295.5 21.2 all-gather.16
  1347.2 20.3 reduce-scatter.8
  1379.8 21.2 all-gather.18
  1446.9 20.3 reduce-scatter.10
  1486.6 20.3 all-gather.20
  1508.6 21.2 all-gather.14
  1531.5 21.2 all-gather.16
  1583.5 20.3 reduce-scatter.8
  1615.8 21.2 all-gather.18
  1682.9 20.3 reduce-scatter.10
  1722.8 20.3 all-gather.20
  1744.6 21.2 all-gather.14
  1767.4 21.2 all-gather.16
  1819.0 20.3 reduce-scatter.8
  1851.3 21.2 all-gather.18
  1918.6 20.3 reduce-scatter.10
Sparse Core Ops, SparseCore 1:
  1986.7 335.6 all-reduce.10
where the time goes:
time: 2370 us; the launch traced here: 2350 us
  waiting for transfers between devices  987 us (42%)
  matrix products  793 us (33%)
  other arithmetic  287 us (12%)
  local copies, waits for them, and re-layouts  143 us (6%)
  blocking collectives  90.4 us (4%)
  starting transfers between devices  28.1 us (1%)
    psum x1, waiting for transfers between devices, on_device(): lax.psum(qkv_total.astype(jnp.bfloat16), 'dp').astype(jnp.float32)  244 us
    all_gather x10, waiting for transfers between devices, gather_normed(): lax.all_gather(normed.astype(jnp.bfloat16), 'tensor', axis=0, tiled=True)  187 us
    all_gather x10, waiting for transfers between devices, gather_inputs(): lax.all_gather(values.astype(jnp.bfloat16), 'tensor', axis=0, tiled=True)  134 us
    ppermute x10, waiting for transfers between devices, shifted(): lax.ppermute(value, axis, [(source, source + steps) for source in range(f...  103 us
    reduce_scatter x5, waiting for transfers between devices, attention_forward(): lax.psum_scatter(term(jnp.int32(0), shard_rows * lax.axis_size('tensor'))...  102 us
    all_gather x5, waiting for transfers between devices, ffn_backward(): lax.all_gather(grad_lowered.astype(jnp.bfloat16), 'tensor', axis=0, tiled...  85.9 us
    sub x10, matrix products, attention_core(): weights = jax.nn.softmax(scores, axis=-1)  85.7 us
    dot_general x5, matrix products, attention_back(): jnp.einsum('hqk,khd->qhd', grad_scores, key, preferred_element_type=jnp.f...  73 us
  transfers between devices with their start and end apart: 61, of which 56 were waited for; matrix products, arithmetic and copies ran while one was open for 20% of the time, Pallas kernels for 0%

commit v1 on v0

--- a/solution.py
+++ b/solution.py
@@ -1,15 +1,511 @@
+import functools
 import math
 
 import jax
 import jax.numpy as jnp
 from jax import lax
+from jax.experimental import pallas as pl
+from jax.experimental.pallas import tpu as pltpu
 from jax.sharding import PartitionSpec as P
 
 H = 16
 HD = 64
-
-
 EPS = 1e-05
+BF = jnp.bfloat16
+F32 = jnp.float32
+VMEM_LIMIT = 62 * 1024 * 1024
+ANY = pl.BlockSpec(memory_space=pl.ANY)
+NN = (((1,), (0,)), ((), ()))
+NT = (((1,), (1,)), ((), ()))
+TN = (((0,), (0,)), ((), ()))
+
+
+def dot(a, b, dims=NN):
+    return lax.dot_general(a, b, dims, preferred_element_type=F32)
+
+
+def call(kernel, grid, inputs, outputs, scratch, meta, chain, deps, name, flops, nbytes):
+    args = [a for a, _ in inputs]
+    specs = [s for _, s in inputs]
+    n_in = len(args)
+    aliases = {}
+    if chain is not None:
+        chained = [index for index, item in enumerate(outputs) if item[3]]
+        for buffer, index in zip(chain, chained):
+            aliases[1 + len(args)] = index
+            args.append(buffer)
+            specs.append(ANY)
+    for item in deps:
+        args.append(item)
+        specs.append(ANY)
+    n_args = len(args)
+
+    def body(meta_ref, *refs):
+        kernel(meta_ref, refs[:n_in], refs[n_args : n_args + len(outputs)], refs[n_args + len(outputs) :])
+
+    return pl.pallas_call(
+        body,
+        grid_spec=pltpu.PrefetchScalarGridSpec(
+            num_scalar_prefetch=1,
+            grid=grid,
+            in_specs=specs,
+            out_specs=[o[2] for o in outputs],
+            scratch_shapes=scratch,
+        ),
+        out_shape=[jax.ShapeDtypeStruct(o[0], o[1]) for o in outputs],
+        input_output_aliases=aliases,
+        compiler_params=pltpu.CompilerParams(
+            dimension_semantics=("arbitrary",) * len(grid), vmem_limit_bytes=VMEM_LIMIT
+        ),
+        cost_estimate=pl.CostEstimate(flops=flops, bytes_accessed=nbytes, transcendentals=0),
+        name=name,
+    )(meta, *args)
+
+
+def own_map(count, make):
+    return lambda i, meta: make(jnp.minimum(i, count - 1) * meta[1])
+
+
+def oth_map(count, make):
+    return lambda i, meta: make(jnp.maximum(i - count, 0) * meta[1])
+
+
+def tile_map(make):
+    return lambda i, meta: make(meta[0], i * meta[1])
+
+
+def fixed(shape):
+    zeros = (0,) * len(shape)
+    return pl.BlockSpec(shape, lambda i, meta: zeros, pipeline_mode=pl.Buffered(1))
+
+
+def fill_distance(dist_ref, length):
+    rows = dist_ref.shape[0]
+    keys = lax.broadcasted_iota(jnp.int32, (rows, rows), 0)
+    places = lax.broadcasted_iota(jnp.int32, (rows, rows), 1)
+    distance = jnp.abs(keys - places).astype(F32)
+    dist_ref[...] = jnp.where(keys < length, distance, 1e12)
+
+
+def attention_forward(x, w_own, w_oth, bias, slopes, meta, chain, deps, slots):
+    rows, width = x.shape
+    local = w_own.shape[2]
+    cw = 256
+    per = cw // HD
+    count = local // cw
+    steps = 2 * count
+    total = 2 * local
+
+    def kernel(meta_ref, ins, outs, scratch):
+        x_ref, own_ref, oth_ref, bias_ref, slope_ref = ins
+        q_ref, k_ref, v_ref, mixed_ref, lse_ref = outs
+        (dist_ref,) = scratch
+        i = pl.program_id(0)
+
+        def work(w_ref):
+            values = x_ref[...]
+            b = bias_ref[...]
+            q_ref[0] = (dot(values, w_ref[0]) + b[0:1]).astype(BF)
+            k_ref[0] = dot(values, w_ref[1]).astype(BF)
+            v_ref[0] = (dot(values, w_ref[2]) + b[1:2]).astype(BF)
+            for head in range(per):
+                cols = slice(head * HD, (head + 1) * HD)
+                query = q_ref[0, :, cols] * BF(1.0 / math.sqrt(HD))
+                scores = dot(k_ref[0, :, cols], query, NT)
+                scores = scores - dist_ref[...] * slope_ref[i * per + head]
+                top = jnp.max(scores, axis=0, keepdims=True)
+                weights = jnp.exp(scores - top)
+                total_weight = jnp.sum(weights, axis=0, keepdims=True)
+                low = (weights * (1.0 / total_weight)).astype(BF)
+                mixed_ref[0, :, cols] = dot(low, v_ref[0, :, cols], TN).astype(BF)
+                lse_ref[0, 0, head : head + 1, :] = top + jnp.log(total_weight)
+
+        @pl.when(meta_ref[1] == 1)
+        def _():
+            @pl.when(i == 0)
+            def _():
+                fill_distance(dist_ref, meta_ref[2])
+
+            @pl.when(i < count)
+            def _():
+                work(own_ref)
+
+            @pl.when(i >= count)
+            def _():
+                work(oth_ref)
+
+    wide = pl.BlockSpec((1, rows, cw), tile_map(lambda s, i: (s, 0, i)))
+    return call(
+        kernel,
+        (steps,),
+        [
+            (x, fixed((rows, width))),
+            (w_own, pl.BlockSpec((3, width, cw), own_map(count, lambda i: (0, 0, i)))),
+            (w_oth, pl.BlockSpec((3, width, cw), oth_map(count, lambda i: (0, 0, i)))),
+            (bias, pl.BlockSpec((2, cw), lambda i, meta: (0, i * meta[1]))),
+            (slopes, pl.BlockSpec(memory_space=pltpu.SMEM)),
+        ],
+        [((slots, rows, total), BF, wide, True)] * 4
+        + [
+            (
+                (slots, steps, 8, rows),
+                F32,
+                pl.BlockSpec((1, 1, 8, rows), tile_map(lambda s, i: (s, i, 0, 0))),
+                True,
+            )
+        ],
+        [pltpu.VMEM((rows, rows), F32)],
+        meta,
+        chain,
+        deps,
+        "attention_forward",
+        2 * rows * width * 3 * total + 4 * rows * rows * total,
+        12 << 20,
+    )
+
+
+def normalize(v):
+    mean = jnp.mean(v, axis=1, keepdims=True)
+    centred = v - mean
+    rstd = lax.rsqrt(jnp.mean(centred * centred, axis=1, keepdims=True) + EPS)
+    return centred * rstd, rstd
+
+
+def ffn_forward(x, mixed, o_own, o_oth, up_own, up_oth, down_own, down_oth, vecs, up_bias, meta, chain, deps, slots):
+    rows, width = x.shape
+    local = o_own.shape[0]
+    units = up_own.shape[2]
+    ft = min(512, units)
+    count = units // ft
+    steps = 2 * count
+
+    def kernel(meta_ref, ins, outs, scratch):
+        x_ref, mixed_ref, o_own_ref, o_oth_ref, u_own_ref, u_oth_ref, d_own_ref, d_oth_ref, vec_ref, ub_ref = ins
+        a_ref, b_ref, h_ref, n_ref, u1_ref, u2_ref, r1_ref, r2_ref, y_ref = outs
+        normed_ref, acc_ref = scratch
+        i = pl.program_id(0)
+        vec = vec_ref[...]
+
+        def work(up_ref, down_ref):
+            for part in range(2):
+                rs = slice(part * rows // 2, (part + 1) * rows // 2)
+                low = n_ref[0, rs, :]
+                gate = dot(low, up_ref[0]) + ub_ref[0:1]
+                lift = dot(low, up_ref[1]) + ub_ref[1:2]
+                cdf = 0.5 * lax.erf(gate * (1.0 / math.sqrt(2.0))) + 0.5
+                act = gate * cdf
+                slope = cdf + gate * (jnp.exp(gate * gate * -0.5) * (1.0 / math.sqrt(2.0 * math.pi)))
+                a_ref[0, rs, :] = act.astype(BF)
+                b_ref[0, rs, :] = (lift * slope).astype(BF)
+                hidden = (act * lift).astype(BF)
+                h_ref[0, rs, :] = hidden
+                acc_ref[rs, :] += dot(hidden, down_ref[...], NT)
+
+        @pl.when(meta_ref[1] == 1)
+        def _():
+            @pl.when(i == 0)
+            def _():
+                attended = dot(mixed_ref[0, :, :local], o_own_ref[...])
+                attended += dot(mixed_ref[0, :, local:], o_oth_ref[...])
+                u, rstd = normalize(x_ref[...].astype(F32) + attended + vec[0:1])
+                normed = u * vec[1:2] + vec[2:3]
+                normed_ref[...] = normed
+                n_ref[0] = normed.astype(BF)
+                u1_ref[0] = u.astype(BF)
+                r1_ref[0] = jnp.broadcast_to(rstd, (rows, 128))
+                acc_ref[...] = jnp.zeros_like(acc_ref)
+
+            @pl.when(i < count)
+            def _():
+                work(u_own_ref, d_own_ref)
+
+            @pl.when(i >= count)
+            def _():
+                work(u_oth_ref, d_oth_ref)
+
+            @pl.when(i == steps - 1)
+            def _():
+                u, rstd = normalize(normed_ref[...] + acc_ref[...] + vec[3:4])
+                u2_ref[0] = u.astype(BF)
+                r2_ref[0] = jnp.broadcast_to(rstd, (rows, 128))
+                y_ref[...] = (u * vec[4:5] + vec[5:6]).astype(BF)
+
+    tile = pl.BlockSpec((1, rows, ft), tile_map(lambda s, i: (s, 0, i)))
+    whole = pl.BlockSpec((1, rows, width), lambda i, meta: (meta[0], 0, 0))
+    stat = pl.BlockSpec((1, rows, 128), lambda i, meta: (meta[0], 0, 0))
+    return call(
+        kernel,
+        (steps,),
+        [
+            (x, fixed((rows, width))),
+            (mixed, pl.BlockSpec((1, rows, 2 * local), lambda i, meta: (meta[0], 0, 0), pipeline_mode=pl.Buffered(1))),
+            (o_own, fixed((local, width))),
+            (o_oth, fixed((local, width))),
+            (up_own, pl.BlockSpec((2, width, ft), own_map(count, lambda i: (0, 0, i)))),
+            (up_oth, pl.BlockSpec((2, width, ft), oth_map(count, lambda i: (0, 0, i)))),
+            (down_own, pl.BlockSpec((width, ft), own_map(count, lambda i: (0, i)))),
+            (down_oth, pl.BlockSpec((width, ft), oth_map(count, lambda i: (0, i)))),
+            (vecs, fixed((8, width))),
+            (up_bias, pl.BlockSpec((2, ft), lambda i, meta: (0, i * meta[1]))),
+        ],
+        [((slots, rows, 2 * units), BF, tile, True)] * 3
+        + [((slots, rows, width), BF, whole, True)] * 3
+        + [((slots, rows, 128), F32, stat, True)] * 2
+        + [((rows, width), BF, pl.BlockSpec((rows, width), lambda i, meta: (0, 0)), False)],
+        [pltpu.VMEM((rows, width), F32), pltpu.VMEM((rows, width), F32)],
+        meta,
+        chain,
+        deps,
+        "ffn_forward",
+        2 * rows * width * (6 * units + 2 * local),
+        45 << 20,
+    )
+
+
+def ffn_backward(grad, u2, r2, u1, r1, act, slope, up_own, up_oth, down_own, down_oth, vecs, meta, chain, deps, slots):
+    rows, width = grad.shape
+    units = up_own.shape[2]
+    ft = min(512, units)
+    count = units // ft
+    steps = 2 * count
+
+    def kernel(meta_ref, ins, outs, scratch):
+        g_ref, u2_ref, r2_ref, u1_ref, r1_ref, a_ref, b_ref, u_own_ref, u_oth_ref, d_own_ref, d_oth_ref, vec_ref = ins
+        gg0_ref, gg1_ref, gl_ref, ga_ref, gaf_ref, sums_ref, ub_ref = outs
+        (acc_ref,) = scratch
+        i = pl.program_id(0)
+        vec = vec_ref[...]
+
+        def norm_back(grad_z, u, rstd, gain):
+            t = grad_z * gain
+            return rstd * (
+                t - jnp.mean(t, axis=1, keepdims=True) - u * jnp.mean(t * u, axis=1, keepdims=True)
+            )
+
+        def work(up_ref, down_ref):
+            s0 = jnp.zeros((1, ft), F32)
+            s1 = jnp.zeros((1, ft), F32)
+            for part in range(2):
+                rs = slice(part * rows // 2, (part + 1) * rows // 2)
+                gh = dot(gl_ref[0, rs, :], down_ref[...])
+                g0 = (gh * b_ref[0, rs, :].astype(F32)).astype(BF)
+                g1 = (gh * a_ref[0, rs, :].astype(F32)).astype(BF)
+                gg0_ref[0, rs, :] = g0
+                gg1_ref[0, rs, :] = g1
+                s0 += jnp.sum(g0.astype(F32), axis=0, keepdims=True)
+                s1 += jnp.sum(g1.astype(F32), axis=0, keepdims=True)
+                acc_ref[rs, :] += dot(g0, up_ref[0], NT) + dot(g1, up_ref[1], NT)
+            ub_ref[...] = jnp.concatenate([s0, s1, jnp.zeros((6, ft), F32)], axis=0)
+
+        @pl.when(meta_ref[1] == 1)
+        def _():
+            @pl.when(i == 0)
+            def _():
+                grad_y = g_ref[...].astype(F32)
+                u = u2_ref[0].astype(F32)
+                grad_c = norm_back(grad_y, u, r2_ref[0, :, 0:1], vec[4:5])
+                acc_ref[...] = grad_c
+                gl_ref[0] = grad_c.astype(BF)
+                sums_ref[0:1, :] = jnp.sum(grad_y * u, axis=0, keepdims=True)
+                sums_ref[1:2, :] = jnp.sum(grad_y, axis=0, keepdims=True)
+                sums_ref[2:3, :] = jnp.sum(grad_c, axis=0, keepdims=True)
+
+            @pl.when(i < count)
+            def _():
+                work(u_own_ref, d_own_ref)
+
+            @pl.when(i >= count)
+            def _():
+                work(u_oth_ref, d_oth_ref)
+
+            @pl.when(i == steps - 1)
+            def _():
+                grad_n = acc_ref[...]
+                u = u1_ref[0].astype(F32)
+                grad_a = norm_back(grad_n, u, r1_ref[0, :, 0:1], vec[1:2])
+                ga_ref[0] = grad_a.astype(BF)
+                gaf_ref[...] = grad_a
+                sums_ref[3:4, :] = jnp.sum(grad_n * u, axis=0, keepdims=True)
+                sums_ref[4:5, :] = jnp.sum(grad_n, axis=0, keepdims=True)
+                sums_ref[5:6, :] = jnp.sum(grad_a, axis=0, keepdims=True)
+                sums_ref[6:8, :] = jnp.zeros((2, width), F32)
+
+    tile = pl.BlockSpec((1, rows, ft), tile_map(lambda s, i: (s, 0, i)))
+    whole = pl.BlockSpec((1, rows, width), lambda i, meta: (meta[0], 0, 0))
+    whole1 = pl.BlockSpec((1, rows, width), lambda i, meta: (meta[0], 0, 0), pipeline_mode=pl.Buffered(1))
+    stat = pl.BlockSpec((1, rows, 128), lambda i, meta: (meta[0], 0, 0))
+    return call(
+        kernel,
+        (steps,),
+        [
+            (grad, fixed((rows, width))),
+            (u2, whole1),
+            (r2, stat),
+            (u1, whole1),
+            (r1, stat),
+            (act, tile),
+            (slope, tile),
+            (up_own, pl.BlockSpec((2, width, ft), own_map(count, lambda i: (0, 0, i)))),
+            (up_oth, pl.BlockSpec((2, width, ft), oth_map(count, lambda i: (0, 0, i)))),
+            (down_own, pl.BlockSpec((width, ft), own_map(count, lambda i: (0, i)))),
+            (down_oth, pl.BlockSpec((width, ft), oth_map(count, lambda i: (0, i)))),
+            (vecs, fixed((8, width))),
+        ],
+        [((slots, rows, 2 * units), BF, tile, True)] * 2
+        + [((slots, rows, width), BF, whole, True)] * 2
+        + [
+            ((rows, width), F32, pl.BlockSpec((rows, width), lambda i, meta: (0, 0)), False),
+            ((8, width), F32, pl.BlockSpec((8, width), lambda i, meta: (0, 0)), False),
+            ((8, 2 * units), F32, pl.BlockSpec((8, ft), lambda i, meta: (0, i)), False),
+        ],
+        [pltpu.VMEM((rows, width), F32)],
+        meta,
+        chain,
+        deps,
+        "ffn_backward",
+        2 * rows * width * 6 * units,
+        50 << 20,
+    )
+
+
+def attention_backward(ga, gaf, q, k, v, lse, o_own, o_oth, w_own, w_oth, slopes, meta, chain, deps, slots):
+    rows, width = gaf.shape
+    local = w_own.shape[2]
+    cw = 256
+    per = cw // HD
+    count = local // cw
+    steps = 2 * count
+    total = 2 * local
+
+    def kernel(meta_ref, ins, outs, scratch):
+        ga_ref, gaf_ref, q_ref, k_ref, v_ref, lse_ref, o_own_ref, o_oth_ref, w_own_ref, w_oth_ref, slope_ref = ins
+        gq_ref, gk_ref, gv_ref, gx_ref, gxl_ref, sums_ref = outs
+        dist_ref, gm_ref, acc_ref = scratch
+        i = pl.program_id(0)
+        scale = BF(1.0 / math.sqrt(HD))
+
+        def work(o_ref, w_ref):
+            gm_ref[...] = dot(ga_ref[0], o_ref[...], NT).astype(BF)
+            for head in range(per):
+                cols = slice(head * HD, (head + 1) * HD)
+                query = q_ref[0, :, cols] * scale
+                key = k_ref[0, :, cols]
+                gm = gm_ref[:, cols]
+                scores = dot(key, query, NT)
+                scores = scores - dist_ref[...] * slope_ref[i * per + head]
+                weights = jnp.exp(scores - lse_ref[0, 0, head : head + 1, :])
+                gv_ref[0, :, cols] = dot(weights.astype(BF), gm).astype(BF)
+                gw = dot(v_ref[0, :, cols], gm, NT)
+                t = weights * gw
+                inner = jnp.sum(t, axis=0, keepdims=True)
+                gs = (t - weights * inner).astype(BF)
+                gk_ref[0, :, cols] = dot(gs, query).astype(BF)
+                gq_ref[0, :, cols] = dot(gs, key * scale, TN).astype(BF)
+            acc_ref[...] += (
+                dot(gq_ref[0], w_ref[0], NT) + dot(gk_ref[0], w_ref[1], NT) + dot(gv_ref[0], w_ref[2], NT)
+            )
+            sums_ref[...] = jnp.concatenate(
+                [
+                    jnp.sum(gq_ref[0].astype(F32), axis=0, keepdims=True),
+                    jnp.sum(gv_ref[0].astype(F32), axis=0, keepdims=True),
+                    jnp.zeros((6, cw), F32),
+                ],
+                axis=0,
+            )
+
+        @pl.when(meta_ref[1] == 1)
+        def _():
+            @pl.when(i == 0)
+            def _():
+                fill_distance(dist_ref, meta_ref[2])
+                acc_ref[...] = gaf_ref[...]
+
+            @pl.when(i < count)
+            def _():
+                work(o_own_ref, w_own_ref)
+
+            @pl.when(i >= count)
+            def _():
+                work(o_oth_ref, w_oth_ref)
+
+            @pl.when(i == steps - 1)
+            def _():
+                gx_ref[...] = acc_ref[...]
+                gxl_ref[...] = acc_ref[...].astype(BF)
+
+    tile = pl.BlockSpec((1, rows, cw), tile_map(lambda s, i: (s, 0, i)))
+    return call(
+        kernel,
+        (steps,),
+        [
+            (ga, pl.BlockSpec((1, rows, width), lambda i, meta: (meta[0], 0, 0), pipeline_mode=pl.Buffered(1))),
+            (gaf, fixed((rows, width))),
+            (q, tile),
+            (k, tile),
+            (v, tile),
+            (lse, pl.BlockSpec((1, 1, 8, rows), tile_map(lambda s, i: (s, i, 0, 0)))),
+            (o_own, pl.BlockSpec((cw, width), own_map(count, lambda i: (i, 0)))),
+            (o_oth, pl.BlockSpec((cw, width), oth_map(count, lambda i: (i, 0)))),
+            (w_own, pl.BlockSpec((3, width, cw), own_map(count, lambda i: (0, 0, i)))),
+            (w_oth, pl.BlockSpec((3, width, cw), oth_map(count, lambda i: (0, 0, i)))),
+            (slopes, pl.BlockSpec(memory_space=pltpu.SMEM)),
+        ],
+        [((slots, rows, total), BF, tile, True)] * 3
+        + [
+            ((rows, width), F32, pl.BlockSpec((rows, width), lambda i, meta: (0, 0)), False),
+            ((rows, width), BF, pl.BlockSpec((rows, width), lambda i, meta: (0, 0)), False),
+            ((8, total), F32, pl.BlockSpec((8, cw), lambda i, meta: (0, i)), False),
+        ],
+        [pltpu.VMEM((rows, rows), F32), pltpu.VMEM((rows, cw), BF), pltpu.VMEM((rows, width), F32)],
+        meta,
+        chain,
+        deps,
+        "attention_backward",
+        2 * rows * width * 4 * total + 10 * rows * rows * total,
+        20 << 20,
+    )
+
+
+def weight_grads(left, rights, seqs, name):
+    rows, depth = left.shape[1:]
+    width = rights[0].shape[2]
+    nt = 512
+    n = len(rights)
+
+    def kernel(*refs):
+        left_ref, ins, outs, flip_ref = refs[0], refs[1 : 1 + n], refs[1 + n : 1 + 2 * n], refs[1 + 2 * n]
+
+        @pl.when(pl.program_id(0) == 0)
+        def _():
+            for s in range(seqs):
+                flip_ref[:, s * rows : (s + 1) * rows] = left_ref[s].T
+
+        for a, b in zip(ins, outs):
+            total = dot(flip_ref[:, :rows], a[0])
+            for s in range(1, seqs):
+                total += dot(flip_ref[:, s * rows : (s + 1) * rows], a[s])
+            b[...] = total.astype(BF)
+
+    return pl.pallas_call(
+        kernel,
+        grid=(width // nt,),
+        in_specs=[pl.BlockSpec((seqs, rows, depth), lambda j: (0, 0, 0), pipeline_mode=pl.Buffered(1))]
+        + [pl.BlockSpec((seqs, rows, nt), lambda j: (0, 0, j))] * n,
+        out_specs=[pl.BlockSpec((depth, nt), lambda j: (0, j))] * n,
+        out_shape=[jax.ShapeDtypeStruct((depth, width), BF)] * n,
+        scratch_shapes=[pltpu.VMEM((depth, seqs * rows), BF)],
+        compiler_params=pltpu.CompilerParams(
+            dimension_semantics=("arbitrary",), vmem_limit_bytes=VMEM_LIMIT
+        ),
+        cost_estimate=pl.CostEstimate(
+            flops=2 * seqs * rows * depth * width * n,
+            bytes_accessed=(seqs * rows + depth) * width * n * 2,
+            transcendentals=0,
+        ),
+        name=name,
+    )(left, *rights)
+
+
 MASKED = -1000000000.0
 
 
@@ -422,9 +918,221 @@
     )
 
 
+def join(first, second, swapped):
+    return jnp.where(
+        swapped, jnp.concatenate([second, first], axis=0), jnp.concatenate([first, second], axis=0)
+    )
+
+
+def by_sequence(
+    inputs,
+    cotangent,
+    lengths,
+    w_qkv,
+    b_qv,
+    w_out,
+    b_out,
+    ln_gain,
+    ln_bias,
+    w_up,
+    b_up,
+    w_down,
+    b_down,
+):
+    batches, shard_rows, width = inputs.shape
+    place = lax.axis_index("tensor")
+    section = lax.axis_index("section")
+    groups = lax.axis_size("dp")
+    group = lax.axis_index("dp")
+    core = group % 2
+    rows = 2 * shard_rows
+    seqs = batches // 2
+    slots = seqs + 1
+    local = w_qkv.shape[3]
+    units = w_up.shape[3]
+    heads = local // HD
+    pair = [(index, index ^ 1) for index in range(groups)]
+
+    def across(value):
+        return lax.ppermute(value, "tensor", [(0, 1), (1, 0)])
+
+    def partner(value):
+        return lax.ppermute(value, "dp", pair)
+
+    def whole_rows(value):
+        mine = lax.dynamic_slice_in_dim(value, place * seqs, seqs, 0)
+        sent = lax.dynamic_slice_in_dim(value, (1 - place) * seqs, seqs, 0)
+        got = across(sent)
+        return [join(mine[m], got[m], place == 1) for m in range(seqs)]
+
+    def own_rows(values, low):
+        kept = [lax.dynamic_slice_in_dim(v, place * shard_rows, shard_rows, 0) for v in values]
+        sent = [lax.dynamic_slice_in_dim(v, (1 - place) * shard_rows, shard_rows, 0) for v in low]
+        got = [across(v) for v in sent]
+        return join(jnp.stack(kept), jnp.stack(got).astype(values[0].dtype), place == 1)
+
+    def fetch(weight):
+        half = weight.shape[0] // 2
+        got = across(lax.dynamic_slice_in_dim(weight, core * half, half, 0))
+        return join(got, partner(got), core == 1)
+
+    def fetch_wide(weight):
+        part = weight.shape[0] // groups
+        got = across(lax.dynamic_slice_in_dim(weight, group * part, part, 0))
+        return lax.all_gather(got, "dp", axis=0, tiled=True)
+
+    qkv_own = jnp.transpose(w_qkv[0], (1, 0, 2))
+    out_own = w_out[0]
+    up_own = w_up[0]
+    down_own = w_down[0]
+    x_first = whole_rows(inputs)
+    small = across(jnp.concatenate([b_qv[0], b_up[0]], axis=1))
+    qkv_oth = fetch(qkv_own.reshape(3 * width, local)).reshape(3, width, local)
+    out_oth = fetch(out_own)
+    up_oth = fetch_wide(up_own.reshape(2 * width, units)).reshape(2, width, units)
+    down_oth = fetch(down_own)
+    outer = whole_rows(cotangent)
+
+    bias = jnp.concatenate([b_qv[0], small[:, :local]], axis=1).astype(F32)
+    up_bias = jnp.concatenate([b_up[0], small[:, local:]], axis=1).astype(F32)
+    vecs = jnp.stack(
+        [b_out[0], ln_gain[0, 0], ln_bias[0, 0], b_down[0], ln_gain[0, 1], ln_bias[0, 1], b_out[0], b_out[0]]
+    ).astype(F32)
+    slopes = jnp.concatenate(
+        [alibi_slopes(place * heads, heads, H), alibi_slopes((1 - place) * heads, heads, H)]
+    )
+    own_lengths = lax.dynamic_slice_in_dim(lengths, place * seqs, seqs, 0)
+
+    def meta(m, turn):
+        active = section == turn
+        return jnp.stack([jnp.where(active, m, seqs), active.astype(jnp.int32), own_lengths[m]])
+
+    metas = [[meta(m, turn) for m in range(seqs)] for turn in range(2)]
+    att = ffn = None
+    deps = []
+
+    def attention(x, m, turn):
+        nonlocal att, deps
+        att = attention_forward(x, qkv_own, qkv_oth, bias, slopes, metas[turn][m], att, deps, slots)
+        deps = [att[4]]
+
+    def feed(x, m, turn):
+        nonlocal ffn, deps
+        ffn = ffn_forward(
+            x, att[3], out_own, out_oth, up_own, up_oth, down_own, down_oth, vecs, up_bias,
+            metas[turn][m], ffn, deps, slots,
+        )
+        *ffn, y = ffn
+        deps = [y]
+        return y
+
+    for m in range(seqs):
+        attention(x_first[m], m, 0)
+    y_first = [feed(x_first[m], m, 0) for m in range(seqs)]
+    x_second = [lax.ppermute(y, "section", [(0, 1)]) for y in y_first]
+    y_second = []
+    for m in range(seqs):
+        attention(x_second[m], m, 1)
+        y_second.append(feed(x_second[m], m, 1))
+
+    bff = bat = None
+    sums = [[None] * seqs, [None] * seqs]
+
+    def back(grad, m, turn):
+        nonlocal bff, bat, deps
+        act, slope, hidden, normed, u1, u2, r1, r2 = ffn
+        *bff, gaf, norm_sums, up_sums = ffn_backward(
+            grad, u2, r2, u1, r1, act, slope, up_own, up_oth, down_own, down_oth, vecs,
+            metas[turn][m], bff, deps, slots,
+        )
+        deps = [norm_sums]
+        *bat, gx, gx_low, qv_sums = attention_backward(
+            bff[3], gaf, att[0], att[1], att[2], att[4], out_own, out_oth, qkv_own, qkv_oth, slopes,
+            metas[turn][m], bat, deps, slots,
+        )
+        deps = [qv_sums]
+        sums[turn][m] = (norm_sums, up_sums, qv_sums)
+        return gx, gx_low
+
+    row = jnp.arange(rows)[:, None]
+    gx_second = [
+        back(jnp.where(row < own_lengths[m], outer[m], 0), m, 1) for m in range(seqs)
+    ]
+    grad_middle = [lax.ppermute(gx_second[m][1], "section", [(1, 0)]) for m in range(seqs)]
+    gx_first = [back(grad_middle[m], m, 0) for m in range(seqs)]
+
+    first = section == 0
+    hidden, normed = ffn[2], ffn[3]
+    mixed = att[3]
+    x_all = jnp.stack([jnp.where(first, x_first[m], x_second[m]) for m in range(seqs)])
+    gg0, gg1, gl, ga = bff
+    d_up = weight_grads(normed, [gg0, gg1], seqs, "grad_up")
+    (d_down,) = weight_grads(gl, [hidden], seqs, "grad_down")
+    d_qkv = weight_grads(x_all, bat, seqs, "grad_qkv")
+    (d_out,) = weight_grads(mixed, [ga], seqs, "grad_out")
+
+    produced = own_rows(*[[jnp.where(first, a, b) for a, b in zip(y_first, y_second)]] * 2)
+    grads_in = own_rows(
+        [jnp.where(first, a[0], b[0]) for a, b in zip(gx_first, gx_second)],
+        [jnp.where(first, a[1], b[1]) for a, b in zip(gx_first, gx_second)],
+    )
+
+    def reduce_columns(grad, count):
+        total = grad[:, :count] + across(grad[:, count:])
+        return lax.psum(total, "dp").astype(F32)
+
+    up_sum = jnp.stack([reduce_columns(g, units) for g in d_up])
+    down_sum = reduce_columns(d_down, units)
+    qkv_sum = jnp.stack([reduce_columns(g, local) for g in d_qkv], axis=1)
+    out_sum = lax.psum(d_out[:local] + across(d_out[local:]), "dp").astype(F32)
+
+    picked = [
+        sum(jnp.where(first, sums[0][m][index], sums[1][m][index]) for m in range(seqs))
+        for index in range(3)
+    ]
+    norm_sums, up_sums, qv_sums = picked
+
+    def ordered(values, count):
+        return jnp.where(
+            place == 0, values, jnp.concatenate([values[:, count:], values[:, :count]], axis=1)
+        )
+
+    packed = jnp.concatenate(
+        [norm_sums[:6].reshape(-1), ordered(up_sums[:2], units).reshape(-1), ordered(qv_sums[:2], local).reshape(-1)]
+    )
+    packed = lax.psum(packed, ("tensor", "dp"))
+    norm_total = packed[: 6 * width].reshape(6, width)
+    up_total = packed[6 * width : 6 * width + 4 * units].reshape(2, 2 * units)
+    qv_total = packed[6 * width + 4 * units :].reshape(2, 2 * local)
+    up_bias_sum = lax.dynamic_slice_in_dim(up_total, place * units, units, 1)
+    qv_sum = lax.dynamic_slice_in_dim(qv_total, place * local, local, 1)
+    gain_sum = jnp.stack([norm_total[3], norm_total[0]])
+    shift_sum = jnp.stack([norm_total[4], norm_total[1]])
+    return (
+        produced[None],
+        grads_in[None],
+        qkv_sum[None],
+        qv_sum[None],
+        out_sum[None],
+        norm_total[5][None],
+        gain_sum[None],
+        shift_sum[None],
+        up_sum[None],
+        up_bias_sum[None],
+        down_sum[None],
+        norm_total[2][None],
+    )
+
+
 def solution(mesh):
+    sections, parts, groups = (mesh.shape[name] for name in ("section", "tensor", "dp"))
+
+    def run(*args):
+        paired = sections == 2 and parts == 2 and groups % 2 == 0 and args[0].shape[0] == 4
+        return (by_sequence if paired else on_device)(*args)
+
     return jax.shard_map(
-        on_device,
+        run,
         mesh=mesh,
         in_specs=(
             P("dp", "tensor", None),

time: 2370 us -> 1350 us (0.57)
  matrix products: 793 us -> 0 us
  Pallas kernels: 0 us -> 324 us
  other arithmetic: 287 us -> 89.8 us
  waiting for transfers between devices: 987 us -> 835 us
  local copies, waits for them, and re-layouts: 143 us -> 44 us
  blocking collectives: 90.4 us -> 0 us
    dot_general x100 -> x0, matrix products: 708 us -> none  [the longest x5 73 us: attention_back(): jnp.einsum('hqk,khd->qhd', grad_scores, key, preferred_element_type=jnp.f...]
    ppermute x10 -> x25, waiting for transfers between devices: 103 us -> 550 us  [the longest x18 450 us: across(): return lax.ppermute(value, 'tensor', [(0, 1), (1, 0)])]
    all_gather x30 -> x1, waiting for transfers between devices: 429 us -> 0.01 us  [fetch_wide(): return lax.all_gather(got, 'dp', axis=0, tiled=True)]
    pallas_call x0 -> x20, Pallas kernels: none -> 324 us  [the longest x16 268 us: call(): pl.pallas_call(body, grid_spec=pltpu.PrefetchScalarGridSpec(num_scalar_pr...]
    reduce_scatter x20 -> x0, waiting for transfers between devices: 207 us -> none  [the longest x5 102 us: attention_forward(): lax.psum_scatter(term(jnp.int32(0), shard_rows * lax.axis_size('tensor'))...]
    reduce_sum x70 -> x0, other arithmetic: 111 us -> none  [the longest x20 36.8 us: layer_norm(): mean = jnp.mean(values, axis=-1, keepdims=True)]
    psum x2 -> x0, blocking collectives: 90.4 us -> none  [the longest x1 61.4 us: on_device(): lax.psum((out_bias_total, gain_total, shift_total, down_bias_total), ('te...]
    sub x10 -> x0, matrix products: 85.7 us -> none  [attention_core(): weights = jax.nn.softmax(scores, axis=-1)]
  transfers between devices with their start and end apart: 61 -> 28, of which waited for: 56 -> 14; matrix products, arithmetic and copies ran while one was open for 20% -> 8% of each run, Pallas kernels for 0% -> 17%
where the time goes in v1:
time: 1350 us; the launch traced here: 1340 us
  waiting for transfers between devices  835 us (62%)
  Pallas kernels  324 us (24%)
  other arithmetic  89.8 us (7%)
  local copies, waits for them, and re-layouts  44 us (3%)
  starting transfers between devices  27.3 us (2%)
  between operations  14.7 us (1%)
    ppermute x18, waiting for transfers between devices, across(): return lax.ppermute(value, 'tensor', [(0, 1), (1, 0)])  450 us
    psum x1, waiting for transfers between devices, reduce_columns(): return lax.psum(total, 'dp').astype(F32)  285 us
    pallas_call x16, Pallas kernels, call(): pl.pallas_call(body, grid_spec=pltpu.PrefetchScalarGridSpec(num_scalar_pr...  268 us
    ppermute x2, waiting for transfers between devices, by_sequence(): lax.ppermute(gx_second[m][1], 'section', [(1, 0)])  95.7 us
    pallas_call x4, Pallas kernels, weight_grads(): pl.pallas_call(kernel, grid=(width // nt,), in_specs=[pl.BlockSpec((seqs,...  56.1 us
  transfers between devices with their start and end apart: 28, of which 14 were waited for; matrix products, arithmetic and copies ran while one was open for 8% of the time, Pallas kernels for 17%

profile of v1, /device:TPU:0, one launch (start us, length us, event | category | flops | bytes accessed | tf_op | source)
XLA Modules:
  0.0 1335.5 jit_solution(3906890556904398993)
XLA Ops:
  8.7 3.0 collective-permute-start.6
  11.7 23.3 %collective-permute-done.6 = bf16[256,2048]{1,0:T(8,128)(2,1)} collective-permute-done((bf16[256,2048]{1,0:T(8,128)(2,1)S(1)}, bf16[256,2048]{1,0:T(8,128)(2,1)}, u32[]{:S(2)}, u32[]{:S(2)}) %collective-permute-start.6) | collective-permute-done | bytes 1048608 | tf_op jit(solution)/shard_map/ppermute | solution.py:957
  39.1 2.3 constant_dynamic-slice_fusion.6
  44.6 3.5 dynamic-slice_bitcast_fusion
  51.2 1.9 add_add_fusion.2
  53.1 1.9 add_add_fusion
  55.1 2.3 constant_dynamic-slice_fusion.1
  60.0 50.1 %collective-permute-done.1 = bf16[1536,512]{1,0:T(8,128)(2,1)} collective-permute-done((bf16[1536,512]{1,0:T(8,128)(2,1)}, bf16[1536,512]{1,0:T(8,128)(2,1)}, u32[]{:S(2)}, u32[]{:S(2)}) %collective-permute-start.1) | collective-permute-done | bytes 1572896 | tf_op jit(solution)/shard_map/ppermute | solution.py:957
  112.6 42.4 %collective-permute-done.7 = bf16[512,2048]{1,0:T(8,128)(2,1)} collective-permute-done((bf16[512,2048]{1,0:T(8,128)(2,1)}, bf16[512,2048]{1,0:T(8,128)(2,1)}, u32[]{:S(2)}, u32[]{:S(2)}) %collective-permute-start.7) | collective-permute-done | bytes 2097184 | tf_op jit(solution)/shard_map/ppermute | solution.py:957
  155.1 2.6 maximum_select_fusion.6.refs_3_.refs_7_
  157.7 2.3 maximum_select_fusion.4
  160.0 15.1 %collective-permute-done.13 = bf16[2,256,1024]{2,1,0:T(8,128)(2,1)S(1)} collective-permute-done((bf16[2,256,1024]{2,1,0:T(8,128)(2,1)}, bf16[2,256,1024]{2,1,0:T(8,128)(2,1)S(1)}, u32[]{:S(2)}, u32[]{:S(2)}) %collective-permute-start.13) | collective-permute-done | bytes 1048608 | tf_op jit(solution)/shard_map/ppermute | solution.py:957
  175.2 3.9 fusion.6
  179.1 3.4 maximum_select_fusion.2
  182.5 17.6 %attention_forward.4 = (bf16[3,512,1024]{2,1,0:T(8,128)(2,1)}, bf16[3,512,1024]{2,1,0:T(8,128)(2,1)}, bf16[3,512,1024]{2,1,0:T(8,128)(2,1)}, bf16[3,512,1024]{2,1,0:T(8,128)(2,1)}, f32[3,4,8,512]{3,2,1,0:T(8,128)}) custom-call(s32[3]{0:T(128)} %get-tuple-element.273.meta_ref, bf16[512,1024]{1,0:T(8,128)(2,1)} %get-tuple-element.277.refs_0_, ...), custom_call_target="tpu_custom_call" | custom-call | flops 4294967296 | bytes 12582912 | tf_op jit(solution)/shard_map/attention_forward/pallas_call | solution.py:46
  201.8 17.8 %attention_forward.5 = (bf16[3,512,1024]{2,1,0:T(8,128)(2,1)}, bf16[3,512,1024]{2,1,0:T(8,128)(2,1)}, bf16[3,512,1024]{2,1,0:T(8,128)(2,1)}, bf16[3,512,1024]{2,1,0:T(8,128)(2,1)}, f32[3,4,8,512]{3,2,1,0:T(8,128)}) custom-call(s32[3]{0:T(128)} %get-tuple-element.274.meta_ref, ...), custom_call_target="tpu_custom_call", output_to_operand_aliasing={{0}: (6, {}), {1}: (7, {}), {2}: (8, {}), {3}: (9, {}), {4}... | custom-call | flops 4294967296 | bytes 12582912 | tf_op jit(solution)/shard_map/attention_forward/pallas_call | solution.py:46
  219.6 6.2 maximum_select_fusion.refs_7_.refs_10_
  225.8 28.6 %ffn_forward.4 = (bf16[3,512,4096]{2,1,0:T(8,128)(2,1)}, bf16[3,512,4096]{2,1,0:T(8,128)(2,1)}, bf16[3,512,4096]{2,1,0:T(8,128)(2,1)}, bf16[3,512,1024]{2,1,0:T(...) custom-call(s32[3]{0:T(128)} %get-tuple-element.273.meta_ref, ...), custom_call_target="tpu_custom_call" | custom-call | flops 13958643712 | bytes 47185920 | tf_op jit(solution)/shard_map/ffn_forward/pallas_call | solution.py:46
  255.8 28.7 %ffn_forward.5 = (bf16[3,512,4096]{2,1,0:T(8,128)(2,1)}, bf16[3,512,4096]{2,1,0:T(8,128)(2,1)}, bf16[3,512,4096]{2,1,0:T(8,128)(2,1)}, bf16[3,512,1024]{2,1,0:T(...) custom-call(s32[3]{0:T(128)} %get-tuple-element.274.meta_ref, ...), custom_call_target="tpu_custom_call", output_to_operand_aliasing={{0}: (11, {}), {1}: (12, {}), {2}: (13, {}), {3}: (14, {}),... | custom-call | flops 13958643712 | bytes 47185920 | tf_op jit(solution)/shard_map/ffn_forward/pallas_call | solution.py:46
  284.4 2.3 collective-permute-start.11
  287.8 4.6 attention_forward.6
  292.4 9.7 ffn_forward.6
  302.1 4.6 collective-permute-done.11.refs_0_
  306.7 4.5 attention_forward.7
  311.2 9.4 ffn_forward.7
  320.6 9.6 ffn_backward.4
  330.2 7.5 attention_backward.4
  338.9 9.9 ffn_backward.5
  348.8 7.3 attention_backward.5
  359.4 92.8 %collective-permute-done.14.refs_0_ = bf16[512,1024]{1,0:T(8,128)(2,1)} collective-permute-done((bf16[512,1024]{1,0:T(8,128)(2,1)}, bf16[512,1024]{1,0:T(8,128)(2,1)}, u32[]{:S(2)}, u32[]{:S(2)}) %collective-permute-start.14) | collective-permute-done | bytes 1048608 | tf_op jit(solution)/shard_map/ppermute | solution.py:1061
  452.2 28.7 %ffn_backward.6 = (bf16[3,512,4096]{2,1,0:T(8,128)(2,1)}, bf16[3,512,4096]{2,1,0:T(8,128)(2,1)}, bf16[3,512,1024]{2,1,0:T(8,128)(2,1)}, bf16[3,512,1024]{2,1,0:T...) custom-call(s32[3]{0:T(128)} %get-tuple-element.273.meta_ref, ...), custom_call_target="tpu_custom_call", output_to_operand_aliasing={{0}: (13, {}), {1}: (14, {}), {2}: (15, {}), {3}: (16, {})} | custom-call | flops 12884901888 | bytes 52428800 | tf_op jit(solution)/shard_map/ffn_backward/pallas_call | solution.py:46
  480.9 27.7 %attention_backward.6 = (bf16[3,512,1024]{2,1,0:T(8,128)(2,1)}, bf16[3,512,1024]{2,1,0:T(8,128)(2,1)}, bf16[3,512,1024]{2,1,0:T(8,128)(2,1)}, f32[512,1024]{1,0:...) custom-call(s32[3]{0:T(128)} %get-tuple-element.273.meta_ref, ...), custom_call_target="tpu_custom_call", output_to_operand_aliasing={{0}: (12, {}), {1}: (13, {}), {2}: (14, {})} | custom-call | flops 6979321856 | bytes 20971520 | tf_op jit(solution)/shard_map/attention_backward/pallas_call | solution.py:46
  508.6 2.9 collective-permute-done.16.refs_0_
  511.6 28.8 %ffn_backward.7 = (bf16[3,512,4096]{2,1,0:T(8,128)(2,1)}, bf16[3,512,4096]{2,1,0:T(8,128)(2,1)}, bf16[3,512,1024]{2,1,0:T(8,128)(2,1)}, bf16[3,512,1024]{2,1,0:T...) custom-call(s32[3]{0:T(128)} %get-tuple-element.274.meta_ref, ...), custom_call_target="tpu_custom_call", output_to_operand_aliasing={{0}: (13, {}), {1}: (14, {}), {2}: (15, {}), {3}: (16, {})} | custom-call | flops 12884901888 | bytes 52428800 | tf_op jit(solution)/shard_map/ffn_backward/pallas_call | solution.py:46
  541.2 6.1 grad_out.1
  547.3 2.3 slice.248
  550.8 15.0 %grad_down.1 = bf16[1024,4096]{1,0:T(8,128)(2,1)} custom-call(bf16[3,512,1024]{2,1,0:T(8,128)(2,1)} %get-tuple-element.236.refs_0_, bf16[3,512,4096]{2,1,0:T(8,128)(2,1)} %get-tuple-element.237.refs_1_), custom_call_target="tpu_custom_call" | custom-call | flops 8589934592 | bytes 16777216 | tf_op jit(solution)/shard_map/grad_down/pallas_call | solution.py:489
  565.8 4.8 slice.256
  570.6 27.9 %attention_backward.7 = (bf16[3,512,1024]{2,1,0:T(8,128)(2,1)}, bf16[3,512,1024]{2,1,0:T(8,128)(2,1)}, bf16[3,512,1024]{2,1,0:T(8,128)(2,1)}, f32[512,1024]{1,0:...) custom-call(s32[3]{0:T(128)} %get-tuple-element.274.meta_ref, ...), custom_call_target="tpu_custom_call", output_to_operand_aliasing={{0}: (12, {}), {1}: (13, {}), {2}: (14, {})} | custom-call | flops 6979321856 | bytes 20971520 | tf_op jit(solution)/shard_map/attention_backward/pallas_call | solution.py:46
  598.5 12.0 grad_qkv.1
  610.5 2.3 slice.199
  614.8 23.0 %grad_up.1 = (bf16[1024,4096]{1,0:T(8,128)(2,1)}, bf16[1024,4096]{1,0:T(8,128)(2,1)}) custom-call(bf16[3,512,1024]{2,1,0:T(8,128)(2,1)} %get-tuple-element.231.refs_0_, bf16[3,512,4096]{2,1,0:T(8,128)(2,1)} %get-tuple-element.232.refs_1_, bf16[3,512,4096]{2,1,0:T(8,128)(2,1)} %get-tuple-element.233.refs_2_), custom_call_target="tpu_custom_call" | custom-call | flops 17179869184 | bytes 33554432 | tf_op jit(solution)/shard_map/grad_up/pallas_call | solution.py:489
  637.8 5.1 slice.222
  644.0 2.4 slice.224
  654.8 2.8 add_bitcast_fusion.2
  657.6 274.4 %collective-permute-done.19 = bf16[1024,512]{1,0:T(8,128)(2,1)} collective-permute-done((bf16[1024,512]{1,0:T(8,128)(2,1)}, bf16[1024,512]{1,0:T(8,128)(2,1)}, u32[]{:S(2)}, u32[]{:S(2)}) %collective-permute-start.19) | collective-permute-done | bytes 1048608 | tf_op jit(solution)/shard_map/ppermute | solution.py:957
  932.0 2.4 add_bitcast_fusion.3
  934.4 15.6 %collective-permute-done.18 = bf16[1024,512]{1,0:T(8,128)(2,1)} collective-permute-done((bf16[1024,512]{1,0:T(8,128)(2,1)}, bf16[1024,512]{1,0:T(8,128)(2,1)}, u32[]{:S(2)}, u32[]{:S(2)}) %collective-permute-start.18) | collective-permute-done | bytes 1048608 | tf_op jit(solution)/shard_map/ppermute | solution.py:957
  950.0 2.5 add_bitcast_fusion.4
  952.5 6.2 fusion.1
  958.7 5.0 add_bitcast_fusion
  963.7 4.8 add_bitcast_fusion.1
  973.0 12.9 collective-permute-done.10
  985.9 5.7 collective-permute-done.12
  991.6 3.0 maximum_select_fusion.3
  996.5 2.2 dynamic-slice_select_fusion.3
  1006.1 4.3 collective-permute-done.17
  1010.4 5.7 collective-permute-done.15
  1017.3 2.3 maximum_select_fusion.1
  1019.7 285.4 %all-reduce.6.cloned.1.call-done = (bf16[1024,1,512]{2,0,1:T(8,128)(2,1)}, bf16[1024,1,512]{2,0,1:T(8,128)(2,1)}, bf16[1024,1,512]{2,0,1:T(8,128)(2,1)}, bf16[1,...) async-done(((bf16[1024,1,512]{2,0,1:T(8,128)(2,1)}, bf16[1024,1,512]{2,0,1:T(8,128)(2,1)}, ...) | async-done | bytes 16777232 | tf_op jit(solution)/shard_map/psum | solution.py:1082
  1305.1 2.8 broadcast_in_dim.64
  1307.9 6.8 broadcast_in_dim.71
  1314.7 9.6 fusion
  1324.3 4.4 fusion.2
  (192 shorter events, 53.7 us)
Async XLA Ops:
  7.2 27.9 %copy-start.35 = (bf16[1,2,2048]{2,1,0:T(2,128)(2,1)S(1)}, bf16[1,2,2048]{2,1,0:T(2,128)(2,1)}, u32[]{:S(2)}) copy-start(bf16[1,2,2048]{2,1,0:T(2,128)(2,1)} %param.23) | copy-start | bytes 24580
  7.2 27.9 %copy-start.38 = (bf16[1,2,512]{2,1,0:T(2,128)(2,1)S(1)}, bf16[1,2,512]{2,1,0:T(2,128)(2,1)}, u32[]{:S(2)}) copy-start(bf16[1,2,512]{2,1,0:T(2,128)(2,1)} %param.17) | copy-start | bytes 6148
  7.2 218.6 %all-gather.2.cloned.1.call-start = ((), (), s32[]{:S(2)}) async-start(), calls=%async_computation | async-start | bytes 9437184 | tf_op jit(solution)/shard_map/all_gather | solution.py:982
  7.2 35.8 %copy-start = (bf16[1,1024,3,512]{3,1,2,0:T(8,128)(2,1)S(1)}, bf16[1,1024,3,512]{3,1,2,0:T(8,128)(2,1)}, u32[]{:S(2)}) copy-start(bf16[1,1024,3,512]{3,1,2,0:T(8,128)(2,1)} %param.16) | copy-start | bytes 9437188
  8.7 26.3 %collective-permute-start.6 = (bf16[256,2048]{1,0:T(8,128)(2,1)S(1)}, bf16[256,2048]{1,0:T(8,128)(2,1)}, u32[]{:S(2)}, u32[]{:S(2)}) collective-permute-start(bf16[256,2048]{1,0:T(8,128)(2,1)S(1)} %constant_dynamic-slice_fusion.4), channel_id=1, source_target_pairs={{0,8},{8,0},{1,9},{9,1},{2,10},{10,2},{3,11},{11,3},{4,12},{12,4},... | collective-permute-start | bytes 3145736 | tf_op jit(solution)/shard_map/ppermute | solution.py:957
  35.0 965.9 %all-reduce.4.cloned.1.call-start = ((), (), s32[]{:S(2)}) async-start(), calls=%async_computation.1 | async-start | bytes 131072 | tf_op jit(solution)/shard_map/psum | solution.py:1103
  35.1 24.4 %collective-permute-start.3 = (bf16[2,2560]{1,0:T(2,128)(2,1)S(1)}, bf16[2,2560]{1,0:T(2,128)(2,1)S(1)}, u32[]{:S(2)}, u32[]{:S(2)}) collective-permute-start(bf16[2,2560]{1,0:T(2,128)(2,1)S(1)} %pad_maximum_fusion.2), channel_id=1, source_target_pairs={{0,8},{8,0},{1,9},{9,1},{2,10},{10,2},{3,11},{11,3},{4,12},{12,4},... | collective-permute-start | bytes 30728 | tf_op jit(solution)/shard_map/ppermute | solution.py:957
  38.8 21.1 %collective-permute-start.4 = (bf16[256,1024]{1,0:T(8,128)(2,1)}, bf16[256,1024]{1,0:T(8,128)(2,1)}, u32[]{:S(2)}, u32[]{:S(2)}) collective-permute-start(bf16[256,1024]{1,0:T(8,128)(2,1)} %dynamic-slice_bitcast_fusion.7), channel_id=1, source_target_pairs={{0,8},{8,0},{1,9},{9,1},{2,10},{10,2},{3,11},{11,3},{4,12},{12,4},... | collective-permute-start | bytes 1572872 | tf_op jit(solution)/shard_map/ppermute | solution.py:957
  41.3 70.0 %collective-permute-start = (bf16[2,256,1024]{2,1,0:T(8,128)(2,1)}, bf16[2,256,1024]{2,1,0:T(8,128)(2,1)}, u32[]{:S(2)}, u32[]{:S(2)}) collective-permute-start(bf16[2,256,1024]{2,1,0:T(8,128)(2,1)} %constant_dynamic-slice_fusion.6), channel_id=1, source_target_pairs={{0,8},{8,0},{1,9},{9,1},{2,10},{10,2},{3,11},{11,3},{4,12},{12,4},... | collective-permute-start | bytes 3145736 | tf_op jit(solution)/shard_map/ppermute | solution.py:957
  43.1 6.8 copy-start.40
  44.3 65.8 %collective-permute-start.1 = (bf16[1536,512]{1,0:T(8,128)(2,1)}, bf16[1536,512]{1,0:T(8,128)(2,1)}, u32[]{:S(2)}, u32[]{:S(2)}) collective-permute-start(bf16[1536,512]{1,0:T(8,128)(2,1)} %constant_dynamic-slice_fusion.5), channel_id=1, source_target_pairs={{0,8},{8,0},{1,9},{9,1},{2,10},{10,2},{3,11},{11,3},{4,12},{12,4},... | collective-permute-start | bytes 4718600 | tf_op jit(solution)/shard_map/ppermute | solution.py:957
  44.6 12.8 copy-start.15
  48.1 106.9 %collective-permute-start.7 = (bf16[512,2048]{1,0:T(8,128)(2,1)}, bf16[512,2048]{1,0:T(8,128)(2,1)}, u32[]{:S(2)}, u32[]{:S(2)}) collective-permute-start(bf16[512,2048]{1,0:T(8,128)(2,1)} %dynamic-slice_bitcast_fusion), channel_id=1, source_target_pairs={{0,8},{8,0},{1,9},{9,1},{2,10},{10,2},{3,11},{11,3},{4,12},{12,4},... | collective-permute-start | bytes 6291464 | tf_op jit(solution)/shard_map/ppermute | solution.py:957
  49.8 8.3 copy-start.16
  55.1 3.8 copy-start.39
  59.5 115.6 %collective-permute-start.13 = (bf16[2,256,1024]{2,1,0:T(8,128)(2,1)}, bf16[2,256,1024]{2,1,0:T(8,128)(2,1)S(1)}, u32[]{:S(2)}, u32[]{:S(2)}) collective-permute-start(bf16[2,256,1024]{2,1,0:T(8,128)(2,1)} %constant_dynamic-slice_fusion.1), channel_id=1, source_target_pairs={{0,8},{8,0},{1,9},{9,1},{2,10},{10,2},{3,11},{11,3},{4,12},{12,4},... | collective-permute-start | bytes 3145736 | tf_op jit(solution)/shard_map/ppermute | solution.py:957
  59.9 95.2 %collective-permute-start.5 = (bf16[256,1024]{1,0:T(8,128)(2,1)}, bf16[256,1024]{1,0:T(8,128)(2,1)S(1)}, u32[]{:S(2)}, u32[]{:S(2)}) collective-permute-start(bf16[256,1024]{1,0:T(8,128)(2,1)} %collective-permute-done.4), channel_id=1, source_target_pairs={{0,1},{1,0},{2,3},{3,2},{4,5},{5,4},{6,7},{7,6},{8,9},{9,8},{10,11... | collective-permute-start | bytes 1572872 | tf_op jit(solution)/shard_map/ppermute | solution.py:960
  110.1 69.0 %collective-permute-start.2 = (bf16[1536,512]{1,0:T(8,128)(2,1)}, bf16[1536,512]{1,0:T(8,128)(2,1)S(1)}, u32[]{:S(2)}, u32[]{:S(2)}) collective-permute-start(bf16[1536,512]{1,0:T(8,128)(2,1)} %collective-permute-done.1), channel_id=1, source_target_pairs={{0,1},{1,0},{2,3},{3,2},{4,5},{5,4},{6,7},{7,6},{8,9},{9,8},{10,11... | collective-permute-start | bytes 4718600 | tf_op jit(solution)/shard_map/ppermute | solution.py:960
  155.1 64.5 %collective-permute-start.8 = (bf16[512,2048]{1,0:T(8,128)(2,1)}, bf16[512,2048]{1,0:T(8,128)(2,1)}, u32[]{:S(2)}, u32[]{:S(2)}) collective-permute-start(bf16[512,2048]{1,0:T(8,128)(2,1)} %collective-permute-done.7), channel_id=1, source_target_pairs={{0,1},{1,0},{2,3},{3,2},{4,5},{5,4},{6,7},{7,6},{8,9},{9,8},{10,11... | collective-permute-start | bytes 6291464 | tf_op jit(solution)/shard_map/ppermute | solution.py:960
  254.4 32.3 %collective-permute-start.9 = (bf16[512,1024]{1,0:T(8,128)(2,1)}, bf16[512,1024]{1,0:T(8,128)(2,1)S(1)}, u32[]{:S(2)}, u32[]{:S(2)}) collective-permute-start(bf16[512,1024]{1,0:T(8,128)(2,1)} %get-tuple-element.132.refs_18_), channel_id=1, source_target_pairs={{0,16},{1,17},{2,18},{3,19},{4,20},{5,21},{6,22},{7,23},{8,24},{9,... | collective-permute-start | bytes 3145736 | tf_op jit(solution)/shard_map/ppermute | solution.py:1032
  284.4 22.2 %collective-permute-start.11 = (bf16[512,1024]{1,0:T(8,128)(2,1)}, bf16[512,1024]{1,0:T(8,128)(2,1)}, u32[]{:S(2)}, u32[]{:S(2)}) collective-permute-start(bf16[512,1024]{1,0:T(8,128)(2,1)} %get-tuple-element.144.refs_10_), channel_id=1, source_target_pairs={{0,16},{1,17},{2,18},{3,19},{4,20},{5,21},{6,22},{7,23},{8,24},{9,... | collective-permute-start | bytes 3145736 | tf_op jit(solution)/shard_map/ppermute | solution.py:1032
  337.6 114.5 %collective-permute-start.14 = (bf16[512,1024]{1,0:T(8,128)(2,1)}, bf16[512,1024]{1,0:T(8,128)(2,1)}, u32[]{:S(2)}, u32[]{:S(2)}) collective-permute-start(bf16[512,1024]{1,0:T(8,128)(2,1)} %get-tuple-element.182), channel_id=1, source_target_pairs={{16,0},{17,1},{18,2},{19,3},{20,4},{21,5},{22,6},{23,7},{24,8},{25... | collective-permute-start | bytes 3145736 | tf_op jit(solution)/shard_map/ppermute | solution.py:1061
  348.8 8.8 copy-start.1
  356.2 155.4 %collective-permute-start.16 = (bf16[512,1024]{1,0:T(8,128)(2,1)}, bf16[512,1024]{1,0:T(8,128)(2,1)}, u32[]{:S(2)}, u32[]{:S(2)}) collective-permute-start(bf16[512,1024]{1,0:T(8,128)(2,1)} %get-tuple-element.204), channel_id=1, source_target_pairs={{16,0},{17,1},{18,2},{19,3},{20,4},{21,5},{22,6},{23,7},{24,8},{25... | collective-permute-start | bytes 3145736 | tf_op jit(solution)/shard_map/ppermute | solution.py:1061
  511.6 28.8 %copy-start.30 = (f32[8,1024]{1,0:T(8,128)S(1)}, f32[8,1024]{1,0:T(8,128)}, u32[]{:S(2)}) copy-start(f32[8,1024]{1,0:T(8,128)} %get-tuple-element.195.refs_14_) | copy-start | bytes 98308
  511.6 28.8 %copy-start.31 = (f32[8,1024]{1,0:T(8,128)S(1)}, f32[8,1024]{1,0:T(8,128)}, u32[]{:S(2)}) copy-start(f32[8,1024]{1,0:T(8,128)} %get-tuple-element.202.refs_14_) | copy-start | bytes 98308
  511.6 28.9 %copy-start.33 = (f32[8,1024]{1,0:T(8,128)S(1)}, f32[8,1024]{1,0:T(8,128)}, u32[]{:S(2)}) copy-start(f32[8,1024]{1,0:T(8,128)} %get-tuple-element.181.refs_11_) | copy-start | bytes 98308
  549.6 100.2 %collective-permute-start.21 = (bf16[512,1024]{1,0:T(8,128)(2,1)}, bf16[512,1024]{1,0:T(8,128)(2,1)S(1)}, u32[]{:S(2)}, u32[]{:S(2)}) collective-permute-start(bf16[512,1024]{1,0:T(8,128)(2,1)} %slice.248), channel_id=1, source_target_pairs={{0,8},{8,0},{1,9},{9,1},{2,10},{10,2},{3,11},{11,3},{4,12},{12,4},... | collective-permute-start | bytes 3145736 | tf_op jit(solution)/shard_map/ppermute | solution.py:957
  612.7 39.0 %collective-permute-start.20 = (bf16[1024,512]{1,0:T(8,128)(2,1)}, bf16[1024,512]{1,0:T(8,128)(2,1)}, u32[]{:S(2)}, u32[]{:S(2)}) collective-permute-start(bf16[1024,512]{1,0:T(8,128)(2,1)} %slice.199), channel_id=1, source_target_pairs={{0,8},{8,0},{1,9},{9,1},{2,10},{10,2},{3,11},{11,3},{4,12},{12,4},... | collective-permute-start | bytes 3145736 | tf_op jit(solution)/shard_map/ppermute | solution.py:957
  613.5 338.9 %collective-permute-start.24 = (bf16[1024,2048]{1,0:T(8,128)(2,1)}, bf16[1024,2048]{1,0:T(8,128)(2,1)}, u32[]{:S(2)}, u32[]{:S(2)}) collective-permute-start(bf16[1024,2048]{1,0:T(8,128)(2,1)} %slice.256), channel_id=1, source_target_pairs={{0,8},{8,0},{1,9},{9,1},{2,10},{10,2},{3,11},{11,3},{4,12},{12,4},... | collective-permute-start | bytes 12582920 | tf_op jit(solution)/shard_map/ppermute | solution.py:957
  637.8 6.2 copy-start.4
  644.0 4.5 copy-start.26
  644.0 4.5 copy-start.27
  644.0 4.5 copy-start.28
  644.0 4.5 copy-start.29
  644.0 4.6 copy-start.23
  644.0 4.6 copy-start.24
  644.0 4.6 copy-start.25
  644.0 4.6 copy-start.34
  644.0 4.6 copy-start.13
  644.0 6.7 copy-start.11
  646.5 7.3 copy-start.5
  646.5 312.2 %collective-permute-start.23 = (bf16[1024,2048]{1,0:T(8,128)(2,1)}, bf16[1024,2048]{1,0:T(8,128)(2,1)}, u32[]{:S(2)}, u32[]{:S(2)}) collective-permute-start(bf16[1024,2048]{1,0:T(8,128)(2,1)} %slice.224), channel_id=1, source_target_pairs={{0,8},{8,0},{1,9},{9,1},{2,10},{10,2},{3,11},{11,3},{4,12},{12,4},... | collective-permute-start | bytes 12582920 | tf_op jit(solution)/shard_map/ppermute | solution.py:957
  647.3 316.4 %collective-permute-start.22 = (bf16[1024,2048]{1,0:T(8,128)(2,1)}, bf16[1024,2048]{1,0:T(8,128)(2,1)}, u32[]{:S(2)}, u32[]{:S(2)}) collective-permute-start(bf16[1024,2048]{1,0:T(8,128)(2,1)} %slice.222), channel_id=1, source_target_pairs={{0,8},{8,0},{1,9},{9,1},{2,10},{10,2},{3,11},{11,3},{4,12},{12,4},... | collective-permute-start | bytes 12582920 | tf_op jit(solution)/shard_map/ppermute | solution.py:957
  649.8 282.2 %collective-permute-start.19 = (bf16[1024,512]{1,0:T(8,128)(2,1)}, bf16[1024,512]{1,0:T(8,128)(2,1)}, u32[]{:S(2)}, u32[]{:S(2)}) collective-permute-start(bf16[1024,512]{1,0:T(8,128)(2,1)} %slice.197), channel_id=1, source_target_pairs={{0,8},{8,0},{1,9},{9,1},{2,10},{10,2},{3,11},{11,3},{4,12},{12,4},... | collective-permute-start | bytes 3145736 | tf_op jit(solution)/shard_map/ppermute | solution.py:957
  651.8 298.2 %collective-permute-start.18 = (bf16[1024,512]{1,0:T(8,128)(2,1)}, bf16[1024,512]{1,0:T(8,128)(2,1)}, u32[]{:S(2)}, u32[]{:S(2)}) collective-permute-start(bf16[1024,512]{1,0:T(8,128)(2,1)} %slice.195), channel_id=1, source_target_pairs={{0,8},{8,0},{1,9},{9,1},{2,10},{10,2},{3,11},{11,3},{4,12},{12,4},... | collective-permute-start | bytes 3145736 | tf_op jit(solution)/shard_map/ppermute | solution.py:957
  653.7 651.4 %all-reduce.6.cloned.1.call-start = ((), (), s32[]{:S(2)}) async-start(), calls=%async_computation.2 | async-start | bytes 33554432 | tf_op jit(solution)/shard_map/psum | solution.py:1082
  653.7 278.3 %copy-start.14 = (bf16[1024,1024]{1,0:T(8,128)(2,1)S(1)}, bf16[1024,1024]{1,0:T(8,128)(2,1)}, u32[]{:S(2)}) copy-start(bf16[1024,1024]{1,0:T(8,128)(2,1)} %get-tuple-element.224) | copy-start | bytes 6291460
  654.8 295.2 %copy-start.12 = (bf16[1024,1024]{1,0:T(8,128)(2,1)S(1)}, bf16[1024,1024]{1,0:T(8,128)(2,1)}, u32[]{:S(2)}) copy-start(bf16[1024,1024]{1,0:T(8,128)(2,1)} %get-tuple-element.223) | copy-start | bytes 6291460
  950.0 8.7 slice-start.2
  952.5 6.2 slice-start.3
  952.5 11.2 slice-start
  958.6 5.0 slice-start.1
  970.7 15.2 %collective-permute-start.10 = (bf16[256,1024]{1,0:T(8,128)(2,1)}, bf16[256,1024]{1,0:T(8,128)(2,1)}, u32[]{:S(2)}, u32[]{:S(2)}) collective-permute-start(bf16[256,1024]{1,0:T(8,128)(2,1)} %get-tuple-element.251), channel_id=1, source_target_pairs={{0,8},{8,0},{1,9},{9,1},{2,10},{10,2},{3,11},{11,3},{4,12},{12,4},... | collective-permute-start | bytes 1572872 | tf_op jit(solution)/shard_map/ppermute | solution.py:957
  971.4 20.2 %collective-permute-start.12 = (bf16[256,1024]{1,0:T(8,128)(2,1)S(1)}, bf16[256,1024]{1,0:T(8,128)(2,1)S(1)}, u32[]{:S(2)}, u32[]{:S(2)}) collective-permute-start(bf16[256,1024]{1,0:T(8,128)(2,1)S(1)} %get-tuple-element.253), channel_id=1, source_target_pairs={{0,8},{8,0},{1,9},{9,1},{2,10},{10,2},{3,11},{11,3},{4,12},{12,4},... | collective-permute-start | bytes 1572872 | tf_op jit(solution)/shard_map/ppermute | solution.py:957
  991.6 8.9 copy-start.19
  991.6 8.9 copy-start.21
  994.6 6.1 copy-start.20
  994.6 6.1 copy-start.22
  996.1 14.3 %collective-permute-start.17 = (bf16[256,1024]{1,0:T(8,128)(2,1)S(1)}, bf16[256,1024]{1,0:T(8,128)(2,1)S(1)}, u32[]{:S(2)}, u32[]{:S(2)}) collective-permute-start(bf16[256,1024]{1,0:T(8,128)(2,1)S(1)} %dynamic-slice_select_fusion.2), channel_id=1, source_target_pairs={{0,8},{8,0},{1,9},{9,1},{2,10},{10,2},{3,11},{11,3},{4,12},{12,4},... | collective-permute-start | bytes 1572872 | tf_op jit(solution)/shard_map/ppermute | solution.py:957
  998.8 17.4 %collective-permute-start.15 = (bf16[256,1024]{1,0:T(8,128)(2,1)}, bf16[256,1024]{1,0:T(8,128)(2,1)}, u32[]{:S(2)}, u32[]{:S(2)}) collective-permute-start(bf16[256,1024]{1,0:T(8,128)(2,1)} %dynamic-slice_select_fusion.3), channel_id=1, source_target_pairs={{0,8},{8,0},{1,9},{9,1},{2,10},{10,2},{3,11},{11,3},{4,12},{12,4},... | collective-permute-start | bytes 1572872 | tf_op jit(solution)/shard_map/ppermute | solution.py:957
  1307.9 6.8 copy-start.10
  1314.7 9.6 copy-start.17
  1314.7 9.6 copy-start.18
  (9 other events, 20.8 us)
Sparse Core Ops, SparseCore 0:
  35.1 83.5 all-gather.1
  653.8 84.4 all-reduce.3
  968.6 336.3 all-reduce.5

commit v2 on v1

--- a/solution.py
+++ b/solution.py
@@ -466,11 +466,12 @@
     )
 
 
-def weight_grads(left, rights, seqs, name):
+def weight_grads(left, rights, seqs, name, packed=False):
     rows, depth = left.shape[1:]
     width = rights[0].shape[2]
     nt = 512
     n = len(rights)
+    fold = 2 if packed else 1
 
     def kernel(*refs):
         left_ref, ins, outs, flip_ref = refs[0], refs[1 : 1 + n], refs[1 + n : 1 + 2 * n], refs[1 + 2 * n]
@@ -484,15 +485,19 @@
             total = dot(flip_ref[:, :rows], a[0])
             for s in range(1, seqs):
                 total += dot(flip_ref[:, s * rows : (s + 1) * rows], a[s])
-            b[...] = total.astype(BF)
+            if packed:
+                b[:, :nt] = total[: depth // 2].astype(BF)
+                b[:, nt:] = total[depth // 2 :].astype(BF)
+            else:
+                b[...] = total.astype(BF)
 
     return pl.pallas_call(
         kernel,
         grid=(width // nt,),
         in_specs=[pl.BlockSpec((seqs, rows, depth), lambda j: (0, 0, 0), pipeline_mode=pl.Buffered(1))]
         + [pl.BlockSpec((seqs, rows, nt), lambda j: (0, 0, j))] * n,
-        out_specs=[pl.BlockSpec((depth, nt), lambda j: (0, j))] * n,
-        out_shape=[jax.ShapeDtypeStruct((depth, width), BF)] * n,
+        out_specs=[pl.BlockSpec((depth // fold, nt * fold), lambda j: (0, j))] * n,
+        out_shape=[jax.ShapeDtypeStruct((depth // fold, width * fold), BF)] * n,
         scratch_shapes=[pltpu.VMEM((depth, seqs * rows), BF)],
         compiler_params=pltpu.CompilerParams(
             dimension_semantics=("arbitrary",), vmem_limit_bytes=VMEM_LIMIT
@@ -504,6 +509,219 @@
         ),
         name=name,
     )(left, *rights)
+
+
+def reduce_grads(bigs, packs, out_grad, step_rows=32):
+    depth, double = bigs[0].shape
+    columns = double // 2
+    half = columns // 2
+    r = step_rows
+    per_core = depth // 2
+    quarter = packs[0].shape[0] // 2
+    n_big = per_core // r
+    n_small = quarter // (2 * r)
+    smalls = len(packs) + 1
+    total = len(bigs) * n_big + smalls * n_small
+    n_in = len(bigs) + smalls
+    n_out = n_in
+
+    def kernel(*refs):
+        ins = refs[:n_in]
+        outs = refs[n_in : n_in + n_out]
+        (own, oth, from_x, from_z, final, mine, send_sem, core_sem, x_sem, z_sem, f_sem, load_sem, store_sem, give_sem) = refs[
+            n_in + n_out :
+        ]
+        t = lax.axis_index("tensor")
+        d = lax.axis_index("dp")
+        chips = lax.axis_size("dp") // 2
+        c = lax.rem(d, 2)
+        z = d // 2
+        last = chips - 1
+        other_core = {"dp": d + 1 - 2 * c}
+        other_x = {"tensor": 1 - t}
+        above = {"dp": d + 2}
+        below = {"dp": d - 2}
+        MESH = pl.DeviceIdType.MESH
+
+        barrier = pltpu.get_barrier_semaphore()
+        pl.semaphore_signal(barrier, inc=1, device_id=other_core, device_id_type=MESH)
+        pl.semaphore_signal(barrier, inc=1, device_id=other_x, device_id_type=MESH)
+
+        @pl.when(z < last)
+        def _():
+            pl.semaphore_signal(barrier, inc=1, device_id=above, device_id_type=MESH)
+
+        @pl.when(z > 0)
+        def _():
+            pl.semaphore_signal(barrier, inc=1, device_id=below, device_id_type=MESH)
+
+        pl.semaphore_wait(barrier, 2 + jnp.where(z < last, 1, 0) + jnp.where(z > 0, 1, 0))
+
+        def pieces(k, core, side, visit):
+            for m in range(len(bigs)):
+                @pl.when((k >= m * n_big) & (k < (m + 1) * n_big))
+                def _(m=m):
+                    start = pl.multiple_of(core * per_core + (k - m * n_big) * r, r)
+                    visit(m, ins[m].at[pl.ds(start, r), pl.ds(side * columns, columns)], pl.ds(start, r), slice(0, columns))
+
+            for m in range(smalls):
+                base = len(bigs) * n_big + m * n_small
+
+                @pl.when((k >= base) & (k < base + n_small))
+                def _(m=m, base=base):
+                    for part in range(2):
+                        start = pl.multiple_of(core * quarter + (2 * (k - base) + part) * r, r)
+                        index = len(bigs) + m
+                        if m < len(packs):
+                            source = ins[index].at[pl.ds(start, r), pl.ds(side * half, half)]
+                        else:
+                            source = ins[index].at[pl.ds(side * 2 * quarter + start, r), :]
+                        visit(index, source, pl.ds(start, r), slice(part * half, (part + 1) * half))
+
+        def remote(src, dst, kind, sem, device):
+            return pltpu.make_async_remote_copy(
+                src_ref=src, dst_ref=dst, send_sem=send_sem.at[kind], recv_sem=sem, device_id=device, device_id_type=MESH
+            )
+
+        def arrived(dst, sem):
+            pltpu.make_async_copy(dst, dst, sem).wait()
+
+        up = slice(0, half)
+        down = slice(half, columns)
+        sides = ((up, 0, z, above, below), (down, 1, last - z, below, above))
+
+        def guarded(k, extra=None):
+            ok = (k >= 0) & (k < total)
+            return ok if extra is None else ok & extra
+
+        @pl.loop(0, total + 2 * last + 3)
+        def _(s):
+            @pl.when(guarded(s))
+            def _():
+                k = s
+                slot = lax.rem(k, 2)
+
+                def visit_oth(index, source, rows, cols):
+                    remote(source, oth.at[k, :, cols], 0, core_sem.at[0, k], other_core).start()
+
+                def visit_own(index, source, rows, cols):
+                    remote(source, own.at[k, :, cols], 1, core_sem.at[1, k], other_core).start()
+
+                def load_oth(index, source, rows, cols):
+                    pltpu.make_async_copy(source, mine.at[slot, 0, :, cols], load_sem.at[slot, 0]).start()
+
+                def load_own(index, source, rows, cols):
+                    pltpu.make_async_copy(source, mine.at[slot, 1, :, cols], load_sem.at[slot, 1]).start()
+
+                pieces(k, 1 - c, 1, visit_oth)
+                pieces(k, 1 - c, 0, visit_own)
+                pieces(k, c, 1, load_oth)
+                pieces(k, c, 0, load_own)
+
+            k1 = s - 1
+
+            @pl.when(guarded(k1))
+            def _():
+                slot = lax.rem(k1, 2)
+                arrived(oth.at[k1], core_sem.at[0, k1])
+                arrived(mine.at[slot, 0], load_sem.at[slot, 0])
+                oth[k1] = (oth[k1].astype(F32) + mine[slot, 0].astype(F32)).astype(BF)
+                arrived(own.at[k1], core_sem.at[1, k1])
+                arrived(mine.at[slot, 1], load_sem.at[slot, 1])
+                own[k1] = (own[k1].astype(F32) + mine[slot, 1].astype(F32)).astype(BF)
+                remote(oth.at[k1], from_x.at[k1], 2, x_sem.at[k1], other_x).start()
+
+            k2 = s - 2
+
+            @pl.when(guarded(k2))
+            def _():
+                arrived(from_x.at[k2], x_sem.at[k2])
+                own[k2] = (own[k2].astype(F32) + from_x[k2].astype(F32)).astype(BF)
+
+            for cols, way, place, ahead, behind in sides:
+                k3 = s - 2 - place
+
+                @pl.when(guarded(k3, place > 0))
+                def _(cols=cols, way=way, k3=k3):
+                    arrived(from_z.at[k3, :, cols], z_sem.at[way, k3])
+                    own[k3, :, cols] = (own[k3, :, cols].astype(F32) + from_z[k3, :, cols].astype(F32)).astype(BF)
+
+                @pl.when(guarded(k3, place < last))
+                def _(cols=cols, way=way, k3=k3, ahead=ahead):
+                    remote(own.at[k3, :, cols], from_z.at[k3, :, cols], 3 + way, z_sem.at[way, k3], ahead).start()
+
+                k4 = s - 2 - last - (last - place)
+
+                @pl.when(guarded(k4, place == last))
+                def _(cols=cols, k4=k4):
+                    final[k4, :, cols] = own[k4, :, cols]
+
+                @pl.when(guarded(k4, place < last))
+                def _(cols=cols, way=way, k4=k4):
+                    arrived(final.at[k4, :, cols], f_sem.at[way, k4])
+
+                @pl.when(guarded(k4, place > 0))
+                def _(cols=cols, way=way, k4=k4, behind=behind):
+                    remote(final.at[k4, :, cols], final.at[k4, :, cols], 5 + way, f_sem.at[way, k4], behind).start()
+
+            k5 = s - 2 - 2 * last
+
+            @pl.when(guarded(k5))
+            def _():
+                def store(index, source, rows, cols):
+                    pltpu.make_async_copy(final.at[k5, :, cols], target(index, rows, cols), store_sem).start()
+                    remote(final.at[k5, :, cols], target(index, rows, cols), 7, give_sem, other_core).start()
+
+                def target(index, rows, cols):
+                    return outs[index].at[rows, :]
+
+                pieces(k5, c, 0, store)
+
+        def drained(ref, sem):
+            pltpu.make_async_copy(ref, ref, sem).wait()
+
+        drained(oth, send_sem.at[0])
+        drained(own, send_sem.at[1])
+        drained(oth, send_sem.at[2])
+        for cols, way, place, ahead, behind in sides:
+            @pl.when(place < last)
+            def _(cols=cols, way=way):
+                drained(from_z.at[:, :, cols], send_sem.at[3 + way])
+
+            @pl.when(place > 0)
+            def _(cols=cols, way=way):
+                drained(final.at[:, :, cols], send_sem.at[5 + way])
+
+        drained(final, send_sem.at[7])
+        drained(final, store_sem)
+        drained(final, give_sem)
+
+    buffer = pltpu.VMEM((total, r, columns), BF)
+    moved = 2 * total * r * columns
+    return pl.pallas_call(
+        kernel,
+        in_specs=[ANY] * n_in,
+        out_specs=[ANY] * n_out,
+        out_shape=[jax.ShapeDtypeStruct((depth, columns), BF)] * len(bigs)
+        + [jax.ShapeDtypeStruct((2 * quarter, half), BF)] * smalls,
+        scratch_shapes=[buffer] * 5
+        + [
+            pltpu.VMEM((2, 2, r, columns), BF),
+            pltpu.SemaphoreType.DMA((8,)),
+            pltpu.SemaphoreType.DMA((2, total)),
+            pltpu.SemaphoreType.DMA((total,)),
+            pltpu.SemaphoreType.DMA((2, total)),
+            pltpu.SemaphoreType.DMA((2, total)),
+            pltpu.SemaphoreType.DMA((2, 2)),
+            pltpu.SemaphoreType.DMA,
+            pltpu.SemaphoreType.DMA,
+        ],
+        compiler_params=pltpu.CompilerParams(
+            collective_id=0, has_side_effects=True, vmem_limit_bytes=VMEM_LIMIT
+        ),
+        cost_estimate=pl.CostEstimate(flops=4 * moved, bytes_accessed=12 * moved, transcendentals=0),
+        name="reduce_grads",
+    )(*bigs, *packs, out_grad)
 
 
 MASKED = -1000000000.0
@@ -1068,7 +1286,7 @@
     gg0, gg1, gl, ga = bff
     d_up = weight_grads(normed, [gg0, gg1], seqs, "grad_up")
     (d_down,) = weight_grads(gl, [hidden], seqs, "grad_down")
-    d_qkv = weight_grads(x_all, bat, seqs, "grad_qkv")
+    d_qkv = weight_grads(x_all, bat, seqs, "grad_qkv", packed=True)
     (d_out,) = weight_grads(mixed, [ga], seqs, "grad_out")
 
     produced = own_rows(*[[jnp.where(first, a, b) for a, b in zip(y_first, y_second)]] * 2)
@@ -1077,14 +1295,17 @@
         [jnp.where(first, a[1], b[1]) for a, b in zip(gx_first, gx_second)],
     )
 
-    def reduce_columns(grad, count):
-        total = grad[:, :count] + across(grad[:, count:])
-        return lax.psum(total, "dp").astype(F32)
-
-    up_sum = jnp.stack([reduce_columns(g, units) for g in d_up])
-    down_sum = reduce_columns(d_down, units)
-    qkv_sum = jnp.stack([reduce_columns(g, local) for g in d_qkv], axis=1)
-    out_sum = lax.psum(d_out[:local] + across(d_out[local:]), "dp").astype(F32)
+    *sums_big, sum_q, sum_k, sum_v, out_sum = reduce_grads([*d_up, d_down], d_qkv, d_out)
+    up_sum = jnp.stack(sums_big[:2]).astype(F32)
+    down_sum = sums_big[2].astype(F32)
+    qkv_sum = jnp.stack(
+        [
+            jnp.concatenate([item[:, :local], item[:, local:]], axis=0)
+            for item in (sum_q, sum_k, sum_v)
+        ],
+        axis=1,
+    ).astype(F32)
+    out_sum = out_sum.astype(F32)
 
     picked = [
         sum(jnp.where(first, sums[0][m][index], sums[1][m][index]) for m in range(seqs))

time: 1350 us -> 945 us (0.70)
  waiting for transfers between devices: 835 us -> 230 us
  Pallas kernels: 324 us -> 579 us
  other arithmetic: 89.8 us -> 62.9 us
  local copies, waits for them, and re-layouts: 44 us -> 28.6 us
    ppermute x18 -> x11, waiting for transfers between devices: 450 us -> 131 us  [across(): return lax.ppermute(value, 'tensor', [(0, 1), (1, 0)])]
    psum x1 -> x0, waiting for transfers between devices: 285 us -> none  [reduce_columns(): return lax.psum(total, 'dp').astype(F32)]
    pallas_call x0 -> x1, Pallas kernels: none -> 254 us  [reduce_grads(): pl.pallas_call(kernel, in_specs=[ANY] * n_in, out_specs=[ANY] * n_out, ou...]
    another operation x5 -> x3, other arithmetic: 17.4 us -> 0.21 us  [by_sequence(): jnp.stack([jnp.concatenate([item[:, :local], item[:, local:]], axis=0) fo...]
    slice x7 -> x3, local copies, waits for them, and re-layouts: 19 us -> 2.76 us  [by_sequence(): item[:, :local]]
    convert_element_type x0 -> x2, other arithmetic: none -> 14.2 us  [the longest x1 10.7 us: by_sequence(): up_sum = jnp.stack(sums_big[:2]).astype(F32)]
    broadcast_in_dim x2 -> x0, other arithmetic: 14 us -> none  [the longest x1 9.58 us: by_sequence(): up_sum[None]]
  transfers between devices with their start and end apart: 28 -> 20, of which waited for: 14 -> 7; matrix products, arithmetic and copies ran while one was open for 8% -> 8% of each run, Pallas kernels for 17% -> 51%
where the time goes in v2:
time: 945 us; the launch traced here: 935 us
  Pallas kernels  579 us (61%)
  waiting for transfers between devices  230 us (24%)
  other arithmetic  62.9 us (7%)
  local copies, waits for them, and re-layouts  28.6 us (3%)
  starting transfers between devices  19.8 us (2%)
  between operations  15 us (2%)
    pallas_call x16, Pallas kernels, call(): pl.pallas_call(body, grid_spec=pltpu.PrefetchScalarGridSpec(num_scalar_pr...  269 us
    pallas_call x1, Pallas kernels, reduce_grads(): pl.pallas_call(kernel, in_specs=[ANY] * n_in, out_specs=[ANY] * n_out, ou...  254 us
    ppermute x11, waiting for transfers between devices, across(): return lax.ppermute(value, 'tensor', [(0, 1), (1, 0)])  131 us
    ppermute x2, waiting for transfers between devices, by_sequence(): lax.ppermute(gx_second[m][1], 'section', [(1, 0)])  95.2 us
    pallas_call x4, Pallas kernels, weight_grads(): pl.pallas_call(kernel, grid=(width // nt,), in_specs=[pl.BlockSpec((seqs,...  56.1 us
    select_n x6, other arithmetic, join(): jnp.where(swapped, jnp.concatenate([second, first], axis=0), jnp.concaten...  20.2 us
  transfers between devices with their start and end apart: 20, of which 7 were waited for; matrix products, arithmetic and copies ran while one was open for 8% of the time, Pallas kernels for 51%

profile of v2, /device:TPU:0, one launch (start us, length us, event | category | flops | bytes accessed | tf_op | source)
XLA Modules:
  0.0 935.2 jit_solution(3145178431849693183)
XLA Ops:
  7.3 1.4 constant_dynamic-slice_fusion.4
  8.7 3.0 collective-permute-start.6
  11.7 23.3 %collective-permute-done.6 = bf16[256,2048]{1,0:T(8,128)(2,1)} collective-permute-done((bf16[256,2048]{1,0:T(8,128)(2,1)S(1)}, bf16[256,2048]{1,0:T(8,128)(2,1)}, u32[]{:S(2)}, u32[]{:S(2)}) %collective-permute-start.6) | collective-permute-done | bytes 1048608 | tf_op jit(solution)/shard_map/ppermute | solution.py:1175
  35.1 1.8 collective-permute-start.3
  36.9 1.9 dynamic-slice_bitcast_fusion.7
  39.1 2.3 constant_dynamic-slice_fusion.6
  41.3 1.7 collective-permute-start
  44.6 3.5 dynamic-slice_bitcast_fusion
  48.1 1.7 collective-permute-start.7
  51.2 1.9 add_add_fusion.2
  53.1 1.9 add_add_fusion
  55.0 2.3 constant_dynamic-slice_fusion.1
  59.9 50.2 %collective-permute-done.1 = bf16[1536,512]{1,0:T(8,128)(2,1)} collective-permute-done((bf16[1536,512]{1,0:T(8,128)(2,1)}, bf16[1536,512]{1,0:T(8,128)(2,1)}, u32[]{:S(2)}, u32[]{:S(2)}) %collective-permute-start.1) | collective-permute-done | bytes 1572896 | tf_op jit(solution)/shard_map/ppermute | solution.py:1175
  111.4 1.3 slice_bitcast_fusion.3
  112.6 42.4 %collective-permute-done.7 = bf16[512,2048]{1,0:T(8,128)(2,1)} collective-permute-done((bf16[512,2048]{1,0:T(8,128)(2,1)}, bf16[512,2048]{1,0:T(8,128)(2,1)}, u32[]{:S(2)}, u32[]{:S(2)}) %collective-permute-start.7) | collective-permute-done | bytes 2097184 | tf_op jit(solution)/shard_map/ppermute | solution.py:1175
  155.1 2.6 maximum_select_fusion.6.refs_3_.refs_7_
  157.7 2.3 maximum_select_fusion.4
  160.0 15.1 %collective-permute-done.13 = bf16[2,256,1024]{2,1,0:T(8,128)(2,1)S(1)} collective-permute-done((bf16[2,256,1024]{2,1,0:T(8,128)(2,1)}, bf16[2,256,1024]{2,1,0:T(8,128)(2,1)S(1)}, u32[]{:S(2)}, u32[]{:S(2)}) %collective-permute-start.13) | collective-permute-done | bytes 1048608 | tf_op jit(solution)/shard_map/ppermute | solution.py:1175
  175.2 3.9 fusion.2
  179.1 3.5 maximum_select_fusion.2
  182.5 17.6 %attention_forward.4 = (bf16[3,512,1024]{2,1,0:T(8,128)(2,1)}, bf16[3,512,1024]{2,1,0:T(8,128)(2,1)}, bf16[3,512,1024]{2,1,0:T(8,128)(2,1)}, bf16[3,512,1024]{2,1,0:T(8,128)(2,1)}, f32[3,4,8,512]{3,2,1,0:T(8,128)}) custom-call(s32[3]{0:T(128)} %get-tuple-element.286.meta_ref, bf16[512,1024]{1,0:T(8,128)(2,1)} %get-tuple-element.290.refs_0_, ...), custom_call_target="tpu_custom_call" | custom-call | flops 4294967296 | bytes 12582912 | tf_op jit(solution)/shard_map/attention_forward/pallas_call | solution.py:46
  200.2 1.6 copy.93.refs_9_
  201.8 17.8 %attention_forward.5 = (bf16[3,512,1024]{2,1,0:T(8,128)(2,1)}, bf16[3,512,1024]{2,1,0:T(8,128)(2,1)}, bf16[3,512,1024]{2,1,0:T(8,128)(2,1)}, bf16[3,512,1024]{2,1,0:T(8,128)(2,1)}, f32[3,4,8,512]{3,2,1,0:T(8,128)}) custom-call(s32[3]{0:T(128)} %get-tuple-element.287.meta_ref, ...), custom_call_target="tpu_custom_call", output_to_operand_aliasing={{0}: (6, {}), {1}: (7, {}), {2}: (8, {}), {3}: (9, {}), {4}... | custom-call | flops 4294967296 | bytes 12582912 | tf_op jit(solution)/shard_map/attention_forward/pallas_call | solution.py:46
  219.6 6.2 maximum_select_fusion.refs_7_.refs_10_
  225.8 28.7 %ffn_forward.4 = (bf16[3,512,4096]{2,1,0:T(8,128)(2,1)}, bf16[3,512,4096]{2,1,0:T(8,128)(2,1)}, bf16[3,512,4096]{2,1,0:T(8,128)(2,1)}, bf16[3,512,1024]{2,1,0:T(...) custom-call(s32[3]{0:T(128)} %get-tuple-element.286.meta_ref, ...), custom_call_target="tpu_custom_call" | custom-call | flops 13958643712 | bytes 47185920 | tf_op jit(solution)/shard_map/ffn_forward/pallas_call | solution.py:46
  254.5 1.4 collective-permute-start.9
  255.9 28.6 %ffn_forward.5 = (bf16[3,512,4096]{2,1,0:T(8,128)(2,1)}, bf16[3,512,4096]{2,1,0:T(8,128)(2,1)}, bf16[3,512,4096]{2,1,0:T(8,128)(2,1)}, bf16[3,512,1024]{2,1,0:T(...) custom-call(s32[3]{0:T(128)} %get-tuple-element.287.meta_ref, ...), custom_call_target="tpu_custom_call", output_to_operand_aliasing={{0}: (11, {}), {1}: (12, {}), {2}: (13, {}), {3}: (14, {}),... | custom-call | flops 13958643712 | bytes 47185920 | tf_op jit(solution)/shard_map/ffn_forward/pallas_call | solution.py:46
  284.5 2.3 collective-permute-start.11
  287.8 4.6 attention_forward.6
  292.5 9.8 %ffn_forward.6 = (bf16[3,512,4096]{2,1,0:T(8,128)(2,1)}, bf16[3,512,4096]{2,1,0:T(8,128)(2,1)}, bf16[3,512,4096]{2,1,0:T(8,128)(2,1)}, bf16[3,512,1024]{2,1,0:T(...) custom-call(s32[3]{0:T(128)} %get-tuple-element.288.meta_ref, ...), custom_call_target="tpu_custom_call", output_to_operand_aliasing={{0}: (11, {}), {1}: (12, {}), {2}: (13, {}), {3}: (14, {}),... | custom-call | flops 13958643712 | bytes 47185920 | tf_op jit(solution)/shard_map/ffn_forward/pallas_call | solution.py:46
  303.4 3.3 collective-permute-done.11.refs_0_
  306.7 4.5 attention_forward.7
  311.2 9.7 %ffn_forward.7 = (bf16[3,512,4096]{2,1,0:T(8,128)(2,1)}, bf16[3,512,4096]{2,1,0:T(8,128)(2,1)}, bf16[3,512,4096]{2,1,0:T(8,128)(2,1)}, bf16[3,512,1024]{2,1,0:T(...) custom-call(s32[3]{0:T(128)} %get-tuple-element.289.meta_ref, ...), custom_call_target="tpu_custom_call", output_to_operand_aliasing={{0}: (11, {}), {1}: (12, {}), {2}: (13, {}), {3}: (14, {}),... | custom-call | flops 13958643712 | bytes 47185920 | tf_op jit(solution)/shard_map/ffn_forward/pallas_call | solution.py:46
  325.4 9.6 %ffn_backward.4 = (bf16[3,512,4096]{2,1,0:T(8,128)(2,1)}, bf16[3,512,4096]{2,1,0:T(8,128)(2,1)}, bf16[3,512,1024]{2,1,0:T(8,128)(2,1)}, bf16[3,512,1024]{2,1,0:T...) custom-call(s32[3]{0:T(128)} %get-tuple-element.288.meta_ref, ...), custom_call_target="tpu_custom_call" | custom-call | flops 12884901888 | bytes 52428800 | tf_op jit(solution)/shard_map/ffn_backward/pallas_call | solution.py:46
  335.0 7.3 attention_backward.4
  342.3 1.3 collective-permute-start.14
  343.6 9.9 %ffn_backward.5 = (bf16[3,512,4096]{2,1,0:T(8,128)(2,1)}, bf16[3,512,4096]{2,1,0:T(8,128)(2,1)}, bf16[3,512,1024]{2,1,0:T(8,128)(2,1)}, bf16[3,512,1024]{2,1,0:T...) custom-call(s32[3]{0:T(128)} %get-tuple-element.289.meta_ref, ...), custom_call_target="tpu_custom_call", output_to_operand_aliasing={{0}: (13, {}), {1}: (14, {}), {2}: (15, {}), {3}: (16, {})} | custom-call | flops 12884901888 | bytes 52428800 | tf_op jit(solution)/shard_map/ffn_backward/pallas_call | solution.py:46
  353.5 7.4 attention_backward.5
  360.9 1.4 collective-permute-start.16
  362.7 1.5 pad_maximum_fusion.refs_0_
  364.2 3.3 maximum_select_fusion.3
  367.5 92.0 %collective-permute-done.14.refs_0_ = bf16[512,1024]{1,0:T(8,128)(2,1)} collective-permute-done((bf16[512,1024]{1,0:T(8,128)(2,1)}, bf16[512,1024]{1,0:T(8,128)(2,1)}, u32[]{:S(2)}, u32[]{:S(2)}) %collective-permute-start.14) | collective-permute-done | bytes 1048608 | tf_op jit(solution)/shard_map/ppermute | solution.py:1279
  459.5 28.3 %ffn_backward.6 = (bf16[3,512,4096]{2,1,0:T(8,128)(2,1)}, bf16[3,512,4096]{2,1,0:T(8,128)(2,1)}, bf16[3,512,1024]{2,1,0:T(8,128)(2,1)}, bf16[3,512,1024]{2,1,0:T...) custom-call(s32[3]{0:T(128)} %get-tuple-element.286.meta_ref, ...), custom_call_target="tpu_custom_call", output_to_operand_aliasing={{0}: (13, {}), {1}: (14, {}), {2}: (15, {}), {3}: (16, {})} | custom-call | flops 12884901888 | bytes 52428800 | tf_op jit(solution)/shard_map/ffn_backward/pallas_call | solution.py:46
  487.8 28.1 %attention_backward.6 = (bf16[3,512,1024]{2,1,0:T(8,128)(2,1)}, bf16[3,512,1024]{2,1,0:T(8,128)(2,1)}, bf16[3,512,1024]{2,1,0:T(8,128)(2,1)}, f32[512,1024]{1,0:...) custom-call(s32[3]{0:T(128)} %get-tuple-element.286.meta_ref, ...), custom_call_target="tpu_custom_call", output_to_operand_aliasing={{0}: (12, {}), {1}: (13, {}), {2}: (14, {})} | custom-call | flops 6979321856 | bytes 20971520 | tf_op jit(solution)/shard_map/attention_backward/pallas_call | solution.py:46
  515.8 3.2 collective-permute-done.16.refs_0_
  519.0 29.0 %ffn_backward.7 = (bf16[3,512,4096]{2,1,0:T(8,128)(2,1)}, bf16[3,512,4096]{2,1,0:T(8,128)(2,1)}, bf16[3,512,1024]{2,1,0:T(8,128)(2,1)}, bf16[3,512,1024]{2,1,0:T...) custom-call(s32[3]{0:T(128)} %get-tuple-element.287.meta_ref, ...), custom_call_target="tpu_custom_call", output_to_operand_aliasing={{0}: (13, {}), {1}: (14, {}), {2}: (15, {}), {3}: (16, {})} | custom-call | flops 12884901888 | bytes 52428800 | tf_op jit(solution)/shard_map/ffn_backward/pallas_call | solution.py:46
  548.8 6.1 grad_out.1.refs_6_
  554.9 1.4 dynamic-slice_select_fusion.3
  556.4 28.1 %attention_backward.7 = (bf16[3,512,1024]{2,1,0:T(8,128)(2,1)}, bf16[3,512,1024]{2,1,0:T(8,128)(2,1)}, bf16[3,512,1024]{2,1,0:T(8,128)(2,1)}, f32[512,1024]{1,0:...) custom-call(s32[3]{0:T(128)} %get-tuple-element.287.meta_ref, ...), custom_call_target="tpu_custom_call", output_to_operand_aliasing={{0}: (12, {}), {1}: (13, {}), {2}: (14, {})} | custom-call | flops 6979321856 | bytes 20971520 | tf_op jit(solution)/shard_map/attention_backward/pallas_call | solution.py:46
  585.3 1.4 dynamic-slice_select_fusion.2
  587.5 1.3 collective-permute-start.17
  589.6 15.0 %grad_down.1.refs_2_ = bf16[1024,4096]{1,0:T(8,128)(2,1)} custom-call(bf16[3,512,1024]{2,1,0:T(8,128)(2,1)} %get-tuple-element.232.refs_0_, bf16[3,512,4096]{2,1,0:T(8,128)(2,1)} %get-tuple-element.233.refs_1_), custom_call_target="tpu_custom_call" | custom-call | flops 8589934592 | bytes 16777216 | tf_op jit(solution)/shard_map/grad_down/pallas_call | solution.py:494
  604.6 23.3 %grad_up.1 = (bf16[1024,4096]{1,0:T(8,128)(2,1)}, bf16[1024,4096]{1,0:T(8,128)(2,1)}) custom-call(bf16[3,512,1024]{2,1,0:T(8,128)(2,1)} %get-tuple-element.227.refs_0_, bf16[3,512,4096]{2,1,0:T(8,128)(2,1)} %get-tuple-element.228.refs_1_, bf16[3,512,4096]{2,1,0:T(8,128)(2,1)} %get-tuple-element.229.refs_2_), custom_call_target="tpu_custom_call" | custom-call | flops 17179869184 | bytes 33554432 | tf_op jit(solution)/shard_map/grad_up/pallas_call | solution.py:494
  627.8 11.8 %grad_qkv.1 = (bf16[512,2048]{1,0:T(8,128)(2,1)}, bf16[512,2048]{1,0:T(8,128)(2,1)}, bf16[512,2048]{1,0:T(8,128)(2,1)}) custom-call(bf16[2,512,1024]{2,1,0:T(8,128)(2,1)} %pad_maximum_fusion.refs_0_, bf16[3,512,1024]{2,1,0:T(8,128)(2,1)} %get-tuple-element.234.refs_1_, bf16[3,512,1024]{2,1,0:T(8,128)(2,1)} %get-tuple-element.235.refs_2_, ...), custom_call_target="tpu_custom_call" | custom-call | flops 6442450944 | bytes 12582912 | tf_op jit(solution)/shard_map/grad_qkv/pallas_call | solution.py:494
  639.6 254.2 %reduce_grads.1 = (bf16[1024,2048]{1,0:T(8,128)(2,1)}, bf16[1024,2048]{1,0:T(8,128)(2,1)}, bf16[1024,2048]{1,0:T(8,128)(2,1)}, bf16[512,1024]{1,0:T(8,128)(2,1)}...) custom-call(bf16[1024,4096]{1,0:T(8,128)(2,1)} %get-tuple-element.230.refs_0_, ...), custom_call_target="tpu_custom_call" | custom-call | flops 33554432 | bytes 100663296 | tf_op jit(solution)/shard_map/reduce_grads/pallas_call | solution.py:701
  893.8 1.4 fusion.9
  895.2 1.3 fusion.10
  896.6 1.6 bitcast_convert_fusion.1
  899.4 4.4 bitcast_convert_fusion
  904.3 10.7 %maximum_convert_fusion = f32[1,2,1024,2048]{3,2,1,0:T(8,128)} fusion(bf16[1,1,1024,2048]{3,2,1,0:T(8,128)(2,1)} %bitcast.157, bf16[1,1,1024,2048]{3,2,1,0:T(8,128)(2,1)} %bitcast.156), kind=kLoop, calls=%fused_computation | loop fusion | flops 8388608 | bytes 25165824 | tf_op jit(solution)/shard_map/convert_element_type | solution.py:1299
  915.0 3.5 maximum_convert_fusion.1
  920.7 1.3 fusion.13
  924.5 1.3 fusion.4
  925.8 2.3 maximum_select_fusion.1
  (146 shorter events, 23.4 us)
Async XLA Ops:
  7.2 27.9 %copy-start.29 = (bf16[1,2,2048]{2,1,0:T(2,128)(2,1)S(1)}, bf16[1,2,2048]{2,1,0:T(2,128)(2,1)}, u32[]{:S(2)}) copy-start(bf16[1,2,2048]{2,1,0:T(2,128)(2,1)} %param.23) | copy-start | bytes 24580
  7.2 27.9 %copy-start.32 = (bf16[1,2,512]{2,1,0:T(2,128)(2,1)S(1)}, bf16[1,2,512]{2,1,0:T(2,128)(2,1)}, u32[]{:S(2)}) copy-start(bf16[1,2,512]{2,1,0:T(2,128)(2,1)} %param.17) | copy-start | bytes 6148
  7.2 218.6 %all-gather.2.cloned.1.call-start = ((), (), s32[]{:S(2)}) async-start(), calls=%async_computation | async-start | bytes 9437184 | tf_op jit(solution)/shard_map/all_gather | solution.py:1200
  7.2 35.8 %copy-start = (bf16[1,1024,3,512]{3,1,2,0:T(8,128)(2,1)S(1)}, bf16[1,1024,3,512]{3,1,2,0:T(8,128)(2,1)}, u32[]{:S(2)}) copy-start(bf16[1,1024,3,512]{3,1,2,0:T(8,128)(2,1)} %param.16) | copy-start | bytes 9437188
  8.7 26.3 %collective-permute-start.6 = (bf16[256,2048]{1,0:T(8,128)(2,1)S(1)}, bf16[256,2048]{1,0:T(8,128)(2,1)}, u32[]{:S(2)}, u32[]{:S(2)}) collective-permute-start(bf16[256,2048]{1,0:T(8,128)(2,1)S(1)} %constant_dynamic-slice_fusion.4), channel_id=1, source_target_pairs={{0,8},{8,0},{1,9},{9,1},{2,10},{10,2},{3,11},{11,3},{4,12},{12,4},... | collective-permute-start | bytes 3145736 | tf_op jit(solution)/shard_map/ppermute | solution.py:1175
  35.0 884.2 %all-reduce.2.cloned.1.call-start = ((), (), s32[]{:S(2)}) async-start(), calls=%async_computation.1 | async-start | bytes 131072 | tf_op jit(solution)/shard_map/psum | solution.py:1324
  35.1 24.3 %collective-permute-start.3 = (bf16[2,2560]{1,0:T(2,128)(2,1)S(1)}, bf16[2,2560]{1,0:T(2,128)(2,1)S(1)}, u32[]{:S(2)}, u32[]{:S(2)}) collective-permute-start(bf16[2,2560]{1,0:T(2,128)(2,1)S(1)} %pad_maximum_fusion.2), channel_id=1, source_target_pairs={{0,8},{8,0},{1,9},{9,1},{2,10},{10,2},{3,11},{11,3},{4,12},{12,4},... | collective-permute-start | bytes 30728 | tf_op jit(solution)/shard_map/ppermute | solution.py:1175
  38.8 21.0 %collective-permute-start.4 = (bf16[256,1024]{1,0:T(8,128)(2,1)}, bf16[256,1024]{1,0:T(8,128)(2,1)}, u32[]{:S(2)}, u32[]{:S(2)}) collective-permute-start(bf16[256,1024]{1,0:T(8,128)(2,1)} %dynamic-slice_bitcast_fusion.7), channel_id=1, source_target_pairs={{0,8},{8,0},{1,9},{9,1},{2,10},{10,2},{3,11},{11,3},{4,12},{12,4},... | collective-permute-start | bytes 1572872 | tf_op jit(solution)/shard_map/ppermute | solution.py:1175
  41.3 70.0 %collective-permute-start = (bf16[2,256,1024]{2,1,0:T(8,128)(2,1)}, bf16[2,256,1024]{2,1,0:T(8,128)(2,1)}, u32[]{:S(2)}, u32[]{:S(2)}) collective-permute-start(bf16[2,256,1024]{2,1,0:T(8,128)(2,1)} %constant_dynamic-slice_fusion.6), channel_id=1, source_target_pairs={{0,8},{8,0},{1,9},{9,1},{2,10},{10,2},{3,11},{11,3},{4,12},{12,4},... | collective-permute-start | bytes 3145736 | tf_op jit(solution)/shard_map/ppermute | solution.py:1175
  43.1 6.8 copy-start.34
  44.3 65.8 %collective-permute-start.1 = (bf16[1536,512]{1,0:T(8,128)(2,1)}, bf16[1536,512]{1,0:T(8,128)(2,1)}, u32[]{:S(2)}, u32[]{:S(2)}) collective-permute-start(bf16[1536,512]{1,0:T(8,128)(2,1)} %constant_dynamic-slice_fusion.5), channel_id=1, source_target_pairs={{0,8},{8,0},{1,9},{9,1},{2,10},{10,2},{3,11},{11,3},{4,12},{12,4},... | collective-permute-start | bytes 4718600 | tf_op jit(solution)/shard_map/ppermute | solution.py:1175
  44.6 12.7 %copy-start.9 = (bf16[4,256,1024]{2,1,0:T(8,128)(2,1)S(1)}, bf16[4,256,1024]{2,1,0:T(8,128)(2,1)}, u32[]{:S(2)}) copy-start(bf16[4,256,1024]{2,1,0:T(8,128)(2,1)} %param.13) | copy-start | bytes 6291460
  48.1 106.9 %collective-permute-start.7 = (bf16[512,2048]{1,0:T(8,128)(2,1)}, bf16[512,2048]{1,0:T(8,128)(2,1)}, u32[]{:S(2)}, u32[]{:S(2)}) collective-permute-start(bf16[512,2048]{1,0:T(8,128)(2,1)} %dynamic-slice_bitcast_fusion), channel_id=1, source_target_pairs={{0,8},{8,0},{1,9},{9,1},{2,10},{10,2},{3,11},{11,3},{4,12},{12,4},... | collective-permute-start | bytes 6291464 | tf_op jit(solution)/shard_map/ppermute | solution.py:1175
  49.8 8.2 copy-start.10
  55.0 3.2 copy-start.30
  55.0 3.2 copy-start.31
  55.0 3.8 copy-start.27
  55.0 3.8 copy-start.33
  59.4 115.6 %collective-permute-start.13 = (bf16[2,256,1024]{2,1,0:T(8,128)(2,1)}, bf16[2,256,1024]{2,1,0:T(8,128)(2,1)S(1)}, u32[]{:S(2)}, u32[]{:S(2)}) collective-permute-start(bf16[2,256,1024]{2,1,0:T(8,128)(2,1)} %constant_dynamic-slice_fusion.1), channel_id=1, source_target_pairs={{0,8},{8,0},{1,9},{9,1},{2,10},{10,2},{3,11},{11,3},{4,12},{12,4},... | collective-permute-start | bytes 3145736 | tf_op jit(solution)/shard_map/ppermute | solution.py:1175
  59.8 95.3 %collective-permute-start.5 = (bf16[256,1024]{1,0:T(8,128)(2,1)}, bf16[256,1024]{1,0:T(8,128)(2,1)S(1)}, u32[]{:S(2)}, u32[]{:S(2)}) collective-permute-start(bf16[256,1024]{1,0:T(8,128)(2,1)} %collective-permute-done.4), channel_id=1, source_target_pairs={{0,1},{1,0},{2,3},{3,2},{4,5},{5,4},{6,7},{7,6},{8,9},{9,8},{10,11... | collective-permute-start | bytes 1572872 | tf_op jit(solution)/shard_map/ppermute | solution.py:1178
  110.1 69.0 %collective-permute-start.2 = (bf16[1536,512]{1,0:T(8,128)(2,1)}, bf16[1536,512]{1,0:T(8,128)(2,1)S(1)}, u32[]{:S(2)}, u32[]{:S(2)}) collective-permute-start(bf16[1536,512]{1,0:T(8,128)(2,1)} %collective-permute-done.1), channel_id=1, source_target_pairs={{0,1},{1,0},{2,3},{3,2},{4,5},{5,4},{6,7},{7,6},{8,9},{9,8},{10,11... | collective-permute-start | bytes 4718600 | tf_op jit(solution)/shard_map/ppermute | solution.py:1178
  155.1 64.5 %collective-permute-start.8 = (bf16[512,2048]{1,0:T(8,128)(2,1)}, bf16[512,2048]{1,0:T(8,128)(2,1)}, u32[]{:S(2)}, u32[]{:S(2)}) collective-permute-start(bf16[512,2048]{1,0:T(8,128)(2,1)} %collective-permute-done.7), channel_id=1, source_target_pairs={{0,1},{1,0},{2,3},{3,2},{4,5},{5,4},{6,7},{7,6},{8,9},{9,8},{10,11... | collective-permute-start | bytes 6291464 | tf_op jit(solution)/shard_map/ppermute | solution.py:1178
  254.5 32.3 %collective-permute-start.9 = (bf16[512,1024]{1,0:T(8,128)(2,1)}, bf16[512,1024]{1,0:T(8,128)(2,1)S(1)}, u32[]{:S(2)}, u32[]{:S(2)}) collective-permute-start(bf16[512,1024]{1,0:T(8,128)(2,1)} %get-tuple-element.139.refs_18_), channel_id=1, source_target_pairs={{0,16},{1,17},{2,18},{3,19},{4,20},{5,21},{6,22},{7,23},{8,24},{9,... | collective-permute-start | bytes 3145736 | tf_op jit(solution)/shard_map/ppermute | solution.py:1250
  284.5 22.2 %collective-permute-start.11 = (bf16[512,1024]{1,0:T(8,128)(2,1)}, bf16[512,1024]{1,0:T(8,128)(2,1)}, u32[]{:S(2)}, u32[]{:S(2)}) collective-permute-start(bf16[512,1024]{1,0:T(8,128)(2,1)} %get-tuple-element.151.refs_10_), channel_id=1, source_target_pairs={{0,16},{1,17},{2,18},{3,19},{4,20},{5,21},{6,22},{7,23},{8,24},{9,... | collective-permute-start | bytes 3145736 | tf_op jit(solution)/shard_map/ppermute | solution.py:1250
  286.8 1.0 copy-start.2
  292.4 9.8 %copy-start.4 = (bf16[512,1024]{1,0:T(8,128)(2,1)S(1)}, bf16[512,1024]{1,0:T(8,128)(2,1)}, u32[]{:S(2)}) copy-start(bf16[512,1024]{1,0:T(8,128)(2,1)} %get-tuple-element.139.refs_18_) | copy-start | bytes 3145732
  311.2 9.7 %copy-start.7 = (bf16[512,1024]{1,0:T(8,128)(2,1)S(1)}, bf16[512,1024]{1,0:T(8,128)(2,1)}, u32[]{:S(2)}) copy-start(bf16[512,1024]{1,0:T(8,128)(2,1)} %get-tuple-element.151.refs_10_) | copy-start | bytes 3145732
  320.9 1.4 copy-start.8
  323.4 40.8 %collective-permute-start.10 = (bf16[256,1024]{1,0:T(8,128)(2,1)}, bf16[256,1024]{1,0:T(8,128)(2,1)}, u32[]{:S(2)}, u32[]{:S(2)}) collective-permute-start(bf16[256,1024]{1,0:T(8,128)(2,1)} %get-tuple-element.264), channel_id=1, source_target_pairs={{0,8},{8,0},{1,9},{9,1},{2,10},{10,2},{3,11},{11,3},{4,12},{12,4},... | collective-permute-start | bytes 1572872 | tf_op jit(solution)/shard_map/ppermute | solution.py:1175
  324.3 39.9 %collective-permute-start.12 = (bf16[256,1024]{1,0:T(8,128)(2,1)}, bf16[256,1024]{1,0:T(8,128)(2,1)}, u32[]{:S(2)}, u32[]{:S(2)}) collective-permute-start(bf16[256,1024]{1,0:T(8,128)(2,1)} %get-tuple-element.266), channel_id=1, source_target_pairs={{0,8},{8,0},{1,9},{9,1},{2,10},{10,2},{3,11},{11,3},{4,12},{12,4},... | collective-permute-start | bytes 1572872 | tf_op jit(solution)/shard_map/ppermute | solution.py:1175
  342.3 117.1 %collective-permute-start.14 = (bf16[512,1024]{1,0:T(8,128)(2,1)}, bf16[512,1024]{1,0:T(8,128)(2,1)}, u32[]{:S(2)}, u32[]{:S(2)}) collective-permute-start(bf16[512,1024]{1,0:T(8,128)(2,1)} %get-tuple-element.189), channel_id=1, source_target_pairs={{16,0},{17,1},{18,2},{19,3},{20,4},{21,5},{22,6},{23,7},{24,8},{25... | collective-permute-start | bytes 3145736 | tf_op jit(solution)/shard_map/ppermute | solution.py:1279
  353.5 8.9 copy-start.1
  360.9 1.6 copy-start.3
  360.9 1.6 copy-start.6
  360.9 158.1 %collective-permute-start.16 = (bf16[512,1024]{1,0:T(8,128)(2,1)}, bf16[512,1024]{1,0:T(8,128)(2,1)}, u32[]{:S(2)}, u32[]{:S(2)}) collective-permute-start(bf16[512,1024]{1,0:T(8,128)(2,1)} %get-tuple-element.211), channel_id=1, source_target_pairs={{16,0},{17,1},{18,2},{19,3},{20,4},{21,5},{22,6},{23,7},{24,8},{25... | collective-permute-start | bytes 3145736 | tf_op jit(solution)/shard_map/ppermute | solution.py:1279
  362.5 1.7 copy-start.11
  519.0 29.0 %copy-start.25 = (f32[8,1024]{1,0:T(8,128)S(1)}, f32[8,1024]{1,0:T(8,128)}, u32[]{:S(2)}) copy-start(f32[8,1024]{1,0:T(8,128)} %get-tuple-element.202.refs_14_) | copy-start | bytes 98308
  519.0 29.0 %copy-start.26 = (f32[8,1024]{1,0:T(8,128)S(1)}, f32[8,1024]{1,0:T(8,128)}, u32[]{:S(2)}) copy-start(f32[8,1024]{1,0:T(8,128)} %get-tuple-element.209.refs_14_) | copy-start | bytes 98308
  519.0 29.0 %copy-start.28 = (f32[8,1024]{1,0:T(8,128)S(1)}, f32[8,1024]{1,0:T(8,128)}, u32[]{:S(2)}) copy-start(f32[8,1024]{1,0:T(8,128)} %get-tuple-element.188.refs_11_) | copy-start | bytes 98308
  556.3 28.1 %copy-start.18 = (f32[8,1024]{1,0:T(8,128)S(1)}, f32[8,1024]{1,0:T(8,128)}, u32[]{:S(2)}) copy-start(f32[8,1024]{1,0:T(8,128)} %get-tuple-element.193.refs_16_) | copy-start | bytes 98308
  556.3 28.1 %copy-start.19 = (f32[8,1024]{1,0:T(8,128)S(1)}, f32[8,1024]{1,0:T(8,128)}, u32[]{:S(2)}) copy-start(f32[8,1024]{1,0:T(8,128)} %get-tuple-element.203.refs_16_) | copy-start | bytes 98308
  556.3 28.1 %copy-start.20 = (f32[8,1024]{1,0:T(8,128)S(1)}, f32[8,1024]{1,0:T(8,128)}, u32[]{:S(2)}) copy-start(f32[8,1024]{1,0:T(8,128)} %get-tuple-element.215.refs_16_) | copy-start | bytes 98308
  556.4 30.4 %copy-start.21 = (f32[8,4096]{1,0:T(8,128)S(1)}, f32[8,4096]{1,0:T(8,128)}, u32[]{:S(2)}) copy-start(f32[8,4096]{1,0:T(8,128)} %get-tuple-element.244) | copy-start | bytes 393220
  556.4 30.4 %copy-start.22 = (f32[8,4096]{1,0:T(8,128)S(1)}, f32[8,4096]{1,0:T(8,128)}, u32[]{:S(2)}) copy-start(f32[8,4096]{1,0:T(8,128)} %get-tuple-element.246) | copy-start | bytes 393220
  556.4 30.4 %copy-start.23 = (f32[8,4096]{1,0:T(8,128)S(1)}, f32[8,4096]{1,0:T(8,128)}, u32[]{:S(2)}) copy-start(f32[8,4096]{1,0:T(8,128)} %get-tuple-element.243) | copy-start | bytes 393220
  556.4 30.4 %copy-start.24 = (f32[8,4096]{1,0:T(8,128)S(1)}, f32[8,4096]{1,0:T(8,128)}, u32[]{:S(2)}) copy-start(f32[8,4096]{1,0:T(8,128)} %get-tuple-element.245) | copy-start | bytes 393220
  587.5 337.0 %collective-permute-start.17 = (bf16[256,1024]{1,0:T(8,128)(2,1)S(1)}, bf16[256,1024]{1,0:T(8,128)(2,1)}, u32[]{:S(2)}, u32[]{:S(2)}) collective-permute-start(bf16[256,1024]{1,0:T(8,128)(2,1)S(1)} %dynamic-slice_select_fusion.2), channel_id=1, source_target_pairs={{0,8},{8,0},{1,9},{9,1},{2,10},{10,2},{3,11},{11,3},{4,12},{12,4},... | collective-permute-start | bytes 1572872 | tf_op jit(solution)/shard_map/ppermute | solution.py:1175
  588.8 335.7 %collective-permute-start.15 = (bf16[256,1024]{1,0:T(8,128)(2,1)S(1)}, bf16[256,1024]{1,0:T(8,128)(2,1)}, u32[]{:S(2)}, u32[]{:S(2)}) collective-permute-start(bf16[256,1024]{1,0:T(8,128)(2,1)S(1)} %dynamic-slice_select_fusion.3), channel_id=1, source_target_pairs={{0,8},{8,0},{1,9},{9,1},{2,10},{10,2},{3,11},{11,3},{4,12},{12,4},... | collective-permute-start | bytes 1572872 | tf_op jit(solution)/shard_map/ppermute | solution.py:1175
  893.8 2.7 copy-start.13
  893.8 2.8 copy-start.12
  896.5 2.9 copy-start.5
  899.4 4.5 copy-start.14
  899.4 4.5 copy-start.16
  915.0 3.5 copy-start.15
  915.0 4.1 copy-start.17
Sparse Core Ops, SparseCore 0:
  35.1 83.5 all-gather.1
  587.6 84.3 all-reduce.1

commit v3 on v1

--- a/solution.py
+++ b/solution.py
@@ -466,44 +466,461 @@
     )
 
 
-def weight_grads(left, rights, seqs, name):
-    rows, depth = left.shape[1:]
-    width = rights[0].shape[2]
-    nt = 512
-    n = len(rights)
+MESH = pl.DeviceIdType.MESH
+CORE_LAG = 3
+CROSS_LAG = 3
+CHAIN_LAG = 2
+
+
+def arrived(ref, sem):
+    pltpu.make_async_copy(ref, ref, sem).wait()
+
+
+def neighbours():
+    t = lax.axis_index("tensor")
+    d = lax.axis_index("dp")
+    last = lax.axis_size("dp") // 2 - 1
+    c = lax.rem(d, 2)
+    z = d // 2
+    return t, c, z, last, {"dp": d + 1 - 2 * c}, {"tensor": 1 - t}, {"dp": d + 2}, {"dp": d - 2}
+
+
+def greet(c, z, chips, core, cross):
+    barrier = pltpu.get_barrier_semaphore()
+    pl.semaphore_signal(barrier, inc=1, device_id=core, device_id_type=MESH)
+    pl.semaphore_signal(barrier, inc=1, device_id=cross, device_id_type=MESH)
+    for shift in range(1, chips):
+        chip = lax.rem(z + shift, chips)
+        pl.semaphore_signal(barrier, inc=1, device_id={"dp": chip * 2 + c}, device_id_type=MESH)
+    pl.semaphore_wait(barrier, 1 + chips)
+
+
+def fetch_other_half(qkv, out, up, down, held, chips):
+    weights = [qkv, out, up, down]
+    seqs = held.shape[0] // 2
+    shard_rows = held.shape[1]
+    groups = 2 * chips
+
+    def rows_of(item):
+        return weights[item].shape[0]
+
+    plan = []
+    up_piece = rows_of(2) // groups
+    parts = 4
+    for part in range(parts):
+        plan.append((2, True, 0, up_piece, part * up_piece // parts, up_piece // parts))
+    spread = rows_of(3) // 2
+    plan.append((3, True, 0, spread // groups, 0, spread // groups))
+    n_spread = len(plan)
+    plan.append((-1, False, 0, 0, 0, 0))
+    for part in range(3):
+        size = rows_of(0) // 6
+        plan.append((0, False, 0, rows_of(0) // 2, part * size, size))
+    plan.append((1, False, 0, rows_of(1) // 2, 0, rows_of(1) // 2))
+    plan.append((-1, False, 0, 0, 0, 1))
+    direct = (rows_of(3) - spread) // 2
+    for part in range(2):
+        plan.append((3, False, spread, direct, part * direct // 2, direct // 2))
+    n = len(plan)
 
     def kernel(*refs):
-        left_ref, ins, outs, flip_ref = refs[0], refs[1 : 1 + n], refs[1 + n : 1 + 2 * n], refs[1 + 2 * n]
-
-        @pl.when(pl.program_id(0) == 0)
-        def _():
-            for s in range(seqs):
-                flip_ref[:, s * rows : (s + 1) * rows] = left_ref[s].T
-
-        for a, b in zip(ins, outs):
-            total = dot(flip_ref[:, :rows], a[0])
-            for s in range(1, seqs):
-                total += dot(flip_ref[:, s * rows : (s + 1) * rows], a[s])
-            b[...] = total.astype(BF)
-
+        ins, held_ref = refs[:4], refs[4]
+        outs, rows_ref = refs[5:9], refs[9]
+        stage, x_send, x_recv, c_send, c_recv, u_send, u_recv, d_send, d_recv, l_sem = refs[10:]
+        t, c, z, last, core, cross, above, below = neighbours()
+        greet(c, z, chips, core, cross)
+
+        def rows(index, chip, on):
+            item, is_spread, base, piece, offset, size = plan[index]
+            place = chip * 2 + on if is_spread else on
+            return item, pl.ds(pl.multiple_of(base + place * piece + offset, size), size)
+
+        def cross_copy(index):
+            if plan[index][0] < 0:
+                m = plan[index][5]
+                src = held_ref.at[(1 - t) * seqs + m]
+                dst = rows_ref.at[m, pl.ds(pl.multiple_of(t * shard_rows, shard_rows), shard_rows)]
+            else:
+                item, where = rows(index, z, c)
+                src, dst = ins[item].at[where], outs[item].at[where]
+            return pltpu.make_async_remote_copy(
+                src_ref=src, dst_ref=dst, send_sem=x_send.at[index], recv_sem=x_recv.at[index],
+                device_id=cross, device_id_type=MESH,
+            )
+
+        def pass_on(index, chip, send, recv, device):
+            item, where = rows(index, chip, c)
+            place = outs[item].at[where]
+            return pltpu.make_async_remote_copy(
+                src_ref=place, dst_ref=place, send_sem=send.at[index, chip], recv_sem=recv.at[index, chip],
+                device_id=device, device_id_type=MESH,
+            )
+
+        def got(index, chip, on, sem):
+            item, where = rows(index, chip, on)
+            arrived(outs[item].at[where], sem)
+
+        for index in range(n):
+            cross_copy(index).start()
+        mine = pltpu.make_async_copy(held_ref.at[pl.ds(t * seqs, seqs)], stage, l_sem)
+        mine.start()
+        mine.wait()
+        for m in range(seqs):
+            pltpu.make_async_copy(
+                stage.at[m], rows_ref.at[m, pl.ds(pl.multiple_of(t * shard_rows, shard_rows), shard_rows)], l_sem
+            ).start()
+
+        def handle(index, hop):
+            if hop == 0:
+                if plan[index][0] < 0:
+                    m = plan[index][5]
+                    arrived(
+                        rows_ref.at[m, pl.ds(pl.multiple_of((1 - t) * shard_rows, shard_rows), shard_rows)],
+                        x_recv.at[index],
+                    )
+                    return
+                got(index, z, c, x_recv.at[index])
+                pass_on(index, z, c_send, c_recv, core).start()
+                if plan[index][1]:
+                    @pl.when(z < last)
+                    def _():
+                        pass_on(index, z, u_send, u_recv, above).start()
+
+                    @pl.when(z > 0)
+                    def _():
+                        pass_on(index, z, d_send, d_recv, below).start()
+                return
+
+            @pl.when(z - hop >= 0)
+            def _():
+                got(index, z - hop, c, u_recv.at[index, z - hop])
+
+                @pl.when(z < last)
+                def _():
+                    pass_on(index, z - hop, u_send, u_recv, above).start()
+
+                pass_on(index, z - hop, c_send, c_recv, core).start()
+
+            @pl.when(z + hop <= last)
+            def _():
+                got(index, z + hop, c, d_recv.at[index, z + hop])
+
+                @pl.when(z > 0)
+                def _():
+                    pass_on(index, z + hop, d_send, d_recv, below).start()
+
+                pass_on(index, z + hop, c_send, c_recv, core).start()
+
+        for round_ in range(max(n, n_spread + chips - 1)):
+            if round_ < n:
+                handle(round_, 0)
+            for hop in range(1, chips):
+                if 0 <= round_ - hop < n_spread:
+                    handle(round_ - hop, hop)
+
+        for m in range(seqs):
+            arrived(stage.at[m], l_sem)
+        for index in range(n):
+            item, is_spread = plan[index][:2]
+            cross_copy(index).wait_send()
+            if item < 0:
+                continue
+            if not is_spread:
+                got(index, z, 1 - c, c_recv.at[index, z])
+                pass_on(index, z, c_send, c_recv, core).wait_send()
+                continue
+            for chip in range(chips):
+                got(index, chip, 1 - c, c_recv.at[index, chip])
+                pass_on(index, chip, c_send, c_recv, core).wait_send()
+
+                @pl.when((chip <= z) & (z < last))
+                def _(chip=chip):
+                    pass_on(index, chip, u_send, u_recv, above).wait_send()
+
+                @pl.when((chip >= z) & (z > 0))
+                def _(chip=chip):
+                    pass_on(index, chip, d_send, d_recv, below).wait_send()
+
+    sem = pltpu.SemaphoreType.DMA
+    moved = sum(w.size for w in weights) * 2
     return pl.pallas_call(
         kernel,
-        grid=(width // nt,),
-        in_specs=[pl.BlockSpec((seqs, rows, depth), lambda j: (0, 0, 0), pipeline_mode=pl.Buffered(1))]
-        + [pl.BlockSpec((seqs, rows, nt), lambda j: (0, 0, j))] * n,
-        out_specs=[pl.BlockSpec((depth, nt), lambda j: (0, j))] * n,
-        out_shape=[jax.ShapeDtypeStruct((depth, width), BF)] * n,
-        scratch_shapes=[pltpu.VMEM((depth, seqs * rows), BF)],
+        in_specs=[ANY] * 5,
+        out_specs=[ANY] * 5,
+        out_shape=[jax.ShapeDtypeStruct(w.shape, BF) for w in weights]
+        + [jax.ShapeDtypeStruct((seqs, 2 * shard_rows, held.shape[2]), BF)],
+        scratch_shapes=[pltpu.VMEM((seqs,) + held.shape[1:], BF)]
+        + [sem((n,)), sem((n,))]
+        + [sem((n, chips))] * 6
+        + [sem],
+        compiler_params=pltpu.CompilerParams(collective_id=1, has_side_effects=True),
+        cost_estimate=pl.CostEstimate(flops=0, bytes_accessed=2 * moved, transcendentals=0),
+        name="fetch_other_half",
+    )(*weights, held)
+
+
+def weight_grads_reduced(groups, sums, chips):
+    seqs = 2
+    rows, depth = groups[0][0].shape[1:]
+    lefts = [g[0] for g in groups]
+    rights = [r for g in groups for r in g[1]]
+    bt = 128
+    half = depth // 2
+    quarter = half // 2
+    blocks = [r.shape[2] // (2 * bt) for r in rights]
+    starts = [sum(blocks[:index]) for index in range(len(rights))]
+    total = sum(blocks)
+    group_starts = []
+    index = 0
+    for _, members in groups:
+        group_starts.append(starts[index])
+        index += len(members)
+    n_left, n_right = len(lefts), len(rights)
+    tiles, mines, gives = 4, CORE_LAG + 1, 4
+    last_static = chips - 1
+    drain = CORE_LAG + CROSS_LAG + 2 * last_static * CHAIN_LAG + 1
+    vec_shape = sums.shape
+
+    def kernel(*refs):
+        left_refs = refs[:n_left]
+        right_refs = refs[n_left : n_left + n_right]
+        sums_ref = refs[n_left + n_right]
+        outs = refs[n_left + n_right + 1 : n_left + 2 * n_right + 1]
+        sums_out = refs[n_left + 2 * n_right + 1]
+        (
+            acc, from_x, from_z, final, flip, stage, tile, mine, give, vec, vec_in, vec_all,
+            tile_sem, stage_sem, give_send, core_recv, x_send, x_recv, z_send, z_recv, f_send, f_recv,
+            store_sem, out_send, out_recv, v_load, v_send, v_recv,
+        ) = refs[n_left + 2 * n_right + 2 :]
+        t, c, z, last, core, cross, above, below = neighbours()
+        greet(c, z, chips, core, cross)
+
+        def remote(src, dst, send, recv, device):
+            return pltpu.make_async_remote_copy(
+                src_ref=src, dst_ref=dst, send_sem=send, recv_sem=recv, device_id=device, device_id_type=MESH
+            )
+
+        def valid(k):
+            return (k >= 0) & (k < total)
+
+        def member(k, visit):
+            for m in range(n_right):
+                @pl.when((k >= starts[m]) & (k < starts[m] + blocks[m]))
+                def _(m=m):
+                    visit(m, k - starts[m])
+
+        def load_tile(k):
+            slot = lax.rem(k, tiles)
+
+            def visit(m, j):
+                for side in range(2):
+                    at = pl.multiple_of((side * blocks[m] + j) * bt, bt)
+                    pltpu.make_async_copy(
+                        right_refs[m].at[pl.ds(0, seqs), :, pl.ds(at, bt)],
+                        tile.at[slot, :, :, pl.ds(side * bt, bt)],
+                        tile_sem.at[slot],
+                    ).start()
+
+            member(k, visit)
+
+        def load_left(g):
+            return pltpu.make_async_copy(left_refs[g].at[pl.ds(0, seqs)], stage, stage_sem)
+
+        vec_load = pltpu.make_async_copy(sums_ref, vec.at[0], v_load)
+        vec_load.start()
+        load_left(0).start()
+        for k in range(tiles - 1):
+            load_tile(jnp.int32(k))
+        vec_load.wait()
+        vec_core = remote(vec.at[0], vec_in.at[0], v_send.at[0], v_recv.at[0], core)
+        vec_cross = remote(vec.at[1], vec_in.at[1], v_send.at[1], v_recv.at[1], cross)
+        vec_core.start()
+
+        up = pl.ds(0, quarter)
+        down = pl.ds(quarter, quarter)
+        sides = ((up, 0, z, above, below), (down, 1, last - z, below, above))
+
+        @pl.loop(0, total + drain)
+        def _(s):
+            @pl.when(valid(s))
+            def _():
+                for g in range(n_left):
+                    @pl.when(s == group_starts[g])
+                    def _(g=g):
+                        load_left(g).wait()
+                        for m in range(seqs):
+                            flip[:, m * rows : (m + 1) * rows] = stage[m].T
+                        if g + 1 < n_left:
+                            load_left(g + 1).start()
+
+                slot = lax.rem(s, tiles)
+                arrived(tile.at[slot], tile_sem.at[slot])
+                give_slot = lax.rem(s, gives)
+
+                @pl.when(s >= gives)
+                def _():
+                    arrived(give.at[give_slot], give_send.at[give_slot])
+
+                for place, ring, at in ((1 - c, give, give_slot), (c, mine, lax.rem(s, mines))):
+                    here = pl.ds(pl.multiple_of(place * half, half), half)
+                    block = dot(flip[here, :rows], tile[slot, 0])
+                    for m in range(1, seqs):
+                        block += dot(flip[here, m * rows : (m + 1) * rows], tile[slot, m])
+                    ring[at, 1] = block[:, :bt].astype(BF)
+                    ring[at, 0] = block[:, bt:].astype(BF)
+
+            @pl.when(s + tiles - 1 < total)
+            def _():
+                load_tile(s + tiles - 1)
+
+            k1 = s - CORE_LAG
+
+            @pl.when(valid(k1))
+            def _():
+                arrived(acc.at[k1], core_recv.at[k1])
+                at = lax.rem(k1, mines)
+                for side in range(2):
+                    acc[k1, side] = (acc[k1, side].astype(F32) + mine[at, side].astype(F32)).astype(BF)
+
+            k2 = k1 - CROSS_LAG
+
+            @pl.when(valid(k2))
+            def _():
+                arrived(from_x.at[k2], x_recv.at[k2])
+                acc[k2, 1] = (acc[k2, 1].astype(F32) + from_x[k2].astype(F32)).astype(BF)
+
+            for span, way, place, ahead, behind in sides:
+                k3 = k2 - CHAIN_LAG * place
+
+                @pl.when(valid(k3) & (place > 0))
+                def _(span=span, way=way, k3=k3):
+                    arrived(from_z.at[k3, span], z_recv.at[way, k3])
+                    acc[k3, 1, span] = (acc[k3, 1, span].astype(F32) + from_z[k3, span].astype(F32)).astype(BF)
+
+                k4 = k2 - CHAIN_LAG * (2 * last - place)
+
+                @pl.when(valid(k4) & (place == last))
+                def _(span=span, k4=k4):
+                    final[k4, span] = acc[k4, 1, span]
+
+                @pl.when(valid(k4) & (place < last))
+                def _(span=span, way=way, k4=k4):
+                    arrived(final.at[k4, span], f_recv.at[way, k4])
+
+            @pl.when(valid(s))
+            def _():
+                at = lax.rem(s, gives)
+                remote(give.at[at], acc.at[s], give_send.at[at], core_recv.at[s], core).start()
+
+            @pl.when(valid(k1))
+            def _():
+                remote(acc.at[k1, 0], from_x.at[k1], x_send, x_recv.at[k1], cross).start()
+
+            for span, way, place, ahead, behind in sides:
+                k3 = k2 - CHAIN_LAG * place
+
+                @pl.when(valid(k3) & (place < last))
+                def _(span=span, way=way, k3=k3, ahead=ahead):
+                    remote(acc.at[k3, 1, span], from_z.at[k3, span], z_send.at[way], z_recv.at[way, k3], ahead).start()
+
+                k4 = k2 - CHAIN_LAG * (2 * last - place)
+
+                @pl.when(valid(k4) & (place > 0))
+                def _(span=span, way=way, k4=k4, behind=behind):
+                    remote(final.at[k4, span], final.at[k4, span], f_send.at[way], f_recv.at[way, k4], behind).start()
+
+            k5 = k2 - CHAIN_LAG * 2 * last
+
+            @pl.when(valid(k5))
+            def _():
+                def visit(m, j):
+                    dst = outs[m].at[
+                        pl.ds(pl.multiple_of(c * half, half), half), pl.ds(pl.multiple_of(j * bt, bt), bt)
+                    ]
+                    pltpu.make_async_copy(final.at[k5], dst, store_sem).start()
+                    remote(final.at[k5], dst, out_send, out_recv, core).start()
+
+                member(k5, visit)
+
+            @pl.when(s == 4)
+            def _():
+                vec_core.wait_recv()
+                vec[1] = vec[0] + vec_in[0]
+
+            @pl.when(s == 5)
+            def _():
+                vec_cross.start()
+
+            @pl.when(s == 10)
+            def _():
+                vec_cross.wait_recv()
+                vec_all[z] = vec[1] + vec_in[1]
+
+            @pl.when(s == 11)
+            def _():
+                for shift in range(1, chips):
+                    to = lax.rem(z + shift, chips)
+                    remote(
+                        vec_all.at[z], vec_all.at[z], v_send.at[1 + shift], v_recv.at[1 + shift], {"dp": to * 2 + c}
+                    ).start()
+
+        vec_core.wait_send()
+        vec_cross.wait_send()
+        for shift in range(1, chips):
+            origin = lax.rem(z + chips - shift, chips)
+            arrived(vec_all.at[origin], v_recv.at[1 + shift])
+            arrived(vec_all.at[z], v_send.at[1 + shift])
+        whole = vec_all[0]
+        for chip in range(1, chips):
+            whole += vec_all[chip]
+        sums_out[...] = whole
+        for at in range(gives):
+            arrived(give.at[at], give_send.at[at])
+        arrived(acc.at[:, 0], x_send)
+        for span, way, place, ahead, behind in sides:
+            @pl.when(place < last)
+            def _(span=span, way=way):
+                arrived(from_z.at[:, span], z_send.at[way])
+
+            @pl.when(place > 0)
+            def _(span=span, way=way):
+                arrived(final.at[:, span], f_send.at[way])
+
+        arrived(final, out_send)
+        arrived(final, store_sem)
+        arrived(final, out_recv)
+
+    sem = pltpu.SemaphoreType.DMA
+    flops = 2 * seqs * rows * depth * 2 * bt * total
+    return pl.pallas_call(
+        kernel,
+        in_specs=[ANY] * (n_left + n_right + 1),
+        out_specs=[ANY] * n_right + [pl.BlockSpec(memory_space=pltpu.VMEM)],
+        out_shape=[jax.ShapeDtypeStruct((depth, r.shape[2] // 2), BF) for r in rights]
+        + [jax.ShapeDtypeStruct(vec_shape, F32)],
+        scratch_shapes=[
+            pltpu.VMEM((total, 2, half, bt), BF),
+            pltpu.VMEM((total, half, bt), BF),
+            pltpu.VMEM((total, half, bt), BF),
+            pltpu.VMEM((total, half, bt), BF),
+            pltpu.VMEM((depth, seqs * rows), BF),
+            pltpu.VMEM((seqs, rows, depth), BF),
+            pltpu.VMEM((tiles, seqs, rows, 2 * bt), BF),
+            pltpu.VMEM((mines, 2, half, bt), BF),
+            pltpu.VMEM((gives, 2, half, bt), BF),
+            pltpu.VMEM((2,) + vec_shape, F32),
+            pltpu.VMEM((2,) + vec_shape, F32),
+            pltpu.VMEM((chips,) + vec_shape, F32),
+            sem((tiles,)), sem, sem((gives,)), sem((total,)), sem, sem((total,)),
+            sem((2,)), sem((2, total)), sem((2,)), sem((2, total)),
+            sem, sem, sem, sem, sem((chips + 1,)), sem((chips + 1,)),
+        ],
         compiler_params=pltpu.CompilerParams(
-            dimension_semantics=("arbitrary",), vmem_limit_bytes=VMEM_LIMIT
+            collective_id=0, has_side_effects=True, vmem_limit_bytes=VMEM_LIMIT
         ),
-        cost_estimate=pl.CostEstimate(
-            flops=2 * seqs * rows * depth * width * n,
-            bytes_accessed=(seqs * rows + depth) * width * n * 2,
-            transcendentals=0,
-        ),
-        name=name,
-    )(left, *rights)
+        cost_estimate=pl.CostEstimate(flops=flops, bytes_accessed=64 << 20, transcendentals=0),
+        name="weight_grads_reduced",
+    )(*lefts, *rights, sums)
 
 
 MASKED = -1000000000.0
@@ -943,27 +1360,16 @@
     place = lax.axis_index("tensor")
     section = lax.axis_index("section")
     groups = lax.axis_size("dp")
-    group = lax.axis_index("dp")
-    core = group % 2
     rows = 2 * shard_rows
     seqs = batches // 2
     slots = seqs + 1
     local = w_qkv.shape[3]
     units = w_up.shape[3]
     heads = local // HD
-    pair = [(index, index ^ 1) for index in range(groups)]
+    chips = groups // 2
 
     def across(value):
         return lax.ppermute(value, "tensor", [(0, 1), (1, 0)])
-
-    def partner(value):
-        return lax.ppermute(value, "dp", pair)
-
-    def whole_rows(value):
-        mine = lax.dynamic_slice_in_dim(value, place * seqs, seqs, 0)
-        sent = lax.dynamic_slice_in_dim(value, (1 - place) * seqs, seqs, 0)
-        got = across(sent)
-        return [join(mine[m], got[m], place == 1) for m in range(seqs)]
 
     def own_rows(values, low):
         kept = [lax.dynamic_slice_in_dim(v, place * shard_rows, shard_rows, 0) for v in values]
@@ -971,27 +1377,23 @@
         got = [across(v) for v in sent]
         return join(jnp.stack(kept), jnp.stack(got).astype(values[0].dtype), place == 1)
 
-    def fetch(weight):
-        half = weight.shape[0] // 2
-        got = across(lax.dynamic_slice_in_dim(weight, core * half, half, 0))
-        return join(got, partner(got), core == 1)
-
-    def fetch_wide(weight):
-        part = weight.shape[0] // groups
-        got = across(lax.dynamic_slice_in_dim(weight, group * part, part, 0))
-        return lax.all_gather(got, "dp", axis=0, tiled=True)
-
     qkv_own = jnp.transpose(w_qkv[0], (1, 0, 2))
     out_own = w_out[0]
     up_own = w_up[0]
     down_own = w_down[0]
-    x_first = whole_rows(inputs)
     small = across(jnp.concatenate([b_qv[0], b_up[0]], axis=1))
-    qkv_oth = fetch(qkv_own.reshape(3 * width, local)).reshape(3, width, local)
-    out_oth = fetch(out_own)
-    up_oth = fetch_wide(up_own.reshape(2 * width, units)).reshape(2, width, units)
-    down_oth = fetch(down_own)
-    outer = whole_rows(cotangent)
+    first = section == 0
+    qkv_oth, out_oth, up_oth, down_oth, held = fetch_other_half(
+        qkv_own.reshape(3 * width, local),
+        out_own,
+        up_own.reshape(2 * width, units),
+        down_own,
+        jnp.where(first, inputs, cotangent),
+        chips,
+    )
+    qkv_oth = qkv_oth.reshape(3, width, local)
+    up_oth = up_oth.reshape(2, width, units)
+    x_first = outer = [held[m] for m in range(seqs)]
 
     bias = jnp.concatenate([b_qv[0], small[:, :local]], axis=1).astype(F32)
     up_bias = jnp.concatenate([b_up[0], small[:, local:]], axis=1).astype(F32)
@@ -1061,30 +1463,15 @@
     grad_middle = [lax.ppermute(gx_second[m][1], "section", [(1, 0)]) for m in range(seqs)]
     gx_first = [back(grad_middle[m], m, 0) for m in range(seqs)]
 
-    first = section == 0
     hidden, normed = ffn[2], ffn[3]
     mixed = att[3]
     x_all = jnp.stack([jnp.where(first, x_first[m], x_second[m]) for m in range(seqs)])
     gg0, gg1, gl, ga = bff
-    d_up = weight_grads(normed, [gg0, gg1], seqs, "grad_up")
-    (d_down,) = weight_grads(gl, [hidden], seqs, "grad_down")
-    d_qkv = weight_grads(x_all, bat, seqs, "grad_qkv")
-    (d_out,) = weight_grads(mixed, [ga], seqs, "grad_out")
-
     produced = own_rows(*[[jnp.where(first, a, b) for a, b in zip(y_first, y_second)]] * 2)
     grads_in = own_rows(
         [jnp.where(first, a[0], b[0]) for a, b in zip(gx_first, gx_second)],
         [jnp.where(first, a[1], b[1]) for a, b in zip(gx_first, gx_second)],
     )
-
-    def reduce_columns(grad, count):
-        total = grad[:, :count] + across(grad[:, count:])
-        return lax.psum(total, "dp").astype(F32)
-
-    up_sum = jnp.stack([reduce_columns(g, units) for g in d_up])
-    down_sum = reduce_columns(d_down, units)
-    qkv_sum = jnp.stack([reduce_columns(g, local) for g in d_qkv], axis=1)
-    out_sum = lax.psum(d_out[:local] + across(d_out[local:]), "dp").astype(F32)
 
     picked = [
         sum(jnp.where(first, sums[0][m][index], sums[1][m][index]) for m in range(seqs))
@@ -1095,15 +1482,19 @@
     def ordered(values, count):
         return jnp.where(
             place == 0, values, jnp.concatenate([values[:, count:], values[:, :count]], axis=1)
-        )
-
-    packed = jnp.concatenate(
-        [norm_sums[:6].reshape(-1), ordered(up_sums[:2], units).reshape(-1), ordered(qv_sums[:2], local).reshape(-1)]
-    )
-    packed = lax.psum(packed, ("tensor", "dp"))
-    norm_total = packed[: 6 * width].reshape(6, width)
-    up_total = packed[6 * width : 6 * width + 4 * units].reshape(2, 2 * units)
-    qv_total = packed[6 * width + 4 * units :].reshape(2, 2 * local)
+        ).reshape(-1, width)
+
+    packed = jnp.concatenate([norm_sums[:6], ordered(up_sums[:2], units), ordered(qv_sums[:2], local)])
+    down_sum, *up_sum, sum_q, sum_k, sum_v, out_sum, packed = weight_grads_reduced(
+        [(gl, [hidden]), (normed, [gg0, gg1]), (x_all, bat), (ga, [mixed])], packed, chips
+    )
+    up_sum = jnp.stack(up_sum).astype(F32)
+    down_sum = down_sum.astype(F32)
+    qkv_sum = jnp.stack([sum_q, sum_k, sum_v], axis=1).astype(F32)
+    out_sum = out_sum.T.astype(F32)
+    norm_total = packed[:6]
+    up_total = packed[6 : 6 + 4 * units // width].reshape(2, 2 * units)
+    qv_total = packed[6 + 4 * units // width :].reshape(2, 2 * local)
     up_bias_sum = lax.dynamic_slice_in_dim(up_total, place * units, units, 1)
     qv_sum = lax.dynamic_slice_in_dim(qv_total, place * local, local, 1)
     gain_sum = jnp.stack([norm_total[3], norm_total[0]])

time: 1350 us -> 819 us (0.61)
  waiting for transfers between devices: 835 us -> 104 us
  Pallas kernels: 324 us -> 622 us
  other arithmetic: 89.8 us -> 52.3 us
  local copies, waits for them, and re-layouts: 44 us -> 17.9 us
  starting transfers between devices: 27.3 us -> 13.5 us
    ppermute x18 -> x5, waiting for transfers between devices: 450 us -> 0.01 us  [across(): return lax.ppermute(value, 'tensor', [(0, 1), (1, 0)])]
    pallas_call x4 -> x2, Pallas kernels: 56.1 us -> 353 us  [the longest x1 226 us: weight_grads_reduced(): pl.pallas_call(kernel, in_specs=[ANY] * (n_left + n_right + 1), out_specs...]
    psum x2 -> x0, waiting for transfers between devices: 285 us -> none  [the longest x1 285 us: reduce_columns(): return lax.psum(total, 'dp').astype(F32)]
    slice x10 -> x2, local copies, waits for them, and re-layouts: 20.5 us -> 1.7 us  [the longest x1 0.85 us: by_sequence(): qv_total = packed[6 + 4 * units // width:].reshape(2, 2 * local)]
    another operation x5 -> x0, other arithmetic: 17.4 us -> none  [the longest x2 9.81 us: by_sequence(): up_sum = jnp.stack([reduce_columns(g, units) for g in d_up])]
    select_n x6 -> x2, other arithmetic: 19.9 us -> 5.5 us  [join(): jnp.where(swapped, jnp.concatenate([second, first], axis=0), jnp.concaten...]
    broadcast_in_dim x2 -> x0, other arithmetic: 14 us -> none  [the longest x1 9.58 us: by_sequence(): up_sum[None]]
    ppermute x18 -> x5, starting transfers between devices: 20.7 us -> 7.07 us  [across(): return lax.ppermute(value, 'tensor', [(0, 1), (1, 0)])]
  transfers between devices with their start and end apart: 28 -> 9, of which waited for: 14 -> 3; matrix products, arithmetic and copies ran while one was open for 8% -> 6% of each run, Pallas kernels for 17% -> 32%
where the time goes in v3:
time: 819 us; the launch traced here: 811 us
  Pallas kernels  622 us (76%)
  waiting for transfers between devices  104 us (13%)
  other arithmetic  52.3 us (6%)
  local copies, waits for them, and re-layouts  17.9 us (2%)
  starting transfers between devices  13.5 us (2%)
    pallas_call x16, Pallas kernels, call(): pl.pallas_call(body, grid_spec=pltpu.PrefetchScalarGridSpec(num_scalar_pr...  269 us
    pallas_call x1, Pallas kernels, weight_grads_reduced(): pl.pallas_call(kernel, in_specs=[ANY] * (n_left + n_right + 1), out_specs...  226 us
    pallas_call x1, Pallas kernels, fetch_other_half(): pl.pallas_call(kernel, in_specs=[ANY] * 5, out_specs=[ANY] * 5, out_shape...  127 us
    ppermute x2, waiting for transfers between devices, by_sequence(): lax.ppermute(gx_second[m][1], 'section', [(1, 0)])  97.7 us
  transfers between devices with their start and end apart: 9, of which 3 were waited for; matrix products, arithmetic and copies ran while one was open for 6% of the time, Pallas kernels for 32%

profile of v3, /device:TPU:0, one launch (start us, length us, event | category | flops | bytes accessed | tf_op | source)
XLA Modules:
  0.0 811.4 jit_solution(5626645826678273407)
XLA Ops:
  0.6 0.7 pad_maximum_fusion.2
  1.4 3.0 collective-permute-start
  4.4 0.7 dynamic_slice.33
  5.7 3.1 broadcast_select_fusion.refs_4_
  8.8 127.5 %fetch_other_half.1 = (bf16[3072,512]{1,0:T(8,128)(2,1)}, bf16[512,1024]{1,0:T(8,128)(2,1)}, bf16[2048,2048]{1,0:T(8,128)(2,1)}, bf16[1024,2048]{1,0:T(8,128)(2,1)}, bf16[2,512,1024]{2,1,0:T(8,128)(2,1)}) custom-call(bf16[3072,512]{1,0:T(8,128)(2,1)} %bitcast.108, bf16[512,1024]{1,0:T(8,128)(2,1)} %bitcast.125, bf16[2048,2048]{1,0:T(8,128)(2,1)} %bitcast.82, ...), custom_call_target="tpu_custom_call" | custom-call | bytes 33554432 | tf_op jit(solution)/shard_map/fetch_other_half/pallas_call | solution.py:646
  136.3 3.0 slice_bitcast_fusion.1
  139.4 1.3 iota_compare_fusion
  140.7 1.9 add_add_fusion
  142.6 2.0 add_add_fusion.2
  145.2 0.6 convert_element_type.60.refs_8_.refs_11_
  145.9 0.6 maximum_convert_fusion.3.refs_3_
  146.5 17.7 %attention_forward.4 = (bf16[3,512,1024]{2,1,0:T(8,128)(2,1)}, bf16[3,512,1024]{2,1,0:T(8,128)(2,1)}, bf16[3,512,1024]{2,1,0:T(8,128)(2,1)}, bf16[3,512,1024]{2,1,0:T(8,128)(2,1)}, f32[3,4,8,512]{3,2,1,0:T(8,128)}) custom-call(s32[3]{0:T(128)} %get-tuple-element.292.meta_ref, bf16[512,1024]{1,0:T(8,128)(2,1)} %get-tuple-element.270.refs_0_, ...), custom_call_target="tpu_custom_call" | custom-call | flops 4294967296 | bytes 12582912 | tf_op jit(solution)/shard_map/attention_forward/pallas_call | solution.py:46
  164.2 1.6 copy.90.refs_9_
  165.9 0.6 maximum_convert_fusion.2.refs_9_
  166.5 18.1 %attention_forward.5 = (bf16[3,512,1024]{2,1,0:T(8,128)(2,1)}, bf16[3,512,1024]{2,1,0:T(8,128)(2,1)}, bf16[3,512,1024]{2,1,0:T(8,128)(2,1)}, bf16[3,512,1024]{2,1,0:T(8,128)(2,1)}, f32[3,4,8,512]{3,2,1,0:T(8,128)}) custom-call(s32[3]{0:T(128)} %get-tuple-element.293.meta_ref, ...), custom_call_target="tpu_custom_call", output_to_operand_aliasing={{0}: (6, {}), {1}: (7, {}), {2}: (8, {}), {3}: (9, {}), {4}... | custom-call | flops 4294967296 | bytes 12582912 | tf_op jit(solution)/shard_map/attention_forward/pallas_call | solution.py:46
  184.6 28.6 %ffn_forward.4 = (bf16[3,512,4096]{2,1,0:T(8,128)(2,1)}, bf16[3,512,4096]{2,1,0:T(8,128)(2,1)}, bf16[3,512,4096]{2,1,0:T(8,128)(2,1)}, bf16[3,512,1024]{2,1,0:T(...) custom-call(s32[3]{0:T(128)} %get-tuple-element.292.meta_ref, ...), custom_call_target="tpu_custom_call" | custom-call | flops 13958643712 | bytes 47185920 | tf_op jit(solution)/shard_map/ffn_forward/pallas_call | solution.py:46
  213.3 1.4 collective-permute-start.1
  214.6 28.6 %ffn_forward.5 = (bf16[3,512,4096]{2,1,0:T(8,128)(2,1)}, bf16[3,512,4096]{2,1,0:T(8,128)(2,1)}, bf16[3,512,4096]{2,1,0:T(8,128)(2,1)}, bf16[3,512,1024]{2,1,0:T(...) custom-call(s32[3]{0:T(128)} %get-tuple-element.293.meta_ref, ...), custom_call_target="tpu_custom_call", output_to_operand_aliasing={{0}: (11, {}), {1}: (12, {}), {2}: (13, {}), {3}: (14, {}),... | custom-call | flops 13958643712 | bytes 47185920 | tf_op jit(solution)/shard_map/ffn_forward/pallas_call | solution.py:46
  243.2 2.3 collective-permute-start.3
  245.6 1.0 copy-done
  246.5 4.6 attention_forward.6
  251.1 9.6 %ffn_forward.6 = (bf16[3,512,4096]{2,1,0:T(8,128)(2,1)}, bf16[3,512,4096]{2,1,0:T(8,128)(2,1)}, bf16[3,512,4096]{2,1,0:T(8,128)(2,1)}, bf16[3,512,1024]{2,1,0:T(...) custom-call(s32[3]{0:T(128)} %get-tuple-element.294.meta_ref, ...), custom_call_target="tpu_custom_call", output_to_operand_aliasing={{0}: (11, {}), {1}: (12, {}), {2}: (13, {}), {3}: (14, {}),... | custom-call | flops 13958643712 | bytes 47185920 | tf_op jit(solution)/shard_map/ffn_forward/pallas_call | solution.py:46
  260.7 1.2 broadcast_select_fusion.4
  261.9 6.2 collective-permute-done.3.refs_0_
  268.1 4.8 attention_forward.7
  272.9 9.9 %ffn_forward.7 = (bf16[3,512,4096]{2,1,0:T(8,128)(2,1)}, bf16[3,512,4096]{2,1,0:T(8,128)(2,1)}, bf16[3,512,4096]{2,1,0:T(8,128)(2,1)}, bf16[3,512,1024]{2,1,0:T(...) custom-call(s32[3]{0:T(128)} %get-tuple-element.295.meta_ref, ...), custom_call_target="tpu_custom_call", output_to_operand_aliasing={{0}: (11, {}), {1}: (12, {}), {2}: (13, {}), {3}: (14, {}),... | custom-call | flops 13958643712 | bytes 47185920 | tf_op jit(solution)/shard_map/ffn_forward/pallas_call | solution.py:46
  283.0 0.9 constant_dynamic-slice_fusion
  284.2 1.1 constant_dynamic-slice_fusion.1
  285.3 1.5 collective-permute-start.4
  287.3 2.0 select_bitcast_fusion.1
  289.3 9.5 %ffn_backward.4 = (bf16[3,512,4096]{2,1,0:T(8,128)(2,1)}, bf16[3,512,4096]{2,1,0:T(8,128)(2,1)}, bf16[3,512,1024]{2,1,0:T(8,128)(2,1)}, bf16[3,512,1024]{2,1,0:T...) custom-call(s32[3]{0:T(128)} %get-tuple-element.294.meta_ref, ...), custom_call_target="tpu_custom_call" | custom-call | flops 12884901888 | bytes 52428800 | tf_op jit(solution)/shard_map/ffn_backward/pallas_call | solution.py:46
  298.8 7.4 attention_backward.4
  306.2 1.3 collective-permute-start.5
  307.5 9.8 %ffn_backward.5 = (bf16[3,512,4096]{2,1,0:T(8,128)(2,1)}, bf16[3,512,4096]{2,1,0:T(8,128)(2,1)}, bf16[3,512,1024]{2,1,0:T(8,128)(2,1)}, bf16[3,512,1024]{2,1,0:T...) custom-call(s32[3]{0:T(128)} %get-tuple-element.295.meta_ref, ...), custom_call_target="tpu_custom_call", output_to_operand_aliasing={{0}: (13, {}), {1}: (14, {}), {2}: (15, {}), {3}: (16, {})} | custom-call | flops 12884901888 | bytes 52428800 | tf_op jit(solution)/shard_map/ffn_backward/pallas_call | solution.py:46
  317.3 7.3 attention_backward.5
  324.6 1.4 collective-permute-start.7
  326.1 2.7 pad_maximum_fusion.refs_2_
  328.8 3.2 maximum_select_fusion.1
  332.0 94.8 %collective-permute-done.5.refs_0_ = bf16[512,1024]{1,0:T(8,128)(2,1)} collective-permute-done((bf16[512,1024]{1,0:T(8,128)(2,1)}, bf16[512,1024]{1,0:T(8,128)(2,1)}, u32[]{:S(2)}, u32[]{:S(2)}) %collective-permute-start.5) | collective-permute-done | bytes 1048608 | tf_op jit(solution)/shard_map/ppermute | solution.py:1463
  426.8 28.3 %ffn_backward.6 = (bf16[3,512,4096]{2,1,0:T(8,128)(2,1)}, bf16[3,512,4096]{2,1,0:T(8,128)(2,1)}, bf16[3,512,1024]{2,1,0:T(8,128)(2,1)}, bf16[3,512,1024]{2,1,0:T...) custom-call(s32[3]{0:T(128)} %get-tuple-element.292.meta_ref, ...), custom_call_target="tpu_custom_call", output_to_operand_aliasing={{0}: (13, {}), {1}: (14, {}), {2}: (15, {}), {3}: (16, {})} | custom-call | flops 12884901888 | bytes 52428800 | tf_op jit(solution)/shard_map/ffn_backward/pallas_call | solution.py:46
  455.1 28.0 %attention_backward.6 = (bf16[3,512,1024]{2,1,0:T(8,128)(2,1)}, bf16[3,512,1024]{2,1,0:T(8,128)(2,1)}, bf16[3,512,1024]{2,1,0:T(8,128)(2,1)}, f32[512,1024]{1,0:...) custom-call(s32[3]{0:T(128)} %get-tuple-element.292.meta_ref, ...), custom_call_target="tpu_custom_call", output_to_operand_aliasing={{0}: (12, {}), {1}: (13, {}), {2}: (14, {})} | custom-call | flops 6979321856 | bytes 20971520 | tf_op jit(solution)/shard_map/attention_backward/pallas_call | solution.py:46
  483.1 2.9 collective-permute-done.7.refs_0_
  486.0 29.0 %ffn_backward.7 = (bf16[3,512,4096]{2,1,0:T(8,128)(2,1)}, bf16[3,512,4096]{2,1,0:T(8,128)(2,1)}, bf16[3,512,1024]{2,1,0:T(8,128)(2,1)}, bf16[3,512,1024]{2,1,0:T...) custom-call(s32[3]{0:T(128)} %get-tuple-element.293.meta_ref, ...), custom_call_target="tpu_custom_call", output_to_operand_aliasing={{0}: (13, {}), {1}: (14, {}), {2}: (15, {}), {3}: (16, {})} | custom-call | flops 12884901888 | bytes 52428800 | tf_op jit(solution)/shard_map/ffn_backward/pallas_call | solution.py:46
  515.0 0.8 fusion.3
  515.8 28.1 %attention_backward.7 = (bf16[3,512,1024]{2,1,0:T(8,128)(2,1)}, bf16[3,512,1024]{2,1,0:T(8,128)(2,1)}, bf16[3,512,1024]{2,1,0:T(8,128)(2,1)}, f32[512,1024]{1,0:...) custom-call(s32[3]{0:T(128)} %get-tuple-element.293.meta_ref, ...), custom_call_target="tpu_custom_call", output_to_operand_aliasing={{0}: (12, {}), {1}: (13, {}), {2}: (14, {})} | custom-call | flops 6979321856 | bytes 20971520 | tf_op jit(solution)/shard_map/attention_backward/pallas_call | solution.py:46
  544.0 0.8 select_add_fusion.1
  544.9 0.6 pad_maximum_fusion.1.refs_11_
  545.6 225.6 %weight_grads_reduced.1 = (bf16[1024,2048]{1,0:T(8,128)(2,1)}, bf16[1024,2048]{1,0:T(8,128)(2,1)}, bf16[1024,2048]{1,0:T(8,128)(2,1)}, bf16[1024,512]{1,0:T(8,12...) custom-call(bf16[3,512,1024]{2,1,0:T(8,128)(2,1)} %get-tuple-element, ...), custom_call_target="tpu_custom_call" | custom-call | flops 34359738368 | bytes 67108864 | tf_op jit(solution)/shard_map/weight_grads_reduced/pallas_call | solution.py:895
  771.2 0.9 slice.107
  772.0 1.7 fusion.5
  773.7 0.8 slice.113
  774.5 2.2 dynamic-slice_select_fusion.2
  776.7 1.4 collective-permute-start.8
  778.2 2.0 dynamic-slice_select_fusion.3
  781.1 1.8 copy.85
  783.0 6.8 bitcast_convert_fusion
  790.0 1.4 copy-done.12
  792.2 0.6 maximum_bitcast_fusion.1
  792.8 0.6 maximum_bitcast_fusion.2
  793.4 0.6 dynamic-slice_bitcast_fusion.2
  794.0 3.5 maximum_convert_fusion.1
  798.0 9.4 %maximum_convert_fusion = f32[1,2,1024,2048]{3,2,1,0:T(8,128)} fusion(bf16[1,1,1024,2048]{3,2,1,0:T(8,128)(2,1)} %bitcast.135, bf16[1,1,1024,2048]{3,2,1,0:T(8,128)(2,1)S(1)} %bitcast.134), kind=kLoop, calls=%fused_computation | loop fusion | flops 8388608 | bytes 25165824 | tf_op jit(solution)/shard_map/convert_element_type | solution.py:1491
  807.5 1.3 fusion.2
  808.8 2.3 maximum_select_fusion
  (91 shorter events, 4.9 us)
Async XLA Ops:
  1.4 144.5 %collective-permute-start = (bf16[2,2560]{1,0:T(2,128)(2,1)S(1)}, bf16[2,2560]{1,0:T(2,128)(2,1)S(1)}, u32[]{:S(2)}, u32[]{:S(2)}) collective-permute-start(bf16[2,2560]{1,0:T(2,128)(2,1)S(1)} %pad_maximum_fusion.2), channel_id=1, source_target_pairs={{0,8},{8,0},{1,9},{9,1},{2,10},{10,2},{3,11},{11,3},{4,12},{12,4},... | collective-permute-start | bytes 30728 | tf_op jit(solution)/shard_map/ppermute | solution.py:1372
  136.3 3.1 copy-start.29
  136.3 3.1 copy-start.30
  136.3 8.9 %copy-start.26 = (bf16[1,1024]{1,0:T(2,128)(2,1)S(1)}, bf16[1,1024]{1,0:T(2,128)(2,1)}, u32[]{:S(2)}) copy-start(bf16[1,1024]{1,0:T(2,128)(2,1)} %param.19) | copy-start | bytes 6148
  136.3 8.9 %copy-start.32 = (bf16[1,1024]{1,0:T(2,128)(2,1)S(1)}, bf16[1,1024]{1,0:T(2,128)(2,1)}, u32[]{:S(2)}) copy-start(bf16[1,1024]{1,0:T(2,128)(2,1)} %param.25) | copy-start | bytes 6148
  136.3 9.5 %copy-start.31 = (bf16[1,2,512]{2,1,0:T(2,128)(2,1)S(1)}, bf16[1,2,512]{2,1,0:T(2,128)(2,1)}, u32[]{:S(2)}) copy-start(bf16[1,2,512]{2,1,0:T(2,128)(2,1)} %param.17) | copy-start | bytes 6148
  146.5 19.4 %copy-start.28 = (bf16[1,2,2048]{2,1,0:T(2,128)(2,1)S(1)}, bf16[1,2,2048]{2,1,0:T(2,128)(2,1)}, u32[]{:S(2)}) copy-start(bf16[1,2,2048]{2,1,0:T(2,128)(2,1)} %param.23) | copy-start | bytes 24580
  213.3 32.3 %collective-permute-start.1 = (bf16[512,1024]{1,0:T(8,128)(2,1)}, bf16[512,1024]{1,0:T(8,128)(2,1)S(1)}, u32[]{:S(2)}, u32[]{:S(2)}) collective-permute-start(bf16[512,1024]{1,0:T(8,128)(2,1)} %get-tuple-element.145.refs_18_), channel_id=1, source_target_pairs={{0,16},{1,17},{2,18},{3,19},{4,20},{5,21},{6,22},{7,23},{8,24},{9,... | collective-permute-start | bytes 3145736 | tf_op jit(solution)/shard_map/ppermute | solution.py:1434
  243.2 24.8 %collective-permute-start.3 = (bf16[512,1024]{1,0:T(8,128)(2,1)}, bf16[512,1024]{1,0:T(8,128)(2,1)}, u32[]{:S(2)}, u32[]{:S(2)}) collective-permute-start(bf16[512,1024]{1,0:T(8,128)(2,1)} %get-tuple-element.157.refs_10_), channel_id=1, source_target_pairs={{0,16},{1,17},{2,18},{3,19},{4,20},{5,21},{6,22},{7,23},{8,24},{9,... | collective-permute-start | bytes 3145736 | tf_op jit(solution)/shard_map/ppermute | solution.py:1434
  245.6 1.0 copy-start
  251.1 9.6 %copy-start.3 = (bf16[512,1024]{1,0:T(8,128)(2,1)S(1)}, bf16[512,1024]{1,0:T(8,128)(2,1)}, u32[]{:S(2)}) copy-start(bf16[512,1024]{1,0:T(8,128)(2,1)} %get-tuple-element.145.refs_18_) | copy-start | bytes 3145732
  272.9 9.9 %copy-start.4 = (bf16[512,1024]{1,0:T(8,128)(2,1)S(1)}, bf16[512,1024]{1,0:T(8,128)(2,1)}, u32[]{:S(2)}) copy-start(bf16[512,1024]{1,0:T(8,128)(2,1)} %get-tuple-element.157.refs_10_) | copy-start | bytes 3145732
  282.8 1.3 copy-start.5
  282.8 4.4 copy-start.1
  282.9 4.4 copy-start.2
  285.3 43.5 %collective-permute-start.4 = (bf16[256,1024]{1,0:T(8,128)(2,1)}, bf16[256,1024]{1,0:T(8,128)(2,1)}, u32[]{:S(2)}, u32[]{:S(2)}) collective-permute-start(bf16[256,1024]{1,0:T(8,128)(2,1)} %get-tuple-element.274), channel_id=1, source_target_pairs={{0,8},{8,0},{1,9},{9,1},{2,10},{10,2},{3,11},{11,3},{4,12},{12,4},... | collective-permute-start | bytes 1572872 | tf_op jit(solution)/shard_map/ppermute | solution.py:1372
  286.8 42.0 %collective-permute-start.2 = (bf16[256,1024]{1,0:T(8,128)(2,1)}, bf16[256,1024]{1,0:T(8,128)(2,1)}, u32[]{:S(2)}, u32[]{:S(2)}) collective-permute-start(bf16[256,1024]{1,0:T(8,128)(2,1)} %get-tuple-element.272), channel_id=1, source_target_pairs={{0,8},{8,0},{1,9},{9,1},{2,10},{10,2},{3,11},{11,3},{4,12},{12,4},... | collective-permute-start | bytes 1572872 | tf_op jit(solution)/shard_map/ppermute | solution.py:1372
  306.2 120.5 %collective-permute-start.5 = (bf16[512,1024]{1,0:T(8,128)(2,1)}, bf16[512,1024]{1,0:T(8,128)(2,1)}, u32[]{:S(2)}, u32[]{:S(2)}) collective-permute-start(bf16[512,1024]{1,0:T(8,128)(2,1)} %get-tuple-element.195), channel_id=1, source_target_pairs={{16,0},{17,1},{18,2},{19,3},{20,4},{21,5},{22,6},{23,7},{24,8},{25... | collective-permute-start | bytes 3145736 | tf_op jit(solution)/shard_map/ppermute | solution.py:1463
  324.6 4.2 copy-start.7
  324.6 161.3 %collective-permute-start.7 = (bf16[512,1024]{1,0:T(8,128)(2,1)}, bf16[512,1024]{1,0:T(8,128)(2,1)}, u32[]{:S(2)}, u32[]{:S(2)}) collective-permute-start(bf16[512,1024]{1,0:T(8,128)(2,1)} %get-tuple-element.217), channel_id=1, source_target_pairs={{16,0},{17,1},{18,2},{19,3},{20,4},{21,5},{22,6},{23,7},{24,8},{25... | collective-permute-start | bytes 3145736 | tf_op jit(solution)/shard_map/ppermute | solution.py:1463
  486.0 29.0 %copy-start.24 = (f32[8,1024]{1,0:T(8,128)S(1)}, f32[8,1024]{1,0:T(8,128)}, u32[]{:S(2)}) copy-start(f32[8,1024]{1,0:T(8,128)} %get-tuple-element.208.refs_14_) | copy-start | bytes 98308
  486.0 29.0 %copy-start.25 = (f32[8,1024]{1,0:T(8,128)S(1)}, f32[8,1024]{1,0:T(8,128)}, u32[]{:S(2)}) copy-start(f32[8,1024]{1,0:T(8,128)} %get-tuple-element.215.refs_14_) | copy-start | bytes 98308
  486.0 29.0 %copy-start.27 = (f32[8,1024]{1,0:T(8,128)S(1)}, f32[8,1024]{1,0:T(8,128)}, u32[]{:S(2)}) copy-start(f32[8,1024]{1,0:T(8,128)} %get-tuple-element.194.refs_11_) | copy-start | bytes 98308
  515.8 28.2 %copy-start.17 = (f32[8,1024]{1,0:T(8,128)S(1)}, f32[8,1024]{1,0:T(8,128)}, u32[]{:S(2)}) copy-start(f32[8,1024]{1,0:T(8,128)} %get-tuple-element.199.refs_16_) | copy-start | bytes 98308
  515.8 28.2 %copy-start.18 = (f32[8,1024]{1,0:T(8,128)S(1)}, f32[8,1024]{1,0:T(8,128)}, u32[]{:S(2)}) copy-start(f32[8,1024]{1,0:T(8,128)} %get-tuple-element.209.refs_16_) | copy-start | bytes 98308
  515.8 28.2 %copy-start.19 = (f32[8,1024]{1,0:T(8,128)S(1)}, f32[8,1024]{1,0:T(8,128)}, u32[]{:S(2)}) copy-start(f32[8,1024]{1,0:T(8,128)} %get-tuple-element.221.refs_16_) | copy-start | bytes 98308
  515.8 29.0 %copy-start.20 = (f32[8,4096]{1,0:T(8,128)S(1)}, f32[8,4096]{1,0:T(8,128)}, u32[]{:S(2)}) copy-start(f32[8,4096]{1,0:T(8,128)} %get-tuple-element.242) | copy-start | bytes 393220
  515.8 29.0 %copy-start.21 = (f32[8,4096]{1,0:T(8,128)S(1)}, f32[8,4096]{1,0:T(8,128)}, u32[]{:S(2)}) copy-start(f32[8,4096]{1,0:T(8,128)} %get-tuple-element.244) | copy-start | bytes 393220
  515.8 29.0 %copy-start.22 = (f32[8,4096]{1,0:T(8,128)S(1)}, f32[8,4096]{1,0:T(8,128)}, u32[]{:S(2)}) copy-start(f32[8,4096]{1,0:T(8,128)} %get-tuple-element.241) | copy-start | bytes 393220
  515.8 29.0 %copy-start.23 = (f32[8,4096]{1,0:T(8,128)S(1)}, f32[8,4096]{1,0:T(8,128)}, u32[]{:S(2)}) copy-start(f32[8,4096]{1,0:T(8,128)} %get-tuple-element.243) | copy-start | bytes 393220
  545.6 232.6 %copy-start.16 = (bf16[512,1024]{1,0:T(8,128)(2,1)S(1)}, bf16[512,1024]{1,0:T(8,128)(2,1)}, u32[]{:S(2)}) copy-start(bf16[512,1024]{1,0:T(8,128)(2,1)} %get-tuple-element.195) | copy-start | bytes 3145732
  771.2 9.7 %copy-start.11 = (bf16[1024,512]{1,0:T(8,128)(2,1)S(1)}, bf16[1024,512]{1,0:T(8,128)(2,1)}, u32[]{:S(2)}) copy-start(bf16[1024,512]{1,0:T(8,128)(2,1)} %get-tuple-element.250) | copy-start | bytes 3145732
  776.7 30.7 %collective-permute-start.8 = (bf16[256,1024]{1,0:T(8,128)(2,1)}, bf16[256,1024]{1,0:T(8,128)(2,1)}, u32[]{:S(2)}, u32[]{:S(2)}) collective-permute-start(bf16[256,1024]{1,0:T(8,128)(2,1)} %dynamic-slice_select_fusion.2), channel_id=1, source_target_pairs={{0,8},{8,0},{1,9},{9,1},{2,10},{10,2},{3,11},{11,3},{4,12},{12,4},... | collective-permute-start | bytes 1572872 | tf_op jit(solution)/shard_map/ppermute | solution.py:1372
  780.2 27.2 %collective-permute-start.6 = (bf16[256,1024]{1,0:T(8,128)(2,1)}, bf16[256,1024]{1,0:T(8,128)(2,1)}, u32[]{:S(2)}, u32[]{:S(2)}) collective-permute-start(bf16[256,1024]{1,0:T(8,128)(2,1)} %dynamic-slice_select_fusion.3), channel_id=1, source_target_pairs={{0,8},{8,0},{1,9},{9,1},{2,10},{10,2},{3,11},{11,3},{4,12},{12,4},... | collective-permute-start | bytes 1572872 | tf_op jit(solution)/shard_map/ppermute | solution.py:1372
  783.0 6.8 copy-start.13
  783.0 6.8 copy-start.15
  783.0 7.0 copy-start.14
  789.8 1.6 copy-start.12
  789.8 4.2 copy-start.8
  789.8 4.2 copy-start.9
  789.8 4.2 copy-start.10
  794.0 4.1 copy-start.6

commit v4 on v3

--- a/solution.py
+++ b/solution.py
@@ -1,4 +1,3 @@
-import functools
 import math
 
 import jax
@@ -15,68 +14,74 @@
 F32 = jnp.float32
 VMEM_LIMIT = 62 * 1024 * 1024
 ANY = pl.BlockSpec(memory_space=pl.ANY)
+SMEM = pl.BlockSpec(memory_space=pltpu.SMEM)
+WHOLE = pl.BlockSpec(memory_space=pltpu.VMEM)
 NN = (((1,), (0,)), ((), ()))
 NT = (((1,), (1,)), ((), ()))
 TN = (((0,), (0,)), ((), ()))
+CW = 256
+PER = CW // HD
 
 
 def dot(a, b, dims=NN):
     return lax.dot_general(a, b, dims, preferred_element_type=F32)
 
 
-def call(kernel, grid, inputs, outputs, scratch, meta, chain, deps, name, flops, nbytes):
-    args = [a for a, _ in inputs]
-    specs = [s for _, s in inputs]
+def arrived(ref, sem):
+    pltpu.make_async_copy(ref, ref, sem).wait()
+
+
+def call(kernel, inputs, outputs, scratch, meta, chain, deps, name, flops, nbytes):
+    pairs = [item if isinstance(item, tuple) else (item, ANY) for item in inputs]
+    args = [meta] + [p[0] for p in pairs]
+    specs = [SMEM] + [p[1] for p in pairs]
     n_in = len(args)
     aliases = {}
     if chain is not None:
-        chained = [index for index, item in enumerate(outputs) if item[3]]
-        for buffer, index in zip(chain, chained):
-            aliases[1 + len(args)] = index
+        for buffer, index in zip(chain, [index for index, item in enumerate(outputs) if item[2]]):
+            aliases[len(args)] = index
             args.append(buffer)
             specs.append(ANY)
-    for item in deps:
-        args.append(item)
-        specs.append(ANY)
-    n_args = len(args)
-
-    def body(meta_ref, *refs):
-        kernel(meta_ref, refs[:n_in], refs[n_args : n_args + len(outputs)], refs[n_args + len(outputs) :])
+    args += deps
+    specs += [ANY] * len(deps)
+    n_args, n_out = len(args), len(outputs)
+
+    def body(*refs):
+        @pl.when(refs[0][1] == 1)
+        def _():
+            kernel(refs[0], refs[1:n_in], refs[n_args : n_args + n_out], refs[n_args + n_out :])
 
     return pl.pallas_call(
         body,
-        grid_spec=pltpu.PrefetchScalarGridSpec(
-            num_scalar_prefetch=1,
-            grid=grid,
-            in_specs=specs,
-            out_specs=[o[2] for o in outputs],
-            scratch_shapes=scratch,
-        ),
+        in_specs=specs,
+        out_specs=[ANY] * n_out,
         out_shape=[jax.ShapeDtypeStruct(o[0], o[1]) for o in outputs],
+        scratch_shapes=scratch,
         input_output_aliases=aliases,
-        compiler_params=pltpu.CompilerParams(
-            dimension_semantics=("arbitrary",) * len(grid), vmem_limit_bytes=VMEM_LIMIT
-        ),
+        compiler_params=pltpu.CompilerParams(vmem_limit_bytes=VMEM_LIMIT),
         cost_estimate=pl.CostEstimate(flops=flops, bytes_accessed=nbytes, transcendentals=0),
         name=name,
-    )(meta, *args)
-
-
-def own_map(count, make):
-    return lambda i, meta: make(jnp.minimum(i, count - 1) * meta[1])
-
-
-def oth_map(count, make):
-    return lambda i, meta: make(jnp.maximum(i - count, 0) * meta[1])
-
-
-def tile_map(make):
-    return lambda i, meta: make(meta[0], i * meta[1])
-
-
-def fixed(shape):
-    zeros = (0,) * len(shape)
-    return pl.BlockSpec(shape, lambda i, meta: zeros, pipeline_mode=pl.Buffered(1))
+    )(*args)
+
+
+def pick(k, count, own, oth, make):
+    @pl.when(k < count)
+    def _():
+        for src, dst, sem in make(own, k):
+            pltpu.make_async_copy(src, dst, sem).start()
+
+    @pl.when(k >= count)
+    def _():
+        for src, dst, sem in make(oth, k - count):
+            pltpu.make_async_copy(src, dst, sem).start()
+
+
+def block(index, size):
+    return pl.ds(pl.multiple_of(index * size, size), size)
+
+
+def copy(src, dst, sem):
+    return pltpu.make_async_copy(src, dst, sem)
 
 
 def fill_distance(dist_ref, length):
@@ -87,83 +92,6 @@
     dist_ref[...] = jnp.where(keys < length, distance, 1e12)
 
 
-def attention_forward(x, w_own, w_oth, bias, slopes, meta, chain, deps, slots):
-    rows, width = x.shape
-    local = w_own.shape[2]
-    cw = 256
-    per = cw // HD
-    count = local // cw
-    steps = 2 * count
-    total = 2 * local
-
-    def kernel(meta_ref, ins, outs, scratch):
-        x_ref, own_ref, oth_ref, bias_ref, slope_ref = ins
-        q_ref, k_ref, v_ref, mixed_ref, lse_ref = outs
-        (dist_ref,) = scratch
-        i = pl.program_id(0)
-
-        def work(w_ref):
-            values = x_ref[...]
-            b = bias_ref[...]
-            q_ref[0] = (dot(values, w_ref[0]) + b[0:1]).astype(BF)
-            k_ref[0] = dot(values, w_ref[1]).astype(BF)
-            v_ref[0] = (dot(values, w_ref[2]) + b[1:2]).astype(BF)
-            for head in range(per):
-                cols = slice(head * HD, (head + 1) * HD)
-                query = q_ref[0, :, cols] * BF(1.0 / math.sqrt(HD))
-                scores = dot(k_ref[0, :, cols], query, NT)
-                scores = scores - dist_ref[...] * slope_ref[i * per + head]
-                top = jnp.max(scores, axis=0, keepdims=True)
-                weights = jnp.exp(scores - top)
-                total_weight = jnp.sum(weights, axis=0, keepdims=True)
-                low = (weights * (1.0 / total_weight)).astype(BF)
-                mixed_ref[0, :, cols] = dot(low, v_ref[0, :, cols], TN).astype(BF)
-                lse_ref[0, 0, head : head + 1, :] = top + jnp.log(total_weight)
-
-        @pl.when(meta_ref[1] == 1)
-        def _():
-            @pl.when(i == 0)
-            def _():
-                fill_distance(dist_ref, meta_ref[2])
-
-            @pl.when(i < count)
-            def _():
-                work(own_ref)
-
-            @pl.when(i >= count)
-            def _():
-                work(oth_ref)
-
-    wide = pl.BlockSpec((1, rows, cw), tile_map(lambda s, i: (s, 0, i)))
-    return call(
-        kernel,
-        (steps,),
-        [
-            (x, fixed((rows, width))),
-            (w_own, pl.BlockSpec((3, width, cw), own_map(count, lambda i: (0, 0, i)))),
-            (w_oth, pl.BlockSpec((3, width, cw), oth_map(count, lambda i: (0, 0, i)))),
-            (bias, pl.BlockSpec((2, cw), lambda i, meta: (0, i * meta[1]))),
-            (slopes, pl.BlockSpec(memory_space=pltpu.SMEM)),
-        ],
-        [((slots, rows, total), BF, wide, True)] * 4
-        + [
-            (
-                (slots, steps, 8, rows),
-                F32,
-                pl.BlockSpec((1, 1, 8, rows), tile_map(lambda s, i: (s, i, 0, 0))),
-                True,
-            )
-        ],
-        [pltpu.VMEM((rows, rows), F32)],
-        meta,
-        chain,
-        deps,
-        "attention_forward",
-        2 * rows * width * 3 * total + 4 * rows * rows * total,
-        12 << 20,
-    )
-
-
 def normalize(v):
     mean = jnp.mean(v, axis=1, keepdims=True)
     centred = v - mean
@@ -171,298 +99,428 @@
     return centred * rstd, rstd
 
 
-def ffn_forward(x, mixed, o_own, o_oth, up_own, up_oth, down_own, down_oth, vecs, up_bias, meta, chain, deps, slots):
+def halves(rows):
+    return [slice(0, rows // 2), slice(rows // 2, rows)]
+
+
+def layer_forward(x, weights, bias, slopes, vecs, up_bias, meta, chain, deps, slots):
+    qkv_own, qkv_oth, o_own, o_oth, up_own, up_oth, down_own, down_oth = weights
     rows, width = x.shape
-    local = o_own.shape[0]
+    local = qkv_own.shape[2]
     units = up_own.shape[2]
+    heads_steps = local // CW
     ft = min(512, units)
-    count = units // ft
-    steps = 2 * count
+    tiles = units // ft
+    total = 2 * local
 
     def kernel(meta_ref, ins, outs, scratch):
-        x_ref, mixed_ref, o_own_ref, o_oth_ref, u_own_ref, u_oth_ref, d_own_ref, d_oth_ref, vec_ref, ub_ref = ins
-        a_ref, b_ref, h_ref, n_ref, u1_ref, u2_ref, r1_ref, r2_ref, y_ref = outs
-        normed_ref, acc_ref = scratch
-        i = pl.program_id(0)
+        (x_hbm, qkv_own_ref, qkv_oth_ref, o_own_ref, o_oth_ref, up_own_ref, up_oth_ref, down_own_ref, down_oth_ref,
+         bias_ref, slope_ref, vec_ref, ub_ref) = ins
+        q_out, k_out, v_out, mixed_out, lse_out, a_out, b_out, h_out, n_out, u1_out, u2_out, r1_out, r2_out, y_out = outs
+        (x_ref, w_ref, o_ref, up_ref, down_ref, qkv_ref, lse_ref, mixed_ref, dist_ref, normed_ref, acc_ref, low_ref,
+         tile_ref, row_ref, stat_ref, x_sem, w_sem, o_sem, f_sem, q_sem, m_sem, t_sem, r_sem) = scratch
+        slot = meta_ref[0]
+
+        def start_w(k):
+            s = lax.rem(k, 2)
+            pick(k, heads_steps, qkv_own_ref, qkv_oth_ref,
+                 lambda ref, j: [(ref.at[:, :, block(j, CW)], w_ref.at[s], w_sem.at[s])])
+
+        def start_f(k):
+            s = lax.rem(k, 2)
+            pick(k, tiles, (up_own_ref, down_own_ref), (up_oth_ref, down_oth_ref),
+                 lambda ref, j: [(ref[0].at[:, :, block(j, ft)], up_ref.at[s], f_sem.at[s, 0]),
+                                 (ref[1].at[:, block(j, ft)], down_ref.at[s], f_sem.at[s, 1])])
+
+        copy(x_hbm, x_ref, x_sem).start()
+        start_w(jnp.int32(0))
+        start_w(jnp.int32(1))
+        copy(o_own_ref, o_ref.at[pl.ds(0, local)], o_sem).start()
+        copy(o_oth_ref, o_ref.at[pl.ds(local, local)], o_sem).start()
+        start_f(jnp.int32(0))
+        start_f(jnp.int32(1))
+        fill_distance(dist_ref, meta_ref[2])
+        arrived(x_ref, x_sem)
+
+        def write_qkv(i, s):
+            cols = block(i, CW)
+            return [copy(qkv_ref.at[s, c], out.at[slot, :, cols], q_sem.at[s, c])
+                    for c, out in enumerate((q_out, k_out, v_out))] + [
+                copy(lse_ref.at[s], lse_out.at[slot, i], q_sem.at[s, 3])]
+
+        @pl.loop(0, 2 * heads_steps)
+        def _(i):
+            s = lax.rem(i, 2)
+            arrived(w_ref.at[s], w_sem.at[s])
+
+            @pl.when(i >= 2)
+            def _():
+                for item in write_qkv(i - 2, s):
+                    item.wait()
+
+            values = x_ref[...]
+            b = bias_ref[:, block(i, CW)]
+            qkv_ref[s, 0] = (dot(values, w_ref[s, 0]) + b[0:1]).astype(BF)
+            qkv_ref[s, 1] = dot(values, w_ref[s, 1]).astype(BF)
+            qkv_ref[s, 2] = (dot(values, w_ref[s, 2]) + b[1:2]).astype(BF)
+
+            @pl.when(i + 2 < 2 * heads_steps)
+            def _():
+                start_w(i + 2)
+
+            parts = []
+            for head in range(PER):
+                cols = slice(head * HD, (head + 1) * HD)
+                query = qkv_ref[s, 0, :, cols] * BF(1.0 / math.sqrt(HD))
+                scores = dot(qkv_ref[s, 1, :, cols], query, NT)
+                scores = scores - dist_ref[...] * slope_ref[i * PER + head]
+                top = jnp.max(scores, axis=0, keepdims=True)
+                likely = jnp.exp(scores - top)
+                mass = jnp.sum(likely, axis=0, keepdims=True)
+                low = (likely * (1.0 / mass)).astype(BF)
+                parts.append(dot(low, qkv_ref[s, 2, :, cols], TN).astype(BF))
+                lse_ref[s, head : head + 1, :] = top + jnp.log(mass)
+            mixed_ref[:, block(i, CW)] = jnp.concatenate(parts, axis=1)
+            for item in write_qkv(i, s):
+                item.start()
+
+        copy(mixed_ref, mixed_out.at[slot], m_sem).start()
+        arrived(o_ref, o_sem)
         vec = vec_ref[...]
-
-        def work(up_ref, down_ref):
-            for part in range(2):
-                rs = slice(part * rows // 2, (part + 1) * rows // 2)
-                low = n_ref[0, rs, :]
-                gate = dot(low, up_ref[0]) + ub_ref[0:1]
-                lift = dot(low, up_ref[1]) + ub_ref[1:2]
+        for rs in halves(rows):
+            attended = dot(mixed_ref[rs, :], o_ref[...])
+            u, rstd = normalize(x_ref[rs, :].astype(F32) + attended + vec[0:1])
+            normed = u * vec[1:2] + vec[2:3]
+            normed_ref[rs, :] = normed
+            low_ref[rs, :] = normed.astype(BF)
+            row_ref[0, rs, :] = u.astype(BF)
+            stat_ref[0, rs, :] = jnp.broadcast_to(rstd, (rows // 2, 128))
+            acc_ref[rs, :] = jnp.zeros((rows // 2, width), F32)
+        for index, (src, dst) in enumerate(((low_ref, n_out), (row_ref.at[0], u1_out), (stat_ref.at[0], r1_out))):
+            copy(src, dst.at[slot], r_sem.at[index]).start()
+
+        def write_tiles(i, s):
+            return [copy(tile_ref.at[s, c], out.at[slot, :, block(i, ft)], t_sem.at[s, c])
+                    for c, out in enumerate((a_out, b_out, h_out))]
+
+        @pl.loop(0, 2 * tiles)
+        def _(i):
+            s = lax.rem(i, 2)
+            arrived(up_ref.at[s], f_sem.at[s, 0])
+            arrived(down_ref.at[s], f_sem.at[s, 1])
+
+            @pl.when(i >= 2)
+            def _():
+                for item in write_tiles(i - 2, s):
+                    item.wait()
+
+            b = ub_ref[:, block(i, ft)]
+            for rs in halves(rows):
+                low = low_ref[rs, :]
+                gate = dot(low, up_ref[s, 0]) + b[0:1]
+                lift = dot(low, up_ref[s, 1]) + b[1:2]
                 cdf = 0.5 * lax.erf(gate * (1.0 / math.sqrt(2.0))) + 0.5
                 act = gate * cdf
                 slope = cdf + gate * (jnp.exp(gate * gate * -0.5) * (1.0 / math.sqrt(2.0 * math.pi)))
-                a_ref[0, rs, :] = act.astype(BF)
-                b_ref[0, rs, :] = (lift * slope).astype(BF)
+                tile_ref[s, 0, rs, :] = act.astype(BF)
+                tile_ref[s, 1, rs, :] = (lift * slope).astype(BF)
                 hidden = (act * lift).astype(BF)
-                h_ref[0, rs, :] = hidden
-                acc_ref[rs, :] += dot(hidden, down_ref[...], NT)
-
-        @pl.when(meta_ref[1] == 1)
-        def _():
-            @pl.when(i == 0)
-            def _():
-                attended = dot(mixed_ref[0, :, :local], o_own_ref[...])
-                attended += dot(mixed_ref[0, :, local:], o_oth_ref[...])
-                u, rstd = normalize(x_ref[...].astype(F32) + attended + vec[0:1])
-                normed = u * vec[1:2] + vec[2:3]
-                normed_ref[...] = normed
-                n_ref[0] = normed.astype(BF)
-                u1_ref[0] = u.astype(BF)
-                r1_ref[0] = jnp.broadcast_to(rstd, (rows, 128))
-                acc_ref[...] = jnp.zeros_like(acc_ref)
-
-            @pl.when(i < count)
-            def _():
-                work(u_own_ref, d_own_ref)
-
-            @pl.when(i >= count)
-            def _():
-                work(u_oth_ref, d_oth_ref)
-
-            @pl.when(i == steps - 1)
-            def _():
-                u, rstd = normalize(normed_ref[...] + acc_ref[...] + vec[3:4])
-                u2_ref[0] = u.astype(BF)
-                r2_ref[0] = jnp.broadcast_to(rstd, (rows, 128))
-                y_ref[...] = (u * vec[4:5] + vec[5:6]).astype(BF)
-
-    tile = pl.BlockSpec((1, rows, ft), tile_map(lambda s, i: (s, 0, i)))
-    whole = pl.BlockSpec((1, rows, width), lambda i, meta: (meta[0], 0, 0))
-    stat = pl.BlockSpec((1, rows, 128), lambda i, meta: (meta[0], 0, 0))
+                tile_ref[s, 2, rs, :] = hidden
+                acc_ref[rs, :] += dot(hidden, down_ref[s], NT)
+
+            @pl.when(i + 2 < 2 * tiles)
+            def _():
+                start_f(i + 2)
+
+            for item in write_tiles(i, s):
+                item.start()
+
+        for rs in halves(rows):
+            u, rstd = normalize(normed_ref[rs, :] + acc_ref[rs, :] + vec[3:4])
+            row_ref[1, rs, :] = u.astype(BF)
+            stat_ref[1, rs, :] = jnp.broadcast_to(rstd, (rows // 2, 128))
+            row_ref[2, rs, :] = (u * vec[4:5] + vec[5:6]).astype(BF)
+        ends = [(row_ref.at[1], u2_out.at[slot]), (stat_ref.at[1], r2_out.at[slot]), (row_ref.at[2], y_out)]
+        for index, (src, dst) in enumerate(ends):
+            copy(src, dst, r_sem.at[3 + index]).start()
+        for index, (src, dst) in enumerate(
+            [(low_ref, n_out.at[slot]), (row_ref.at[0], u1_out.at[slot]), (stat_ref.at[0], r1_out.at[slot])] + ends
+        ):
+            copy(src, dst, r_sem.at[index]).wait()
+        copy(mixed_ref, mixed_out.at[slot], m_sem).wait()
+        for i in (2 * heads_steps - 2, 2 * heads_steps - 1):
+            for item in write_qkv(jnp.int32(i), i % 2):
+                item.wait()
+        for i in (2 * tiles - 2, 2 * tiles - 1):
+            for item in write_tiles(jnp.int32(i), i % 2):
+                item.wait()
+
+    sem = pltpu.SemaphoreType.DMA
     return call(
         kernel,
-        (steps,),
+        [x, *weights, (bias, WHOLE), (slopes, SMEM), (vecs, WHOLE), (up_bias, WHOLE)],
+        [((slots, rows, total), BF, True)] * 4
+        + [((slots, 2 * heads_steps, 8, rows), F32, True)]
+        + [((slots, rows, 2 * units), BF, True)] * 3
+        + [((slots, rows, width), BF, True)] * 3
+        + [((slots, rows, 128), F32, True)] * 2
+        + [((rows, width), BF, False)],
         [
-            (x, fixed((rows, width))),
-            (mixed, pl.BlockSpec((1, rows, 2 * local), lambda i, meta: (meta[0], 0, 0), pipeline_mode=pl.Buffered(1))),
-            (o_own, fixed((local, width))),
-            (o_oth, fixed((local, width))),
-            (up_own, pl.BlockSpec((2, width, ft), own_map(count, lambda i: (0, 0, i)))),
-            (up_oth, pl.BlockSpec((2, width, ft), oth_map(count, lambda i: (0, 0, i)))),
-            (down_own, pl.BlockSpec((width, ft), own_map(count, lambda i: (0, i)))),
-            (down_oth, pl.BlockSpec((width, ft), oth_map(count, lambda i: (0, i)))),
-            (vecs, fixed((8, width))),
-            (up_bias, pl.BlockSpec((2, ft), lambda i, meta: (0, i * meta[1]))),
+            pltpu.VMEM((rows, width), BF),
+            pltpu.VMEM((2, 3, width, CW), BF),
+            pltpu.VMEM((total, width), BF),
+            pltpu.VMEM((2, 2, width, ft), BF),
+            pltpu.VMEM((2, width, ft), BF),
+            pltpu.VMEM((2, 3, rows, CW), BF),
+            pltpu.VMEM((2, 8, rows), F32),
+            pltpu.VMEM((rows, total), BF),
+            pltpu.VMEM((rows, rows), F32),
+            pltpu.VMEM((rows, width), F32),
+            pltpu.VMEM((rows, width), F32),
+            pltpu.VMEM((rows, width), BF),
+            pltpu.VMEM((2, 3, rows, ft), BF),
+            pltpu.VMEM((3, rows, width), BF),
+            pltpu.VMEM((2, rows, 128), F32),
+            sem, sem((2,)), sem, sem((2, 2)), sem((2, 4)), sem, sem((2, 3)), sem((6,)),
         ],
-        [((slots, rows, 2 * units), BF, tile, True)] * 3
-        + [((slots, rows, width), BF, whole, True)] * 3
-        + [((slots, rows, 128), F32, stat, True)] * 2
-        + [((rows, width), BF, pl.BlockSpec((rows, width), lambda i, meta: (0, 0)), False)],
-        [pltpu.VMEM((rows, width), F32), pltpu.VMEM((rows, width), F32)],
         meta,
         chain,
         deps,
-        "ffn_forward",
-        2 * rows * width * (6 * units + 2 * local),
-        45 << 20,
-    )
-
-
-def ffn_backward(grad, u2, r2, u1, r1, act, slope, up_own, up_oth, down_own, down_oth, vecs, meta, chain, deps, slots):
+        "layer_forward",
+        2 * rows * width * (4 * total + 6 * units) + 4 * rows * rows * total,
+        54 << 20,
+    )
+
+
+def layer_backward(grad, kept, weights, slopes, vecs, meta, chain, deps, slots):
+    qkv_own, qkv_oth, o_own, o_oth, up_own, up_oth, down_own, down_oth = weights
+    q, k, v, _, lse, act, slope, _, _, u1, u2, r1, r2 = kept
     rows, width = grad.shape
+    local = qkv_own.shape[2]
     units = up_own.shape[2]
+    heads_steps = local // CW
     ft = min(512, units)
-    count = units // ft
-    steps = 2 * count
+    tiles = units // ft
+    total = 2 * local
+
+    def norm_back(grad_z, u, rstd, gain):
+        t = grad_z * gain
+        return rstd * (t - jnp.mean(t, axis=1, keepdims=True) - u * jnp.mean(t * u, axis=1, keepdims=True))
+
+    def row_sum(values):
+        return jnp.sum(values, axis=0, keepdims=True)
 
     def kernel(meta_ref, ins, outs, scratch):
-        g_ref, u2_ref, r2_ref, u1_ref, r1_ref, a_ref, b_ref, u_own_ref, u_oth_ref, d_own_ref, d_oth_ref, vec_ref = ins
-        gg0_ref, gg1_ref, gl_ref, ga_ref, gaf_ref, sums_ref, ub_ref = outs
-        (acc_ref,) = scratch
-        i = pl.program_id(0)
+        (g_hbm, q_hbm, k_hbm, v_hbm, lse_hbm, a_hbm, b_hbm, u1_hbm, u2_hbm, r1_hbm, r2_hbm,
+         qkv_own_ref, qkv_oth_ref, o_own_ref, o_oth_ref, up_own_ref, up_oth_ref, down_own_ref, down_oth_ref,
+         slope_ref, vec_ref) = ins
+        gg0_out, gg1_out, gl_out, ga_out, gq_out, gk_out, gv_out, gx_out, gxl_out, sums_out, ub_out, qv_out = outs
+        (g_ref, u_ref, r_ref, up_ref, down_ref, ab_ref, gg_ref, low_ref, acc_ref, sums_ref, ub_ref, qv_ref,
+         w_ref, o_ref, qkv_ref, lse_ref, gm_ref, dist_ref, gqkv_ref,
+         g_sem, f_sem, t_sem, w_sem, q_sem, r_sem) = scratch
+        slot = meta_ref[0]
+
+        def start_f(i):
+            s = lax.rem(i, 2)
+            pick(i, tiles, (up_own_ref, down_own_ref), (up_oth_ref, down_oth_ref),
+                 lambda ref, j: [(ref[0].at[:, :, block(j, ft)], up_ref.at[s], f_sem.at[s, 0]),
+                                 (ref[1].at[:, block(j, ft)], down_ref.at[s], f_sem.at[s, 1])])
+            for c, ref in enumerate((a_hbm, b_hbm)):
+                copy(ref.at[slot, :, block(i, ft)], ab_ref.at[s, c], f_sem.at[s, 2 + c]).start()
+
+        def start_w(i):
+            s = lax.rem(i, 2)
+            pick(i, heads_steps, (qkv_own_ref, o_own_ref), (qkv_oth_ref, o_oth_ref),
+                 lambda ref, j: [(ref[0].at[:, :, block(j, CW)], w_ref.at[s], w_sem.at[s, 0]),
+                                 (ref[1].at[block(j, CW)], o_ref.at[s], w_sem.at[s, 1])])
+            for c, ref in enumerate((q_hbm, k_hbm, v_hbm)):
+                copy(ref.at[slot, :, block(i, CW)], qkv_ref.at[s, c], w_sem.at[s, 2 + c]).start()
+            copy(lse_hbm.at[slot, i], lse_ref.at[s], w_sem.at[s, 5]).start()
+
+        firsts = [(g_hbm, g_ref), (u2_hbm.at[slot], u_ref.at[1]), (r2_hbm.at[slot], r_ref.at[1]),
+                  (u1_hbm.at[slot], u_ref.at[0]), (r1_hbm.at[slot], r_ref.at[0])]
+        for index, (src, dst) in enumerate(firsts):
+            copy(src, dst, g_sem.at[index]).start()
+            if index == 2:
+                start_f(jnp.int32(0))
+                start_f(jnp.int32(1))
+        start_w(jnp.int32(0))
+        start_w(jnp.int32(1))
         vec = vec_ref[...]
-
-        def norm_back(grad_z, u, rstd, gain):
-            t = grad_z * gain
-            return rstd * (
-                t - jnp.mean(t, axis=1, keepdims=True) - u * jnp.mean(t * u, axis=1, keepdims=True)
-            )
-
-        def work(up_ref, down_ref):
+        fill_distance(dist_ref, meta_ref[2])
+        for index, (src, dst) in enumerate(firsts[:3]):
+            copy(src, dst, g_sem.at[index]).wait()
+        sums = [jnp.zeros((1, width), F32)] * 3
+        for rs in halves(rows):
+            grad_y = g_ref[rs, :].astype(F32)
+            u = u_ref[1, rs, :].astype(F32)
+            grad_c = norm_back(grad_y, u, r_ref[1, rs, 0:1], vec[4:5])
+            acc_ref[rs, :] = grad_c
+            low_ref[0, rs, :] = grad_c.astype(BF)
+            for index, values in enumerate((grad_y * u, grad_y, grad_c)):
+                sums[index] += row_sum(values)
+        for index in range(3):
+            sums_ref[index : index + 1, :] = sums[index]
+        copy(low_ref.at[0], gl_out.at[slot], r_sem.at[0]).start()
+
+        def write_tiles(i, s):
+            return [copy(gg_ref.at[s, c], out.at[slot, :, block(i, ft)], t_sem.at[s, c])
+                    for c, out in enumerate((gg0_out, gg1_out))]
+
+        @pl.loop(0, 2 * tiles)
+        def _(i):
+            s = lax.rem(i, 2)
+            arrived(up_ref.at[s], f_sem.at[s, 0])
+            arrived(down_ref.at[s], f_sem.at[s, 1])
+            for c in range(2):
+                arrived(ab_ref.at[s, c], f_sem.at[s, 2 + c])
+
+            @pl.when(i >= 2)
+            def _():
+                for item in write_tiles(i - 2, s):
+                    item.wait()
+
             s0 = jnp.zeros((1, ft), F32)
             s1 = jnp.zeros((1, ft), F32)
-            for part in range(2):
-                rs = slice(part * rows // 2, (part + 1) * rows // 2)
-                gh = dot(gl_ref[0, rs, :], down_ref[...])
-                g0 = (gh * b_ref[0, rs, :].astype(F32)).astype(BF)
-                g1 = (gh * a_ref[0, rs, :].astype(F32)).astype(BF)
-                gg0_ref[0, rs, :] = g0
-                gg1_ref[0, rs, :] = g1
-                s0 += jnp.sum(g0.astype(F32), axis=0, keepdims=True)
-                s1 += jnp.sum(g1.astype(F32), axis=0, keepdims=True)
-                acc_ref[rs, :] += dot(g0, up_ref[0], NT) + dot(g1, up_ref[1], NT)
-            ub_ref[...] = jnp.concatenate([s0, s1, jnp.zeros((6, ft), F32)], axis=0)
-
-        @pl.when(meta_ref[1] == 1)
-        def _():
-            @pl.when(i == 0)
-            def _():
-                grad_y = g_ref[...].astype(F32)
-                u = u2_ref[0].astype(F32)
-                grad_c = norm_back(grad_y, u, r2_ref[0, :, 0:1], vec[4:5])
-                acc_ref[...] = grad_c
-                gl_ref[0] = grad_c.astype(BF)
-                sums_ref[0:1, :] = jnp.sum(grad_y * u, axis=0, keepdims=True)
-                sums_ref[1:2, :] = jnp.sum(grad_y, axis=0, keepdims=True)
-                sums_ref[2:3, :] = jnp.sum(grad_c, axis=0, keepdims=True)
-
-            @pl.when(i < count)
-            def _():
-                work(u_own_ref, d_own_ref)
-
-            @pl.when(i >= count)
-            def _():
-                work(u_oth_ref, d_oth_ref)
-
-            @pl.when(i == steps - 1)
-            def _():
-                grad_n = acc_ref[...]
-                u = u1_ref[0].astype(F32)
-                grad_a = norm_back(grad_n, u, r1_ref[0, :, 0:1], vec[1:2])
-                ga_ref[0] = grad_a.astype(BF)
-                gaf_ref[...] = grad_a
-                sums_ref[3:4, :] = jnp.sum(grad_n * u, axis=0, keepdims=True)
-                sums_ref[4:5, :] = jnp.sum(grad_n, axis=0, keepdims=True)
-                sums_ref[5:6, :] = jnp.sum(grad_a, axis=0, keepdims=True)
-                sums_ref[6:8, :] = jnp.zeros((2, width), F32)
-
-    tile = pl.BlockSpec((1, rows, ft), tile_map(lambda s, i: (s, 0, i)))
-    whole = pl.BlockSpec((1, rows, width), lambda i, meta: (meta[0], 0, 0))
-    whole1 = pl.BlockSpec((1, rows, width), lambda i, meta: (meta[0], 0, 0), pipeline_mode=pl.Buffered(1))
-    stat = pl.BlockSpec((1, rows, 128), lambda i, meta: (meta[0], 0, 0))
+            for rs in halves(rows):
+                gh = dot(low_ref[0, rs, :], down_ref[s])
+                g0 = (gh * ab_ref[s, 1, rs, :].astype(F32)).astype(BF)
+                g1 = (gh * ab_ref[s, 0, rs, :].astype(F32)).astype(BF)
+                gg_ref[s, 0, rs, :] = g0
+                gg_ref[s, 1, rs, :] = g1
+                s0 += row_sum(g0.astype(F32))
+                s1 += row_sum(g1.astype(F32))
+                acc_ref[rs, :] += dot(g0, up_ref[s, 0], NT) + dot(g1, up_ref[s, 1], NT)
+            ub_ref[0:1, block(i, ft)] = s0
+            ub_ref[1:2, block(i, ft)] = s1
+
+            @pl.when(i + 2 < 2 * tiles)
+            def _():
+                start_f(i + 2)
+
+            for item in write_tiles(i, s):
+                item.start()
+
+        for index, (src, dst) in enumerate(firsts[3:]):
+            copy(src, dst, g_sem.at[3 + index]).wait()
+        sums = [jnp.zeros((1, width), F32)] * 3
+        for rs in halves(rows):
+            grad_n = acc_ref[rs, :]
+            u = u_ref[0, rs, :].astype(F32)
+            grad_a = norm_back(grad_n, u, r_ref[0, rs, 0:1], vec[1:2])
+            low_ref[1, rs, :] = grad_a.astype(BF)
+            acc_ref[rs, :] = grad_a
+            for index, values in enumerate((grad_n * u, grad_n, grad_a)):
+                sums[index] += row_sum(values)
+        for index in range(3):
+            sums_ref[3 + index : 4 + index, :] = sums[index]
+        sums_ref[6:8, :] = jnp.zeros((2, width), F32)
+        copy(low_ref.at[1], ga_out.at[slot], r_sem.at[1]).start()
+        scale = BF(1.0 / math.sqrt(HD))
+
+        def write_heads(i, s):
+            return [copy(gqkv_ref.at[s, c], out.at[slot, :, block(i, CW)], q_sem.at[s, c])
+                    for c, out in enumerate((gq_out, gk_out, gv_out))]
+
+        @pl.loop(0, 2 * heads_steps)
+        def _(i):
+            s = lax.rem(i, 2)
+            for index, ref in enumerate((w_ref.at[s], o_ref.at[s], qkv_ref.at[s, 0], qkv_ref.at[s, 1], qkv_ref.at[s, 2], lse_ref.at[s])):
+                arrived(ref, w_sem.at[s, index])
+
+            @pl.when(i >= 2)
+            def _():
+                for item in write_heads(i - 2, s):
+                    item.wait()
+
+            gm_ref[...] = dot(low_ref[1], o_ref[s], NT).astype(BF)
+            parts = [[], [], []]
+            for head in range(PER):
+                cols = slice(head * HD, (head + 1) * HD)
+                query = qkv_ref[s, 0, :, cols] * scale
+                key = qkv_ref[s, 1, :, cols]
+                gm = gm_ref[:, cols]
+                scores = dot(key, query, NT)
+                scores = scores - dist_ref[...] * slope_ref[i * PER + head]
+                likely = jnp.exp(scores - lse_ref[s, head : head + 1, :])
+                parts[2].append(dot(likely.astype(BF), gm).astype(BF))
+                t = likely * dot(qkv_ref[s, 2, :, cols], gm, NT)
+                inner = jnp.sum(t, axis=0, keepdims=True)
+                gs = (t - likely * inner).astype(BF)
+                parts[1].append(dot(gs, query).astype(BF))
+                parts[0].append(dot(gs, key * scale, TN).astype(BF))
+            for c in range(3):
+                gqkv_ref[s, c] = jnp.concatenate(parts[c], axis=1)
+            for index, c in enumerate((0, 2)):
+                qv_ref[index : index + 1, block(i, CW)] = row_sum(gqkv_ref[s, c].astype(F32))
+            acc_ref[...] += (
+                dot(gqkv_ref[s, 0], w_ref[s, 0], NT)
+                + dot(gqkv_ref[s, 1], w_ref[s, 1], NT)
+                + dot(gqkv_ref[s, 2], w_ref[s, 2], NT)
+            )
+
+            @pl.when(i + 2 < 2 * heads_steps)
+            def _():
+                start_w(i + 2)
+
+            for item in write_heads(i, s):
+                item.start()
+
+        g_ref[...] = acc_ref[...].astype(BF)
+        ends = [(g_ref, gxl_out), (acc_ref, gx_out), (sums_ref, sums_out), (ub_ref, ub_out), (qv_ref, qv_out)]
+        for index, (src, dst) in enumerate(ends):
+            copy(src, dst, r_sem.at[2 + index]).start()
+        for index, (src, dst) in enumerate([(low_ref.at[0], gl_out.at[slot]), (low_ref.at[1], ga_out.at[slot])] + ends):
+            copy(src, dst, r_sem.at[index]).wait()
+        for i in (2 * tiles - 2, 2 * tiles - 1):
+            for item in write_tiles(jnp.int32(i), i % 2):
+                item.wait()
+        for i in (2 * heads_steps - 2, 2 * heads_steps - 1):
+            for item in write_heads(jnp.int32(i), i % 2):
+                item.wait()
+
+    sem = pltpu.SemaphoreType.DMA
     return call(
         kernel,
-        (steps,),
+        [grad, q, k, v, lse, act, slope, u1, u2, r1, r2, *weights, (slopes, SMEM), (vecs, WHOLE)],
+        [((slots, rows, 2 * units), BF, True)] * 2
+        + [((slots, rows, width), BF, True)] * 2
+        + [((slots, rows, total), BF, True)] * 3
+        + [
+            ((rows, width), F32, False),
+            ((rows, width), BF, False),
+            ((8, width), F32, False),
+            ((2, 2 * units), F32, False),
+            ((2, total), F32, False),
+        ],
         [
-            (grad, fixed((rows, width))),
-            (u2, whole1),
-            (r2, stat),
-            (u1, whole1),
-            (r1, stat),
-            (act, tile),
-            (slope, tile),
-            (up_own, pl.BlockSpec((2, width, ft), own_map(count, lambda i: (0, 0, i)))),
-            (up_oth, pl.BlockSpec((2, width, ft), oth_map(count, lambda i: (0, 0, i)))),
-            (down_own, pl.BlockSpec((width, ft), own_map(count, lambda i: (0, i)))),
-            (down_oth, pl.BlockSpec((width, ft), oth_map(count, lambda i: (0, i)))),
-            (vecs, fixed((8, width))),
+            pltpu.VMEM((rows, width), BF),
+            pltpu.VMEM((2, rows, width), BF),
+            pltpu.VMEM((2, rows, 128), F32),
+            pltpu.VMEM((2, 2, width, ft), BF),
+            pltpu.VMEM((2, width, ft), BF),
+            pltpu.VMEM((2, 2, rows, ft), BF),
+            pltpu.VMEM((2, 2, rows, ft), BF),
+            pltpu.VMEM((2, rows, width), BF),
+            pltpu.VMEM((rows, width), F32),
+            pltpu.VMEM((8, width), F32),
+            pltpu.VMEM((2, 2 * units), F32),
+            pltpu.VMEM((2, total), F32),
+            pltpu.VMEM((2, 3, width, CW), BF),
+            pltpu.VMEM((2, CW, width), BF),
+            pltpu.VMEM((2, 3, rows, CW), BF),
+            pltpu.VMEM((2, 8, rows), F32),
+            pltpu.VMEM((rows, CW), BF),
+            pltpu.VMEM((rows, rows), F32),
+            pltpu.VMEM((2, 3, rows, CW), BF),
+            sem((5,)), sem((2, 4)), sem((2, 2)), sem((2, 6)), sem((2, 3)), sem((7,)),
         ],
-        [((slots, rows, 2 * units), BF, tile, True)] * 2
-        + [((slots, rows, width), BF, whole, True)] * 2
-        + [
-            ((rows, width), F32, pl.BlockSpec((rows, width), lambda i, meta: (0, 0)), False),
-            ((8, width), F32, pl.BlockSpec((8, width), lambda i, meta: (0, 0)), False),
-            ((8, 2 * units), F32, pl.BlockSpec((8, ft), lambda i, meta: (0, i)), False),
-        ],
-        [pltpu.VMEM((rows, width), F32)],
         meta,
         chain,
         deps,
-        "ffn_backward",
-        2 * rows * width * 6 * units,
-        50 << 20,
-    )
-
-
-def attention_backward(ga, gaf, q, k, v, lse, o_own, o_oth, w_own, w_oth, slopes, meta, chain, deps, slots):
-    rows, width = gaf.shape
-    local = w_own.shape[2]
-    cw = 256
-    per = cw // HD
-    count = local // cw
-    steps = 2 * count
-    total = 2 * local
-
-    def kernel(meta_ref, ins, outs, scratch):
-        ga_ref, gaf_ref, q_ref, k_ref, v_ref, lse_ref, o_own_ref, o_oth_ref, w_own_ref, w_oth_ref, slope_ref = ins
-        gq_ref, gk_ref, gv_ref, gx_ref, gxl_ref, sums_ref = outs
-        dist_ref, gm_ref, acc_ref = scratch
-        i = pl.program_id(0)
-        scale = BF(1.0 / math.sqrt(HD))
-
-        def work(o_ref, w_ref):
-            gm_ref[...] = dot(ga_ref[0], o_ref[...], NT).astype(BF)
-            for head in range(per):
-                cols = slice(head * HD, (head + 1) * HD)
-                query = q_ref[0, :, cols] * scale
-                key = k_ref[0, :, cols]
-                gm = gm_ref[:, cols]
-                scores = dot(key, query, NT)
-                scores = scores - dist_ref[...] * slope_ref[i * per + head]
-                weights = jnp.exp(scores - lse_ref[0, 0, head : head + 1, :])
-                gv_ref[0, :, cols] = dot(weights.astype(BF), gm).astype(BF)
-                gw = dot(v_ref[0, :, cols], gm, NT)
-                t = weights * gw
-                inner = jnp.sum(t, axis=0, keepdims=True)
-                gs = (t - weights * inner).astype(BF)
-                gk_ref[0, :, cols] = dot(gs, query).astype(BF)
-                gq_ref[0, :, cols] = dot(gs, key * scale, TN).astype(BF)
-            acc_ref[...] += (
-                dot(gq_ref[0], w_ref[0], NT) + dot(gk_ref[0], w_ref[1], NT) + dot(gv_ref[0], w_ref[2], NT)
-            )
-            sums_ref[...] = jnp.concatenate(
-                [
-                    jnp.sum(gq_ref[0].astype(F32), axis=0, keepdims=True),
-                    jnp.sum(gv_ref[0].astype(F32), axis=0, keepdims=True),
-                    jnp.zeros((6, cw), F32),
-                ],
-                axis=0,
-            )
-
-        @pl.when(meta_ref[1] == 1)
-        def _():
-            @pl.when(i == 0)
-            def _():
-                fill_distance(dist_ref, meta_ref[2])
-                acc_ref[...] = gaf_ref[...]
-
-            @pl.when(i < count)
-            def _():
-                work(o_own_ref, w_own_ref)
-
-            @pl.when(i >= count)
-            def _():
-                work(o_oth_ref, w_oth_ref)
-
-            @pl.when(i == steps - 1)
-            def _():
-                gx_ref[...] = acc_ref[...]
-                gxl_ref[...] = acc_ref[...].astype(BF)
-
-    tile = pl.BlockSpec((1, rows, cw), tile_map(lambda s, i: (s, 0, i)))
-    return call(
-        kernel,
-        (steps,),
-        [
-            (ga, pl.BlockSpec((1, rows, width), lambda i, meta: (meta[0], 0, 0), pipeline_mode=pl.Buffered(1))),
-            (gaf, fixed((rows, width))),
-            (q, tile),
-            (k, tile),
-            (v, tile),
-            (lse, pl.BlockSpec((1, 1, 8, rows), tile_map(lambda s, i: (s, i, 0, 0)))),
-            (o_own, pl.BlockSpec((cw, width), own_map(count, lambda i: (i, 0)))),
-            (o_oth, pl.BlockSpec((cw, width), oth_map(count, lambda i: (i, 0)))),
-            (w_own, pl.BlockSpec((3, width, cw), own_map(count, lambda i: (0, 0, i)))),
-            (w_oth, pl.BlockSpec((3, width, cw), oth_map(count, lambda i: (0, 0, i)))),
-            (slopes, pl.BlockSpec(memory_space=pltpu.SMEM)),
-        ],
-        [((slots, rows, total), BF, tile, True)] * 3
-        + [
-            ((rows, width), F32, pl.BlockSpec((rows, width), lambda i, meta: (0, 0)), False),
-            ((rows, width), BF, pl.BlockSpec((rows, width), lambda i, meta: (0, 0)), False),
-            ((8, total), F32, pl.BlockSpec((8, cw), lambda i, meta: (0, i)), False),
-        ],
-        [pltpu.VMEM((rows, rows), F32), pltpu.VMEM((rows, cw), BF), pltpu.VMEM((rows, width), F32)],
-        meta,
-        chain,
-        deps,
-        "attention_backward",
-        2 * rows * width * 4 * total + 10 * rows * rows * total,
-        20 << 20,
+        "layer_backward",
+        2 * rows * width * (4 * total + 6 * units) + 10 * rows * rows * total,
+        70 << 20,
     )
 
 
@@ -470,10 +528,6 @@
 CORE_LAG = 3
 CROSS_LAG = 3
 CHAIN_LAG = 2
-
-
-def arrived(ref, sem):
-    pltpu.make_async_copy(ref, ref, sem).wait()
 
 
 def neighbours():
@@ -676,6 +730,7 @@
         group_starts.append(starts[index])
         index += len(members)
     n_left, n_right = len(lefts), len(rights)
+    homes = [(g, index) for g, (_, members) in enumerate(groups) for index in range(len(members))]
     tiles, mines, gives = 4, CORE_LAG + 1, 4
     last_static = chips - 1
     drain = CORE_LAG + CROSS_LAG + 2 * last_static * CHAIN_LAG + 1
@@ -685,13 +740,13 @@
         left_refs = refs[:n_left]
         right_refs = refs[n_left : n_left + n_right]
         sums_ref = refs[n_left + n_right]
-        outs = refs[n_left + n_right + 1 : n_left + 2 * n_right + 1]
-        sums_out = refs[n_left + 2 * n_right + 1]
+        outs = refs[n_left + n_right + 1 : 2 * n_left + n_right + 1]
+        sums_out = refs[2 * n_left + n_right + 1]
         (
             acc, from_x, from_z, final, flip, stage, tile, mine, give, vec, vec_in, vec_all,
             tile_sem, stage_sem, give_send, core_recv, x_send, x_recv, z_send, z_recv, f_send, f_recv,
             store_sem, out_send, out_recv, v_load, v_send, v_recv,
-        ) = refs[n_left + 2 * n_right + 2 :]
+        ) = refs[2 * n_left + n_right + 2 :]
         t, c, z, last, core, cross, above, below = neighbours()
         greet(c, z, chips, core, cross)
 
@@ -834,8 +889,8 @@
             @pl.when(valid(k5))
             def _():
                 def visit(m, j):
-                    dst = outs[m].at[
-                        pl.ds(pl.multiple_of(c * half, half), half), pl.ds(pl.multiple_of(j * bt, bt), bt)
+                    dst = outs[homes[m][0]].at[
+                        homes[m][1], pl.ds(pl.multiple_of(c * half, half), half), pl.ds(pl.multiple_of(j * bt, bt), bt)
                     ]
                     pltpu.make_async_copy(final.at[k5], dst, store_sem).start()
                     remote(final.at[k5], dst, out_send, out_recv, core).start()
@@ -895,8 +950,8 @@
     return pl.pallas_call(
         kernel,
         in_specs=[ANY] * (n_left + n_right + 1),
-        out_specs=[ANY] * n_right + [pl.BlockSpec(memory_space=pltpu.VMEM)],
-        out_shape=[jax.ShapeDtypeStruct((depth, r.shape[2] // 2), BF) for r in rights]
+        out_specs=[ANY] * n_left + [WHOLE],
+        out_shape=[jax.ShapeDtypeStruct((len(g[1]), depth, g[1][0].shape[2] // 2), BF) for g in groups]
         + [jax.ShapeDtypeStruct(vec_shape, F32)],
         scratch_shapes=[
             pltpu.VMEM((total, 2, half, bt), BF),
@@ -1362,7 +1417,6 @@
     groups = lax.axis_size("dp")
     rows = 2 * shard_rows
     seqs = batches // 2
-    slots = seqs + 1
     local = w_qkv.shape[3]
     units = w_up.shape[3]
     heads = local // HD
@@ -1371,11 +1425,12 @@
     def across(value):
         return lax.ppermute(value, "tensor", [(0, 1), (1, 0)])
 
-    def own_rows(values, low):
-        kept = [lax.dynamic_slice_in_dim(v, place * shard_rows, shard_rows, 0) for v in values]
-        sent = [lax.dynamic_slice_in_dim(v, (1 - place) * shard_rows, shard_rows, 0) for v in low]
-        got = [across(v) for v in sent]
-        return join(jnp.stack(kept), jnp.stack(got).astype(values[0].dtype), place == 1)
+    def part_rows(value, part):
+        return lax.dynamic_slice_in_dim(value, part * shard_rows, shard_rows, 0)
+
+    def own_rows(values, got):
+        kept_rows = jnp.stack([part_rows(v, place) for v in values])
+        return join(kept_rows, jnp.stack(got).astype(kept_rows.dtype), place == 1)
 
     qkv_own = jnp.transpose(w_qkv[0], (1, 0, 2))
     out_own = w_out[0]
@@ -1407,71 +1462,50 @@
 
     def meta(m, turn):
         active = section == turn
-        return jnp.stack([jnp.where(active, m, seqs), active.astype(jnp.int32), own_lengths[m]])
+        return jnp.stack([jnp.int32(m), active.astype(jnp.int32), own_lengths[m]])
 
     metas = [[meta(m, turn) for m in range(seqs)] for turn in range(2)]
-    att = ffn = None
+    weights = (qkv_own, qkv_oth, out_own, out_oth, up_own, up_oth, down_own, down_oth)
+    kept = None
     deps = []
 
-    def attention(x, m, turn):
-        nonlocal att, deps
-        att = attention_forward(x, qkv_own, qkv_oth, bias, slopes, metas[turn][m], att, deps, slots)
-        deps = [att[4]]
-
-    def feed(x, m, turn):
-        nonlocal ffn, deps
-        ffn = ffn_forward(
-            x, att[3], out_own, out_oth, up_own, up_oth, down_own, down_oth, vecs, up_bias,
-            metas[turn][m], ffn, deps, slots,
-        )
-        *ffn, y = ffn
+    def forward(x, m, turn):
+        nonlocal kept, deps
+        *kept, y = layer_forward(x, weights, bias, slopes, vecs, up_bias, metas[turn][m], kept, deps, seqs)
         deps = [y]
         return y
 
-    for m in range(seqs):
-        attention(x_first[m], m, 0)
-    y_first = [feed(x_first[m], m, 0) for m in range(seqs)]
+    y_first = [forward(x_first[m], m, 0) for m in range(seqs)]
     x_second = [lax.ppermute(y, "section", [(0, 1)]) for y in y_first]
-    y_second = []
-    for m in range(seqs):
-        attention(x_second[m], m, 1)
-        y_second.append(feed(x_second[m], m, 1))
-
-    bff = bat = None
+    y_second = [forward(x_second[m], m, 1) for m in range(seqs)]
+
+    back = None
     sums = [[None] * seqs, [None] * seqs]
 
-    def back(grad, m, turn):
-        nonlocal bff, bat, deps
-        act, slope, hidden, normed, u1, u2, r1, r2 = ffn
-        *bff, gaf, norm_sums, up_sums = ffn_backward(
-            grad, u2, r2, u1, r1, act, slope, up_own, up_oth, down_own, down_oth, vecs,
-            metas[turn][m], bff, deps, slots,
+    def backward(grad, m, turn):
+        nonlocal back, deps
+        *back, gx, gx_low, norm_sums, up_sums, qv_sums = layer_backward(
+            grad, kept, weights, slopes, vecs, metas[turn][m], back, deps, seqs
         )
         deps = [norm_sums]
-        *bat, gx, gx_low, qv_sums = attention_backward(
-            bff[3], gaf, att[0], att[1], att[2], att[4], out_own, out_oth, qkv_own, qkv_oth, slopes,
-            metas[turn][m], bat, deps, slots,
-        )
-        deps = [qv_sums]
         sums[turn][m] = (norm_sums, up_sums, qv_sums)
         return gx, gx_low
 
     row = jnp.arange(rows)[:, None]
     gx_second = [
-        back(jnp.where(row < own_lengths[m], outer[m], 0), m, 1) for m in range(seqs)
+        backward(jnp.where(row < own_lengths[m], outer[m], 0), m, 1) for m in range(seqs)
     ]
     grad_middle = [lax.ppermute(gx_second[m][1], "section", [(1, 0)]) for m in range(seqs)]
-    gx_first = [back(grad_middle[m], m, 0) for m in range(seqs)]
-
-    hidden, normed = ffn[2], ffn[3]
-    mixed = att[3]
+    gx_first = [backward(grad_middle[m], m, 0) for m in range(seqs)]
+
+    mixed, hidden, normed = kept[3], kept[7], kept[8]
     x_all = jnp.stack([jnp.where(first, x_first[m], x_second[m]) for m in range(seqs)])
-    gg0, gg1, gl, ga = bff
-    produced = own_rows(*[[jnp.where(first, a, b) for a, b in zip(y_first, y_second)]] * 2)
-    grads_in = own_rows(
-        [jnp.where(first, a[0], b[0]) for a, b in zip(gx_first, gx_second)],
-        [jnp.where(first, a[1], b[1]) for a, b in zip(gx_first, gx_second)],
-    )
+    gg0, gg1, gl, ga, *gqkv = back
+
+    y_own = [jnp.where(first, a, b) for a, b in zip(y_first, y_second)]
+    produced = own_rows(y_own, [across(part_rows(y, 1 - place)) for y in y_own])
+    gx_own = [jnp.where(first, a[0], b[0]) for a, b in zip(gx_first, gx_second)]
+    gx_sent = [part_rows(jnp.where(first, a[1], b[1]), 1 - place) for a, b in zip(gx_first, gx_second)]
 
     picked = [
         sum(jnp.where(first, sums[0][m][index], sums[1][m][index]) for m in range(seqs))
@@ -1485,13 +1519,16 @@
         ).reshape(-1, width)
 
     packed = jnp.concatenate([norm_sums[:6], ordered(up_sums[:2], units), ordered(qv_sums[:2], local)])
-    down_sum, *up_sum, sum_q, sum_k, sum_v, out_sum, packed = weight_grads_reduced(
-        [(gl, [hidden]), (normed, [gg0, gg1]), (x_all, bat), (ga, [mixed])], packed, chips
-    )
-    up_sum = jnp.stack(up_sum).astype(F32)
-    down_sum = down_sum.astype(F32)
-    qkv_sum = jnp.stack([sum_q, sum_k, sum_v], axis=1).astype(F32)
-    out_sum = out_sum.T.astype(F32)
+    packed, produced, gx_sent = lax.optimization_barrier((packed, produced, gx_sent))
+    gx_got = [across(value) for value in gx_sent]
+    down_sum, up_sum, qkv_sum, out_sum, packed = weight_grads_reduced(
+        [(gl, [hidden]), (normed, [gg0, gg1]), (x_all, gqkv), (ga, [mixed])], packed, chips
+    )
+    grads_in = own_rows(gx_own, gx_got)
+    up_sum = up_sum.astype(F32)
+    down_sum = down_sum[0].astype(F32)
+    qkv_sum = jnp.transpose(qkv_sum, (1, 0, 2)).astype(F32)
+    out_sum = out_sum[0].T.astype(F32)
     norm_total = packed[:6]
     up_total = packed[6 : 6 + 4 * units // width].reshape(2, 2 * units)
     qv_total = packed[6 + 4 * units // width :].reshape(2, 2 * local)

time: 819 us -> 755 us (0.922)
  Pallas kernels: 622 us -> 540 us
  waiting for transfers between devices: 104 us -> 119 us
    pallas_call x16 -> x8, Pallas kernels: 269 us -> 186 us  [call(): pl.pallas_call(body, in_specs=specs, out_specs=[ANY] * n_out, out_shape=[...]
    ppermute x2, waiting for transfers between devices: 6.18 us -> 17.7 us  [by_sequence(): x_second = [lax.ppermute(y, 'section', [(0, 1)]) for y in y_first]]
    broadcast_in_dim x1 -> x2, other arithmetic: 6.81 us -> 15.4 us  [the longest x1 11.8 us: by_sequence(): up_sum[None]]
    ppermute x5, waiting for transfers between devices: 0.01 us -> 8.35 us  [across(): return lax.ppermute(value, 'tensor', [(0, 1), (1, 0)])]
  transfers between devices with their start and end apart: 9 -> 9, of which waited for: 3 -> 4; matrix products, arithmetic and copies ran while one was open for 6% -> 7% of each run, Pallas kernels for 32% -> 30%
where the time goes in v4:
time: 755 us; the launch traced here: 747 us
  Pallas kernels  540 us (72%)
  waiting for transfers between devices  119 us (16%)
  other arithmetic  57.6 us (8%)
  local copies, waits for them, and re-layouts  15.5 us (2%)
  starting transfers between devices  13.4 us (2%)
    pallas_call x1, Pallas kernels, weight_grads_reduced(): pl.pallas_call(kernel, in_specs=[ANY] * (n_left + n_right + 1), out_specs...  226 us
    pallas_call x8, Pallas kernels, call(): pl.pallas_call(body, in_specs=specs, out_specs=[ANY] * n_out, out_shape=[...  186 us
    pallas_call x1, Pallas kernels, fetch_other_half(): pl.pallas_call(kernel, in_specs=[ANY] * 5, out_specs=[ANY] * 5, out_shape...  127 us
    ppermute x2, waiting for transfers between devices, by_sequence(): lax.ppermute(gx_second[m][1], 'section', [(1, 0)])  93 us
    ppermute x2, waiting for transfers between devices, by_sequence(): x_second = [lax.ppermute(y, 'section', [(0, 1)]) for y in y_first]  17.7 us
  transfers between devices with their start and end apart: 9, of which 4 were waited for; matrix products, arithmetic and copies ran while one was open for 7% of the time, Pallas kernels for 30%

profile of v4, /device:TPU:0, one launch (start us, length us, event | category | flops | bytes accessed | tf_op | source)
XLA Modules:
  0.0 746.8 jit_solution(7647488701143351867)
XLA Ops:
  0.6 0.7 pad_maximum_fusion.2
  1.4 3.0 collective-permute-start
  4.4 0.7 dynamic_slice.33
  5.1 0.6 fusion.11
  5.7 1.9 fusion.4
  7.6 2.0 fusion.5
  9.5 3.1 broadcast_select_fusion.refs_4_
  12.6 127.5 %fetch_other_half.1 = (bf16[3072,512]{1,0:T(8,128)(2,1)}, bf16[512,1024]{1,0:T(8,128)(2,1)}, bf16[2048,2048]{1,0:T(8,128)(2,1)}, bf16[1024,2048]{1,0:T(8,128)(2,1)}, bf16[2,512,1024]{2,1,0:T(8,128)(2,1)}) custom-call(bf16[3072,512]{1,0:T(8,128)(2,1)} %bitcast.107, bf16[512,1024]{1,0:T(8,128)(2,1)} %bitcast.124, bf16[2048,2048]{1,0:T(8,128)(2,1)} %bitcast.81, ...), custom_call_target="tpu_custom_call" | custom-call | bytes 33554432 | tf_op jit(solution)/shard_map/fetch_other_half/pallas_call | solution.py:700
  140.2 3.1 slice_bitcast_fusion.1
  143.3 1.3 iota_compare_fusion
  144.6 0.6 pad_maximum_fusion.3.refs_11_.refs_20_
  145.3 0.6 convert_element_type.51.refs_12_.refs_21_
  145.9 0.6 maximum_convert_fusion.1.refs_10_
  146.5 0.6 maximum_convert_fusion.refs_13_
  147.1 39.8 %layer_forward.4 = (bf16[2,512,1024]{2,1,0:T(8,128)(2,1)}, bf16[2,512,1024]{2,1,0:T(8,128)(2,1)}, bf16[2,512,1024]{2,1,0:T(8,128)(2,1)}, bf16[2,512,1024]{2,1,0:...) custom-call(s32[3]{0:T(128)} %get-tuple-element.289.refs_0_, ...), custom_call_target="tpu_custom_call" | custom-call | flops 18253611008 | bytes 56623104 | tf_op jit(solution)/shard_map/layer_forward/pallas_call | solution.py:54
  186.9 1.4 collective-permute-start.2
  188.3 39.4 %layer_forward.5 = (bf16[2,512,1024]{2,1,0:T(8,128)(2,1)}, bf16[2,512,1024]{2,1,0:T(8,128)(2,1)}, bf16[2,512,1024]{2,1,0:T(8,128)(2,1)}, bf16[2,512,1024]{2,1,0:...) custom-call(s32[3]{0:T(128)} %get-tuple-element.288.refs_0_, ...), custom_call_target="tpu_custom_call", output_to_operand_aliasing={{0}: (14, {}), {1}: (15, {}), {2}: (16, {}), {3}: (17, {}),... | custom-call | flops 18253611008 | bytes 56623104 | tf_op jit(solution)/shard_map/layer_forward/pallas_call | solution.py:54
  227.7 2.3 collective-permute-start.1
  230.0 1.0 copy-done.1
  230.9 1.6 layer_forward.6
  232.5 2.3 broadcast_select_fusion.4
  234.8 17.7 %collective-permute-done.1.refs_1_ = bf16[512,1024]{1,0:T(8,128)(2,1)} collective-permute-done((bf16[512,1024]{1,0:T(8,128)(2,1)}, bf16[512,1024]{1,0:T(8,128)(2,1)}, u32[]{:S(2)}, u32[]{:S(2)}) %collective-permute-start.1) | collective-permute-done | bytes 1048608 | tf_op jit(solution)/shard_map/ppermute | solution.py:1479
  252.5 1.3 layer_forward.7
  254.0 0.9 constant_dynamic-slice_fusion
  254.9 0.3 copy-done.4
  255.2 1.0 constant_dynamic-slice_fusion.1
  256.3 1.5 collective-permute-start.5
  257.8 0.5 collective-permute-start.6
  258.3 2.0 select_bitcast_fusion.1
  260.3 1.4 layer_backward.4
  261.6 1.3 collective-permute-start.3
  262.9 6.0 layer_backward.5
  269.0 1.3 collective-permute-start.4
  270.3 2.8 pad_maximum_fusion.refs_2_
  273.1 8.3 %collective-permute-done.6 = bf16[256,1024]{1,0:T(8,128)(2,1)} collective-permute-done((bf16[256,1024]{1,0:T(8,128)(2,1)}, bf16[256,1024]{1,0:T(8,128)(2,1)}, u32[]{:S(2)}, u32[]{:S(2)}) %collective-permute-start.6) | collective-permute-done | bytes 524320 | tf_op jit(solution)/shard_map/ppermute | solution.py:1426
  281.4 3.1 maximum_select_fusion.1
  284.5 92.7 %collective-permute-done.3.refs_1_ = bf16[512,1024]{1,0:T(8,128)(2,1)} collective-permute-done((bf16[512,1024]{1,0:T(8,128)(2,1)}, bf16[512,1024]{1,0:T(8,128)(2,1)}, u32[]{:S(2)}, u32[]{:S(2)}) %collective-permute-start.3) | collective-permute-done | bytes 1048608 | tf_op jit(solution)/shard_map/ppermute | solution.py:1498
  377.2 48.3 %layer_backward.6 = (bf16[2,512,4096]{2,1,0:T(8,128)(2,1)}, bf16[2,512,4096]{2,1,0:T(8,128)(2,1)}, bf16[2,512,1024]{2,1,0:T(8,128)(2,1)}, bf16[2,512,1024]{2,1,0...) custom-call(s32[3]{0:T(128)} %get-tuple-element.289.refs_0_, ...), custom_call_target="tpu_custom_call", output_to_operand_aliasing={{0}: (22, {}), {1}: (23, {}), {2}: (24, {}), {3}: (25, {}),... | custom-call | flops 19864223744 | bytes 73400320 | tf_op jit(solution)/shard_map/layer_backward/pallas_call | solution.py:54
  425.5 2.1 dynamic-slice_select_fusion.3
  427.6 0.3 collective-permute-done.4.refs_1_
  428.0 48.6 %layer_backward.7 = (bf16[2,512,4096]{2,1,0:T(8,128)(2,1)}, bf16[2,512,4096]{2,1,0:T(8,128)(2,1)}, bf16[2,512,1024]{2,1,0:T(8,128)(2,1)}, bf16[2,512,1024]{2,1,0...) custom-call(s32[3]{0:T(128)} %get-tuple-element.288.refs_0_, ...), custom_call_target="tpu_custom_call", output_to_operand_aliasing={{0}: (22, {}), {1}: (23, {}), {2}: (24, {}), {3}: (25, {}),... | custom-call | flops 19864223744 | bytes 73400320 | tf_op jit(solution)/shard_map/layer_backward/pallas_call | solution.py:54
  476.6 2.0 dynamic-slice_select_fusion.2
  478.7 0.8 fusion.3
  479.5 0.7 select_add_fusion.1
  480.2 0.8 select_add_fusion
  481.1 0.6 pad_maximum_fusion.1.refs_11_
  481.8 225.9 %weight_grads_reduced.1 = (bf16[1,1024,2048]{2,1,0:T(8,128)(2,1)}, bf16[2,1024,2048]{2,1,0:T(8,128)(2,1)}, bf16[3,1024,512]{2,1,0:T(8,128)(2,1)}, bf16[1,1024,512]{2,1,0:T(8,128)(2,1)}, f32[16,1024]{1,0:T(8,128)}) custom-call(bf16[2,512,1024]{2,1,0:T(8,128)(2,1)} %get-tuple-element.232.refs_0_, bf16[2,512,1024]{2,1,0:T(8,128)(2,1)} %get-tuple-element.233.refs_1_, ...), custom_call_target="tpu_custom_call" | custom-call | flops 34359738368 | bytes 67108864 | tf_op jit(solution)/shard_map/weight_grads_reduced/pallas_call | solution.py:950
  707.7 0.8 slice.95
  708.4 1.6 fusion.8
  710.0 0.8 slice.101
  710.9 1.1 collective-permute-start.7
  712.1 1.0 collective-permute-start.8
  713.0 1.5 convert_bitcast_fusion.1
  714.5 1.8 copy.85
  716.3 6.7 convert_element_type.56
  723.0 11.8 %bitcast_convert_fusion = f32[1,2,1024,2048]{3,2,1,0:T(8,128)} fusion(bf16[2,1024,2048]{2,1,0:T(8,128)(2,1)} %get-tuple-element.246), kind=kLoop, calls=%fused_computation | loop fusion | flops 4194304 | bytes 25165824 | tf_op jit(solution)/shard_map/broadcast_in_dim | solution.py:1548
  735.0 1.4 copy-done.8
  736.6 0.6 dynamic-slice_bitcast_fusion.2
  737.2 0.6 maximum_bitcast_fusion.2
  737.8 0.6 maximum_bitcast_fusion.1
  738.4 0.6 dynamic-slice_bitcast_fusion.3
  739.0 3.6 convert_bitcast_fusion
  742.6 1.3 fusion.2
  744.0 2.4 maximum_select_fusion
  (72 shorter events, 0.8 us)
Async XLA Ops:
  1.4 144.5 %collective-permute-start = (bf16[2,2560]{1,0:T(2,128)(2,1)S(1)}, bf16[2,2560]{1,0:T(2,128)(2,1)S(1)}, u32[]{:S(2)}, u32[]{:S(2)}) collective-permute-start(bf16[2,2560]{1,0:T(2,128)(2,1)S(1)} %pad_maximum_fusion.2), channel_id=1, source_target_pairs={{0,8},{8,0},{1,9},{9,1},{2,10},{10,2},{3,11},{11,3},{4,12},{12,4},... | collective-permute-start | bytes 30728 | tf_op jit(solution)/shard_map/ppermute | solution.py:1426
  140.1 4.5 copy-start.21
  140.1 4.5 copy-start.22
  140.1 5.1 copy-start.16
  140.1 5.1 copy-start.27
  140.2 5.7 copy-start.23
  140.2 6.3 copy-start.20
  186.9 43.0 %collective-permute-start.2 = (bf16[512,1024]{1,0:T(8,128)(2,1)}, bf16[512,1024]{1,0:T(8,128)(2,1)S(1)}, u32[]{:S(2)}, u32[]{:S(2)}) collective-permute-start(bf16[512,1024]{1,0:T(8,128)(2,1)} %get-tuple-element.148.refs_27_), channel_id=1, source_target_pairs={{0,16},{1,17},{2,18},{3,19},{4,20},{5,21},{6,22},{7,23},{8,24},{9,... | collective-permute-start | bytes 3145736 | tf_op jit(solution)/shard_map/ppermute | solution.py:1479
  227.7 24.8 %collective-permute-start.1 = (bf16[512,1024]{1,0:T(8,128)(2,1)}, bf16[512,1024]{1,0:T(8,128)(2,1)}, u32[]{:S(2)}, u32[]{:S(2)}) collective-permute-start(bf16[512,1024]{1,0:T(8,128)(2,1)} %get-tuple-element.149.refs_27_), channel_id=1, source_target_pairs={{0,16},{1,17},{2,18},{3,19},{4,20},{5,21},{6,22},{7,23},{8,24},{9,... | collective-permute-start | bytes 3145736 | tf_op jit(solution)/shard_map/ppermute | solution.py:1479
  230.0 1.0 copy-start.1
  252.5 1.3 copy-start.3
  253.8 1.4 copy-start.4
  254.0 4.3 copy-start
  254.0 4.3 copy-start.2
  256.3 16.8 %collective-permute-start.5 = (bf16[256,1024]{1,0:T(8,128)(2,1)}, bf16[256,1024]{1,0:T(8,128)(2,1)}, u32[]{:S(2)}, u32[]{:S(2)}) collective-permute-start(bf16[256,1024]{1,0:T(8,128)(2,1)} %get-tuple-element.266), channel_id=1, source_target_pairs={{0,8},{8,0},{1,9},{9,1},{2,10},{10,2},{3,11},{11,3},{4,12},{12,4},... | collective-permute-start | bytes 1572872 | tf_op jit(solution)/shard_map/ppermute | solution.py:1426
  257.8 23.7 %collective-permute-start.6 = (bf16[256,1024]{1,0:T(8,128)(2,1)}, bf16[256,1024]{1,0:T(8,128)(2,1)}, u32[]{:S(2)}, u32[]{:S(2)}) collective-permute-start(bf16[256,1024]{1,0:T(8,128)(2,1)} %get-tuple-element.268), channel_id=1, source_target_pairs={{0,8},{8,0},{1,9},{9,1},{2,10},{10,2},{3,11},{11,3},{4,12},{12,4},... | collective-permute-start | bytes 1572872 | tf_op jit(solution)/shard_map/ppermute | solution.py:1426
  261.6 115.5 %collective-permute-start.3 = (bf16[512,1024]{1,0:T(8,128)(2,1)}, bf16[512,1024]{1,0:T(8,128)(2,1)}, u32[]{:S(2)}, u32[]{:S(2)}) collective-permute-start(bf16[512,1024]{1,0:T(8,128)(2,1)} %get-tuple-element.188), channel_id=1, source_target_pairs={{16,0},{17,1},{18,2},{19,3},{20,4},{21,5},{22,6},{23,7},{24,8},{25... | collective-permute-start | bytes 3145736 | tf_op jit(solution)/shard_map/ppermute | solution.py:1498
  269.0 158.9 %collective-permute-start.4 = (bf16[512,1024]{1,0:T(8,128)(2,1)}, bf16[512,1024]{1,0:T(8,128)(2,1)}, u32[]{:S(2)}, u32[]{:S(2)}) collective-permute-start(bf16[512,1024]{1,0:T(8,128)(2,1)} %get-tuple-element.206), channel_id=1, source_target_pairs={{16,0},{17,1},{18,2},{19,3},{20,4},{21,5},{22,6},{23,7},{24,8},{25... | collective-permute-start | bytes 3145736 | tf_op jit(solution)/shard_map/ppermute | solution.py:1498
  270.3 11.2 %copy-start.6 = (bf16[1,256,1024]{2,1,0:T(8,128)(2,1)S(1)}, bf16[1,256,1024]{2,1,0:T(8,128)(2,1)}, u32[]{:S(2)}) copy-start(bf16[1,256,1024]{2,1,0:T(8,128)(2,1)} %get-tuple-element.267) | copy-start | bytes 1572868
  377.2 48.3 %copy-start.12 = (bf16[512,1024]{1,0:T(8,128)(2,1)S(1)}, bf16[512,1024]{1,0:T(8,128)(2,1)}, u32[]{:S(2)}) copy-start(bf16[512,1024]{1,0:T(8,128)(2,1)} %get-tuple-element.188) | copy-start | bytes 3145732
  427.9 48.7 %copy-start.11 = (bf16[512,1024]{1,0:T(8,128)(2,1)S(1)}, bf16[512,1024]{1,0:T(8,128)(2,1)}, u32[]{:S(2)}) copy-start(bf16[512,1024]{1,0:T(8,128)(2,1)} %get-tuple-element.206) | copy-start | bytes 3145732
  427.9 50.8 %copy-start.13 = (f32[8,1024]{1,0:T(8,128)S(1)}, f32[8,1024]{1,0:T(8,128)}, u32[]{:S(2)}) copy-start(f32[8,1024]{1,0:T(8,128)} %get-tuple-element.196.refs_29_) | copy-start | bytes 98308
  427.9 50.8 %copy-start.14 = (f32[8,1024]{1,0:T(8,128)S(1)}, f32[8,1024]{1,0:T(8,128)}, u32[]{:S(2)}) copy-start(f32[8,1024]{1,0:T(8,128)} %get-tuple-element.204.refs_29_) | copy-start | bytes 98308
  427.9 50.8 %copy-start.15 = (f32[8,1024]{1,0:T(8,128)S(1)}, f32[8,1024]{1,0:T(8,128)}, u32[]{:S(2)}) copy-start(f32[8,1024]{1,0:T(8,128)} %get-tuple-element.205.refs_29_) | copy-start | bytes 98308
  427.9 51.5 %copy-start.24 = (f32[2,1024]{1,0:T(2,128)S(1)}, f32[2,1024]{1,0:T(2,128)}, u32[]{:S(2)}) copy-start(f32[2,1024]{1,0:T(2,128)} %get-tuple-element.220) | copy-start | bytes 24580
  427.9 51.5 %copy-start.25 = (f32[2,1024]{1,0:T(2,128)S(1)}, f32[2,1024]{1,0:T(2,128)}, u32[]{:S(2)}) copy-start(f32[2,1024]{1,0:T(2,128)} %get-tuple-element.222) | copy-start | bytes 24580
  427.9 51.5 %copy-start.26 = (f32[2,1024]{1,0:T(2,128)S(1)}, f32[2,1024]{1,0:T(2,128)}, u32[]{:S(2)}) copy-start(f32[2,1024]{1,0:T(2,128)} %get-tuple-element.219) | copy-start | bytes 24580
  427.9 52.2 %copy-start.17 = (f32[2,4096]{1,0:T(2,128)S(1)}, f32[2,4096]{1,0:T(2,128)}, u32[]{:S(2)}) copy-start(f32[2,4096]{1,0:T(2,128)} %get-tuple-element.216) | copy-start | bytes 98308
  428.0 52.2 %copy-start.18 = (f32[2,4096]{1,0:T(2,128)S(1)}, f32[2,4096]{1,0:T(2,128)}, u32[]{:S(2)}) copy-start(f32[2,4096]{1,0:T(2,128)} %get-tuple-element.218) | copy-start | bytes 98308
  428.0 52.2 %copy-start.19 = (f32[2,4096]{1,0:T(2,128)S(1)}, f32[2,4096]{1,0:T(2,128)}, u32[]{:S(2)}) copy-start(f32[2,4096]{1,0:T(2,128)} %get-tuple-element.215) | copy-start | bytes 98308
  710.9 31.7 %collective-permute-start.7 = (bf16[256,1024]{1,0:T(8,128)(2,1)}, bf16[256,1024]{1,0:T(8,128)(2,1)}, u32[]{:S(2)}, u32[]{:S(2)}) collective-permute-start(bf16[256,1024]{1,0:T(8,128)(2,1)} %dynamic-slice_select_fusion.3), channel_id=1, source_target_pairs={{0,8},{8,0},{1,9},{9,1},{2,10},{10,2},{3,11},{11,3},{4,12},{12,4},... | collective-permute-start | bytes 1572872 | tf_op jit(solution)/shard_map/ppermute | solution.py:1426
  712.1 30.6 %collective-permute-start.8 = (bf16[256,1024]{1,0:T(8,128)(2,1)}, bf16[256,1024]{1,0:T(8,128)(2,1)}, u32[]{:S(2)}, u32[]{:S(2)}) collective-permute-start(bf16[256,1024]{1,0:T(8,128)(2,1)} %dynamic-slice_select_fusion.2), channel_id=1, source_target_pairs={{0,8},{8,0},{1,9},{9,1},{2,10},{10,2},{3,11},{11,3},{4,12},{12,4},... | collective-permute-start | bytes 1572872 | tf_op jit(solution)/shard_map/ppermute | solution.py:1426
  723.0 11.9 %copy-start.7 = (f32[512,1024]{1,0:T(8,128)S(1)}, f32[512,1024]{1,0:T(8,128)}, u32[]{:S(2)}) copy-start(f32[512,1024]{1,0:T(8,128)} %get-tuple-element.229) | copy-start | bytes 6291460
  723.0 11.9 %copy-start.9 = (f32[512,1024]{1,0:T(8,128)S(1)}, f32[512,1024]{1,0:T(8,128)}, u32[]{:S(2)}) copy-start(f32[512,1024]{1,0:T(8,128)} %get-tuple-element.228) | copy-start | bytes 6291460
  723.0 12.0 %copy-start.10 = (f32[512,1024]{1,0:T(8,128)S(1)}, f32[512,1024]{1,0:T(8,128)}, u32[]{:S(2)}) copy-start(f32[512,1024]{1,0:T(8,128)} %get-tuple-element.230) | copy-start | bytes 6291460
  734.8 1.6 copy-start.8
  735.0 4.0 copy-start.5

commit v5 on v4

--- a/solution.py
+++ b/solution.py
@@ -2,6 +2,7 @@
 
 import jax
 import jax.numpy as jnp
+import numpy as np
 from jax import lax
 from jax.experimental import pallas as pl
 from jax.experimental.pallas import tpu as pltpu
@@ -352,7 +353,8 @@
             copy(src, dst, g_sem.at[index]).wait()
         sums = [jnp.zeros((1, width), F32)] * 3
         for rs in halves(rows):
-            grad_y = g_ref[rs, :].astype(F32)
+            places = lax.broadcasted_iota(jnp.int32, (rows // 2, width), 0) + rs.start
+            grad_y = jnp.where(places < meta_ref[3], g_ref[rs, :].astype(F32), 0.0)
             u = u_ref[1, rs, :].astype(F32)
             grad_c = norm_back(grad_y, u, r_ref[1, rs, 0:1], vec[4:5])
             acc_ref[rs, :] = grad_c
@@ -549,10 +551,11 @@
     pl.semaphore_wait(barrier, 1 + chips)
 
 
-def fetch_other_half(qkv, out, up, down, held, chips):
+def fetch_other_half(qkv, out, up, down, qv_bias, up_bias, inputs, cotangent, chips):
     weights = [qkv, out, up, down]
-    seqs = held.shape[0] // 2
-    shard_rows = held.shape[1]
+    biases = [qv_bias, up_bias]
+    seqs = inputs.shape[0] // 2
+    shard_rows, width = inputs.shape[1:]
     groups = 2 * chips
 
     def rows_of(item):
@@ -567,6 +570,8 @@
     plan.append((3, True, 0, spread // groups, 0, spread // groups))
     n_spread = len(plan)
     plan.append((-1, False, 0, 0, 0, 0))
+    plan.append((-2, False, 0, 0, 0, 0))
+    plan.append((-2, False, 0, 0, 0, 1))
     for part in range(3):
         size = rows_of(0) // 6
         plan.append((0, False, 0, rows_of(0) // 2, part * size, size))
@@ -578,10 +583,11 @@
     n = len(plan)
 
     def kernel(*refs):
-        ins, held_ref = refs[:4], refs[4]
-        outs, rows_ref = refs[5:9], refs[9]
-        stage, x_send, x_recv, c_send, c_recv, u_send, u_recv, d_send, d_recv, l_sem = refs[10:]
+        ins, bias_ins, held_refs = refs[:4], refs[4:6], refs[6:8]
+        outs, bias_outs, row_refs = refs[8:12], refs[12:14], refs[14 : 14 + seqs]
+        stage, x_send, x_recv, c_send, c_recv, u_send, u_recv, d_send, d_recv, l_sem = refs[14 + seqs :]
         t, c, z, last, core, cross, above, below = neighbours()
+        section = lax.axis_index("section")
         greet(c, z, chips, core, cross)
 
         def rows(index, chip, on):
@@ -589,11 +595,16 @@
             place = chip * 2 + on if is_spread else on
             return item, pl.ds(pl.multiple_of(base + place * piece + offset, size), size)
 
-        def cross_copy(index):
-            if plan[index][0] < 0:
-                m = plan[index][5]
-                src = held_ref.at[(1 - t) * seqs + m]
-                dst = rows_ref.at[m, pl.ds(pl.multiple_of(t * shard_rows, shard_rows), shard_rows)]
+        def span(part):
+            return block(part, shard_rows)
+
+        def cross_copy(index, held_ref=None):
+            m = plan[index][5]
+            if plan[index][0] == -1:
+                src = (held_refs[0] if held_ref is None else held_ref).at[(1 - t) * seqs + m]
+                dst = row_refs[m].at[span(t)]
+            elif plan[index][0] == -2:
+                src, dst = bias_ins[m], bias_outs[m]
             else:
                 item, where = rows(index, z, c)
                 src, dst = ins[item].at[where], outs[item].at[where]
@@ -615,23 +626,30 @@
             arrived(outs[item].at[where], sem)
 
         for index in range(n):
-            cross_copy(index).start()
-        mine = pltpu.make_async_copy(held_ref.at[pl.ds(t * seqs, seqs)], stage, l_sem)
-        mine.start()
-        mine.wait()
+            if plan[index][0] == -1:
+                for turn in range(2):
+                    @pl.when(section == turn)
+                    def _(index=index, turn=turn):
+                        cross_copy(index, held_refs[turn]).start()
+            else:
+                cross_copy(index).start()
+        for turn in range(2):
+            @pl.when(section == turn)
+            def _(turn=turn):
+                copy(held_refs[turn].at[pl.ds(t * seqs, seqs)], stage, l_sem).start()
+
+        arrived(stage, l_sem)
         for m in range(seqs):
-            pltpu.make_async_copy(
-                stage.at[m], rows_ref.at[m, pl.ds(pl.multiple_of(t * shard_rows, shard_rows), shard_rows)], l_sem
-            ).start()
+            copy(stage.at[m], row_refs[m].at[span(t)], l_sem).start()
 
         def handle(index, hop):
             if hop == 0:
-                if plan[index][0] < 0:
-                    m = plan[index][5]
-                    arrived(
-                        rows_ref.at[m, pl.ds(pl.multiple_of((1 - t) * shard_rows, shard_rows), shard_rows)],
-                        x_recv.at[index],
-                    )
+                m = plan[index][5]
+                if plan[index][0] == -1:
+                    arrived(row_refs[m].at[span(1 - t)], x_recv.at[index])
+                    return
+                if plan[index][0] == -2:
+                    arrived(bias_outs[m], x_recv.at[index])
                     return
                 got(index, z, c, x_recv.at[index])
                 pass_on(index, z, c_send, c_recv, core).start()
@@ -699,21 +717,21 @@
     moved = sum(w.size for w in weights) * 2
     return pl.pallas_call(
         kernel,
-        in_specs=[ANY] * 5,
-        out_specs=[ANY] * 5,
-        out_shape=[jax.ShapeDtypeStruct(w.shape, BF) for w in weights]
-        + [jax.ShapeDtypeStruct((seqs, 2 * shard_rows, held.shape[2]), BF)],
-        scratch_shapes=[pltpu.VMEM((seqs,) + held.shape[1:], BF)]
+        in_specs=[ANY] * 8,
+        out_specs=[ANY] * (6 + seqs),
+        out_shape=[jax.ShapeDtypeStruct(w.shape, BF) for w in weights + biases]
+        + [jax.ShapeDtypeStruct((2 * shard_rows, width), BF)] * seqs,
+        scratch_shapes=[pltpu.VMEM((seqs, shard_rows, width), BF)]
         + [sem((n,)), sem((n,))]
         + [sem((n, chips))] * 6
         + [sem],
         compiler_params=pltpu.CompilerParams(collective_id=1, has_side_effects=True),
         cost_estimate=pl.CostEstimate(flops=0, bytes_accessed=2 * moved, transcendentals=0),
         name="fetch_other_half",
-    )(*weights, held)
-
-
-def weight_grads_reduced(groups, sums, chips):
+    )(*weights, *biases, inputs, cotangent)
+
+
+def weight_grads_reduced(groups, sums, row_grads, chips):
     seqs = 2
     rows, depth = groups[0][0].shape[1:]
     lefts = [g[0] for g in groups]
@@ -735,19 +753,23 @@
     last_static = chips - 1
     drain = CORE_LAG + CROSS_LAG + 2 * last_static * CHAIN_LAG + 1
     vec_shape = sums.shape
+    n_in = n_left + n_right + 1 + 2 * seqs
+    shard_rows = rows // 2
 
     def kernel(*refs):
         left_refs = refs[:n_left]
         right_refs = refs[n_left : n_left + n_right]
         sums_ref = refs[n_left + n_right]
-        outs = refs[n_left + n_right + 1 : 2 * n_left + n_right + 1]
-        sums_out = refs[2 * n_left + n_right + 1]
+        row_refs = refs[n_left + n_right + 1 : n_in]
+        outs = refs[n_in : n_in + n_left]
+        sums_out, rows_out = refs[n_in + n_left : n_in + n_left + 2]
         (
             acc, from_x, from_z, final, flip, stage, tile, mine, give, vec, vec_in, vec_all,
             tile_sem, stage_sem, give_send, core_recv, x_send, x_recv, z_send, z_recv, f_send, f_recv,
-            store_sem, out_send, out_recv, v_load, v_send, v_recv,
-        ) = refs[2 * n_left + n_right + 2 :]
+            store_sem, out_send, out_recv, v_load, v_send, v_recv, r_send, r_recv,
+        ) = refs[n_in + n_left + 2 :]
         t, c, z, last, core, cross, above, below = neighbours()
+        section = lax.axis_index("section")
         greet(c, z, chips, core, cross)
 
         def remote(src, dst, send, recv, device):
@@ -790,6 +812,12 @@
         vec_core = remote(vec.at[0], vec_in.at[0], v_send.at[0], v_recv.at[0], core)
         vec_cross = remote(vec.at[1], vec_in.at[1], v_send.at[1], v_recv.at[1], cross)
         vec_core.start()
+        for turn in range(2):
+            @pl.when(section == turn)
+            def _(turn=turn):
+                for m in range(seqs):
+                    source = row_refs[turn * seqs + m].at[block(1 - t, shard_rows)]
+                    remote(source, rows_out.at[m], r_send.at[m], r_recv.at[m], cross).start()
 
         up = pl.ds(0, quarter)
         down = pl.ds(quarter, quarter)
@@ -919,6 +947,9 @@
                         vec_all.at[z], vec_all.at[z], v_send.at[1 + shift], v_recv.at[1 + shift], {"dp": to * 2 + c}
                     ).start()
 
+        for m in range(seqs):
+            arrived(rows_out.at[m], r_recv.at[m])
+            arrived(rows_out.at[m], r_send.at[m])
         vec_core.wait_send()
         vec_cross.wait_send()
         for shift in range(1, chips):
@@ -949,10 +980,10 @@
     flops = 2 * seqs * rows * depth * 2 * bt * total
     return pl.pallas_call(
         kernel,
-        in_specs=[ANY] * (n_left + n_right + 1),
-        out_specs=[ANY] * n_left + [WHOLE],
+        in_specs=[ANY] * n_in,
+        out_specs=[ANY] * n_left + [WHOLE, ANY],
         out_shape=[jax.ShapeDtypeStruct((len(g[1]), depth, g[1][0].shape[2] // 2), BF) for g in groups]
-        + [jax.ShapeDtypeStruct(vec_shape, F32)],
+        + [jax.ShapeDtypeStruct(vec_shape, F32), jax.ShapeDtypeStruct((seqs, shard_rows, depth), BF)],
         scratch_shapes=[
             pltpu.VMEM((total, 2, half, bt), BF),
             pltpu.VMEM((total, half, bt), BF),
@@ -968,14 +999,107 @@
             pltpu.VMEM((chips,) + vec_shape, F32),
             sem((tiles,)), sem, sem((gives,)), sem((total,)), sem, sem((total,)),
             sem((2,)), sem((2, total)), sem((2,)), sem((2, total)),
-            sem, sem, sem, sem, sem((chips + 1,)), sem((chips + 1,)),
+            sem, sem, sem, sem, sem((chips + 1,)), sem((chips + 1,)), sem((seqs,)), sem((seqs,)),
         ],
         compiler_params=pltpu.CompilerParams(
             collective_id=0, has_side_effects=True, vmem_limit_bytes=VMEM_LIMIT
         ),
         cost_estimate=pl.CostEstimate(flops=flops, bytes_accessed=64 << 20, transcendentals=0),
         name="weight_grads_reduced",
-    )(*lefts, *rights, sums)
+    )(*lefts, *rights, sums, *row_grads)
+
+
+def widen(reduced, row_grads, got):
+    seqs, shard_rows, width = got.shape
+    n = len(reduced)
+    jobs = []
+    for index, array in enumerate(reduced):
+        lead, depth, columns = array.shape
+        step = 512 * 1024 // columns
+        if index == n - 1:
+            jobs += [(index, 0, at, depth // 2, columns) for at in range(0, depth, depth // 2)]
+        else:
+            jobs += [(index, part, at, step, columns) for part in range(lead) for at in range(0, depth, step)]
+    jobs += [(n, m, 0, shard_rows, width) for m in range(seqs)] + [(n + 1, m, 0, shard_rows, width) for m in range(seqs)]
+    ring = 3
+    size = 512 * 1024
+
+    def kernel(*refs):
+        ins = refs[:n]
+        grad_refs = refs[n : n + 2 * seqs]
+        got_ref = refs[n + 2 * seqs]
+        outs = refs[n + 2 * seqs + 1 : 2 * n + 2 * seqs + 2]
+        shapes = sorted({(j[3], j[4]) for j in jobs if j[0] != n})
+        buffers = refs[2 * n + 2 * seqs + 2 :]
+        wide_rows, in_sem, out_sem = buffers[0], buffers[1], buffers[2]
+        low = {s: buffers[3 + 2 * i] for i, s in enumerate(shapes)}
+        wide = {s: buffers[4 + 2 * i] for i, s in enumerate(shapes)}
+        t = lax.axis_index("tensor")
+        section = lax.axis_index("section")
+
+        def load(number):
+            index, part, at, rows, columns = jobs[number]
+            s = number % ring
+            if index < n:
+                copy(ins[index].at[part, pl.ds(at, rows)], low[rows, columns].at[s], in_sem.at[s]).start()
+            elif index == n:
+                for turn in range(2):
+                    @pl.when(section == turn)
+                    def _(turn=turn):
+                        source = grad_refs[turn * seqs + part].at[block(t, shard_rows)]
+                        copy(source, wide_rows.at[part], in_sem.at[s]).start()
+            else:
+                copy(got_ref.at[part], low[rows, columns].at[s], in_sem.at[s]).start()
+
+        def store(number):
+            index, part, at, rows, columns = jobs[number]
+            s = number % ring
+            if index < n - 1:
+                return copy(wide[rows, columns].at[s], outs[index].at[part, pl.ds(at, rows)], out_sem.at[s])
+            if index == n - 1:
+                return copy(wide[rows, columns].at[s], outs[index].at[:, pl.ds(at, rows)], out_sem.at[s])
+            if index == n:
+                return copy(wide_rows.at[part], outs[n].at[t * seqs + part], out_sem.at[s])
+            return copy(wide[rows, columns].at[s], outs[n].at[(1 - t) * seqs + part], out_sem.at[s])
+
+        for number in range(ring):
+            load(number)
+        for number, (index, part, at, rows, columns) in enumerate(jobs):
+            s = number % ring
+            if index == n:
+                arrived(wide_rows.at[part], in_sem.at[s])
+            else:
+                arrived(low[rows, columns].at[s], in_sem.at[s])
+            if number >= ring:
+                store(number - ring).wait()
+            if index == n - 1:
+                wide[rows, columns][s] = low[rows, columns][s].astype(F32).T
+            elif index != n:
+                wide[rows, columns][s] = low[rows, columns][s].astype(F32)
+            store(number).start()
+            if number + ring < len(jobs):
+                load(number + ring)
+        for number in range(len(jobs) - ring, len(jobs)):
+            store(number).wait()
+
+    shapes = sorted({(j[3], j[4]) for j in jobs if j[0] != n})
+    square = (reduced[-1].shape[1] // 2, reduced[-1].shape[2])
+    last = reduced[-1].shape
+    sem = pltpu.SemaphoreType.DMA
+    buffers = []
+    for s in shapes:
+        buffers += [pltpu.VMEM((ring,) + s, BF), pltpu.VMEM((ring,) + ((s[1], s[0]) if s == square else s), F32)]
+    return pl.pallas_call(
+        kernel,
+        in_specs=[ANY] * (n + 2 * seqs + 1),
+        out_specs=[ANY] * (n + 1),
+        out_shape=[jax.ShapeDtypeStruct(r.shape, F32) for r in reduced[:-1]]
+        + [jax.ShapeDtypeStruct((last[2], last[1]), F32), jax.ShapeDtypeStruct((2 * seqs, shard_rows, width), F32)],
+        scratch_shapes=[pltpu.VMEM((seqs, shard_rows, width), F32), sem((ring,)), sem((ring,))] + buffers,
+        compiler_params=pltpu.CompilerParams(vmem_limit_bytes=VMEM_LIMIT),
+        cost_estimate=pl.CostEstimate(flops=0, bytes_accessed=56 << 20, transcendentals=0),
+        name="widen",
+    )(*reduced, *row_grads, got)
 
 
 MASKED = -1000000000.0
@@ -1428,41 +1552,38 @@
     def part_rows(value, part):
         return lax.dynamic_slice_in_dim(value, part * shard_rows, shard_rows, 0)
 
-    def own_rows(values, got):
-        kept_rows = jnp.stack([part_rows(v, place) for v in values])
-        return join(kept_rows, jnp.stack(got).astype(kept_rows.dtype), place == 1)
-
     qkv_own = jnp.transpose(w_qkv[0], (1, 0, 2))
     out_own = w_out[0]
     up_own = w_up[0]
     down_own = w_down[0]
-    small = across(jnp.concatenate([b_qv[0], b_up[0]], axis=1))
     first = section == 0
-    qkv_oth, out_oth, up_oth, down_oth, held = fetch_other_half(
+    qkv_oth, out_oth, up_oth, down_oth, qv_oth, ub_oth, *held = fetch_other_half(
         qkv_own.reshape(3 * width, local),
         out_own,
         up_own.reshape(2 * width, units),
         down_own,
-        jnp.where(first, inputs, cotangent),
+        b_qv[0],
+        b_up[0],
+        inputs,
+        cotangent,
         chips,
     )
     qkv_oth = qkv_oth.reshape(3, width, local)
     up_oth = up_oth.reshape(2, width, units)
-    x_first = outer = [held[m] for m in range(seqs)]
-
-    bias = jnp.concatenate([b_qv[0], small[:, :local]], axis=1).astype(F32)
-    up_bias = jnp.concatenate([b_up[0], small[:, local:]], axis=1).astype(F32)
+    x_first = outer = held
+
+    bias = jnp.concatenate([b_qv[0], qv_oth], axis=1).astype(F32)
+    up_bias = jnp.concatenate([b_up[0], ub_oth], axis=1).astype(F32)
     vecs = jnp.stack(
         [b_out[0], ln_gain[0, 0], ln_bias[0, 0], b_down[0], ln_gain[0, 1], ln_bias[0, 1], b_out[0], b_out[0]]
     ).astype(F32)
-    slopes = jnp.concatenate(
-        [alibi_slopes(place * heads, heads, H), alibi_slopes((1 - place) * heads, heads, H)]
-    )
+    slope_table = np.exp2(-8.0 * (np.arange(2 * heads, dtype=np.float32) + 1.0) / H).astype(np.float32)
+    slopes = jnp.where(place == 0, slope_table, np.roll(slope_table, heads))
     own_lengths = lax.dynamic_slice_in_dim(lengths, place * seqs, seqs, 0)
 
     def meta(m, turn):
         active = section == turn
-        return jnp.stack([jnp.int32(m), active.astype(jnp.int32), own_lengths[m]])
+        return jnp.stack([jnp.int32(m), active.astype(jnp.int32), own_lengths[m], own_lengths[m] if turn == 1 else jnp.int32(rows)])
 
     metas = [[meta(m, turn) for m in range(seqs)] for turn in range(2)]
     weights = (qkv_own, qkv_oth, out_own, out_oth, up_own, up_oth, down_own, down_oth)
@@ -1491,21 +1612,19 @@
         sums[turn][m] = (norm_sums, up_sums, qv_sums)
         return gx, gx_low
 
-    row = jnp.arange(rows)[:, None]
-    gx_second = [
-        backward(jnp.where(row < own_lengths[m], outer[m], 0), m, 1) for m in range(seqs)
-    ]
+    gx_second = [backward(outer[m], m, 1) for m in range(seqs)]
     grad_middle = [lax.ppermute(gx_second[m][1], "section", [(1, 0)]) for m in range(seqs)]
+    y_all, _ = lax.optimization_barrier(((y_first, y_second), deps))
+    y_own = [jnp.where(first, a, b) for a, b in zip(*y_all)]
+    y_kept = jnp.stack([part_rows(y, place) for y in y_own])
+    y_got = jnp.stack([across(part_rows(y, 1 - place)) for y in y_own])
+    produced = join(y_kept, y_got, place == 1)
+    x_all = jnp.stack([jnp.where(first, x_first[m], x_second[m]) for m in range(seqs)])
+    deps = deps + [x_all]
     gx_first = [backward(grad_middle[m], m, 0) for m in range(seqs)]
 
     mixed, hidden, normed = kept[3], kept[7], kept[8]
-    x_all = jnp.stack([jnp.where(first, x_first[m], x_second[m]) for m in range(seqs)])
     gg0, gg1, gl, ga, *gqkv = back
-
-    y_own = [jnp.where(first, a, b) for a, b in zip(y_first, y_second)]
-    produced = own_rows(y_own, [across(part_rows(y, 1 - place)) for y in y_own])
-    gx_own = [jnp.where(first, a[0], b[0]) for a, b in zip(gx_first, gx_second)]
-    gx_sent = [part_rows(jnp.where(first, a[1], b[1]), 1 - place) for a, b in zip(gx_first, gx_second)]
 
     picked = [
         sum(jnp.where(first, sums[0][m][index], sums[1][m][index]) for m in range(seqs))
@@ -1519,16 +1638,13 @@
         ).reshape(-1, width)
 
     packed = jnp.concatenate([norm_sums[:6], ordered(up_sums[:2], units), ordered(qv_sums[:2], local)])
-    packed, produced, gx_sent = lax.optimization_barrier((packed, produced, gx_sent))
-    gx_got = [across(value) for value in gx_sent]
-    down_sum, up_sum, qkv_sum, out_sum, packed = weight_grads_reduced(
-        [(gl, [hidden]), (normed, [gg0, gg1]), (x_all, gqkv), (ga, [mixed])], packed, chips
+    low_grads = [g[1] for g in gx_first + gx_second]
+    *reduced, packed, got = weight_grads_reduced(
+        [(gl, [hidden]), (normed, [gg0, gg1]), (x_all, gqkv), (ga, [mixed])], packed, low_grads, chips
     )
-    grads_in = own_rows(gx_own, gx_got)
-    up_sum = up_sum.astype(F32)
-    down_sum = down_sum[0].astype(F32)
-    qkv_sum = jnp.transpose(qkv_sum, (1, 0, 2)).astype(F32)
-    out_sum = out_sum[0].T.astype(F32)
+    down_sum, up_sum, qkv_sum, out_sum, grads_in = widen(reduced, [g[0] for g in gx_first + gx_second], got)
+    down_sum = down_sum[0]
+    qkv_sum = jnp.transpose(qkv_sum, (1, 0, 2))
     norm_total = packed[:6]
     up_total = packed[6 : 6 + 4 * units // width].reshape(2, 2 * units)
     qv_total = packed[6 + 4 * units // width :].reshape(2, 2 * local)

time: 755 us -> 814 us (1.078)
  waiting for transfers between devices: 119 us -> 182 us
  Pallas kernels: 540 us -> 588 us
  other arithmetic: 57.6 us -> 15.3 us
    ppermute x2, waiting for transfers between devices: 93 us -> 145 us  [by_sequence(): lax.ppermute(gx_second[m][1], 'section', [(1, 0)])]
    pallas_call x2 -> x3, Pallas kernels: 353 us -> 394 us  [the longest x1 243 us: weight_grads_reduced(): pl.pallas_call(kernel, in_specs=[ANY] * n_in, out_specs=[ANY] * n_left +...]
    broadcast_in_dim x3 -> x0, other arithmetic: 16.9 us -> none  [the longest x1 11.8 us: by_sequence(): up_sum[None]]
    ppermute x5 -> x2, waiting for transfers between devices: 8.35 us -> 18.4 us  [across(): return lax.ppermute(value, 'tensor', [(0, 1), (1, 0)])]
    select_n x5 -> x3, other arithmetic: 9.69 us -> 0.81 us  [the longest x1 0.57 us: by_sequence(): slopes = jnp.where(place == 0, slope_table, np.roll(slope_table, heads))]
    pallas_call x8, Pallas kernels: 186 us -> 195 us  [call(): pl.pallas_call(body, in_specs=specs, out_specs=[ANY] * n_out, out_shape=[...]
  transfers between devices with their start and end apart: 9 -> 6, of which waited for: 4 -> 4; matrix products, arithmetic and copies ran while one was open for 7% -> 1% of each run, Pallas kernels for 30% -> 11%
where the time goes in v5:
time: 814 us; the launch traced here: 805 us
  Pallas kernels  588 us (72%)
  waiting for transfers between devices  182 us (22%)
  other arithmetic  15.3 us (2%)
  local copies, waits for them, and re-layouts  9.48 us (1%)
  starting transfers between devices  8.34 us (1%)
    pallas_call x1, Pallas kernels, weight_grads_reduced(): pl.pallas_call(kernel, in_specs=[ANY] * n_in, out_specs=[ANY] * n_left +...  243 us
    pallas_call x8, Pallas kernels, call(): pl.pallas_call(body, in_specs=specs, out_specs=[ANY] * n_out, out_shape=[...  195 us
    ppermute x2, waiting for transfers between devices, by_sequence(): lax.ppermute(gx_second[m][1], 'section', [(1, 0)])  145 us
    pallas_call x1, Pallas kernels, fetch_other_half(): pl.pallas_call(kernel, in_specs=[ANY] * 8, out_specs=[ANY] * (6 + seqs),...  131 us
    pallas_call x1, Pallas kernels, widen(): pl.pallas_call(kernel, in_specs=[ANY] * (n + 2 * seqs + 1), out_specs=[AN...  20 us
    ppermute x2, waiting for transfers between devices, across(): return lax.ppermute(value, 'tensor', [(0, 1), (1, 0)])  18.4 us
    ppermute x2, waiting for transfers between devices, by_sequence(): x_second = [lax.ppermute(y, 'section', [(0, 1)]) for y in y_first]  18.3 us
  transfers between devices with their start and end apart: 6, of which 4 were waited for; matrix products, arithmetic and copies ran while one was open for 1% of the time, Pallas kernels for 11%

profile of v5, /device:TPU:0, one launch (start us, length us, event | category | flops | bytes accessed | tf_op | source)
XLA Modules:
  0.0 804.6 jit_solution(17878633170622049838)
XLA Ops:
  0.7 0.7 dynamic_slice.21
  1.4 0.6 fusion.10
  2.0 0.0 copy-start.22
  2.0 0.0 copy-start.12
  2.0 0.0 copy-start.23
  2.0 0.0 copy-start.24
  2.0 130.9 %fetch_other_half.1 = (bf16[3072,512]{1,0:T(8,128)(2,1)}, bf16[512,1024]{1,0:T(8,128)(2,1)}, bf16[2048,2048]{1,0:T(8,128)(2,1)}, bf16[1024,2048]{1,0:T(8,128)(2,...) custom-call(bf16[3072,512]{1,0:T(8,128)(2,1)} %bitcast.73, ...), custom_call_target="tpu_custom_call" | custom-call | bytes 33554432 | tf_op jit(solution)/shard_map/fetch_other_half/pallas_call | solution.py:718
  133.0 1.3 maximum_convert_fusion.1.refs_10_
  134.2 0.0 copy-done.16
  134.3 0.1 stack.53
  134.3 0.6 convert_element_type.14.refs_12_.refs_21_
  134.9 1.3 maximum_convert_fusion.refs_13_
  136.3 0.6 broadcast_select_fusion.2.refs_11_.refs_20_
  136.8 2.0 pad_add_fusion
  138.8 39.7 %layer_forward.4 = (bf16[2,512,1024]{2,1,0:T(8,128)(2,1)}, bf16[2,512,1024]{2,1,0:T(8,128)(2,1)}, bf16[2,512,1024]{2,1,0:T(8,128)(2,1)}, bf16[2,512,1024]{2,1,0:...) custom-call(s32[4]{0:T(128)} %get-tuple-element.287.refs_0_, ...), custom_call_target="tpu_custom_call" | custom-call | flops 18253611008 | bytes 56623104 | tf_op jit(solution)/shard_map/layer_forward/pallas_call | solution.py:55
  178.5 1.4 collective-permute-start
  179.9 39.3 %layer_forward.5 = (bf16[2,512,1024]{2,1,0:T(8,128)(2,1)}, bf16[2,512,1024]{2,1,0:T(8,128)(2,1)}, bf16[2,512,1024]{2,1,0:T(8,128)(2,1)}, bf16[2,512,1024]{2,1,0:...) custom-call(s32[4]{0:T(128)} %get-tuple-element.286.refs_0_, ...), custom_call_target="tpu_custom_call", output_to_operand_aliasing={{0}: (14, {}), {1}: (15, {}), {2}: (16, {}), {3}: (17, {}),... | custom-call | flops 18253611008 | bytes 56623104 | tf_op jit(solution)/shard_map/layer_forward/pallas_call | solution.py:55
  219.2 2.3 collective-permute-start.1
  221.5 1.9 fusion.3
  223.4 0.0 collective-permute-done.refs_1_
  223.4 1.0 copy-done.1
  224.4 1.3 layer_forward.6
  225.7 18.3 %collective-permute-done.1.refs_1_ = bf16[512,1024]{1,0:T(8,128)(2,1)} collective-permute-done((bf16[512,1024]{1,0:T(8,128)(2,1)}, bf16[512,1024]{1,0:T(8,128)(2,1)}, u32[]{:S(2)}, u32[]{:S(2)}) %collective-permute-start.1) | collective-permute-done | bytes 1048608 | tf_op jit(solution)/shard_map/ppermute | solution.py:1600
  244.0 1.5 layer_forward.7
  245.6 7.0 layer_backward.4
  252.6 8.0 layer_backward.5
  260.6 0.0 copy-start.3
  260.6 0.1 broadcast_select_fusion
  260.7 1.1 copy-done.3
  261.8 0.3 copy-done.5
  262.1 0.1 broadcast_select_fusion.1
  262.2 0.1 constant_dynamic-slice_fusion
  262.3 0.1 constant_dynamic-slice_fusion.1
  262.4 0.6 collective-permute-start.3
  263.0 1.5 collective-permute-start.2
  264.5 1.3 collective-permute-start.4
  265.8 1.3 collective-permute-start.5
  267.1 0.2 select_bitcast_fusion
  267.3 0.1 select_bitcast_fusion.1
  267.4 1.5 pad_maximum_fusion.refs_30_.refs_2_
  268.9 8.4 %collective-permute-done.3 = bf16[256,1024]{1,0:T(8,128)(2,1)S(1)} collective-permute-done((bf16[256,1024]{1,0:T(8,128)(2,1)S(1)}, bf16[256,1024]{1,0:T(8,128)(2,1)S(1)}, u32[]{:S(2)}, u32[]{:S(2)}) %collective-permute-start.3) | collective-permute-done | bytes 524320 | tf_op jit(solution)/shard_map/ppermute | solution.py:1550
  277.3 10.1 %collective-permute-done.2 = bf16[256,1024]{1,0:T(8,128)(2,1)S(1)} collective-permute-done((bf16[256,1024]{1,0:T(8,128)(2,1)S(1)}, bf16[256,1024]{1,0:T(8,128)(2,1)S(1)}, u32[]{:S(2)}, u32[]{:S(2)}) %collective-permute-start.2) | collective-permute-done | bytes 524320 | tf_op jit(solution)/shard_map/ppermute | solution.py:1550
  287.4 1.6 maximum_select_fusion
  288.9 145.2 %collective-permute-done.5.refs_1_ = bf16[512,1024]{1,0:T(8,128)(2,1)S(1)} collective-permute-done((bf16[512,1024]{1,0:T(8,128)(2,1)S(1)}, bf16[512,1024]{1,0:T(8,128)(2,1)S(1)}, u32[]{:S(2)}, u32[]{:S(2)}) %collective-permute-start.5) | collective-permute-done | bytes 1048608 | tf_op jit(solution)/shard_map/ppermute | solution.py:1616
  434.2 1.0 copy-done.6
  435.1 48.9 %layer_backward.6 = (bf16[2,512,4096]{2,1,0:T(8,128)(2,1)}, bf16[2,512,4096]{2,1,0:T(8,128)(2,1)}, bf16[2,512,1024]{2,1,0:T(8,128)(2,1)}, bf16[2,512,1024]{2,1,0...) custom-call(s32[4]{0:T(128)} %get-tuple-element.287.refs_0_, ...), custom_call_target="tpu_custom_call", output_to_operand_aliasing={{0}: (22, {}), {1}: (23, {}), {2}: (24, {}), {3}: (25, {}),... | custom-call | flops 19864223744 | bytes 73400320 | tf_op jit(solution)/shard_map/layer_backward/pallas_call | solution.py:55
  484.1 0.0 collective-permute-done.4.refs_1_
  484.1 0.0 copy-start.19
  484.1 0.0 copy-start.20
  484.1 0.0 copy-start.21
  484.2 48.8 %layer_backward.7 = (bf16[2,512,4096]{2,1,0:T(8,128)(2,1)}, bf16[2,512,4096]{2,1,0:T(8,128)(2,1)}, bf16[2,512,1024]{2,1,0:T(8,128)(2,1)}, bf16[2,512,1024]{2,1,0...) custom-call(s32[4]{0:T(128)} %get-tuple-element.286.refs_0_, ...), custom_call_target="tpu_custom_call", output_to_operand_aliasing={{0}: (22, {}), {1}: (23, {}), {2}: (24, {}), {3}: (25, {}),... | custom-call | flops 19864223744 | bytes 73400320 | tf_op jit(solution)/shard_map/layer_backward/pallas_call | solution.py:55
  533.0 0.7 select_add_fusion.1
  533.7 0.8 select_add_fusion
  534.7 0.8 fusion
  535.4 0.6 pad_maximum_fusion.1.refs_11_
  536.1 242.6 %weight_grads_reduced.1 = (bf16[1,1024,2048]{2,1,0:T(8,128)(2,1)}, bf16[2,1024,2048]{2,1,0:T(8,128)(2,1)}, bf16[3,1024,512]{2,1,0:T(8,128)(2,1)}, bf16[1,1024,51...) custom-call(bf16[2,512,1024]{2,1,0:T(8,128)(2,1)} %get-tuple-element.230.refs_0_, ...), custom_call_target="tpu_custom_call" | custom-call | flops 34359738368 | bytes 67108864 | tf_op jit(solution)/shard_map/weight_grads_reduced/pallas_call | solution.py:981
  778.7 0.8 slice.79
  779.5 1.6 fusion.7
  781.1 0.8 slice.85
  782.0 0.6 dynamic-slice_bitcast_fusion.3
  782.6 0.6 maximum_bitcast_fusion
  783.2 0.6 maximum_bitcast_fusion.1
  783.8 0.6 dynamic-slice_bitcast_fusion.2
  784.4 20.0 %widen.1 = (f32[1,1024,2048]{2,1,0:T(8,128)}, f32[2,1024,2048]{2,1,0:T(8,128)}, f32[3,1024,512]{2,1,0:T(8,128)}, f32[512,1024]{1,0:T(8,128)}, f32[4,256,1024]{2,1,0:T(8,128)}) custom-call(bf16[1,1024,2048]{2,1,0:T(8,128)(2,1)} %get-tuple-element.251.refs_0_, bf16[2,1024,2048]{2,1,0:T(8,128)(2,1)} %get-tuple-element.252.refs_1_, ...), custom_call_target="tpu_custom_call" | custom-call | bytes 58720256 | tf_op jit(solution)/shard_map/widen/pallas_call | solution.py:1092
  (46 shorter events, 0.2 us)
Async XLA Ops:
  2.0 131.0 %copy-start.18 = (bf16[1,2,512]{2,1,0:T(2,128)(2,1)S(1)}, bf16[1,2,512]{2,1,0:T(2,128)(2,1)}, u32[]{:S(2)}) copy-start(bf16[1,2,512]{2,1,0:T(2,128)(2,1)} %param.19) | copy-start | bytes 6148
  2.0 132.2 %copy-start.16 = (bf16[1,2,1024]{2,1,0:T(2,128)(2,1)S(1)}, bf16[1,2,1024]{2,1,0:T(2,128)(2,1)}, u32[]{:S(2)}) copy-start(bf16[1,2,1024]{2,1,0:T(2,128)(2,1)} %param.23) | copy-start | bytes 12292
  2.0 132.2 %copy-start.17 = (bf16[1,2,1024]{2,1,0:T(2,128)(2,1)S(1)}, bf16[1,2,1024]{2,1,0:T(2,128)(2,1)}, u32[]{:S(2)}) copy-start(bf16[1,2,1024]{2,1,0:T(2,128)(2,1)} %param.22) | copy-start | bytes 12292
  2.0 132.3 %copy-start.11 = (bf16[1,1024]{1,0:T(2,128)(2,1)S(1)}, bf16[1,1024]{1,0:T(2,128)(2,1)}, u32[]{:S(2)}) copy-start(bf16[1,1024]{1,0:T(2,128)(2,1)} %param.21) | copy-start | bytes 6148
  2.0 132.3 %copy-start.22 = (bf16[1,1024]{1,0:T(2,128)(2,1)S(1)}, bf16[1,1024]{1,0:T(2,128)(2,1)}, u32[]{:S(2)}) copy-start(bf16[1,1024]{1,0:T(2,128)(2,1)} %param.27) | copy-start | bytes 6148
  2.0 132.9 %copy-start.12 = (bf16[1,2,2048]{2,1,0:T(2,128)(2,1)S(1)}, bf16[1,2,2048]{2,1,0:T(2,128)(2,1)}, u32[]{:S(2)}) copy-start(bf16[1,2,2048]{2,1,0:T(2,128)(2,1)} %param.25) | copy-start | bytes 24580
  2.0 134.2 %copy-start.23 = (f32[16]{0:T(128)S(1)}, f32[16]{0:T(128)}, u32[]{:S(2)}) copy-start(f32[16]{0:T(128)} %constant.38.clone) | copy-start | bytes 196
  2.0 134.2 %copy-start.24 = (f32[16]{0:T(128)S(1)}, f32[16]{0:T(128)}, u32[]{:S(2)}) copy-start(f32[16]{0:T(128)} %constant.39.clone) | copy-start | bytes 196
  178.5 44.9 %collective-permute-start = (bf16[512,1024]{1,0:T(8,128)(2,1)}, bf16[512,1024]{1,0:T(8,128)(2,1)S(1)}, u32[]{:S(2)}, u32[]{:S(2)}) collective-permute-start(bf16[512,1024]{1,0:T(8,128)(2,1)} %get-tuple-element.209.refs_27_), channel_id=1, source_target_pairs={{0,16},{1,17},{2,18},{3,19},{4,20},{5,21},{6,22},{7,23},{8,24},{9,... | collective-permute-start | bytes 3145736 | tf_op jit(solution)/shard_map/ppermute | solution.py:1600
  219.2 24.8 %collective-permute-start.1 = (bf16[512,1024]{1,0:T(8,128)(2,1)}, bf16[512,1024]{1,0:T(8,128)(2,1)}, u32[]{:S(2)}, u32[]{:S(2)}) collective-permute-start(bf16[512,1024]{1,0:T(8,128)(2,1)} %get-tuple-element.211.refs_27_), channel_id=1, source_target_pairs={{0,16},{1,17},{2,18},{3,19},{4,20},{5,21},{6,22},{7,23},{8,24},{9,... | collective-permute-start | bytes 3145736 | tf_op jit(solution)/shard_map/ppermute | solution.py:1600
  223.4 1.0 copy-start.1
  252.6 8.0 copy-start.4
  260.6 1.2 copy-start.3
  260.6 1.5 copy-start.5
  262.2 3.6 copy-start.25
  262.2 4.9 copy-start
  262.4 4.9 copy-start.2
  262.4 4.9 copy-start.7
  262.4 14.9 %collective-permute-start.3 = (bf16[256,1024]{1,0:T(8,128)(2,1)S(1)}, bf16[256,1024]{1,0:T(8,128)(2,1)S(1)}, u32[]{:S(2)}, u32[]{:S(2)}) collective-permute-start(bf16[256,1024]{1,0:T(8,128)(2,1)S(1)} %get-tuple-element.268), channel_id=1, source_target_pairs={{0,8},{8,0},{1,9},{9,1},{2,10},{10,2},{3,11},{11,3},{4,12},{12,4},... | collective-permute-start | bytes 1572872 | tf_op jit(solution)/shard_map/ppermute | solution.py:1550
  263.0 24.4 %collective-permute-start.2 = (bf16[256,1024]{1,0:T(8,128)(2,1)S(1)}, bf16[256,1024]{1,0:T(8,128)(2,1)S(1)}, u32[]{:S(2)}, u32[]{:S(2)}) collective-permute-start(bf16[256,1024]{1,0:T(8,128)(2,1)S(1)} %get-tuple-element.266), channel_id=1, source_target_pairs={{0,8},{8,0},{1,9},{9,1},{2,10},{10,2},{3,11},{11,3},{4,12},{12,4},... | collective-permute-start | bytes 1572872 | tf_op jit(solution)/shard_map/ppermute | solution.py:1550
  264.5 219.6 %collective-permute-start.4 = (bf16[512,1024]{1,0:T(8,128)(2,1)}, bf16[512,1024]{1,0:T(8,128)(2,1)}, u32[]{:S(2)}, u32[]{:S(2)}) collective-permute-start(bf16[512,1024]{1,0:T(8,128)(2,1)} %get-tuple-element.213.refs_15_), channel_id=1, source_target_pairs={{16,0},{17,1},{18,2},{19,3},{20,4},{21,5},{22,6},{23,7},{24,8},{25... | collective-permute-start | bytes 3145736 | tf_op jit(solution)/shard_map/ppermute | solution.py:1616
  265.8 168.3 %collective-permute-start.5 = (bf16[512,1024]{1,0:T(8,128)(2,1)S(1)}, bf16[512,1024]{1,0:T(8,128)(2,1)S(1)}, u32[]{:S(2)}, u32[]{:S(2)}) collective-permute-start(bf16[512,1024]{1,0:T(8,128)(2,1)S(1)} %copy-done.25), channel_id=1, source_target_pairs={{16,0},{17,1},{18,2},{19,3},{20,4},{21,5},{22,6},{23,7},{24,8},{25... | collective-permute-start | bytes 3145736 | tf_op jit(solution)/shard_map/ppermute | solution.py:1616
  434.2 1.0 copy-start.6
  484.1 48.9 %copy-start.19 = (f32[2,1024]{1,0:T(2,128)S(1)}, f32[2,1024]{1,0:T(2,128)}, u32[]{:S(2)}) copy-start(f32[2,1024]{1,0:T(2,128)} %get-tuple-element.246) | copy-start | bytes 24580
  484.1 48.9 %copy-start.20 = (f32[2,1024]{1,0:T(2,128)S(1)}, f32[2,1024]{1,0:T(2,128)}, u32[]{:S(2)}) copy-start(f32[2,1024]{1,0:T(2,128)} %get-tuple-element.248) | copy-start | bytes 24580
  484.1 48.9 %copy-start.21 = (f32[2,1024]{1,0:T(2,128)S(1)}, f32[2,1024]{1,0:T(2,128)}, u32[]{:S(2)}) copy-start(f32[2,1024]{1,0:T(2,128)} %get-tuple-element.245) | copy-start | bytes 24580
  484.1 49.6 %copy-start.13 = (f32[2,4096]{1,0:T(2,128)S(1)}, f32[2,4096]{1,0:T(2,128)}, u32[]{:S(2)}) copy-start(f32[2,4096]{1,0:T(2,128)} %get-tuple-element.242) | copy-start | bytes 98308
  484.1 49.6 %copy-start.14 = (f32[2,4096]{1,0:T(2,128)S(1)}, f32[2,4096]{1,0:T(2,128)}, u32[]{:S(2)}) copy-start(f32[2,4096]{1,0:T(2,128)} %get-tuple-element.244) | copy-start | bytes 98308
  484.2 49.6 %copy-start.15 = (f32[2,4096]{1,0:T(2,128)S(1)}, f32[2,4096]{1,0:T(2,128)}, u32[]{:S(2)}) copy-start(f32[2,4096]{1,0:T(2,128)} %get-tuple-element.241) | copy-start | bytes 98308
  484.2 50.5 %copy-start.8 = (f32[8,1024]{1,0:T(8,128)S(1)}, f32[8,1024]{1,0:T(8,128)}, u32[]{:S(2)}) copy-start(f32[8,1024]{1,0:T(8,128)} %get-tuple-element.207.refs_29_) | copy-start | bytes 98308
  484.2 50.5 %copy-start.9 = (f32[8,1024]{1,0:T(8,128)S(1)}, f32[8,1024]{1,0:T(8,128)}, u32[]{:S(2)}) copy-start(f32[8,1024]{1,0:T(8,128)} %get-tuple-element.208.refs_29_) | copy-start | bytes 98308
  484.2 50.5 %copy-start.10 = (f32[8,1024]{1,0:T(8,128)S(1)}, f32[8,1024]{1,0:T(8,128)}, u32[]{:S(2)}) copy-start(f32[8,1024]{1,0:T(8,128)} %get-tuple-element.229.refs_29_) | copy-start | bytes 98308

commit v6 on v5

--- a/solution.py
+++ b/solution.py
@@ -160,7 +160,7 @@
                     item.wait()
 
             values = x_ref[...]
-            b = bias_ref[:, block(i, CW)]
+            b = bias_ref[:, block(i, CW)].astype(F32)
             qkv_ref[s, 0] = (dot(values, w_ref[s, 0]) + b[0:1]).astype(BF)
             qkv_ref[s, 1] = dot(values, w_ref[s, 1]).astype(BF)
             qkv_ref[s, 2] = (dot(values, w_ref[s, 2]) + b[1:2]).astype(BF)
@@ -215,7 +215,7 @@
                 for item in write_tiles(i - 2, s):
                     item.wait()
 
-            b = ub_ref[:, block(i, ft)]
+            b = ub_ref[:, block(i, ft)].astype(F32)
             for rs in halves(rows):
                 low = low_ref[rs, :]
                 gate = dot(low, up_ref[s, 0]) + b[0:1]
@@ -554,6 +554,7 @@
 def fetch_other_half(qkv, out, up, down, qv_bias, up_bias, inputs, cotangent, chips):
     weights = [qkv, out, up, down]
     biases = [qv_bias, up_bias]
+    bias_widths = [b.shape[1] for b in biases]
     seqs = inputs.shape[0] // 2
     shard_rows, width = inputs.shape[1:]
     groups = 2 * chips
@@ -566,8 +567,10 @@
     parts = 4
     for part in range(parts):
         plan.append((2, True, 0, up_piece, part * up_piece // parts, up_piece // parts))
-    spread = rows_of(3) // 2
-    plan.append((3, True, 0, spread // groups, 0, spread // groups))
+    spread = rows_of(3) * 3 // 4
+    down_piece = spread // groups
+    for part in range(3):
+        plan.append((3, True, 0, down_piece, part * down_piece // 3, down_piece // 3))
     n_spread = len(plan)
     plan.append((-1, False, 0, 0, 0, 0))
     plan.append((-2, False, 0, 0, 0, 0))
@@ -585,7 +588,7 @@
     def kernel(*refs):
         ins, bias_ins, held_refs = refs[:4], refs[4:6], refs[6:8]
         outs, bias_outs, row_refs = refs[8:12], refs[12:14], refs[14 : 14 + seqs]
-        stage, x_send, x_recv, c_send, c_recv, u_send, u_recv, d_send, d_recv, l_sem = refs[14 + seqs :]
+        stage, x_send, x_recv, c_send, c_recv, u_send, u_recv, d_send, d_recv, l_sem, b_sem = refs[14 + seqs :]
         t, c, z, last, core, cross, above, below = neighbours()
         section = lax.axis_index("section")
         greet(c, z, chips, core, cross)
@@ -597,6 +600,9 @@
 
         def span(part):
             return block(part, shard_rows)
+
+        def bias_part(m, side):
+            return bias_outs[m].at[:, pl.ds(side * bias_widths[m], bias_widths[m])]
 
         def cross_copy(index, held_ref=None):
             m = plan[index][5]
@@ -604,7 +610,7 @@
                 src = (held_refs[0] if held_ref is None else held_ref).at[(1 - t) * seqs + m]
                 dst = row_refs[m].at[span(t)]
             elif plan[index][0] == -2:
-                src, dst = bias_ins[m], bias_outs[m]
+                src, dst = bias_ins[m], bias_part(m, 1)
             else:
                 item, where = rows(index, z, c)
                 src, dst = ins[item].at[where], outs[item].at[where]
@@ -625,6 +631,8 @@
             item, where = rows(index, chip, on)
             arrived(outs[item].at[where], sem)
 
+        for m in range(2):
+            copy(bias_ins[m], bias_part(m, 0), b_sem.at[m]).start()
         for index in range(n):
             if plan[index][0] == -1:
                 for turn in range(2):
@@ -649,7 +657,7 @@
                     arrived(row_refs[m].at[span(1 - t)], x_recv.at[index])
                     return
                 if plan[index][0] == -2:
-                    arrived(bias_outs[m], x_recv.at[index])
+                    arrived(bias_part(m, 1), x_recv.at[index])
                     return
                 got(index, z, c, x_recv.at[index])
                 pass_on(index, z, c_send, c_recv, core).start()
@@ -690,6 +698,8 @@
                 if 0 <= round_ - hop < n_spread:
                     handle(round_ - hop, hop)
 
+        for m in range(2):
+            copy(bias_ins[m], bias_part(m, 0), b_sem.at[m]).wait()
         for m in range(seqs):
             arrived(stage.at[m], l_sem)
         for index in range(n):
@@ -719,12 +729,13 @@
         kernel,
         in_specs=[ANY] * 8,
         out_specs=[ANY] * (6 + seqs),
-        out_shape=[jax.ShapeDtypeStruct(w.shape, BF) for w in weights + biases]
+        out_shape=[jax.ShapeDtypeStruct(w.shape, BF) for w in weights]
+        + [jax.ShapeDtypeStruct((2, 2 * size), BF) for size in bias_widths]
         + [jax.ShapeDtypeStruct((2 * shard_rows, width), BF)] * seqs,
         scratch_shapes=[pltpu.VMEM((seqs, shard_rows, width), BF)]
         + [sem((n,)), sem((n,))]
         + [sem((n, chips))] * 6
-        + [sem],
+        + [sem, sem((2,))],
         compiler_params=pltpu.CompilerParams(collective_id=1, has_side_effects=True),
         cost_estimate=pl.CostEstimate(flops=0, bytes_accessed=2 * moved, transcendentals=0),
         name="fetch_other_half",
@@ -753,7 +764,7 @@
     last_static = chips - 1
     drain = CORE_LAG + CROSS_LAG + 2 * last_static * CHAIN_LAG + 1
     vec_shape = sums.shape
-    n_in = n_left + n_right + 1 + 2 * seqs
+    n_in = n_left + n_right + 1 + seqs
     shard_rows = rows // 2
 
     def kernel(*refs):
@@ -812,12 +823,9 @@
         vec_core = remote(vec.at[0], vec_in.at[0], v_send.at[0], v_recv.at[0], core)
         vec_cross = remote(vec.at[1], vec_in.at[1], v_send.at[1], v_recv.at[1], cross)
         vec_core.start()
-        for turn in range(2):
-            @pl.when(section == turn)
-            def _(turn=turn):
-                for m in range(seqs):
-                    source = row_refs[turn * seqs + m].at[block(1 - t, shard_rows)]
-                    remote(source, rows_out.at[m], r_send.at[m], r_recv.at[m], cross).start()
+        def row_copy(m):
+            source = row_refs[m].at[block(1 - t, shard_rows)]
+            return remote(source, rows_out.at[m], r_send.at[m], r_recv.at[m], cross)
 
         up = pl.ds(0, quarter)
         down = pl.ds(quarter, quarter)
@@ -899,6 +907,11 @@
             def _():
                 remote(acc.at[k1, 0], from_x.at[k1], x_send, x_recv.at[k1], cross).start()
 
+            @pl.when((k1 == total - 1) & (section == 0))
+            def _():
+                for m in range(seqs):
+                    row_copy(m).start()
+
             for span, way, place, ahead, behind in sides:
                 k3 = k2 - CHAIN_LAG * place
 
@@ -947,9 +960,12 @@
                         vec_all.at[z], vec_all.at[z], v_send.at[1 + shift], v_recv.at[1 + shift], {"dp": to * 2 + c}
                     ).start()
 
-        for m in range(seqs):
-            arrived(rows_out.at[m], r_recv.at[m])
-            arrived(rows_out.at[m], r_send.at[m])
+
+        @pl.when(section == 0)
+        def _():
+            for m in range(seqs):
+                row_copy(m).wait()
+
         vec_core.wait_send()
         vec_cross.wait_send()
         for shift in range(1, chips):
@@ -1009,8 +1025,74 @@
     )(*lefts, *rights, sums, *row_grads)
 
 
-def widen(reduced, row_grads, got):
-    seqs, shard_rows, width = got.shape
+def exchange_rows(first, second, grads):
+    seqs = len(first)
+    rows, width = first[0].shape
+    shard_rows = rows // 2
+
+    def kernel(*refs):
+        outputs = (refs[:seqs], refs[seqs : 2 * seqs])
+        grad_refs = refs[2 * seqs : 3 * seqs]
+        out_ref, got_ref, stage, send, recv, l_sem = refs[3 * seqs :]
+        t = lax.axis_index("tensor")
+        section = lax.axis_index("section")
+        cross = {"tensor": 1 - t}
+        barrier = pltpu.get_barrier_semaphore()
+        pl.semaphore_signal(barrier, inc=1, device_id=cross, device_id_type=MESH)
+        pl.semaphore_wait(barrier, 1)
+
+        def remote(src, dst, index):
+            return pltpu.make_async_remote_copy(
+                src_ref=src, dst_ref=dst, send_sem=send.at[index], recv_sem=recv.at[index],
+                device_id=cross, device_id_type=MESH,
+            )
+
+        for turn in range(2):
+            @pl.when(section == turn)
+            def _(turn=turn):
+                sent = [
+                    remote(outputs[turn][m].at[block(1 - t, shard_rows)], out_ref.at[t * seqs + m], m) for m in range(seqs)
+                ]
+                if turn == 1:
+                    sent += [
+                        remote(grad_refs[m].at[block(1 - t, shard_rows)], got_ref.at[m], seqs + m) for m in range(seqs)
+                    ]
+                for item in sent:
+                    item.start()
+                for m in range(seqs):
+                    copy(outputs[turn][m].at[block(t, shard_rows)], stage.at[m], l_sem.at[m]).start()
+                for m in range(seqs):
+                    arrived(stage.at[m], l_sem.at[m])
+                    copy(stage.at[m], out_ref.at[t * seqs + m], l_sem.at[m]).start()
+                for m in range(seqs):
+                    arrived(stage.at[m], l_sem.at[m])
+                for m in range(seqs):
+                    arrived(out_ref.at[(1 - t) * seqs + m], recv.at[m])
+                    arrived(stage.at[m], send.at[m])
+                if turn == 1:
+                    for m in range(seqs):
+                        sent[seqs + m].wait()
+
+    sem = pltpu.SemaphoreType.DMA
+    return pl.pallas_call(
+        kernel,
+        in_specs=[ANY] * (3 * seqs),
+        out_specs=[ANY] * 2,
+        out_shape=[
+            jax.ShapeDtypeStruct((2 * seqs, shard_rows, width), BF),
+            jax.ShapeDtypeStruct((seqs, shard_rows, width), BF),
+        ],
+        scratch_shapes=[
+            pltpu.VMEM((seqs, shard_rows, width), BF), sem((2 * seqs,)), sem((2 * seqs,)), sem((seqs,)),
+        ],
+        compiler_params=pltpu.CompilerParams(collective_id=2, has_side_effects=True),
+        cost_estimate=pl.CostEstimate(flops=0, bytes_accessed=0, transcendentals=0),
+        name="exchange_rows",
+    )(*first, *second, *grads)
+
+
+def widen(reduced, row_grads, gots, sums, units, local):
+    seqs, shard_rows, width = gots[0].shape
     n = len(reduced)
     jobs = []
     for index, array in enumerate(reduced):
@@ -1022,15 +1104,18 @@
             jobs += [(index, part, at, step, columns) for part in range(lead) for at in range(0, depth, step)]
     jobs += [(n, m, 0, shard_rows, width) for m in range(seqs)] + [(n + 1, m, 0, shard_rows, width) for m in range(seqs)]
     ring = 3
-    size = 512 * 1024
+    n_in = n + 2 * seqs + 3
+    parts = units // width
 
     def kernel(*refs):
         ins = refs[:n]
         grad_refs = refs[n : n + 2 * seqs]
-        got_ref = refs[n + 2 * seqs]
-        outs = refs[n + 2 * seqs + 1 : 2 * n + 2 * seqs + 2]
+        got_refs = refs[n + 2 * seqs : n + 2 * seqs + 2]
+        sums_ref = refs[n + 2 * seqs + 2]
+        outs = refs[n_in : n_in + n + 1]
+        qv_ref, out_bias_ref, gain_ref, shift_ref, ub_ref, down_bias_ref = refs[n_in + n + 1 : n_in + n + 7]
         shapes = sorted({(j[3], j[4]) for j in jobs if j[0] != n})
-        buffers = refs[2 * n + 2 * seqs + 2 :]
+        buffers = refs[n_in + n + 7 :]
         wide_rows, in_sem, out_sem = buffers[0], buffers[1], buffers[2]
         low = {s: buffers[3 + 2 * i] for i, s in enumerate(shapes)}
         wide = {s: buffers[4 + 2 * i] for i, s in enumerate(shapes)}
@@ -1049,7 +1134,10 @@
                         source = grad_refs[turn * seqs + part].at[block(t, shard_rows)]
                         copy(source, wide_rows.at[part], in_sem.at[s]).start()
             else:
-                copy(got_ref.at[part], low[rows, columns].at[s], in_sem.at[s]).start()
+                for turn in range(2):
+                    @pl.when(section == turn)
+                    def _(turn=turn):
+                        copy(got_refs[turn].at[part], low[rows, columns].at[s], in_sem.at[s]).start()
 
         def store(number):
             index, part, at, rows, columns = jobs[number]
@@ -1064,6 +1152,22 @@
 
         for number in range(ring):
             load(number)
+        gain_ref[0:1] = sums_ref[3:4]
+        gain_ref[1:2] = sums_ref[0:1]
+        shift_ref[0:1] = sums_ref[4:5]
+        shift_ref[1:2] = sums_ref[1:2]
+        out_bias_ref[...] = sums_ref[5:6]
+        down_bias_ref[...] = sums_ref[2:3]
+        for half in range(2):
+            @pl.when(t == half)
+            def _(half=half):
+                for g in range(2):
+                    for j in range(parts):
+                        at = 6 + (2 * g + half) * parts + j
+                        ub_ref[g : g + 1, j * width : (j + 1) * width] = sums_ref[at : at + 1]
+                    at = 6 + 4 * parts + g
+                    qv_ref[g : g + 1] = sums_ref[at : at + 1, half * local : (half + 1) * local]
+
         for number, (index, part, at, rows, columns) in enumerate(jobs):
             s = number % ring
             if index == n:
@@ -1091,15 +1195,19 @@
         buffers += [pltpu.VMEM((ring,) + s, BF), pltpu.VMEM((ring,) + ((s[1], s[0]) if s == square else s), F32)]
     return pl.pallas_call(
         kernel,
-        in_specs=[ANY] * (n + 2 * seqs + 1),
-        out_specs=[ANY] * (n + 1),
+        in_specs=[ANY] * (n + 2 * seqs + 2) + [WHOLE],
+        out_specs=[ANY] * (n + 1) + [WHOLE] * 6,
         out_shape=[jax.ShapeDtypeStruct(r.shape, F32) for r in reduced[:-1]]
-        + [jax.ShapeDtypeStruct((last[2], last[1]), F32), jax.ShapeDtypeStruct((2 * seqs, shard_rows, width), F32)],
+        + [jax.ShapeDtypeStruct((last[2], last[1]), F32), jax.ShapeDtypeStruct((2 * seqs, shard_rows, width), F32)]
+        + [
+            jax.ShapeDtypeStruct(shape, F32)
+            for shape in ((2, local), (1, width), (2, width), (2, width), (2, units), (1, width))
+        ],
         scratch_shapes=[pltpu.VMEM((seqs, shard_rows, width), F32), sem((ring,)), sem((ring,))] + buffers,
         compiler_params=pltpu.CompilerParams(vmem_limit_bytes=VMEM_LIMIT),
         cost_estimate=pl.CostEstimate(flops=0, bytes_accessed=56 << 20, transcendentals=0),
         name="widen",
-    )(*reduced, *row_grads, got)
+    )(*reduced, *row_grads, *gots, sums)
 
 
 MASKED = -1000000000.0
@@ -1514,12 +1622,6 @@
     )
 
 
-def join(first, second, swapped):
-    return jnp.where(
-        swapped, jnp.concatenate([second, first], axis=0), jnp.concatenate([first, second], axis=0)
-    )
-
-
 def by_sequence(
     inputs,
     cotangent,
@@ -1546,18 +1648,12 @@
     heads = local // HD
     chips = groups // 2
 
-    def across(value):
-        return lax.ppermute(value, "tensor", [(0, 1), (1, 0)])
-
-    def part_rows(value, part):
-        return lax.dynamic_slice_in_dim(value, part * shard_rows, shard_rows, 0)
-
     qkv_own = jnp.transpose(w_qkv[0], (1, 0, 2))
     out_own = w_out[0]
     up_own = w_up[0]
     down_own = w_down[0]
     first = section == 0
-    qkv_oth, out_oth, up_oth, down_oth, qv_oth, ub_oth, *held = fetch_other_half(
+    qkv_oth, out_oth, up_oth, down_oth, bias, up_bias, *held = fetch_other_half(
         qkv_own.reshape(3 * width, local),
         out_own,
         up_own.reshape(2 * width, units),
@@ -1572,8 +1668,6 @@
     up_oth = up_oth.reshape(2, width, units)
     x_first = outer = held
 
-    bias = jnp.concatenate([b_qv[0], qv_oth], axis=1).astype(F32)
-    up_bias = jnp.concatenate([b_up[0], ub_oth], axis=1).astype(F32)
     vecs = jnp.stack(
         [b_out[0], ln_gain[0, 0], ln_bias[0, 0], b_down[0], ln_gain[0, 1], ln_bias[0, 1], b_out[0], b_out[0]]
     ).astype(F32)
@@ -1614,13 +1708,9 @@
 
     gx_second = [backward(outer[m], m, 1) for m in range(seqs)]
     grad_middle = [lax.ppermute(gx_second[m][1], "section", [(1, 0)]) for m in range(seqs)]
-    y_all, _ = lax.optimization_barrier(((y_first, y_second), deps))
-    y_own = [jnp.where(first, a, b) for a, b in zip(*y_all)]
-    y_kept = jnp.stack([part_rows(y, place) for y in y_own])
-    y_got = jnp.stack([across(part_rows(y, 1 - place)) for y in y_own])
-    produced = join(y_kept, y_got, place == 1)
+    produced, got_second = exchange_rows(y_first, y_second, [g[1] for g in gx_second])
     x_all = jnp.stack([jnp.where(first, x_first[m], x_second[m]) for m in range(seqs)])
-    deps = deps + [x_all]
+    deps = deps + [x_all, produced]
     gx_first = [backward(grad_middle[m], m, 0) for m in range(seqs)]
 
     mixed, hidden, normed = kept[3], kept[7], kept[8]
@@ -1638,33 +1728,25 @@
         ).reshape(-1, width)
 
     packed = jnp.concatenate([norm_sums[:6], ordered(up_sums[:2], units), ordered(qv_sums[:2], local)])
-    low_grads = [g[1] for g in gx_first + gx_second]
-    *reduced, packed, got = weight_grads_reduced(
-        [(gl, [hidden]), (normed, [gg0, gg1]), (x_all, gqkv), (ga, [mixed])], packed, low_grads, chips
+    *reduced, packed, got_first = weight_grads_reduced(
+        [(gl, [hidden]), (normed, [gg0, gg1]), (x_all, gqkv), (ga, [mixed])], packed, [g[1] for g in gx_first], chips
     )
-    down_sum, up_sum, qkv_sum, out_sum, grads_in = widen(reduced, [g[0] for g in gx_first + gx_second], got)
-    down_sum = down_sum[0]
-    qkv_sum = jnp.transpose(qkv_sum, (1, 0, 2))
-    norm_total = packed[:6]
-    up_total = packed[6 : 6 + 4 * units // width].reshape(2, 2 * units)
-    qv_total = packed[6 + 4 * units // width :].reshape(2, 2 * local)
-    up_bias_sum = lax.dynamic_slice_in_dim(up_total, place * units, units, 1)
-    qv_sum = lax.dynamic_slice_in_dim(qv_total, place * local, local, 1)
-    gain_sum = jnp.stack([norm_total[3], norm_total[0]])
-    shift_sum = jnp.stack([norm_total[4], norm_total[1]])
+    down_sum, up_sum, qkv_sum, out_sum, grads_in, qv_sum, out_bias_sum, gain_sum, shift_sum, up_bias_sum, down_bias_sum = (
+        widen(reduced, [g[0] for g in gx_first + gx_second], [got_first, got_second], packed, units, local)
+    )
     return (
         produced[None],
         grads_in[None],
-        qkv_sum[None],
+        jnp.transpose(qkv_sum, (1, 0, 2))[None],
         qv_sum[None],
         out_sum[None],
-        norm_total[5][None],
+        out_bias_sum,
         gain_sum[None],
         shift_sum[None],
         up_sum[None],
         up_bias_sum[None],
-        down_sum[None],
-        norm_total[2][None],
+        down_sum,
+        down_bias_sum,
     )
 
 

time: 814 us -> 758 us (0.931)
  waiting for transfers between devices: 182 us -> 136 us
    ppermute x2, waiting for transfers between devices: 145 us -> 118 us  [by_sequence(): lax.ppermute(gx_second[m][1], 'section', [(1, 0)])]
    pallas_call x1 -> x2, Pallas kernels: 20 us -> 46.8 us  [the longest x1 25.3 us: exchange_rows(): pl.pallas_call(kernel, in_specs=[ANY] * (3 * seqs), out_specs=[ANY] * 2,...]
    ppermute x2 -> x0, waiting for transfers between devices: 18.4 us -> none  [across(): return lax.ppermute(value, 'tensor', [(0, 1), (1, 0)])]
    pallas_call x1, Pallas kernels: 243 us -> 225 us  [weight_grads_reduced(): pl.pallas_call(kernel, in_specs=[ANY] * n_in, out_specs=[ANY] * n_left +...]
    pallas_call x1, Pallas kernels: 131 us -> 123 us  [fetch_other_half(): pl.pallas_call(kernel, in_specs=[ANY] * 8, out_specs=[ANY] * (6 + seqs),...]
  transfers between devices with their start and end apart: 6 -> 4, of which waited for: 4 -> 3; matrix products, arithmetic and copies ran while one was open for 1% -> 0% of each run, Pallas kernels for 11% -> 16%
where the time goes in v6:
time: 758 us; the launch traced here: 749 us
  Pallas kernels  586 us (77%)
  waiting for transfers between devices  136 us (18%)
  other arithmetic  10.4 us (1%)
  local copies, waits for them, and re-layouts  8.08 us (1%)
    pallas_call x1, Pallas kernels, weight_grads_reduced(): pl.pallas_call(kernel, in_specs=[ANY] * n_in, out_specs=[ANY] * n_left +...  225 us
    pallas_call x8, Pallas kernels, call(): pl.pallas_call(body, in_specs=specs, out_specs=[ANY] * n_out, out_shape=[...  192 us
    pallas_call x1, Pallas kernels, fetch_other_half(): pl.pallas_call(kernel, in_specs=[ANY] * 8, out_specs=[ANY] * (6 + seqs),...  123 us
    ppermute x2, waiting for transfers between devices, by_sequence(): lax.ppermute(gx_second[m][1], 'section', [(1, 0)])  118 us
    pallas_call x1, Pallas kernels, exchange_rows(): pl.pallas_call(kernel, in_specs=[ANY] * (3 * seqs), out_specs=[ANY] * 2,...  25.3 us
    pallas_call x1, Pallas kernels, widen(): pl.pallas_call(kernel, in_specs=[ANY] * (n + 2 * seqs + 2) + [WHOLE], out...  21.5 us
    ppermute x2, waiting for transfers between devices, by_sequence(): x_second = [lax.ppermute(y, 'section', [(0, 1)]) for y in y_first]  18.4 us
  transfers between devices with their start and end apart: 4, of which 3 were waited for; matrix products, arithmetic and copies ran while one was open for 0% of the time, Pallas kernels for 16%

profile of v6, /device:TPU:0, one launch (start us, length us, event | category | flops | bytes accessed | tf_op | source)
XLA Modules:
  0.0 748.7 jit_solution(9140694584423478147)
XLA Ops:
  0.7 0.7 dynamic_slice.3
  1.4 0.6 fusion.9
  2.0 0.8 slice_bitcast_fusion
  2.8 0.9 stack.41
  3.6 0.6 convert_element_type.2.refs_12_.refs_21_
  4.2 1.2 broadcast_select_fusion.refs_11_.refs_20_
  5.5 2.0 pad_add_fusion
  7.4 122.5 %fetch_other_half.1 = (bf16[3072,512]{1,0:T(8,128)(2,1)}, bf16[512,1024]{1,0:T(8,128)(2,1)}, bf16[2048,2048]{1,0:T(8,128)(2,1)}, bf16[1024,2048]{1,0:T(8,128)(2,...) custom-call(bf16[3072,512]{1,0:T(8,128)(2,1)} %bitcast.64, ...), custom_call_target="tpu_custom_call" | custom-call | bytes 33554432 | tf_op jit(solution)/shard_map/fetch_other_half/pallas_call | solution.py:728
  129.9 39.5 %layer_forward.4 = (bf16[2,512,1024]{2,1,0:T(8,128)(2,1)}, bf16[2,512,1024]{2,1,0:T(8,128)(2,1)}, bf16[2,512,1024]{2,1,0:T(8,128)(2,1)}, bf16[2,512,1024]{2,1,0:...) custom-call(s32[4]{0:T(128)} %get-tuple-element.285.refs_0_, ...), custom_call_target="tpu_custom_call" | custom-call | flops 18253611008 | bytes 56623104 | tf_op jit(solution)/shard_map/layer_forward/pallas_call | solution.py:55
  169.4 1.4 collective-permute-start
  170.8 39.0 %layer_forward.5 = (bf16[2,512,1024]{2,1,0:T(8,128)(2,1)}, bf16[2,512,1024]{2,1,0:T(8,128)(2,1)}, bf16[2,512,1024]{2,1,0:T(8,128)(2,1)}, bf16[2,512,1024]{2,1,0:...) custom-call(s32[4]{0:T(128)} %get-tuple-element.284.refs_0_, ...), custom_call_target="tpu_custom_call", output_to_operand_aliasing={{0}: (14, {}), {1}: (15, {}), {2}: (16, {}), {3}: (17, {}),... | custom-call | flops 18253611008 | bytes 56623104 | tf_op jit(solution)/shard_map/layer_forward/pallas_call | solution.py:55
  209.7 2.3 collective-permute-start.1
  212.0 1.9 fusion.3
  213.9 0.0 collective-permute-done.refs_1_
  213.9 0.0 copy-start.1
  213.9 1.0 copy-done.1
  214.8 1.3 layer_forward.6
  216.2 18.4 %collective-permute-done.1.refs_1_ = bf16[512,1024]{1,0:T(8,128)(2,1)} collective-permute-done((bf16[512,1024]{1,0:T(8,128)(2,1)}, bf16[512,1024]{1,0:T(8,128)(2,1)}, u32[]{:S(2)}, u32[]{:S(2)}) %collective-permute-start.1) | collective-permute-done | bytes 1048608 | tf_op jit(solution)/shard_map/ppermute | solution.py:1694
  234.6 1.5 layer_forward.7
  236.1 7.1 layer_backward.4
  243.2 1.3 collective-permute-start.3
  244.5 6.1 layer_backward.5
  250.6 0.0 copy-start
  250.6 25.3 %exchange_rows.1 = (bf16[4,256,1024]{2,1,0:T(8,128)(2,1)}, bf16[2,256,1024]{2,1,0:T(8,128)(2,1)}) custom-call(bf16[512,1024]{1,0:T(8,128)(2,1)} %get-tuple-element.150.refs_27_.refs_0_, bf16[512,1024]{1,0:T(8,128)(2,1)} %get-tuple-element.165.refs_27_.refs_1_, bf16[512,1024]{1,0:T(8,128)(2,1)} %get-tuple-element.179.refs_27_.refs_2_, ...), custom_call_target="tpu_custom_call" | custom-call | tf_op jit(solution)/shard_map/exchange_rows/pallas_call | solution.py:1077
  275.9 0.0 copy-start.2
  275.9 0.0 copy-start.4
  275.9 1.4 collective-permute-start.2
  277.3 0.0 copy-done
  277.4 0.1 select_bitcast_fusion
  277.5 0.0 copy-done.2
  277.5 0.0 copy-done.4
  277.5 0.1 select_bitcast_fusion.1
  277.6 1.5 pad_maximum_fusion.refs_30_.refs_2_
  279.1 70.4 %collective-permute-done.3.refs_1_ = bf16[512,1024]{1,0:T(8,128)(2,1)S(1)} collective-permute-done((bf16[512,1024]{1,0:T(8,128)(2,1)}, bf16[512,1024]{1,0:T(8,128)(2,1)S(1)}, u32[]{:S(2)}, u32[]{:S(2)}) %collective-permute-start.3) | collective-permute-done | bytes 1048608 | tf_op jit(solution)/shard_map/ppermute | solution.py:1710
  349.6 0.0 copy-start.3
  349.6 1.0 copy-done.3
  350.5 48.8 %layer_backward.6 = (bf16[2,512,4096]{2,1,0:T(8,128)(2,1)}, bf16[2,512,4096]{2,1,0:T(8,128)(2,1)}, bf16[2,512,1024]{2,1,0:T(8,128)(2,1)}, bf16[2,512,1024]{2,1,0...) custom-call(s32[4]{0:T(128)} %get-tuple-element.285.refs_0_, ...), custom_call_target="tpu_custom_call", output_to_operand_aliasing={{0}: (22, {}), {1}: (23, {}), {2}: (24, {}), {3}: (25, {}),... | custom-call | flops 19864223744 | bytes 73400320 | tf_op jit(solution)/shard_map/layer_backward/pallas_call | solution.py:55
  399.3 47.4 %collective-permute-done.2.refs_1_ = bf16[512,1024]{1,0:T(8,128)(2,1)} collective-permute-done((bf16[512,1024]{1,0:T(8,128)(2,1)}, bf16[512,1024]{1,0:T(8,128)(2,1)}, u32[]{:S(2)}, u32[]{:S(2)}) %collective-permute-start.2) | collective-permute-done | bytes 1048608 | tf_op jit(solution)/shard_map/ppermute | solution.py:1710
  446.7 0.0 copy-start.5
  446.8 0.0 copy-start.6
  446.8 0.0 copy-start.7
  446.8 0.0 copy-start.11
  446.8 0.0 copy-start.12
  446.8 0.0 copy-start.13
  446.8 0.0 copy-start.8
  446.8 0.0 copy-start.9
  446.8 0.0 copy-start.10
  446.8 48.8 %layer_backward.7 = (bf16[2,512,4096]{2,1,0:T(8,128)(2,1)}, bf16[2,512,4096]{2,1,0:T(8,128)(2,1)}, bf16[2,512,1024]{2,1,0:T(8,128)(2,1)}, bf16[2,512,1024]{2,1,0...) custom-call(s32[4]{0:T(128)} %get-tuple-element.284.refs_0_, ...), custom_call_target="tpu_custom_call", output_to_operand_aliasing={{0}: (22, {}), {1}: (23, {}), {2}: (24, {}), {3}: (25, {}),... | custom-call | flops 19864223744 | bytes 73400320 | tf_op jit(solution)/shard_map/layer_backward/pallas_call | solution.py:55
  495.6 0.0 copy-done.5
  495.6 0.0 copy-done.6
  495.6 0.0 copy-done.7
  495.6 0.8 fusion
  496.4 0.0 copy-done.11
  496.4 0.0 copy-done.12
  496.4 0.0 copy-done.13
  496.4 0.7 select_add_fusion.1
  497.2 0.0 copy-done.8
  497.2 0.0 copy-done.9
  497.2 0.0 copy-done.10
  497.2 0.8 select_add_fusion
  498.1 0.6 pad_maximum_fusion.1.refs_11_
  498.7 225.2 %weight_grads_reduced.1 = (bf16[1,1024,2048]{2,1,0:T(8,128)(2,1)}, bf16[2,1024,2048]{2,1,0:T(8,128)(2,1)}, bf16[3,1024,512]{2,1,0:T(8,128)(2,1)}, bf16[1,1024,51...) custom-call(bf16[2,512,1024]{2,1,0:T(8,128)(2,1)} %get-tuple-element.231.refs_0_, ...), custom_call_target="tpu_custom_call" | custom-call | flops 34359738368 | bytes 67108864 | tf_op jit(solution)/shard_map/weight_grads_reduced/pallas_call | solution.py:997
  723.9 21.5 %widen.1 = (f32[1,1024,2048]{2,1,0:T(8,128)}, f32[2,1024,2048]{2,1,0:T(8,128)}, f32[3,1024,512]{2,1,0:T(8,128)}, f32[512,1024]{1,0:T(8,128)}, f32[4,256,1024]{2,...) custom-call(bf16[1,1024,2048]{2,1,0:T(8,128)(2,1)} %get-tuple-elemen, ...), custom_call_target="tpu_custom_call" | custom-call | bytes 58720256 | tf_op jit(solution)/shard_map/widen/pallas_call | solution.py:1196
  745.4 3.1 copy.148
  (5 shorter events, 0.1 us)
Async XLA Ops:
  169.4 44.5 %collective-permute-start = (bf16[512,1024]{1,0:T(8,128)(2,1)}, bf16[512,1024]{1,0:T(8,128)(2,1)S(1)}, u32[]{:S(2)}, u32[]{:S(2)}) collective-permute-start(bf16[512,1024]{1,0:T(8,128)(2,1)} %get-tuple-element.150.refs_27_.refs_0_), channel_id=1, source_target_pairs={{0,16},{1,17},{2,18},{3,19},{4,20},{5,21},{6,22},{7,23},{8,24},{9,... | collective-permute-start | bytes 3145736 | tf_op jit(solution)/shard_map/ppermute | solution.py:1694
  209.7 24.8 %collective-permute-start.1 = (bf16[512,1024]{1,0:T(8,128)(2,1)}, bf16[512,1024]{1,0:T(8,128)(2,1)}, u32[]{:S(2)}, u32[]{:S(2)}) collective-permute-start(bf16[512,1024]{1,0:T(8,128)(2,1)} %get-tuple-element.165.refs_27_.refs_1_), channel_id=1, source_target_pairs={{0,16},{1,17},{2,18},{3,19},{4,20},{5,21},{6,22},{7,23},{8,24},{9,... | collective-permute-start | bytes 3145736 | tf_op jit(solution)/shard_map/ppermute | solution.py:1694
  213.9 1.0 copy-start.1
  243.2 106.4 %collective-permute-start.3 = (bf16[512,1024]{1,0:T(8,128)(2,1)}, bf16[512,1024]{1,0:T(8,128)(2,1)S(1)}, u32[]{:S(2)}, u32[]{:S(2)}) collective-permute-start(bf16[512,1024]{1,0:T(8,128)(2,1)} %get-tuple-element.204.refs_4_), channel_id=1, source_target_pairs={{16,0},{17,1},{18,2},{19,3},{20,4},{21,5},{22,6},{23,7},{24,8},{25... | collective-permute-start | bytes 3145736 | tf_op jit(solution)/shard_map/ppermute | solution.py:1710
  250.6 26.8 %copy-start = (bf16[512,1024]{1,0:T(8,128)(2,1)S(1)}, bf16[512,1024]{1,0:T(8,128)(2,1)}, u32[]{:S(2)}) copy-start(bf16[512,1024]{1,0:T(8,128)(2,1)} %get-tuple-element.151.refs_1_) | copy-start | bytes 3145732
  275.9 1.6 copy-start.2
  275.9 1.6 copy-start.4
  275.9 170.8 %collective-permute-start.2 = (bf16[512,1024]{1,0:T(8,128)(2,1)}, bf16[512,1024]{1,0:T(8,128)(2,1)}, u32[]{:S(2)}, u32[]{:S(2)}) collective-permute-start(bf16[512,1024]{1,0:T(8,128)(2,1)} %get-tuple-element.213.refs_5_), channel_id=1, source_target_pairs={{16,0},{17,1},{18,2},{19,3},{20,4},{21,5},{22,6},{23,7},{24,8},{25... | collective-permute-start | bytes 3145736 | tf_op jit(solution)/shard_map/ppermute | solution.py:1710
  349.6 1.0 copy-start.3
  446.7 48.9 %copy-start.5 = (f32[8,1024]{1,0:T(8,128)S(1)}, f32[8,1024]{1,0:T(8,128)}, u32[]{:S(2)}) copy-start(f32[8,1024]{1,0:T(8,128)} %get-tuple-element.212.refs_29_) | copy-start | bytes 98308
  446.8 48.9 %copy-start.6 = (f32[8,1024]{1,0:T(8,128)S(1)}, f32[8,1024]{1,0:T(8,128)}, u32[]{:S(2)}) copy-start(f32[8,1024]{1,0:T(8,128)} %get-tuple-element.222.refs_29_) | copy-start | bytes 98308
  446.8 48.9 %copy-start.7 = (f32[8,1024]{1,0:T(8,128)S(1)}, f32[8,1024]{1,0:T(8,128)}, u32[]{:S(2)}) copy-start(f32[8,1024]{1,0:T(8,128)} %get-tuple-element.230.refs_29_) | copy-start | bytes 98308
  446.8 49.7 %copy-start.11 = (f32[2,1024]{1,0:T(2,128)S(1)}, f32[2,1024]{1,0:T(2,128)}, u32[]{:S(2)}) copy-start(f32[2,1024]{1,0:T(2,128)} %get-tuple-element.247) | copy-start | bytes 24580
  446.8 49.7 %copy-start.12 = (f32[2,1024]{1,0:T(2,128)S(1)}, f32[2,1024]{1,0:T(2,128)}, u32[]{:S(2)}) copy-start(f32[2,1024]{1,0:T(2,128)} %get-tuple-element.249) | copy-start | bytes 24580
  446.8 49.7 %copy-start.13 = (f32[2,1024]{1,0:T(2,128)S(1)}, f32[2,1024]{1,0:T(2,128)}, u32[]{:S(2)}) copy-start(f32[2,1024]{1,0:T(2,128)} %get-tuple-element.246) | copy-start | bytes 24580
  446.8 50.4 %copy-start.8 = (f32[2,4096]{1,0:T(2,128)S(1)}, f32[2,4096]{1,0:T(2,128)}, u32[]{:S(2)}) copy-start(f32[2,4096]{1,0:T(2,128)} %get-tuple-element.243) | copy-start | bytes 98308
  446.8 50.4 %copy-start.9 = (f32[2,4096]{1,0:T(2,128)S(1)}, f32[2,4096]{1,0:T(2,128)}, u32[]{:S(2)}) copy-start(f32[2,4096]{1,0:T(2,128)} %get-tuple-element.245) | copy-start | bytes 98308
  446.8 50.4 %copy-start.10 = (f32[2,4096]{1,0:T(2,128)S(1)}, f32[2,4096]{1,0:T(2,128)}, u32[]{:S(2)}) copy-start(f32[2,4096]{1,0:T(2,128)} %get-tuple-element.242) | copy-start | bytes 98308

commit v7 on v6

--- a/solution.py
+++ b/solution.py
@@ -1025,21 +1025,19 @@
     )(*lefts, *rights, sums, *row_grads)
 
 
-def exchange_rows(first, second, grads):
-    seqs = len(first)
-    rows, width = first[0].shape
+def exchange_rows(outputs, grads, turn, earlier, deps):
+    seqs = len(outputs)
+    rows, width = outputs[0].shape
     shard_rows = rows // 2
+    n_in = seqs + len(grads) + len(earlier) + len(deps)
+    n_out = 2 if grads else 1
 
     def kernel(*refs):
-        outputs = (refs[:seqs], refs[seqs : 2 * seqs])
-        grad_refs = refs[2 * seqs : 3 * seqs]
-        out_ref, got_ref, stage, send, recv, l_sem = refs[3 * seqs :]
+        y_refs, grad_refs = refs[:seqs], refs[seqs : seqs + len(grads)]
+        out_ref = refs[n_in]
+        stage, send, recv, l_sem = refs[n_in + n_out :]
         t = lax.axis_index("tensor")
-        section = lax.axis_index("section")
         cross = {"tensor": 1 - t}
-        barrier = pltpu.get_barrier_semaphore()
-        pl.semaphore_signal(barrier, inc=1, device_id=cross, device_id_type=MESH)
-        pl.semaphore_wait(barrier, 1)
 
         def remote(src, dst, index):
             return pltpu.make_async_remote_copy(
@@ -1047,48 +1045,48 @@
                 device_id=cross, device_id_type=MESH,
             )
 
-        for turn in range(2):
-            @pl.when(section == turn)
-            def _(turn=turn):
-                sent = [
-                    remote(outputs[turn][m].at[block(1 - t, shard_rows)], out_ref.at[t * seqs + m], m) for m in range(seqs)
-                ]
-                if turn == 1:
-                    sent += [
-                        remote(grad_refs[m].at[block(1 - t, shard_rows)], got_ref.at[m], seqs + m) for m in range(seqs)
-                    ]
-                for item in sent:
-                    item.start()
-                for m in range(seqs):
-                    copy(outputs[turn][m].at[block(t, shard_rows)], stage.at[m], l_sem.at[m]).start()
-                for m in range(seqs):
-                    arrived(stage.at[m], l_sem.at[m])
-                    copy(stage.at[m], out_ref.at[t * seqs + m], l_sem.at[m]).start()
-                for m in range(seqs):
-                    arrived(stage.at[m], l_sem.at[m])
-                for m in range(seqs):
-                    arrived(out_ref.at[(1 - t) * seqs + m], recv.at[m])
-                    arrived(stage.at[m], send.at[m])
-                if turn == 1:
-                    for m in range(seqs):
-                        sent[seqs + m].wait()
+        barrier = pltpu.get_barrier_semaphore()
+        pl.semaphore_signal(barrier, inc=1, device_id=cross, device_id_type=MESH)
+        pl.semaphore_wait(barrier, 1)
+
+        @pl.when(lax.axis_index("section") == turn)
+        def _():
+            sent = [remote(y_refs[m].at[block(1 - t, shard_rows)], out_ref.at[t * seqs + m], m) for m in range(seqs)]
+            for m, ref in enumerate(grad_refs):
+                sent.append(remote(ref.at[block(1 - t, shard_rows)], refs[n_in + 1].at[m], seqs + m))
+            for item in sent:
+                item.start()
+            for m in range(seqs):
+                copy(y_refs[m].at[block(t, shard_rows)], stage.at[m], l_sem.at[m]).start()
+            for m in range(seqs):
+                arrived(stage.at[m], l_sem.at[m])
+                copy(stage.at[m], out_ref.at[t * seqs + m], l_sem.at[m]).start()
+            for m in range(seqs):
+                arrived(stage.at[m], l_sem.at[m])
+            for m in range(seqs):
+                arrived(out_ref.at[(1 - t) * seqs + m], recv.at[m])
+                arrived(stage.at[m], send.at[m])
+            for item in sent[seqs:]:
+                item.wait()
 
     sem = pltpu.SemaphoreType.DMA
+    shapes = [
+        jax.ShapeDtypeStruct((2 * seqs, shard_rows, width), BF),
+        jax.ShapeDtypeStruct((seqs, shard_rows, width), BF),
+    ]
     return pl.pallas_call(
         kernel,
-        in_specs=[ANY] * (3 * seqs),
-        out_specs=[ANY] * 2,
-        out_shape=[
-            jax.ShapeDtypeStruct((2 * seqs, shard_rows, width), BF),
-            jax.ShapeDtypeStruct((seqs, shard_rows, width), BF),
-        ],
+        in_specs=[ANY] * n_in,
+        out_specs=[ANY] * n_out,
+        out_shape=shapes[:n_out],
         scratch_shapes=[
             pltpu.VMEM((seqs, shard_rows, width), BF), sem((2 * seqs,)), sem((2 * seqs,)), sem((seqs,)),
         ],
-        compiler_params=pltpu.CompilerParams(collective_id=2, has_side_effects=True),
+        input_output_aliases={seqs + len(grads): 0} if earlier else {},
+        compiler_params=pltpu.CompilerParams(collective_id=2 + turn, has_side_effects=True),
         cost_estimate=pl.CostEstimate(flops=0, bytes_accessed=0, transcendentals=0),
         name="exchange_rows",
-    )(*first, *second, *grads)
+    )(*outputs, *grads, *earlier, *deps)
 
 
 def widen(reduced, row_grads, gots, sums, units, local):
@@ -1692,7 +1690,10 @@
 
     y_first = [forward(x_first[m], m, 0) for m in range(seqs)]
     x_second = [lax.ppermute(y, "section", [(0, 1)]) for y in y_first]
-    y_second = [forward(x_second[m], m, 1) for m in range(seqs)]
+    y_second = [forward(x_second[0], 0, 1)]
+    (produced,) = exchange_rows(y_first, [], 0, [], deps)
+    deps = [produced]
+    y_second += [forward(x_second[m], m, 1) for m in range(1, seqs)]
 
     back = None
     sums = [[None] * seqs, [None] * seqs]
@@ -1708,10 +1709,10 @@
 
     gx_second = [backward(outer[m], m, 1) for m in range(seqs)]
     grad_middle = [lax.ppermute(gx_second[m][1], "section", [(1, 0)]) for m in range(seqs)]
-    produced, got_second = exchange_rows(y_first, y_second, [g[1] for g in gx_second])
     x_all = jnp.stack([jnp.where(first, x_first[m], x_second[m]) for m in range(seqs)])
-    deps = deps + [x_all, produced]
+    deps = deps + [x_all]
     gx_first = [backward(grad_middle[m], m, 0) for m in range(seqs)]
+    produced, got_second = exchange_rows(y_second, [g[1] for g in gx_second], 1, [produced], deps)
 
     mixed, hidden, normed = kept[3], kept[7], kept[8]
     gg0, gg1, gl, ga, *gqkv = back

time: 758 us -> 712 us (0.939)
  waiting for transfers between devices: 136 us -> 90.6 us
    ppermute x2, waiting for transfers between devices: 118 us -> 90.6 us  [by_sequence(): lax.ppermute(gx_second[m][1], 'section', [(1, 0)])]
    ppermute x2, waiting for transfers between devices: 18.4 us -> 0.01 us  [by_sequence(): x_second = [lax.ppermute(y, 'section', [(0, 1)]) for y in y_first]]
    pallas_call x1 -> x2, Pallas kernels: 25.3 us -> 27.4 us  [exchange_rows(): pl.pallas_call(kernel, in_specs=[ANY] * n_in, out_specs=[ANY] * n_out, ou...]
  transfers between devices with their start and end apart: 4 -> 4, of which waited for: 3 -> 2; matrix products, arithmetic and copies ran while one was open for 0% -> 1% of each run, Pallas kernels for 16% -> 17%
where the time goes in v7:
time: 712 us; the launch traced here: 702 us
  Pallas kernels  588 us (83%)
  waiting for transfers between devices  90.6 us (13%)
  other arithmetic  8.1 us (1%)
  local copies, waits for them, and re-layouts  7.13 us (1%)
    pallas_call x1, Pallas kernels, weight_grads_reduced(): pl.pallas_call(kernel, in_specs=[ANY] * n_in, out_specs=[ANY] * n_left +...  225 us
    pallas_call x8, Pallas kernels, call(): pl.pallas_call(body, in_specs=specs, out_specs=[ANY] * n_out, out_shape=[...  192 us
    pallas_call x1, Pallas kernels, fetch_other_half(): pl.pallas_call(kernel, in_specs=[ANY] * 8, out_specs=[ANY] * (6 + seqs),...  123 us
    ppermute x2, waiting for transfers between devices, by_sequence(): lax.ppermute(gx_second[m][1], 'section', [(1, 0)])  90.6 us
    pallas_call x2, Pallas kernels, exchange_rows(): pl.pallas_call(kernel, in_specs=[ANY] * n_in, out_specs=[ANY] * n_out, ou...  27.4 us
    pallas_call x1, Pallas kernels, widen(): pl.pallas_call(kernel, in_specs=[ANY] * (n + 2 * seqs + 2) + [WHOLE], out...  21.5 us
  transfers between devices with their start and end apart: 4, of which 2 were waited for; matrix products, arithmetic and copies ran while one was open for 1% of the time, Pallas kernels for 17%

profile of v7, /device:TPU:0, one launch (start us, length us, event | category | flops | bytes accessed | tf_op | source)
XLA Modules:
  0.0 701.9 jit_solution(1685936153621428355)
XLA Ops:
  0.7 0.7 dynamic_slice.3
  1.4 0.6 fusion.9
  2.0 0.8 slice_bitcast_fusion
  2.8 0.9 stack.44
  3.6 0.6 convert_element_type.2.refs_12_.refs_21_
  4.2 1.2 broadcast_select_fusion.refs_11_.refs_20_
  5.5 1.9 pad_add_fusion.2
  7.4 122.5 %fetch_other_half.1 = (bf16[3072,512]{1,0:T(8,128)(2,1)}, bf16[512,1024]{1,0:T(8,128)(2,1)}, bf16[2048,2048]{1,0:T(8,128)(2,1)}, bf16[1024,2048]{1,0:T(8,128)(2,...) custom-call(bf16[3072,512]{1,0:T(8,128)(2,1)} %bitcast.64, ...), custom_call_target="tpu_custom_call" | custom-call | bytes 33554432 | tf_op jit(solution)/shard_map/fetch_other_half/pallas_call | solution.py:728
  129.9 39.5 %layer_forward.4 = (bf16[2,512,1024]{2,1,0:T(8,128)(2,1)}, bf16[2,512,1024]{2,1,0:T(8,128)(2,1)}, bf16[2,512,1024]{2,1,0:T(8,128)(2,1)}, bf16[2,512,1024]{2,1,0:...) custom-call(s32[4]{0:T(128)} %get-tuple-element.285.refs_0_, ...), custom_call_target="tpu_custom_call" | custom-call | flops 18253611008 | bytes 56623104 | tf_op jit(solution)/shard_map/layer_forward/pallas_call | solution.py:55
  169.4 1.4 collective-permute-start
  170.8 39.0 %layer_forward.5 = (bf16[2,512,1024]{2,1,0:T(8,128)(2,1)}, bf16[2,512,1024]{2,1,0:T(8,128)(2,1)}, bf16[2,512,1024]{2,1,0:T(8,128)(2,1)}, bf16[2,512,1024]{2,1,0:...) custom-call(s32[4]{0:T(128)} %get-tuple-element.284.refs_0_, ...), custom_call_target="tpu_custom_call", output_to_operand_aliasing={{0}: (14, {}), {1}: (15, {}), {2}: (16, {}), {3}: (17, {}),... | custom-call | flops 18253611008 | bytes 56623104 | tf_op jit(solution)/shard_map/layer_forward/pallas_call | solution.py:55
  209.8 2.3 collective-permute-start.1
  212.0 1.9 fusion.3
  213.9 0.0 collective-permute-done.refs_1_
  213.9 1.0 copy-done.1
  214.9 1.3 layer_forward.6
  216.2 25.9 %exchange_rows.2.refs_27_.refs_4_ = bf16[4,256,1024]{2,1,0:T(8,128)(2,1)} custom-call(bf16[512,1024]{1,0:T(8,128)(2,1)} %get-tuple-element.150.refs_27_.refs_0_, bf16[512,1024]{1,0:T(8,128)(2,1)} %get-tuple-element.178.refs_27_.refs_1_, bf16[512,1024]{1,0:T(8,128)(2,1)} %get-tuple-element.179.refs_2_.refs_0_), custom_call_target="tpu_custom_call" | custom-call | tf_op jit(solution)/shard_map/exchange_rows/pallas_call | solution.py:1077
  242.1 0.0 collective-permute-done.1.refs_1_
  242.1 1.6 layer_forward.7
  243.7 7.1 %layer_backward.4 = (bf16[2,512,4096]{2,1,0:T(8,128)(2,1)}, bf16[2,512,4096]{2,1,0:T(8,128)(2,1)}, bf16[2,512,1024]{2,1,0:T(8,128)(2,1)}, bf16[2,512,1024]{2,1,0...) custom-call(s32[4]{0:T(128)} %get-tuple-element.287.refs_0_, ...), custom_call_target="tpu_custom_call" | custom-call | flops 19864223744 | bytes 73400320 | tf_op jit(solution)/shard_map/layer_backward/pallas_call | solution.py:55
  250.8 1.3 collective-permute-start.3
  252.1 0.0 copy-start
  252.1 6.0 layer_backward.5
  258.1 0.0 copy-start.2
  258.1 0.0 copy-start.3
  258.1 1.4 collective-permute-start.2
  259.5 0.0 copy-done
  259.5 0.1 select_bitcast_fusion
  259.7 0.0 copy-done.2
  259.7 0.0 copy-done.3
  259.7 0.1 select_bitcast_fusion.1
  259.8 1.5 pad_maximum_fusion.refs_30_.refs_2_
  261.3 88.2 %collective-permute-done.3.refs_1_ = bf16[512,1024]{1,0:T(8,128)(2,1)} collective-permute-done((bf16[512,1024]{1,0:T(8,128)(2,1)}, bf16[512,1024]{1,0:T(8,128)(2,1)}, u32[]{:S(2)}, u32[]{:S(2)}) %collective-permute-start.3) | collective-permute-done | bytes 1048608 | tf_op jit(solution)/shard_map/ppermute | solution.py:1711
  349.5 48.6 %layer_backward.6 = (bf16[2,512,4096]{2,1,0:T(8,128)(2,1)}, bf16[2,512,4096]{2,1,0:T(8,128)(2,1)}, bf16[2,512,1024]{2,1,0:T(8,128)(2,1)}, bf16[2,512,1024]{2,1,0...) custom-call(s32[4]{0:T(128)} %get-tuple-element.285.refs_0_, ...), custom_call_target="tpu_custom_call", output_to_operand_aliasing={{0}: (22, {}), {1}: (23, {}), {2}: (24, {}), {3}: (25, {}),... | custom-call | flops 19864223744 | bytes 73400320 | tf_op jit(solution)/shard_map/layer_backward/pallas_call | solution.py:55
  398.2 2.4 collective-permute-done.2.refs_1_
  400.6 48.6 %layer_backward.7 = (bf16[2,512,4096]{2,1,0:T(8,128)(2,1)}, bf16[2,512,4096]{2,1,0:T(8,128)(2,1)}, bf16[2,512,1024]{2,1,0:T(8,128)(2,1)}, bf16[2,512,1024]{2,1,0...) custom-call(s32[4]{0:T(128)} %get-tuple-element.284.refs_0_, ...), custom_call_target="tpu_custom_call", output_to_operand_aliasing={{0}: (22, {}), {1}: (23, {}), {2}: (24, {}), {3}: (25, {}),... | custom-call | flops 19864223744 | bytes 73400320 | tf_op jit(solution)/shard_map/layer_backward/pallas_call | solution.py:55
  449.2 0.0 copy-start.4
  449.2 0.0 copy-start.5
  449.2 0.0 copy-start.6
  449.2 0.0 copy-start.7
  449.3 0.0 copy-start.12
  449.3 0.0 copy-start.13
  449.3 0.0 copy-start.14
  449.3 0.0 copy-start.15
  449.3 0.0 copy-start.8
  449.3 0.0 copy-start.9
  449.3 0.0 copy-start.10
  449.3 0.0 copy-start.11
  449.3 1.6 exchange_rows.3
  450.9 0.0 copy-done.4
  450.9 0.0 copy-done.5
  450.9 0.0 copy-done.6
  450.9 0.0 copy-done.7
  451.0 0.0 copy-done.12
  451.0 0.0 copy-done.13
  451.0 0.0 copy-done.14
  451.0 0.0 copy-done.15
  451.0 0.0 copy-done.8
  451.1 0.0 copy-done.9
  451.1 0.0 copy-done.10
  451.2 0.6 pad_maximum_fusion.1.refs_11_
  451.9 225.2 %weight_grads_reduced.1 = (bf16[1,1024,2048]{2,1,0:T(8,128)(2,1)}, bf16[2,1024,2048]{2,1,0:T(8,128)(2,1)}, bf16[3,1024,512]{2,1,0:T(8,128)(2,1)}, bf16[1,1024,51...) custom-call(bf16[2,512,1024]{2,1,0:T(8,128)(2,1)} %get-tuple-element.232.refs_0_, ...), custom_call_target="tpu_custom_call" | custom-call | flops 34359738368 | bytes 67108864 | tf_op jit(solution)/shard_map/weight_grads_reduced/pallas_call | solution.py:997
  677.1 21.5 %widen.1 = (f32[1,1024,2048]{2,1,0:T(8,128)}, f32[2,1024,2048]{2,1,0:T(8,128)}, f32[3,1024,512]{2,1,0:T(8,128)}, f32[512,1024]{1,0:T(8,128)}, f32[4,256,1024]{2,...) custom-call(bf16[1,1024,2048]{2,1,0:T(8,128)(2,1)} %get-tuple-elemen, ...), custom_call_target="tpu_custom_call" | custom-call | bytes 58720256 | tf_op jit(solution)/shard_map/widen/pallas_call | solution.py:1194
  698.6 3.1 copy.150
  (10 shorter events, 0.1 us)
Async XLA Ops:
  169.4 44.5 %collective-permute-start = (bf16[512,1024]{1,0:T(8,128)(2,1)}, bf16[512,1024]{1,0:T(8,128)(2,1)S(1)}, u32[]{:S(2)}, u32[]{:S(2)}) collective-permute-start(bf16[512,1024]{1,0:T(8,128)(2,1)} %get-tuple-element.150.refs_27_.refs_0_), channel_id=1, source_target_pairs={{0,16},{1,17},{2,18},{3,19},{4,20},{5,21},{6,22},{7,23},{8,24},{9,... | collective-permute-start | bytes 3145736 | tf_op jit(solution)/shard_map/ppermute | solution.py:1692
  209.8 32.4 %collective-permute-start.1 = (bf16[512,1024]{1,0:T(8,128)(2,1)}, bf16[512,1024]{1,0:T(8,128)(2,1)}, u32[]{:S(2)}, u32[]{:S(2)}) collective-permute-start(bf16[512,1024]{1,0:T(8,128)(2,1)} %get-tuple-element.178.refs_27_.refs_1_), channel_id=1, source_target_pairs={{0,16},{1,17},{2,18},{3,19},{4,20},{5,21},{6,22},{7,23},{8,24},{9,... | collective-permute-start | bytes 3145736 | tf_op jit(solution)/shard_map/ppermute | solution.py:1692
  213.9 1.0 copy-start.1
  250.8 98.7 %collective-permute-start.3 = (bf16[512,1024]{1,0:T(8,128)(2,1)}, bf16[512,1024]{1,0:T(8,128)(2,1)}, u32[]{:S(2)}, u32[]{:S(2)}) collective-permute-start(bf16[512,1024]{1,0:T(8,128)(2,1)} %get-tuple-element.204.refs_2_), channel_id=1, source_target_pairs={{16,0},{17,1},{18,2},{19,3},{20,4},{21,5},{22,6},{23,7},{24,8},{25... | collective-permute-start | bytes 3145736 | tf_op jit(solution)/shard_map/ppermute | solution.py:1711
  252.1 7.4 %copy-start = (bf16[512,1024]{1,0:T(8,128)(2,1)S(1)}, bf16[512,1024]{1,0:T(8,128)(2,1)}, u32[]{:S(2)}) copy-start(bf16[512,1024]{1,0:T(8,128)(2,1)} %get-tuple-element.151.refs_1_) | copy-start | bytes 3145732
  258.1 1.6 copy-start.2
  258.1 1.6 copy-start.3
  258.1 142.5 %collective-permute-start.2 = (bf16[512,1024]{1,0:T(8,128)(2,1)}, bf16[512,1024]{1,0:T(8,128)(2,1)}, u32[]{:S(2)}, u32[]{:S(2)}) collective-permute-start(bf16[512,1024]{1,0:T(8,128)(2,1)} %get-tuple-element.213.refs_3_), channel_id=1, source_target_pairs={{16,0},{17,1},{18,2},{19,3},{20,4},{21,5},{22,6},{23,7},{24,8},{25... | collective-permute-start | bytes 3145736 | tf_op jit(solution)/shard_map/ppermute | solution.py:1711
  449.2 1.7 copy-start.4
  449.2 1.7 copy-start.5
  449.2 1.7 copy-start.6
  449.2 1.7 copy-start.7
  449.3 1.7 copy-start.12
  449.3 1.7 copy-start.13
  449.3 1.7 copy-start.14
  449.3 1.7 copy-start.15
  449.3 1.7 copy-start.8
  449.3 1.7 copy-start.9
  449.3 1.7 copy-start.10
  449.3 1.7 copy-start.11

commit v8 on v7

--- a/solution.py
+++ b/solution.py
@@ -104,169 +104,25 @@
     return [slice(0, rows // 2), slice(rows // 2, rows)]
 
 
-def layer_forward(x, weights, bias, slopes, vecs, up_bias, meta, chain, deps, slots):
-    qkv_own, qkv_oth, o_own, o_oth, up_own, up_oth, down_own, down_oth = weights
-    rows, width = x.shape
-    local = qkv_own.shape[2]
-    units = up_own.shape[2]
-    heads_steps = local // CW
-    ft = min(512, units)
-    tiles = units // ft
-    total = 2 * local
-
-    def kernel(meta_ref, ins, outs, scratch):
-        (x_hbm, qkv_own_ref, qkv_oth_ref, o_own_ref, o_oth_ref, up_own_ref, up_oth_ref, down_own_ref, down_oth_ref,
-         bias_ref, slope_ref, vec_ref, ub_ref) = ins
-        q_out, k_out, v_out, mixed_out, lse_out, a_out, b_out, h_out, n_out, u1_out, u2_out, r1_out, r2_out, y_out = outs
-        (x_ref, w_ref, o_ref, up_ref, down_ref, qkv_ref, lse_ref, mixed_ref, dist_ref, normed_ref, acc_ref, low_ref,
-         tile_ref, row_ref, stat_ref, x_sem, w_sem, o_sem, f_sem, q_sem, m_sem, t_sem, r_sem) = scratch
-        slot = meta_ref[0]
-
-        def start_w(k):
-            s = lax.rem(k, 2)
-            pick(k, heads_steps, qkv_own_ref, qkv_oth_ref,
-                 lambda ref, j: [(ref.at[:, :, block(j, CW)], w_ref.at[s], w_sem.at[s])])
-
-        def start_f(k):
-            s = lax.rem(k, 2)
-            pick(k, tiles, (up_own_ref, down_own_ref), (up_oth_ref, down_oth_ref),
-                 lambda ref, j: [(ref[0].at[:, :, block(j, ft)], up_ref.at[s], f_sem.at[s, 0]),
-                                 (ref[1].at[:, block(j, ft)], down_ref.at[s], f_sem.at[s, 1])])
-
-        copy(x_hbm, x_ref, x_sem).start()
-        start_w(jnp.int32(0))
-        start_w(jnp.int32(1))
-        copy(o_own_ref, o_ref.at[pl.ds(0, local)], o_sem).start()
-        copy(o_oth_ref, o_ref.at[pl.ds(local, local)], o_sem).start()
-        start_f(jnp.int32(0))
-        start_f(jnp.int32(1))
-        fill_distance(dist_ref, meta_ref[2])
-        arrived(x_ref, x_sem)
-
-        def write_qkv(i, s):
-            cols = block(i, CW)
-            return [copy(qkv_ref.at[s, c], out.at[slot, :, cols], q_sem.at[s, c])
-                    for c, out in enumerate((q_out, k_out, v_out))] + [
-                copy(lse_ref.at[s], lse_out.at[slot, i], q_sem.at[s, 3])]
-
-        @pl.loop(0, 2 * heads_steps)
-        def _(i):
-            s = lax.rem(i, 2)
-            arrived(w_ref.at[s], w_sem.at[s])
-
-            @pl.when(i >= 2)
-            def _():
-                for item in write_qkv(i - 2, s):
-                    item.wait()
-
-            values = x_ref[...]
-            b = bias_ref[:, block(i, CW)].astype(F32)
-            qkv_ref[s, 0] = (dot(values, w_ref[s, 0]) + b[0:1]).astype(BF)
-            qkv_ref[s, 1] = dot(values, w_ref[s, 1]).astype(BF)
-            qkv_ref[s, 2] = (dot(values, w_ref[s, 2]) + b[1:2]).astype(BF)
-
-            @pl.when(i + 2 < 2 * heads_steps)
-            def _():
-                start_w(i + 2)
-
-            parts = []
-            for head in range(PER):
-                cols = slice(head * HD, (head + 1) * HD)
-                query = qkv_ref[s, 0, :, cols] * BF(1.0 / math.sqrt(HD))
-                scores = dot(qkv_ref[s, 1, :, cols], query, NT)
-                scores = scores - dist_ref[...] * slope_ref[i * PER + head]
-                top = jnp.max(scores, axis=0, keepdims=True)
-                likely = jnp.exp(scores - top)
-                mass = jnp.sum(likely, axis=0, keepdims=True)
-                low = (likely * (1.0 / mass)).astype(BF)
-                parts.append(dot(low, qkv_ref[s, 2, :, cols], TN).astype(BF))
-                lse_ref[s, head : head + 1, :] = top + jnp.log(mass)
-            mixed_ref[:, block(i, CW)] = jnp.concatenate(parts, axis=1)
-            for item in write_qkv(i, s):
-                item.start()
-
-        copy(mixed_ref, mixed_out.at[slot], m_sem).start()
-        arrived(o_ref, o_sem)
-        vec = vec_ref[...]
-        for rs in halves(rows):
-            attended = dot(mixed_ref[rs, :], o_ref[...])
-            u, rstd = normalize(x_ref[rs, :].astype(F32) + attended + vec[0:1])
-            normed = u * vec[1:2] + vec[2:3]
-            normed_ref[rs, :] = normed
-            low_ref[rs, :] = normed.astype(BF)
-            row_ref[0, rs, :] = u.astype(BF)
-            stat_ref[0, rs, :] = jnp.broadcast_to(rstd, (rows // 2, 128))
-            acc_ref[rs, :] = jnp.zeros((rows // 2, width), F32)
-        for index, (src, dst) in enumerate(((low_ref, n_out), (row_ref.at[0], u1_out), (stat_ref.at[0], r1_out))):
-            copy(src, dst.at[slot], r_sem.at[index]).start()
-
-        def write_tiles(i, s):
-            return [copy(tile_ref.at[s, c], out.at[slot, :, block(i, ft)], t_sem.at[s, c])
-                    for c, out in enumerate((a_out, b_out, h_out))]
-
-        @pl.loop(0, 2 * tiles)
-        def _(i):
-            s = lax.rem(i, 2)
-            arrived(up_ref.at[s], f_sem.at[s, 0])
-            arrived(down_ref.at[s], f_sem.at[s, 1])
-
-            @pl.when(i >= 2)
-            def _():
-                for item in write_tiles(i - 2, s):
-                    item.wait()
-
-            b = ub_ref[:, block(i, ft)].astype(F32)
-            for rs in halves(rows):
-                low = low_ref[rs, :]
-                gate = dot(low, up_ref[s, 0]) + b[0:1]
-                lift = dot(low, up_ref[s, 1]) + b[1:2]
-                cdf = 0.5 * lax.erf(gate * (1.0 / math.sqrt(2.0))) + 0.5
-                act = gate * cdf
-                slope = cdf + gate * (jnp.exp(gate * gate * -0.5) * (1.0 / math.sqrt(2.0 * math.pi)))
-                tile_ref[s, 0, rs, :] = act.astype(BF)
-                tile_ref[s, 1, rs, :] = (lift * slope).astype(BF)
-                hidden = (act * lift).astype(BF)
-                tile_ref[s, 2, rs, :] = hidden
-                acc_ref[rs, :] += dot(hidden, down_ref[s], NT)
-
-            @pl.when(i + 2 < 2 * tiles)
-            def _():
-                start_f(i + 2)
-
-            for item in write_tiles(i, s):
-                item.start()
-
-        for rs in halves(rows):
-            u, rstd = normalize(normed_ref[rs, :] + acc_ref[rs, :] + vec[3:4])
-            row_ref[1, rs, :] = u.astype(BF)
-            stat_ref[1, rs, :] = jnp.broadcast_to(rstd, (rows // 2, 128))
-            row_ref[2, rs, :] = (u * vec[4:5] + vec[5:6]).astype(BF)
-        ends = [(row_ref.at[1], u2_out.at[slot]), (stat_ref.at[1], r2_out.at[slot]), (row_ref.at[2], y_out)]
-        for index, (src, dst) in enumerate(ends):
-            copy(src, dst, r_sem.at[3 + index]).start()
-        for index, (src, dst) in enumerate(
-            [(low_ref, n_out.at[slot]), (row_ref.at[0], u1_out.at[slot]), (stat_ref.at[0], r1_out.at[slot])] + ends
-        ):
-            copy(src, dst, r_sem.at[index]).wait()
-        copy(mixed_ref, mixed_out.at[slot], m_sem).wait()
-        for i in (2 * heads_steps - 2, 2 * heads_steps - 1):
-            for item in write_qkv(jnp.int32(i), i % 2):
-                item.wait()
-        for i in (2 * tiles - 2, 2 * tiles - 1):
-            for item in write_tiles(jnp.int32(i), i % 2):
-                item.wait()
-
-    sem = pltpu.SemaphoreType.DMA
-    return call(
-        kernel,
-        [x, *weights, (bias, WHOLE), (slopes, SMEM), (vecs, WHOLE), (up_bias, WHOLE)],
-        [((slots, rows, total), BF, True)] * 4
-        + [((slots, 2 * heads_steps, 8, rows), F32, True)]
-        + [((slots, rows, 2 * units), BF, True)] * 3
-        + [((slots, rows, width), BF, True)] * 3
-        + [((slots, rows, 128), F32, True)] * 2
-        + [((rows, width), BF, False)],
-        [
+class Forward:
+    def __init__(self, rows, width, local, units):
+        self.rows, self.width, self.local, self.units = rows, width, local, units
+        self.ft = min(512, units)
+        self.tiles = units // self.ft
+        self.heads_steps = local // CW
+        self.total = 2 * local
+
+    def kept(self, slots):
+        rows, width = self.rows, self.width
+        shapes = [((slots, rows, self.total), BF)] * 4
+        shapes += [((slots, 2 * self.heads_steps, 8, rows), F32)]
+        shapes += [((slots, rows, 2 * self.units), BF)] * 3
+        return shapes + [((slots, rows, width), BF)] * 3 + [((slots, rows, 128), F32)] * 2
+
+    def scratch(self):
+        rows, width, ft, total = self.rows, self.width, self.ft, self.total
+        sem = pltpu.SemaphoreType.DMA
+        return [
             pltpu.VMEM((rows, width), BF),
             pltpu.VMEM((2, 3, width, CW), BF),
             pltpu.VMEM((total, width), BF),
@@ -282,13 +138,197 @@
             pltpu.VMEM((2, 3, rows, ft), BF),
             pltpu.VMEM((3, rows, width), BF),
             pltpu.VMEM((2, rows, 128), F32),
-            sem, sem((2,)), sem, sem((2, 2)), sem((2, 4)), sem, sem((2, 3)), sem((6,)),
-        ],
+            sem, sem((2,)), sem((2,)), sem((2, 2)), sem((2, 4)), sem, sem((2, 3)), sem((6,)),
+        ]
+
+    def bind(self, x, weights, bias, slopes, vecs, up_bias, slot, outs, scratch):
+        self.x_hbm, self.weights, self.bias, self.slopes, self.vecs, self.up_bias = x, weights, bias, slopes, vecs, up_bias
+        self.slot, self.outs = slot, outs
+        (self.x, self.w, self.o, self.up, self.down, self.qkv, self.lse, self.mixed, self.dist, self.normed, self.acc,
+         self.low, self.tile, self.row, self.stat, self.x_sem, self.w_sem, self.o_sem, self.f_sem, self.q_sem, self.m_sem,
+         self.t_sem, self.r_sem) = scratch
+
+    def start_x(self):
+        copy(self.x_hbm, self.x, self.x_sem).start()
+
+    def start_w(self, k):
+        s = lax.rem(k, 2)
+        pick(k, self.heads_steps, self.weights[0], self.weights[1],
+             lambda ref, j: [(ref.at[:, :, block(j, CW)], self.w.at[s], self.w_sem.at[s])])
+
+    def start_o(self, side):
+        copy(self.weights[2 + side], self.o.at[pl.ds(side * self.local, self.local)], self.o_sem.at[side]).start()
+
+    def start_f(self, k):
+        s = lax.rem(k, 2)
+        ft = self.ft
+        pick(k, self.tiles, (self.weights[4], self.weights[6]), (self.weights[5], self.weights[7]),
+             lambda ref, j: [(ref[0].at[:, :, block(j, ft)], self.up.at[s], self.f_sem.at[s, 0]),
+                             (ref[1].at[:, block(j, ft)], self.down.at[s], self.f_sem.at[s, 1])])
+
+    def write_qkv(self, i, s):
+        cols = block(i, CW)
+        return [copy(self.qkv.at[s, c], out.at[self.slot, :, cols], self.q_sem.at[s, c])
+                for c, out in enumerate(self.outs[:3])] + [
+            copy(self.lse.at[s], self.outs[4].at[self.slot, i], self.q_sem.at[s, 3])]
+
+    def attention_step(self, i, ahead):
+        s = lax.rem(i, 2)
+        qkv = self.qkv
+        arrived(self.w.at[s], self.w_sem.at[s])
+
+        @pl.when(i >= 2)
+        def _():
+            for item in self.write_qkv(i - 2, s):
+                item.wait()
+
+        values = self.x[...]
+        b = self.bias[:, block(i, CW)].astype(F32)
+        qkv[s, 0] = (dot(values, self.w[s, 0]) + b[0:1]).astype(BF)
+        qkv[s, 1] = dot(values, self.w[s, 1]).astype(BF)
+        qkv[s, 2] = (dot(values, self.w[s, 2]) + b[1:2]).astype(BF)
+
+        @pl.when(i + 2 < ahead)
+        def _():
+            self.start_w(i + 2)
+
+        parts = []
+        for head in range(PER):
+            cols = slice(head * HD, (head + 1) * HD)
+            query = qkv[s, 0, :, cols] * BF(1.0 / math.sqrt(HD))
+            scores = dot(qkv[s, 1, :, cols], query, NT)
+            scores = scores - self.dist[...] * self.slopes[i * PER + head]
+            top = jnp.max(scores, axis=0, keepdims=True)
+            likely = jnp.exp(scores - top)
+            mass = jnp.sum(likely, axis=0, keepdims=True)
+            low = (likely * (1.0 / mass)).astype(BF)
+            parts.append(dot(low, qkv[s, 2, :, cols], TN).astype(BF))
+            self.lse[s, head : head + 1, :] = top + jnp.log(mass)
+        self.mixed[:, block(i, CW)] = jnp.concatenate(parts, axis=1)
+        for item in self.write_qkv(i, s):
+            item.start()
+
+    def middle(self):
+        rows, width = self.rows, self.width
+        copy(self.mixed, self.outs[3].at[self.slot], self.m_sem).start()
+        for side in range(2):
+            arrived(self.o.at[pl.ds(side * self.local, self.local)], self.o_sem.at[side])
+        vec = self.vecs[...]
+        for rs in halves(rows):
+            attended = dot(self.mixed[rs, :], self.o[...])
+            u, rstd = normalize(self.x[rs, :].astype(F32) + attended + vec[0:1])
+            normed = u * vec[1:2] + vec[2:3]
+            self.normed[rs, :] = normed
+            self.low[rs, :] = normed.astype(BF)
+            self.row[0, rs, :] = u.astype(BF)
+            self.stat[0, rs, :] = jnp.broadcast_to(rstd, (rows // 2, 128))
+            self.acc[rs, :] = jnp.zeros((rows // 2, width), F32)
+        for index, item in enumerate(self.first_rows()):
+            copy(*item, self.r_sem.at[index]).start()
+
+    def first_rows(self):
+        return [(self.low, self.outs[8].at[self.slot]), (self.row.at[0], self.outs[9].at[self.slot]),
+                (self.stat.at[0], self.outs[11].at[self.slot])]
+
+    def write_tiles(self, i, s):
+        return [copy(self.tile.at[s, c], out.at[self.slot, :, block(i, self.ft)], self.t_sem.at[s, c])
+                for c, out in enumerate(self.outs[5:8])]
+
+    def ffn_step(self, i, ahead):
+        s = lax.rem(i, 2)
+        arrived(self.up.at[s], self.f_sem.at[s, 0])
+        arrived(self.down.at[s], self.f_sem.at[s, 1])
+
+        @pl.when(i >= 2)
+        def _():
+            for item in self.write_tiles(i - 2, s):
+                item.wait()
+
+        b = self.up_bias[:, block(i, self.ft)].astype(F32)
+        low = self.low[...]
+        gate = dot(low, self.up[s, 0]) + b[0:1]
+        lift = dot(low, self.up[s, 1]) + b[1:2]
+        cdf = 0.5 * lax.erf(gate * (1.0 / math.sqrt(2.0))) + 0.5
+        act = gate * cdf
+        slope = cdf + gate * (jnp.exp(gate * gate * -0.5) * (1.0 / math.sqrt(2.0 * math.pi)))
+        self.tile[s, 0] = act.astype(BF)
+        self.tile[s, 1] = (lift * slope).astype(BF)
+        hidden = (act * lift).astype(BF)
+        self.tile[s, 2] = hidden
+        self.acc[...] += dot(hidden, self.down[s], NT)
+
+        @pl.when(i + 2 < ahead)
+        def _():
+            self.start_f(i + 2)
+
+        for item in self.write_tiles(i, s):
+            item.start()
+
+    def finish(self, y_out):
+        rows = self.rows
+        vec = self.vecs[...]
+        for rs in halves(rows):
+            u, rstd = normalize(self.normed[rs, :] + self.acc[rs, :] + vec[3:4])
+            self.row[1, rs, :] = u.astype(BF)
+            self.stat[1, rs, :] = jnp.broadcast_to(rstd, (rows // 2, 128))
+            self.row[2, rs, :] = (u * vec[4:5] + vec[5:6]).astype(BF)
+        ends = [(self.row.at[1], self.outs[10].at[self.slot]), (self.stat.at[1], self.outs[12].at[self.slot]),
+                (self.row.at[2], y_out)]
+        for index, item in enumerate(ends):
+            copy(*item, self.r_sem.at[3 + index]).start()
+        for index, item in enumerate(self.first_rows() + ends):
+            copy(*item, self.r_sem.at[index]).wait()
+        copy(self.mixed, self.outs[3].at[self.slot], self.m_sem).wait()
+        for i in (2 * self.heads_steps - 2, 2 * self.heads_steps - 1):
+            for item in self.write_qkv(jnp.int32(i), i % 2):
+                item.wait()
+        for i in (2 * self.tiles - 2, 2 * self.tiles - 1):
+            for item in self.write_tiles(jnp.int32(i), i % 2):
+                item.wait()
+
+    def flops(self):
+        rows, width, total = self.rows, self.width, self.total
+        return 2 * rows * width * (4 * total + 6 * self.units) + 4 * rows * rows * total
+
+
+def layer_forward(x, weights, bias, slopes, vecs, up_bias, meta, chain, deps, slots):
+    rows, width = x.shape
+    step = Forward(rows, width, weights[0].shape[2], weights[4].shape[2])
+
+    def kernel(meta_ref, ins, outs, scratch):
+        step.bind(ins[0], ins[1:9], *ins[9:13], meta_ref[0], outs[:13], scratch)
+        step.start_x()
+        for k in range(2):
+            step.start_w(jnp.int32(k))
+        for side in range(2):
+            step.start_o(side)
+        for k in range(2):
+            step.start_f(jnp.int32(k))
+        fill_distance(step.dist, meta_ref[2])
+        arrived(step.x, step.x_sem)
+
+        @pl.loop(0, 2 * step.heads_steps)
+        def _(i):
+            step.attention_step(i, 2 * step.heads_steps)
+
+        step.middle()
+
+        @pl.loop(0, 2 * step.tiles)
+        def _(i):
+            step.ffn_step(i, 2 * step.tiles)
+
+        step.finish(outs[13])
+
+    return call(
+        kernel,
+        [x, *weights, (bias, WHOLE), (slopes, SMEM), (vecs, WHOLE), (up_bias, WHOLE)],
+        [shape + (True,) for shape in step.kept(slots)] + [((rows, width), BF, False)],
+        step.scratch(),
         meta,
         chain,
         deps,
         "layer_forward",
-        2 * rows * width * (4 * total + 6 * units) + 4 * rows * rows * total,
+        step.flops(),
         54 << 20,
     )
 
@@ -382,19 +422,14 @@
                 for item in write_tiles(i - 2, s):
                     item.wait()
 
-            s0 = jnp.zeros((1, ft), F32)
-            s1 = jnp.zeros((1, ft), F32)
-            for rs in halves(rows):
-                gh = dot(low_ref[0, rs, :], down_ref[s])
-                g0 = (gh * ab_ref[s, 1, rs, :].astype(F32)).astype(BF)
-                g1 = (gh * ab_ref[s, 0, rs, :].astype(F32)).astype(BF)
-                gg_ref[s, 0, rs, :] = g0
-                gg_ref[s, 1, rs, :] = g1
-                s0 += row_sum(g0.astype(F32))
-                s1 += row_sum(g1.astype(F32))
-                acc_ref[rs, :] += dot(g0, up_ref[s, 0], NT) + dot(g1, up_ref[s, 1], NT)
-            ub_ref[0:1, block(i, ft)] = s0
-            ub_ref[1:2, block(i, ft)] = s1
+            gh = dot(low_ref[0], down_ref[s])
+            g0 = (gh * ab_ref[s, 1].astype(F32)).astype(BF)
+            g1 = (gh * ab_ref[s, 0].astype(F32)).astype(BF)
+            gg_ref[s, 0] = g0
+            gg_ref[s, 1] = g1
+            ub_ref[0:1, block(i, ft)] = row_sum(g0.astype(F32))
+            ub_ref[1:2, block(i, ft)] = row_sum(g1.astype(F32))
+            acc_ref[...] += dot(g0, up_ref[s, 0], NT) + dot(g1, up_ref[s, 1], NT)
 
             @pl.when(i + 2 < 2 * tiles)
             def _():
@@ -551,52 +586,79 @@
     pl.semaphore_wait(barrier, 1 + chips)
 
 
-def fetch_other_half(qkv, out, up, down, qv_bias, up_bias, inputs, cotangent, chips):
-    weights = [qkv, out, up, down]
-    biases = [qv_bias, up_bias]
-    bias_widths = [b.shape[1] for b in biases]
+def fetch_and_forward(weights, biases, inputs, cotangent, slopes, vecs, meta, chips, slots):
     seqs = inputs.shape[0] // 2
     shard_rows, width = inputs.shape[1:]
+    rows = 2 * shard_rows
     groups = 2 * chips
-
-    def rows_of(item):
-        return weights[item].shape[0]
-
-    plan = []
-    up_piece = rows_of(2) // groups
-    parts = 4
-    for part in range(parts):
-        plan.append((2, True, 0, up_piece, part * up_piece // parts, up_piece // parts))
-    spread = rows_of(3) * 3 // 4
-    down_piece = spread // groups
-    for part in range(3):
-        plan.append((3, True, 0, down_piece, part * down_piece // 3, down_piece // 3))
-    n_spread = len(plan)
-    plan.append((-1, False, 0, 0, 0, 0))
-    plan.append((-2, False, 0, 0, 0, 0))
-    plan.append((-2, False, 0, 0, 0, 1))
-    for part in range(3):
-        size = rows_of(0) // 6
-        plan.append((0, False, 0, rows_of(0) // 2, part * size, size))
-    plan.append((1, False, 0, rows_of(1) // 2, 0, rows_of(1) // 2))
-    plan.append((-1, False, 0, 0, 0, 1))
-    direct = (rows_of(3) - spread) // 2
-    for part in range(2):
-        plan.append((3, False, spread, direct, part * direct // 2, direct // 2))
+    qkv, out, up, down = weights
+    local, units = qkv.shape[2], up.shape[2]
+    step = Forward(rows, width, local, units)
+    ft, tiles = step.ft, step.tiles
+    bias_widths = [b.shape[1] for b in biases]
+    QKV, OUT, UP, DOWN, ROWS, BIAS = range(6)
+
+    plan = [(UP, 0, groups), (ROWS, 0, 0), (BIAS, 0, 0), (BIAS, 1, 0)]
+    plan += [(UP, part, groups) for part in range(1, tiles)]
+    plan += [(DOWN, part, groups) for part in range(tiles - 1)]
+    plan += [(QKV, part, 2) for part in range(3)] + [(OUT, 0, 2), (DOWN, tiles - 1, 2)]
+    plan += [(ROWS, part, 0) for part in range(1, seqs)]
     n = len(plan)
+    number = {item[:2]: index for index, item in enumerate(plan)}
+
+    def size(index):
+        kind, part, pieces = plan[index]
+        whole = {QKV: width * local, OUT: local * width, UP: 2 * width * ft, DOWN: width * ft, ROWS: shard_rows * width, BIAS: 64}
+        return whole[kind] / max(1, pieces)
+
+    events, clock, busy = [], 0.0, 0.0
+    for index, (kind, part, pieces) in enumerate(plan):
+        clock += size(index)
+        events.append((clock, index, 0))
+        if pieces == groups:
+            start = max(clock, busy)
+            busy = start + size(index) * (chips - 1)
+            events += [(start + size(index) * hop * 1.001, index, hop) for hop in range(1, chips)]
+    events.sort()
+    when = {event[1:]: event[0] for event in events}
+
+    def ready(*keys):
+        return max(when[key] for k in keys for key in when if key[0] == number[k])
+
+    needs = [[(ROWS, 0), (BIAS, 0)], []] + [[(QKV, part) for part in range(3)], []] + [[(OUT, 0), (BIAS, 1)]]
+    needs += [[] for _ in range(tiles - 1)]
+    fetches = {5 + tiles - 1 + part: tiles + part for part in range(tiles)}
+    needs += [[(UP, part), (DOWN, part)] for part in range(tiles)] + [[]]
+    assert step.heads_steps == 2
+    rounds, taken = [], 0
+    for need in needs:
+        mine = []
+        if need:
+            limit = ready(*need)
+            while taken < len(events) and events[taken][0] <= limit:
+                mine.append(events[taken][1:])
+                taken += 1
+        rounds.append((mine, need))
+    rest = [event[1:] for event in events[taken:]]
+    n_rounds = len(rounds)
+    n_kept = len(step.kept(slots))
 
     def kernel(*refs):
-        ins, bias_ins, held_refs = refs[:4], refs[4:6], refs[6:8]
-        outs, bias_outs, row_refs = refs[8:12], refs[12:14], refs[14 : 14 + seqs]
-        stage, x_send, x_recv, c_send, c_recv, u_send, u_recv, d_send, d_recv, l_sem, b_sem = refs[14 + seqs :]
+        meta_ref, slope_ref, vec_ref = refs[:3]
+        ins, bias_ins, held_refs = refs[3:7], refs[7:9], refs[9:11]
+        outs, bias_outs, row_refs = refs[11:15], refs[15:17], refs[17 : 17 + seqs]
+        kept_refs = refs[17 + seqs : 17 + seqs + n_kept]
+        y_ref = refs[17 + seqs + n_kept]
+        stage, qv_bias, ub_bias, x_send, x_recv, c_send, c_recv, u_send, u_recv, d_send, d_recv, l_sem, b_sem = refs[
+            18 + seqs + n_kept : 31 + seqs + n_kept
+        ]
         t, c, z, last, core, cross, above, below = neighbours()
         section = lax.axis_index("section")
         greet(c, z, chips, core, cross)
-
-        def rows(index, chip, on):
-            item, is_spread, base, piece, offset, size = plan[index]
-            place = chip * 2 + on if is_spread else on
-            return item, pl.ds(pl.multiple_of(base + place * piece + offset, size), size)
+        paired = [item for pair in zip(ins, outs) for item in pair]
+        step.bind(
+            row_refs[0], paired, qv_bias, slope_ref, vec_ref, ub_bias, 0, kept_refs, refs[31 + seqs + n_kept :]
+        )
 
         def span(part):
             return block(part, shard_rows)
@@ -604,37 +666,48 @@
         def bias_part(m, side):
             return bias_outs[m].at[:, pl.ds(side * bias_widths[m], bias_widths[m])]
 
+        def piece(side, index, chip, on):
+            kind, part, pieces = plan[index]
+            place = chip * 2 + on if pieces == groups else on
+            ref = (ins, outs)[side][kind]
+            if kind == QKV:
+                return ref.at[part, block(place, width // pieces)]
+            if kind == OUT:
+                return ref.at[block(place, local // pieces)]
+            cols = pl.ds(part * ft, ft)
+            if kind == DOWN:
+                return ref.at[block(place, width // pieces), cols]
+            per = pieces // 2
+            return ref.at[place // per, block(lax.rem(place, per), width // per), cols]
+
         def cross_copy(index, held_ref=None):
-            m = plan[index][5]
-            if plan[index][0] == -1:
+            kind, m, pieces = plan[index]
+            if kind == ROWS:
                 src = (held_refs[0] if held_ref is None else held_ref).at[(1 - t) * seqs + m]
                 dst = row_refs[m].at[span(t)]
-            elif plan[index][0] == -2:
+            elif kind == BIAS:
                 src, dst = bias_ins[m], bias_part(m, 1)
             else:
-                item, where = rows(index, z, c)
-                src, dst = ins[item].at[where], outs[item].at[where]
+                src, dst = piece(0, index, z, c), piece(1, index, z, c)
             return pltpu.make_async_remote_copy(
                 src_ref=src, dst_ref=dst, send_sem=x_send.at[index], recv_sem=x_recv.at[index],
                 device_id=cross, device_id_type=MESH,
             )
 
         def pass_on(index, chip, send, recv, device):
-            item, where = rows(index, chip, c)
-            place = outs[item].at[where]
+            place = piece(1, index, chip, c)
             return pltpu.make_async_remote_copy(
                 src_ref=place, dst_ref=place, send_sem=send.at[index, chip], recv_sem=recv.at[index, chip],
                 device_id=device, device_id_type=MESH,
             )
 
         def got(index, chip, on, sem):
-            item, where = rows(index, chip, on)
-            arrived(outs[item].at[where], sem)
+            arrived(piece(1, index, chip, on), sem)
 
         for m in range(2):
             copy(bias_ins[m], bias_part(m, 0), b_sem.at[m]).start()
         for index in range(n):
-            if plan[index][0] == -1:
+            if plan[index][0] == ROWS:
                 for turn in range(2):
                     @pl.when(section == turn)
                     def _(index=index, turn=turn):
@@ -644,24 +717,34 @@
         for turn in range(2):
             @pl.when(section == turn)
             def _(turn=turn):
-                copy(held_refs[turn].at[pl.ds(t * seqs, seqs)], stage, l_sem).start()
-
-        arrived(stage, l_sem)
+                copy(held_refs[turn].at[pl.ds(t * seqs, seqs)], stage, l_sem.at[0]).start()
+
+        @pl.when(section == 0)
+        def _():
+            for k in range(2):
+                step.start_w(jnp.int32(k))
+            step.start_o(0)
+            for k in range(2):
+                step.start_f(jnp.int32(k))
+            fill_distance(step.dist, meta_ref[2])
+
+        arrived(stage, l_sem.at[0])
         for m in range(seqs):
-            copy(stage.at[m], row_refs[m].at[span(t)], l_sem).start()
+            copy(stage.at[m], row_refs[m].at[span(t)], l_sem.at[m]).start()
+        for m in range(seqs):
+            arrived(stage.at[m], l_sem.at[m])
+        for m in range(2):
+            copy(bias_ins[m], bias_part(m, 0), b_sem.at[m]).wait()
 
         def handle(index, hop):
-            if hop == 0:
-                m = plan[index][5]
-                if plan[index][0] == -1:
-                    arrived(row_refs[m].at[span(1 - t)], x_recv.at[index])
-                    return
-                if plan[index][0] == -2:
-                    arrived(bias_part(m, 1), x_recv.at[index])
-                    return
+            kind, m, pieces = plan[index]
+            if kind == ROWS:
+                arrived(row_refs[m].at[span(1 - t)], x_recv.at[index])
+            elif kind == BIAS:
+                arrived(bias_part(m, 1), x_recv.at[index])
+            elif hop == 0:
                 got(index, z, c, x_recv.at[index])
-                pass_on(index, z, c_send, c_recv, core).start()
-                if plan[index][1]:
+                if pieces == groups:
                     @pl.when(z < last)
                     def _():
                         pass_on(index, z, u_send, u_recv, above).start()
@@ -669,50 +752,105 @@
                     @pl.when(z > 0)
                     def _():
                         pass_on(index, z, d_send, d_recv, below).start()
-                return
-
-            @pl.when(z - hop >= 0)
+
+                pass_on(index, z, c_send, c_recv, core).start()
+            else:
+                @pl.when(z - hop >= 0)
+                def _():
+                    got(index, z - hop, c, u_recv.at[index, z - hop])
+
+                    @pl.when(z < last)
+                    def _():
+                        pass_on(index, z - hop, u_send, u_recv, above).start()
+
+                    pass_on(index, z - hop, c_send, c_recv, core).start()
+
+                @pl.when(z + hop <= last)
+                def _():
+                    got(index, z + hop, c, d_recv.at[index, z + hop])
+
+                    @pl.when(z > 0)
+                    def _():
+                        pass_on(index, z + hop, d_send, d_recv, below).start()
+
+                    pass_on(index, z + hop, c_send, c_recv, core).start()
+
+        def from_core(key):
+            index = number[key]
+            kind, m, pieces = plan[index]
+            if pieces == groups:
+                for chip in range(chips):
+                    got(index, chip, 1 - c, c_recv.at[index, chip])
+            elif pieces:
+                got(index, z, 1 - c, c_recv.at[index, z])
+
+        @pl.loop(0, n_rounds)
+        def _(tau):
+            for number_, (mine, need) in enumerate(rounds):
+                if not (mine or need):
+                    continue
+
+                @pl.when(tau == number_)
+                def _(number_=number_, mine=mine, need=need):
+                    for index, hop in mine:
+                        handle(index, hop)
+                    for key in need:
+                        from_core(key)
+                    for key in need:
+                        if key == (BIAS, 0):
+                            @pl.when(section == 0)
+                            def _():
+                                step.start_x()
+                                copy(bias_outs[0], qv_bias, b_sem.at[0]).start()
+                                copy(bias_outs[0], qv_bias, b_sem.at[0]).wait()
+                                arrived(step.x, step.x_sem)
+                        elif key == (QKV, 2):
+                            @pl.when(section == 0)
+                            def _():
+                                for k in range(2, 4):
+                                    step.start_w(jnp.int32(k))
+                        elif key == (OUT, 0):
+                            @pl.when(section == 0)
+                            def _():
+                                step.start_o(1)
+                        elif key == (BIAS, 1):
+                            @pl.when(section == 0)
+                            def _():
+                                copy(bias_outs[1], ub_bias, b_sem.at[1]).start()
+                                copy(bias_outs[1], ub_bias, b_sem.at[1]).wait()
+                        elif key[0] == DOWN:
+                            @pl.when(section == 0)
+                            def _(key=key):
+                                step.start_f(jnp.int32(tiles + key[1]))
+
+            @pl.when(section == 0)
             def _():
-                got(index, z - hop, c, u_recv.at[index, z - hop])
-
-                @pl.when(z < last)
+                @pl.when(tau < 4)
                 def _():
-                    pass_on(index, z - hop, u_send, u_recv, above).start()
-
-                pass_on(index, z - hop, c_send, c_recv, core).start()
-
-            @pl.when(z + hop <= last)
-            def _():
-                got(index, z + hop, c, d_recv.at[index, z + hop])
-
-                @pl.when(z > 0)
+                    step.attention_step(tau, 2)
+
+                @pl.when(tau == 4)
                 def _():
-                    pass_on(index, z + hop, d_send, d_recv, below).start()
-
-                pass_on(index, z + hop, c_send, c_recv, core).start()
-
-        for round_ in range(max(n, n_spread + chips - 1)):
-            if round_ < n:
-                handle(round_, 0)
-            for hop in range(1, chips):
-                if 0 <= round_ - hop < n_spread:
-                    handle(round_ - hop, hop)
-
-        for m in range(2):
-            copy(bias_ins[m], bias_part(m, 0), b_sem.at[m]).wait()
-        for m in range(seqs):
-            arrived(stage.at[m], l_sem)
+                    step.middle()
+
+                @pl.when(tau > 4)
+                def _():
+                    step.ffn_step(tau - 5, tiles)
+
+        @pl.when(section == 0)
+        def _():
+            step.finish(y_ref)
+
+        for index, hop in rest:
+            handle(index, hop)
         for index in range(n):
-            item, is_spread = plan[index][:2]
+            kind, part, pieces = plan[index]
             cross_copy(index).wait_send()
-            if item < 0:
-                continue
-            if not is_spread:
-                got(index, z, 1 - c, c_recv.at[index, z])
+            if pieces == 2:
                 pass_on(index, z, c_send, c_recv, core).wait_send()
+            if pieces != groups:
                 continue
             for chip in range(chips):
-                got(index, chip, 1 - c, c_recv.at[index, chip])
                 pass_on(index, chip, c_send, c_recv, core).wait_send()
 
                 @pl.when((chip <= z) & (z < last))
@@ -724,22 +862,25 @@
                     pass_on(index, chip, d_send, d_recv, below).wait_send()
 
     sem = pltpu.SemaphoreType.DMA
-    moved = sum(w.size for w in weights) * 2
     return pl.pallas_call(
         kernel,
-        in_specs=[ANY] * 8,
-        out_specs=[ANY] * (6 + seqs),
+        in_specs=[SMEM, SMEM, WHOLE] + [ANY] * 8,
+        out_specs=[ANY] * (7 + seqs + n_kept),
         out_shape=[jax.ShapeDtypeStruct(w.shape, BF) for w in weights]
-        + [jax.ShapeDtypeStruct((2, 2 * size), BF) for size in bias_widths]
-        + [jax.ShapeDtypeStruct((2 * shard_rows, width), BF)] * seqs,
+        + [jax.ShapeDtypeStruct((2, 2 * size_), BF) for size_ in bias_widths]
+        + [jax.ShapeDtypeStruct((rows, width), BF)] * seqs
+        + [jax.ShapeDtypeStruct(*shape) for shape in step.kept(slots)]
+        + [jax.ShapeDtypeStruct((rows, width), BF)],
         scratch_shapes=[pltpu.VMEM((seqs, shard_rows, width), BF)]
+        + [pltpu.VMEM((2, 2 * size_), BF) for size_ in bias_widths]
         + [sem((n,)), sem((n,))]
         + [sem((n, chips))] * 6
-        + [sem, sem((2,))],
-        compiler_params=pltpu.CompilerParams(collective_id=1, has_side_effects=True),
-        cost_estimate=pl.CostEstimate(flops=0, bytes_accessed=2 * moved, transcendentals=0),
-        name="fetch_other_half",
-    )(*weights, *biases, inputs, cotangent)
+        + [sem((seqs,)), sem((2,))]
+        + step.scratch(),
+        compiler_params=pltpu.CompilerParams(collective_id=1, has_side_effects=True, vmem_limit_bytes=VMEM_LIMIT),
+        cost_estimate=pl.CostEstimate(flops=step.flops(), bytes_accessed=90 << 20, transcendentals=0),
+        name="fetch_and_forward",
+    )(meta, slopes, vecs, *weights, *biases, inputs, cotangent)
 
 
 def weight_grads_reduced(groups, sums, row_grads, chips):
@@ -1651,21 +1792,6 @@
     up_own = w_up[0]
     down_own = w_down[0]
     first = section == 0
-    qkv_oth, out_oth, up_oth, down_oth, bias, up_bias, *held = fetch_other_half(
-        qkv_own.reshape(3 * width, local),
-        out_own,
-        up_own.reshape(2 * width, units),
-        down_own,
-        b_qv[0],
-        b_up[0],
-        inputs,
-        cotangent,
-        chips,
-    )
-    qkv_oth = qkv_oth.reshape(3, width, local)
-    up_oth = up_oth.reshape(2, width, units)
-    x_first = outer = held
-
     vecs = jnp.stack(
         [b_out[0], ln_gain[0, 0], ln_bias[0, 0], b_down[0], ln_gain[0, 1], ln_bias[0, 1], b_out[0], b_out[0]]
     ).astype(F32)
@@ -1678,9 +1804,21 @@
         return jnp.stack([jnp.int32(m), active.astype(jnp.int32), own_lengths[m], own_lengths[m] if turn == 1 else jnp.int32(rows)])
 
     metas = [[meta(m, turn) for m in range(seqs)] for turn in range(2)]
+    qkv_oth, out_oth, up_oth, down_oth, bias, up_bias, *rest = fetch_and_forward(
+        (qkv_own, out_own, up_own, down_own),
+        (b_qv[0], b_up[0]),
+        inputs,
+        cotangent,
+        slopes,
+        vecs,
+        metas[0][0],
+        chips,
+        seqs,
+    )
     weights = (qkv_own, qkv_oth, out_own, out_oth, up_own, up_oth, down_own, down_oth)
-    kept = None
-    deps = []
+    x_first = outer = rest[:seqs]
+    *kept, y = rest[seqs:]
+    deps = [y]
 
     def forward(x, m, turn):
         nonlocal kept, deps
@@ -1688,7 +1826,7 @@
         deps = [y]
         return y
 
-    y_first = [forward(x_first[m], m, 0) for m in range(seqs)]
+    y_first = [y] + [forward(x_first[m], m, 0) for m in range(1, seqs)]
     x_second = [lax.ppermute(y, "section", [(0, 1)]) for y in y_first]
     y_second = [forward(x_second[0], 0, 1)]
     (produced,) = exchange_rows(y_first, [], 0, [], deps)

time: 712 us -> 687 us (0.965)
  Pallas kernels: 588 us -> 565 us
    pallas_call x8 -> x7, Pallas kernels: 192 us -> 149 us  [call(): pl.pallas_call(body, in_specs=specs, out_specs=[ANY] * n_out, out_shape=[...]
    pallas_call x1, Pallas kernels: 123 us -> 144 us  [fetch_and_forward(): pl.pallas_call(kernel, in_specs=[SMEM, SMEM, WHOLE] + [ANY] * 8, out_spec...]
where the time goes in v8:
time: 687 us; the launch traced here: 676 us
  Pallas kernels  565 us (82%)
  waiting for transfers between devices  87.8 us (13%)
  other arithmetic  8.02 us (1%)
  local copies, waits for them, and re-layouts  7.14 us (1%)
    pallas_call x1, Pallas kernels, weight_grads_reduced(): pl.pallas_call(kernel, in_specs=[ANY] * n_in, out_specs=[ANY] * n_left +...  225 us
    pallas_call x7, Pallas kernels, call(): pl.pallas_call(body, in_specs=specs, out_specs=[ANY] * n_out, out_shape=[...  149 us
    pallas_call x1, Pallas kernels, fetch_and_forward(): pl.pallas_call(kernel, in_specs=[SMEM, SMEM, WHOLE] + [ANY] * 8, out_spec...  144 us
    ppermute x2, waiting for transfers between devices, by_sequence(): lax.ppermute(gx_second[m][1], 'section', [(1, 0)])  87.8 us
    pallas_call x2, Pallas kernels, exchange_rows(): pl.pallas_call(kernel, in_specs=[ANY] * n_in, out_specs=[ANY] * n_out, ou...  25.9 us
    pallas_call x1, Pallas kernels, widen(): pl.pallas_call(kernel, in_specs=[ANY] * (n + 2 * seqs + 2) + [WHOLE], out...  21.5 us
  transfers between devices with their start and end apart: 4, of which 2 were waited for; matrix products, arithmetic and copies ran while one was open for 1% of the time, Pallas kernels for 17%

profile of v8, /device:TPU:0, one launch (start us, length us, event | category | flops | bytes accessed | tf_op | source)
XLA Modules:
  0.0 675.9 jit_solution(10276666246635944600)
XLA Ops:
  0.7 0.7 dynamic_slice.3
  1.4 0.6 fusion.9
  2.0 0.8 slice_bitcast_fusion
  2.8 0.9 stack.44
  3.6 0.6 convert_element_type.2.refs_2_.refs_12_.refs_21_
  4.2 1.1 broadcast_select_fusion.refs_1_.refs_11_.refs_20_
  5.4 1.9 pad_add_fusion.2
  7.3 143.5 %fetch_and_forward.1 = (bf16[3,1024,512]{2,1,0:T(8,128)(2,1)}, bf16[512,1024]{1,0:T(8,128)(2,1)}, bf16[2,1024,2048]{2,1,0:T(8,128)(2,1)}, bf16[1024,2048]{1,0:T(...) custom-call(s32[4]{0:T(128)} %get-tuple-element.285.refs_0_, ...), custom_call_target="tpu_custom_call" | custom-call | flops 18253611008 | bytes 94371840 | tf_op jit(solution)/shard_map/fetch_and_forward/pallas_call | solution.py:865
  150.9 1.4 collective-permute-start
  152.2 38.6 %layer_forward.3 = (bf16[2,512,1024]{2,1,0:T(8,128)(2,1)}, bf16[2,512,1024]{2,1,0:T(8,128)(2,1)}, bf16[2,512,1024]{2,1,0:T(8,128)(2,1)}, bf16[2,512,1024]{2,1,0:...) custom-call(s32[4]{0:T(128)} %get-tuple-element.284.refs_0_, ...), custom_call_target="tpu_custom_call", output_to_operand_aliasing={{0}: (14, {}), {1}: (15, {}), {2}: (16, {}), {3}: (17, {}),... | custom-call | flops 18253611008 | bytes 56623104 | tf_op jit(solution)/shard_map/layer_forward/pallas_call | solution.py:55
  190.9 2.3 collective-permute-start.1
  193.1 1.9 fusion.3
  195.0 0.0 collective-permute-done.refs_1_
  195.0 1.0 copy-done.1
  196.0 1.3 layer_forward.4
  197.4 24.2 %exchange_rows.2.refs_27_.refs_4_ = bf16[4,256,1024]{2,1,0:T(8,128)(2,1)} custom-call(bf16[512,1024]{1,0:T(8,128)(2,1)} %get-tuple-element.143.refs_27_.refs_0_, bf16[512,1024]{1,0:T(8,128)(2,1)} %get-tuple-element.177.refs_27_.refs_1_, bf16[512,1024]{1,0:T(8,128)(2,1)} %get-tuple-element.178.refs_2_.refs_0_), custom_call_target="tpu_custom_call" | custom-call | tf_op jit(solution)/shard_map/exchange_rows/pallas_call | solution.py:1218
  221.6 0.0 collective-permute-done.1.refs_1_
  221.6 1.6 layer_forward.5
  223.3 6.8 %layer_backward.4 = (bf16[2,512,4096]{2,1,0:T(8,128)(2,1)}, bf16[2,512,4096]{2,1,0:T(8,128)(2,1)}, bf16[2,512,1024]{2,1,0:T(8,128)(2,1)}, bf16[2,512,1024]{2,1,0...) custom-call(s32[4]{0:T(128)} %get-tuple-element.287.refs_0_, ...), custom_call_target="tpu_custom_call" | custom-call | flops 19864223744 | bytes 73400320 | tf_op jit(solution)/shard_map/layer_backward/pallas_call | solution.py:55
  230.1 1.3 collective-permute-start.3
  231.4 0.0 copy-start
  231.4 5.8 layer_backward.5
  237.2 0.0 copy-start.2
  237.2 0.0 copy-start.3
  237.2 1.4 collective-permute-start.2
  238.6 0.0 copy-done
  238.6 0.1 select_bitcast_fusion
  238.8 0.0 copy-done.2
  238.8 0.0 copy-done.3
  238.8 0.1 select_bitcast_fusion.1
  238.9 1.5 pad_maximum_fusion.refs_30_.refs_2_
  240.4 85.5 %collective-permute-done.3.refs_1_ = bf16[512,1024]{1,0:T(8,128)(2,1)} collective-permute-done((bf16[512,1024]{1,0:T(8,128)(2,1)}, bf16[512,1024]{1,0:T(8,128)(2,1)}, u32[]{:S(2)}, u32[]{:S(2)}) %collective-permute-start.3) | collective-permute-done | bytes 1048608 | tf_op jit(solution)/shard_map/ppermute | solution.py:1849
  325.8 47.6 %layer_backward.6 = (bf16[2,512,4096]{2,1,0:T(8,128)(2,1)}, bf16[2,512,4096]{2,1,0:T(8,128)(2,1)}, bf16[2,512,1024]{2,1,0:T(8,128)(2,1)}, bf16[2,512,1024]{2,1,0...) custom-call(s32[4]{0:T(128)} %get-tuple-element.285.refs_0_, ...), custom_call_target="tpu_custom_call", output_to_operand_aliasing={{0}: (22, {}), {1}: (23, {}), {2}: (24, {}), {3}: (25, {}),... | custom-call | flops 19864223744 | bytes 73400320 | tf_op jit(solution)/shard_map/layer_backward/pallas_call | solution.py:55
  373.4 2.3 collective-permute-done.2.refs_1_
  375.7 47.5 %layer_backward.7 = (bf16[2,512,4096]{2,1,0:T(8,128)(2,1)}, bf16[2,512,4096]{2,1,0:T(8,128)(2,1)}, bf16[2,512,1024]{2,1,0:T(8,128)(2,1)}, bf16[2,512,1024]{2,1,0...) custom-call(s32[4]{0:T(128)} %get-tuple-element.284.refs_0_, ...), custom_call_target="tpu_custom_call", output_to_operand_aliasing={{0}: (22, {}), {1}: (23, {}), {2}: (24, {}), {3}: (25, {}),... | custom-call | flops 19864223744 | bytes 73400320 | tf_op jit(solution)/shard_map/layer_backward/pallas_call | solution.py:55
  423.2 0.0 copy-start.4
  423.2 0.0 copy-start.5
  423.2 0.0 copy-start.6
  423.3 0.0 copy-start.7
  423.3 0.0 copy-start.12
  423.3 0.0 copy-start.13
  423.3 0.0 copy-start.14
  423.3 0.0 copy-start.15
  423.3 0.0 copy-start.8
  423.3 0.0 copy-start.9
  423.3 0.0 copy-start.10
  423.3 0.0 copy-start.11
  423.4 1.6 exchange_rows.3
  425.0 0.0 copy-done.4
  425.0 0.0 copy-done.5
  425.0 0.0 copy-done.6
  425.0 0.0 copy-done.7
  425.0 0.0 copy-done.12
  425.0 0.0 copy-done.13
  425.0 0.0 copy-done.14
  425.1 0.0 copy-done.15
  425.1 0.0 copy-done.8
  425.1 0.0 copy-done.9
  425.1 0.0 copy-done.10
  425.1 0.0 copy-done.11
  425.3 0.6 pad_maximum_fusion.1.refs_11_
  425.9 225.2 %weight_grads_reduced.1 = (bf16[1,1024,2048]{2,1,0:T(8,128)(2,1)}, bf16[2,1024,2048]{2,1,0:T(8,128)(2,1)}, bf16[3,1024,512]{2,1,0:T(8,128)(2,1)}, bf16[1,1024,51...) custom-call(bf16[2,512,1024]{2,1,0:T(8,128)(2,1)} %get-tuple-element.232.refs_0_, ...), custom_call_target="tpu_custom_call" | custom-call | flops 34359738368 | bytes 67108864 | tf_op jit(solution)/shard_map/weight_grads_reduced/pallas_call | solution.py:1138
  651.1 21.5 %widen.1 = (f32[1,1024,2048]{2,1,0:T(8,128)}, f32[2,1024,2048]{2,1,0:T(8,128)}, f32[3,1024,512]{2,1,0:T(8,128)}, f32[512,1024]{1,0:T(8,128)}, f32[4,256,1024]{2,...) custom-call(bf16[1,1024,2048]{2,1,0:T(8,128)(2,1)} %get-tuple-elemen, ...), custom_call_target="tpu_custom_call" | custom-call | bytes 58720256 | tf_op jit(solution)/shard_map/widen/pallas_call | solution.py:1335
  672.6 3.1 copy.150
  (9 shorter events, 0.1 us)
Async XLA Ops:
  150.9 44.2 %collective-permute-start = (bf16[512,1024]{1,0:T(8,128)(2,1)}, bf16[512,1024]{1,0:T(8,128)(2,1)S(1)}, u32[]{:S(2)}, u32[]{:S(2)}) collective-permute-start(bf16[512,1024]{1,0:T(8,128)(2,1)} %get-tuple-element.143.refs_27_.refs_0_), channel_id=1, source_target_pairs={{0,16},{1,17},{2,18},{3,19},{4,20},{5,21},{6,22},{7,23},{8,24},{9,... | collective-permute-start | bytes 3145736 | tf_op jit(solution)/shard_map/ppermute | solution.py:1830
  190.9 30.8 %collective-permute-start.1 = (bf16[512,1024]{1,0:T(8,128)(2,1)}, bf16[512,1024]{1,0:T(8,128)(2,1)}, u32[]{:S(2)}, u32[]{:S(2)}) collective-permute-start(bf16[512,1024]{1,0:T(8,128)(2,1)} %get-tuple-element.177.refs_27_.refs_1_), channel_id=1, source_target_pairs={{0,16},{1,17},{2,18},{3,19},{4,20},{5,21},{6,22},{7,23},{8,24},{9,... | collective-permute-start | bytes 3145736 | tf_op jit(solution)/shard_map/ppermute | solution.py:1830
  195.0 1.0 copy-start.1
  230.1 95.7 %collective-permute-start.3 = (bf16[512,1024]{1,0:T(8,128)(2,1)}, bf16[512,1024]{1,0:T(8,128)(2,1)}, u32[]{:S(2)}, u32[]{:S(2)}) collective-permute-start(bf16[512,1024]{1,0:T(8,128)(2,1)} %get-tuple-element.204.refs_2_), channel_id=1, source_target_pairs={{16,0},{17,1},{18,2},{19,3},{20,4},{21,5},{22,6},{23,7},{24,8},{25... | collective-permute-start | bytes 3145736 | tf_op jit(solution)/shard_map/ppermute | solution.py:1849
  231.4 7.2 %copy-start = (bf16[512,1024]{1,0:T(8,128)(2,1)S(1)}, bf16[512,1024]{1,0:T(8,128)(2,1)}, u32[]{:S(2)}) copy-start(bf16[512,1024]{1,0:T(8,128)(2,1)} %get-tuple-element.150.refs_1_) | copy-start | bytes 3145732
  237.2 1.6 copy-start.2
  237.2 1.6 copy-start.3
  237.2 138.6 %collective-permute-start.2 = (bf16[512,1024]{1,0:T(8,128)(2,1)}, bf16[512,1024]{1,0:T(8,128)(2,1)}, u32[]{:S(2)}, u32[]{:S(2)}) collective-permute-start(bf16[512,1024]{1,0:T(8,128)(2,1)} %get-tuple-element.213.refs_3_), channel_id=1, source_target_pairs={{16,0},{17,1},{18,2},{19,3},{20,4},{21,5},{22,6},{23,7},{24,8},{25... | collective-permute-start | bytes 3145736 | tf_op jit(solution)/shard_map/ppermute | solution.py:1849
  423.2 1.7 copy-start.4
  423.2 1.7 copy-start.5
  423.2 1.7 copy-start.6
  423.3 1.7 copy-start.7
  423.3 1.8 copy-start.12
  423.3 1.8 copy-start.13
  423.3 1.8 copy-start.14
  423.3 1.8 copy-start.15
  423.3 1.8 copy-start.8
  423.3 1.8 copy-start.9
  423.3 1.8 copy-start.10
  423.3 1.8 copy-start.11

commit v9 on v8

--- a/solution.py
+++ b/solution.py
@@ -883,46 +883,72 @@
     )(meta, slopes, vecs, *weights, *biases, inputs, cotangent)
 
 
-def weight_grads_reduced(groups, sums, row_grads, chips):
+def norm_back(grad_z, u, rstd, gain):
+    t = grad_z * gain
+    return rstd * (t - jnp.mean(t, axis=1, keepdims=True) - u * jnp.mean(t * u, axis=1, keepdims=True))
+
+
+def row_sum(values):
+    return jnp.sum(values, axis=0, keepdims=True)
+
+
+def backward_and_reduce(grad, kept, back, x_all, weights, slopes, vecs, meta, sums, low_grad, second, chips):
+    q, k_, v, mixed_all, lse, act, slope, hidden_all, normed_all, u1, u2, r1, r2 = kept
+    gg0, gg1, gl, ga, gq, gk, gv = back
+    rows, width = grad.shape
+    local, units = weights[0].shape[2], weights[4].shape[2]
+    ft = CW
+    tiles = units // ft
+    heads_steps = local // CW
     seqs = 2
-    rows, depth = groups[0][0].shape[1:]
-    lefts = [g[0] for g in groups]
-    rights = [r for g in groups for r in g[1]]
     bt = 128
-    half = depth // 2
+    lefts = [gl, normed_all, x_all, ga]
+    rights = [hidden_all, gg0, gg1, gq, gk, gv, mixed_all]
+    group_of = [0, 1, 1, 2, 2, 2, 3]
+    member_of = [0, 0, 1, 0, 1, 2, 0]
+    half = width // 2
     quarter = half // 2
-    blocks = [r.shape[2] // (2 * bt) for r in rights]
-    starts = [sum(blocks[:index]) for index in range(len(rights))]
-    total = sum(blocks)
-    group_starts = []
-    index = 0
-    for _, members in groups:
-        group_starts.append(starts[index])
-        index += len(members)
-    n_left, n_right = len(lefts), len(rights)
-    homes = [(g, index) for g, (_, members) in enumerate(groups) for index in range(len(members))]
-    tiles, mines, gives = 4, CORE_LAG + 1, 4
-    last_static = chips - 1
-    drain = CORE_LAG + CROSS_LAG + 2 * last_static * CHAIN_LAG + 1
+    per_pair = 2 * ft // bt
+    pairs = tiles // 2
+    ffn_blocks = 3 * per_pair * pairs
+    head_blocks = local // bt
+    total = ffn_blocks + 4 * head_blocks
+    ring, mines, gives = 4, CORE_LAG + 1, 4
+    ahead_of = 4
+    drain = CORE_LAG + CROSS_LAG + 2 * (chips - 1) * CHAIN_LAG + 1
     vec_shape = sums.shape
-    n_in = n_left + n_right + 1 + seqs
     shard_rows = rows // 2
+    norm_at = 2 * tiles
+    head_at = norm_at + 1
+    end_at = head_at + 4 * heads_steps
+    x_flip, ga_flip = ffn_blocks - per_pair, ffn_blocks + per_pair
+    up_rows = units // width
+    assert ahead_of + ffn_blocks - ring > end_at
 
     def kernel(*refs):
-        left_refs = refs[:n_left]
-        right_refs = refs[n_left : n_left + n_right]
-        sums_ref = refs[n_left + n_right]
-        row_refs = refs[n_left + n_right + 1 : n_in]
-        outs = refs[n_in : n_in + n_left]
-        sums_out, rows_out = refs[n_in + n_left : n_in + n_left + 2]
+        meta_ref, slope_ref, vec_ref = refs[:3]
+        g_hbm, q_hbm, k_hbm, v_hbm, lse_hbm, a_hbm, b_hbm, u1_hbm, u2_hbm, r1_hbm, r2_hbm = refs[3:14]
+        (qkv_own_ref, qkv_oth_ref, o_own_ref, o_oth_ref, up_own_ref, up_oth_ref, down_own_ref, down_oth_ref) = refs[14:22]
+        left_refs, right_refs = refs[22:26], refs[26:33]
+        sums_ref, low_grad_ref, second_refs = refs[33], refs[34], refs[35 : 35 + 2 * seqs]
+        outs, sums_out, rows_out = refs[39:43], refs[43], refs[44]
+        fresh = refs[45:50]
+        gx_out, gxl_out = refs[50:52]
         (
-            acc, from_x, from_z, final, flip, stage, tile, mine, give, vec, vec_in, vec_all,
+            acc, from_x, from_z, flip, stage, tile, mine, give, vec, vec_in, vec_all,
+            g_ref, u_ref, r_ref, low_ref, gacc_ref, w_ref, o_ref, qkv_ref, gqkv_ref, lse_ref, gm_ref, dist_ref,
+            part_sums, ub_sums, qv_sums,
             tile_sem, stage_sem, give_send, core_recv, x_send, x_recv, z_send, z_recv, f_send, f_recv,
             store_sem, out_send, out_recv, v_load, v_send, v_recv, r_send, r_recv,
-        ) = refs[n_in + n_left + 2 :]
+            g_sem, w_sem, t_sem, e_sem,
+        ) = refs[52:]
+        final = from_x
         t, c, z, last, core, cross, above, below = neighbours()
         section = lax.axis_index("section")
+        first = section == 0
         greet(c, z, chips, core, cross)
+        fresh_of = {1: fresh[0], 2: fresh[1], 3: fresh[2], 4: fresh[3], 5: fresh[4]}
+        vec_w = vec_ref[...]
 
         def remote(src, dst, send, recv, device):
             return pltpu.make_async_remote_copy(
@@ -933,77 +959,337 @@
             return (k >= 0) & (k < total)
 
         def member(k, visit):
-            for m in range(n_right):
-                @pl.when((k >= starts[m]) & (k < starts[m] + blocks[m]))
+            for m in range(3):
+                @pl.when((k < ffn_blocks) & (lax.rem(k, 3 * per_pair) // per_pair == m))
                 def _(m=m):
-                    visit(m, k - starts[m])
+                    visit(m, k // (3 * per_pair) * per_pair + lax.rem(k, per_pair))
+
+            for m in range(3, 7):
+                base = ffn_blocks + (m - 3) * head_blocks
+
+                @pl.when((k >= base) & (k < base + head_blocks))
+                def _(m=m, base=base):
+                    visit(m, k - base)
 
         def load_tile(k):
-            slot = lax.rem(k, tiles)
+            at = lax.rem(k, ring)
 
             def visit(m, j):
+                count = right_refs[m].shape[2] // (2 * bt)
                 for side in range(2):
-                    at = pl.multiple_of((side * blocks[m] + j) * bt, bt)
-                    pltpu.make_async_copy(
-                        right_refs[m].at[pl.ds(0, seqs), :, pl.ds(at, bt)],
-                        tile.at[slot, :, :, pl.ds(side * bt, bt)],
-                        tile_sem.at[slot],
-                    ).start()
+                    cols = block(side * count + j, bt)
+                    where = pl.ds(side * bt, bt)
+                    copy(right_refs[m].at[0, :, cols], tile.at[at, 0, :, where], tile_sem.at[at]).start()
+                    if m not in fresh_of:
+                        copy(right_refs[m].at[1, :, cols], tile.at[at, 1, :, where], tile_sem.at[at]).start()
+                        continue
+
+                    @pl.when(first)
+                    def _(cols=cols, where=where):
+                        copy(fresh_of[m].at[:, cols], tile.at[at, 1, :, where], tile_sem.at[at]).start()
+
+                    @pl.when(section == 1)
+                    def _(cols=cols, where=where):
+                        copy(right_refs[m].at[1, :, cols], tile.at[at, 1, :, where], tile_sem.at[at]).start()
 
             member(k, visit)
 
-        def load_left(g):
-            return pltpu.make_async_copy(left_refs[g].at[pl.ds(0, seqs)], stage, stage_sem)
-
-        vec_load = pltpu.make_async_copy(sums_ref, vec.at[0], v_load)
+        def take_left(g, at, mine_low):
+            copy(left_refs[g].at[0], stage.at[0], stage_sem.at[0]).start()
+            if mine_low is None:
+                copy(left_refs[g].at[1], stage.at[1], stage_sem.at[1]).start()
+                arrived(stage.at[1], stage_sem.at[1])
+            else:
+                @pl.when(first)
+                def _():
+                    stage[1] = low_ref[mine_low]
+
+                @pl.when(section == 1)
+                def _():
+                    copy(left_refs[g].at[1], stage.at[1], stage_sem.at[1]).start()
+                    arrived(stage.at[1], stage_sem.at[1])
+
+            arrived(stage.at[0], stage_sem.at[0])
+            for m in range(seqs):
+                flip[at, :, m * rows : (m + 1) * rows] = stage[m].T
+
+        def place_of(u):
+            within = lax.rem(u, 4)
+            side = within // 2
+            return side, u // 4 * 2 + lax.rem(within, 2)
+
+        def start_f(u):
+            at = lax.rem(u, 2)
+            side, j = place_of(u)
+            pick(side * tiles + j, tiles, (up_own_ref, down_own_ref), (up_oth_ref, down_oth_ref),
+                 lambda ref, jj: [(ref[0].at[:, :, block(jj, ft)], w_ref.at[at, pl.ds(0, 2)], w_sem.at[at, 0]),
+                                  (ref[1].at[:, block(jj, ft)], w_ref.at[at, 2], w_sem.at[at, 1])])
+            for n, ref in enumerate((a_hbm, b_hbm)):
+                copy(ref.at[1, :, block(side * tiles + j, ft)], qkv_ref.at[at, n], w_sem.at[at, 2 + n]).start()
+
+        def write_tile(u):
+            at = lax.rem(u, 2)
+            side, j = place_of(u)
+            return [copy(gqkv_ref.at[at, n], fresh[n].at[:, block(side * tiles + j, ft)], t_sem.at[at, n]) for n in range(2)]
+
+        def start_w(i):
+            at = lax.rem(i, 2)
+            pick(i, heads_steps, (qkv_own_ref, o_own_ref), (qkv_oth_ref, o_oth_ref),
+                 lambda ref, j: [(ref[0].at[:, :, block(j, CW)], w_ref.at[at], w_sem.at[at, 0]),
+                                 (ref[1].at[block(j, CW)], o_ref.at[at], w_sem.at[at, 1])])
+            for n, ref in enumerate((q_hbm, k_hbm, v_hbm)):
+                copy(ref.at[1, :, block(i, CW)], qkv_ref.at[at, n], w_sem.at[at, 2 + n]).start()
+            copy(lse_hbm.at[1, i], lse_ref.at[at], w_sem.at[at, 5]).start()
+
+        def write_heads(i):
+            at = lax.rem(i, 2)
+            return [copy(gqkv_ref.at[at, n], fresh[2 + n].at[:, block(i, CW)], t_sem.at[at, n]) for n in range(3)]
+
+        def norm_load(index, u_hbm, r_hbm):
+            return [copy(u_hbm.at[1], u_ref, g_sem.at[index]), copy(r_hbm.at[1], r_ref, g_sem.at[index + 1])]
+
+        def begin():
+            copy(g_hbm, g_ref, g_sem.at[0]).start()
+            for item in norm_load(1, u2_hbm, r2_hbm):
+                item.start()
+            start_f(jnp.int32(0))
+            start_f(jnp.int32(1))
+            copy(g_hbm, g_ref, g_sem.at[0]).wait()
+            for item in norm_load(1, u2_hbm, r2_hbm):
+                item.wait()
+            totals = [jnp.zeros((1, width), F32)] * 3
+            for rs in halves(rows):
+                grad_y = g_ref[rs, :].astype(F32)
+                u = u_ref[rs, :].astype(F32)
+                grad_c = norm_back(grad_y, u, r_ref[rs, 0:1], vec_w[4:5])
+                gacc_ref[rs, :] = grad_c
+                low_ref[0, rs, :] = grad_c.astype(BF)
+                for index, values in enumerate((grad_y * u, grad_y, grad_c)):
+                    totals[index] += row_sum(values)
+            for index in range(3):
+                part_sums[index : index + 1, :] = totals[index]
+            for item in norm_load(1, u1_hbm, r1_hbm):
+                item.start()
+
+        def ffn_unit(u):
+            at = lax.rem(u, 2)
+
+            @pl.when(u >= 1)
+            def _():
+                for item in write_tile(u - 1):
+                    item.wait()
+
+            arrived(w_ref.at[at, pl.ds(0, 2)], w_sem.at[at, 0])
+            arrived(w_ref.at[at, 2], w_sem.at[at, 1])
+            for n in range(2):
+                arrived(qkv_ref.at[at, n], w_sem.at[at, 2 + n])
+            gh = dot(low_ref[0], w_ref[at, 2])
+            g0 = (gh * qkv_ref[at, 1].astype(F32)).astype(BF)
+            g1 = (gh * qkv_ref[at, 0].astype(F32)).astype(BF)
+            gqkv_ref[at, 0] = g0
+            gqkv_ref[at, 1] = g1
+            side, j = place_of(u)
+            cols = block(side * tiles + j, ft)
+            ub_sums[0:1, cols] = row_sum(g0.astype(F32))
+            ub_sums[1:2, cols] = row_sum(g1.astype(F32))
+            gacc_ref[...] += dot(g0, w_ref[at, 0], NT) + dot(g1, w_ref[at, 1], NT)
+
+            @pl.when(u + 2 < 2 * tiles)
+            def _():
+                start_f(u + 2)
+
+            for item in write_tile(u):
+                item.start()
+
+        def norm_unit():
+            for item in write_tile(jnp.int32(2 * tiles - 1)):
+                item.wait()
+            for i in range(2):
+                start_w(jnp.int32(i))
+            for item in norm_load(1, u1_hbm, r1_hbm):
+                item.wait()
+            totals = [jnp.zeros((1, width), F32)] * 3
+            for rs in halves(rows):
+                grad_n = gacc_ref[rs, :]
+                u = u_ref[rs, :].astype(F32)
+                grad_a = norm_back(grad_n, u, r_ref[rs, 0:1], vec_w[1:2])
+                low_ref[1, rs, :] = grad_a.astype(BF)
+                gacc_ref[rs, :] = grad_a
+                for index, values in enumerate((grad_n * u, grad_n, grad_a)):
+                    totals[index] += row_sum(values)
+            for index in range(3):
+                part_sums[3 + index : 4 + index, :] = totals[index]
+
+        def head_unit(a):
+            i = a // 2
+            pair = lax.rem(a, 2)
+            at = lax.rem(i, 2)
+            scale = BF(1.0 / math.sqrt(HD))
+
+            @pl.when(pair == 0)
+            def _():
+                for index, ref in enumerate(
+                    (w_ref.at[at], o_ref.at[at], qkv_ref.at[at, 0], qkv_ref.at[at, 1], qkv_ref.at[at, 2], lse_ref.at[at])
+                ):
+                    arrived(ref, w_sem.at[at, index])
+
+                @pl.when(i >= 2)
+                def _():
+                    for item in write_heads(i - 2):
+                        item.wait()
+
+                gm_ref[...] = dot(low_ref[1], o_ref[at], NT).astype(BF)
+
+            cols = block(pair, 2 * HD)
+            query2 = qkv_ref[at, 0, :, cols] * scale
+            key2 = qkv_ref[at, 1, :, cols]
+            value2 = qkv_ref[at, 2, :, cols]
+            gm2 = gm_ref[:, cols]
+            parts = [[], [], []]
+            for head in range(2):
+                here = slice(head * HD, (head + 1) * HD)
+                query, key, gm = query2[:, here], key2[:, here], gm2[:, here]
+                scores = dot(key, query, NT)
+                scores = scores - dist_ref[...] * slope_ref[i * PER + pair * 2 + head]
+                likely = jnp.exp(scores - lse_ref[at, pl.ds(pair * 2 + head, 1), :])
+                parts[2].append(dot(likely.astype(BF), gm).astype(BF))
+                tt = likely * dot(value2[:, here], gm, NT)
+                inner = jnp.sum(tt, axis=0, keepdims=True)
+                gs = (tt - likely * inner).astype(BF)
+                parts[1].append(dot(gs, query).astype(BF))
+                parts[0].append(dot(gs, key * scale, TN).astype(BF))
+            for n in range(3):
+                gqkv_ref[at, n, :, cols] = jnp.concatenate(parts[n], axis=1)
+
+            @pl.when(pair == 1)
+            def _():
+                for index, n in enumerate((0, 2)):
+                    qv_sums[index : index + 1, block(i, CW)] = row_sum(gqkv_ref[at, n].astype(F32))
+                gacc_ref[...] += (
+                    dot(gqkv_ref[at, 0], w_ref[at, 0], NT)
+                    + dot(gqkv_ref[at, 1], w_ref[at, 1], NT)
+                    + dot(gqkv_ref[at, 2], w_ref[at, 2], NT)
+                )
+
+                @pl.when(i + 2 < 2 * heads_steps)
+                def _():
+                    start_w(i + 2)
+
+                for item in write_heads(i):
+                    item.start()
+
+        ends = [(g_ref, gxl_out), (gacc_ref, gx_out)]
+
+        def end_unit():
+            for i in (2 * heads_steps - 2, 2 * heads_steps - 1):
+                for item in write_heads(jnp.int32(i)):
+                    item.wait()
+            g_ref[...] = gacc_ref[...].astype(BF)
+            for index, item in enumerate(ends):
+                copy(*item, e_sem.at[index]).start()
+            vec[0, 0:6] += part_sums[0:6]
+            for own in range(2):
+                @pl.when(t == own)
+                def _(own=own):
+                    for n in range(2):
+                        for side in range(2):
+                            place = own if side == 0 else 1 - own
+                            for j in range(up_rows):
+                                at = 6 + (2 * n + place) * up_rows + j
+                                start = side * units + j * width
+                                vec[0, at : at + 1] += ub_sums[n : n + 1, start : start + width]
+                            at = 6 + 4 * up_rows + n
+                            cols = slice(place * local, (place + 1) * local)
+                            vec[0, at : at + 1, cols] += qv_sums[n : n + 1, side * local : (side + 1) * local]
+
+            for index, item in enumerate(ends):
+                copy(*item, e_sem.at[index]).wait()
+
+        vec_load = copy(sums_ref, vec.at[0], v_load)
         vec_load.start()
-        load_left(0).start()
-        for k in range(tiles - 1):
-            load_tile(jnp.int32(k))
+
+        @pl.when(first)
+        def _():
+            begin()
+            fill_distance(dist_ref, meta_ref[2])
+
+        take_left(0, 0, 0)
         vec_load.wait()
         vec_core = remote(vec.at[0], vec_in.at[0], v_send.at[0], v_recv.at[0], core)
         vec_cross = remote(vec.at[1], vec_in.at[1], v_send.at[1], v_recv.at[1], cross)
-        vec_core.start()
-        def row_copy(m):
-            source = row_refs[m].at[block(1 - t, shard_rows)]
+
+        row_sources = ((low_grad_ref, gxl_out), second_refs)
+
+        def row_copy(sources, m):
+            source = sources[m].at[block(1 - t, shard_rows)]
             return remote(source, rows_out.at[m], r_send.at[m], r_recv.at[m], cross)
 
         up = pl.ds(0, quarter)
         down = pl.ds(quarter, quarter)
         sides = ((up, 0, z, above, below), (down, 1, last - z, below, above))
 
-        @pl.loop(0, total + drain)
-        def _(s):
+        @pl.loop(0, ahead_of + total + drain)
+        def _(turn):
+            s = turn - ahead_of
+
+            @pl.when(first)
+            def _():
+                @pl.when(turn < norm_at)
+                def _():
+                    ffn_unit(turn)
+
+                @pl.when(turn == norm_at)
+                def _():
+                    norm_unit()
+
+                @pl.when((turn >= head_at) & (turn < end_at))
+                def _():
+                    head_unit(turn - head_at)
+
+                @pl.when(turn == end_at)
+                def _():
+                    end_unit()
+
+            @pl.when(s == 0)
+            def _():
+                for k in range(ring - 1):
+                    load_tile(jnp.int32(k))
+
             @pl.when(valid(s))
             def _():
-                for g in range(n_left):
-                    @pl.when(s == group_starts[g])
-                    def _(g=g):
-                        load_left(g).wait()
-                        for m in range(seqs):
-                            flip[:, m * rows : (m + 1) * rows] = stage[m].T
-                        if g + 1 < n_left:
-                            load_left(g + 1).start()
-
-                slot = lax.rem(s, tiles)
-                arrived(tile.at[slot], tile_sem.at[slot])
-                give_slot = lax.rem(s, gives)
+                @pl.when(s == per_pair - 2)
+                def _():
+                    take_left(1, 1, None)
+
+                @pl.when(s == x_flip)
+                def _():
+                    take_left(2, 0, None)
+
+                @pl.when(s == ga_flip)
+                def _():
+                    take_left(3, 1, 1)
+
+                at = lax.rem(s, ring)
+                arrived(tile.at[at], tile_sem.at[at])
+                give_at = lax.rem(s, gives)
 
                 @pl.when(s >= gives)
                 def _():
-                    arrived(give.at[give_slot], give_send.at[give_slot])
-
-                for place, ring, at in ((1 - c, give, give_slot), (c, mine, lax.rem(s, mines))):
-                    here = pl.ds(pl.multiple_of(place * half, half), half)
-                    block = dot(flip[here, :rows], tile[slot, 0])
+                    arrived(give.at[give_at], give_send.at[give_at])
+
+                ffn_flip = jnp.where(lax.rem(s, 3 * per_pair) // per_pair == 0, 0, 1)
+                which = jnp.where(s < ffn_blocks, ffn_flip, jnp.where(s < ffn_blocks + 3 * head_blocks, 0, 1))
+                for place, store, spot in ((1 - c, give, give_at), (c, mine, lax.rem(s, mines))):
+                    here = block(place, half)
+                    product = dot(flip[which, here, :rows], tile[at, 0])
                     for m in range(1, seqs):
-                        block += dot(flip[here, m * rows : (m + 1) * rows], tile[slot, m])
-                    ring[at, 1] = block[:, :bt].astype(BF)
-                    ring[at, 0] = block[:, bt:].astype(BF)
-
-            @pl.when(s + tiles - 1 < total)
+                        product += dot(flip[which, here, m * rows : (m + 1) * rows], tile[at, m])
+                    store[spot, 1] = product[:, :bt].astype(BF)
+                    store[spot, 0] = product[:, bt:].astype(BF)
+
+            @pl.when((s >= 0) & (s + ring - 1 < total))
             def _():
-                load_tile(s + tiles - 1)
+                load_tile(s + ring - 1)
 
             k1 = s - CORE_LAG
 
@@ -1021,23 +1307,23 @@
                 arrived(from_x.at[k2], x_recv.at[k2])
                 acc[k2, 1] = (acc[k2, 1].astype(F32) + from_x[k2].astype(F32)).astype(BF)
 
-            for span, way, place, ahead, behind in sides:
+            for rows_, way, place, ahead, behind in sides:
                 k3 = k2 - CHAIN_LAG * place
 
                 @pl.when(valid(k3) & (place > 0))
-                def _(span=span, way=way, k3=k3):
-                    arrived(from_z.at[k3, span], z_recv.at[way, k3])
-                    acc[k3, 1, span] = (acc[k3, 1, span].astype(F32) + from_z[k3, span].astype(F32)).astype(BF)
+                def _(rows_=rows_, way=way, k3=k3):
+                    arrived(from_z.at[k3, rows_], z_recv.at[way, k3])
+                    acc[k3, 1, rows_] = (acc[k3, 1, rows_].astype(F32) + from_z[k3, rows_].astype(F32)).astype(BF)
 
                 k4 = k2 - CHAIN_LAG * (2 * last - place)
 
                 @pl.when(valid(k4) & (place == last))
-                def _(span=span, k4=k4):
-                    final[k4, span] = acc[k4, 1, span]
+                def _(rows_=rows_, k4=k4):
+                    final[k4, rows_] = acc[k4, 1, rows_]
 
                 @pl.when(valid(k4) & (place < last))
-                def _(span=span, way=way, k4=k4):
-                    arrived(final.at[k4, span], f_recv.at[way, k4])
+                def _(rows_=rows_, way=way, k4=k4):
+                    arrived(final.at[k4, rows_], f_recv.at[way, k4])
 
             @pl.when(valid(s))
             def _():
@@ -1048,52 +1334,55 @@
             def _():
                 remote(acc.at[k1, 0], from_x.at[k1], x_send, x_recv.at[k1], cross).start()
 
-            @pl.when((k1 == total - 1) & (section == 0))
-            def _():
-                for m in range(seqs):
-                    row_copy(m).start()
-
-            for span, way, place, ahead, behind in sides:
+            for number, sources in enumerate(row_sources):
+                @pl.when((k1 == total - 1) & (section == number))
+                def _(sources=sources):
+                    for m in range(len(sources)):
+                        row_copy(sources, m).start()
+
+            for rows_, way, place, ahead, behind in sides:
                 k3 = k2 - CHAIN_LAG * place
 
                 @pl.when(valid(k3) & (place < last))
-                def _(span=span, way=way, k3=k3, ahead=ahead):
-                    remote(acc.at[k3, 1, span], from_z.at[k3, span], z_send.at[way], z_recv.at[way, k3], ahead).start()
+                def _(rows_=rows_, way=way, k3=k3, ahead=ahead):
+                    remote(acc.at[k3, 1, rows_], from_z.at[k3, rows_], z_send.at[way], z_recv.at[way, k3], ahead).start()
 
                 k4 = k2 - CHAIN_LAG * (2 * last - place)
 
                 @pl.when(valid(k4) & (place > 0))
-                def _(span=span, way=way, k4=k4, behind=behind):
-                    remote(final.at[k4, span], final.at[k4, span], f_send.at[way], f_recv.at[way, k4], behind).start()
+                def _(rows_=rows_, way=way, k4=k4, behind=behind):
+                    remote(final.at[k4, rows_], final.at[k4, rows_], f_send.at[way], f_recv.at[way, k4], behind).start()
 
             k5 = k2 - CHAIN_LAG * 2 * last
 
             @pl.when(valid(k5))
             def _():
                 def visit(m, j):
-                    dst = outs[homes[m][0]].at[
-                        homes[m][1], pl.ds(pl.multiple_of(c * half, half), half), pl.ds(pl.multiple_of(j * bt, bt), bt)
-                    ]
-                    pltpu.make_async_copy(final.at[k5], dst, store_sem).start()
+                    dst = outs[group_of[m]].at[member_of[m], block(c, half), block(j, bt)]
+                    copy(final.at[k5], dst, store_sem).start()
                     remote(final.at[k5], dst, out_send, out_recv, core).start()
 
                 member(k5, visit)
 
-            @pl.when(s == 4)
+            @pl.when(turn == end_at + 1)
+            def _():
+                vec_core.start()
+
+            @pl.when(turn == end_at + 6)
             def _():
                 vec_core.wait_recv()
                 vec[1] = vec[0] + vec_in[0]
 
-            @pl.when(s == 5)
+            @pl.when(turn == end_at + 7)
             def _():
                 vec_cross.start()
 
-            @pl.when(s == 10)
+            @pl.when(turn == end_at + 13)
             def _():
                 vec_cross.wait_recv()
                 vec_all[z] = vec[1] + vec_in[1]
 
-            @pl.when(s == 11)
+            @pl.when(turn == end_at + 14)
             def _():
                 for shift in range(1, chips):
                     to = lax.rem(z + shift, chips)
@@ -1101,11 +1390,11 @@
                         vec_all.at[z], vec_all.at[z], v_send.at[1 + shift], v_recv.at[1 + shift], {"dp": to * 2 + c}
                     ).start()
 
-
-        @pl.when(section == 0)
-        def _():
-            for m in range(seqs):
-                row_copy(m).wait()
+        for number, sources in enumerate(row_sources):
+            @pl.when(section == number)
+            def _(sources=sources):
+                for m in range(len(sources)):
+                    row_copy(sources, m).wait()
 
         vec_core.wait_send()
         vec_cross.wait_send()
@@ -1120,83 +1409,96 @@
         for at in range(gives):
             arrived(give.at[at], give_send.at[at])
         arrived(acc.at[:, 0], x_send)
-        for span, way, place, ahead, behind in sides:
+        for rows_, way, place, ahead, behind in sides:
             @pl.when(place < last)
-            def _(span=span, way=way):
-                arrived(from_z.at[:, span], z_send.at[way])
+            def _(rows_=rows_, way=way):
+                arrived(from_z.at[:, rows_], z_send.at[way])
 
             @pl.when(place > 0)
-            def _(span=span, way=way):
-                arrived(final.at[:, span], f_send.at[way])
+            def _(rows_=rows_, way=way):
+                arrived(final.at[:, rows_], f_send.at[way])
 
         arrived(final, out_send)
         arrived(final, store_sem)
         arrived(final, out_recv)
 
     sem = pltpu.SemaphoreType.DMA
-    flops = 2 * seqs * rows * depth * 2 * bt * total
+    flops = 2 * seqs * rows * width * 2 * bt * total
+    members = [member_of[index] for index in range(7)]
+    shapes = [(sum(g == index for g in group_of), width, rights[group_of.index(index)].shape[2] // 2) for index in range(4)]
     return pl.pallas_call(
         kernel,
-        in_specs=[ANY] * n_in,
-        out_specs=[ANY] * n_left + [WHOLE, ANY],
-        out_shape=[jax.ShapeDtypeStruct((len(g[1]), depth, g[1][0].shape[2] // 2), BF) for g in groups]
-        + [jax.ShapeDtypeStruct(vec_shape, F32), jax.ShapeDtypeStruct((seqs, shard_rows, depth), BF)],
+        in_specs=[SMEM, SMEM, WHOLE] + [ANY] * (32 + 2 * seqs),
+        out_specs=[ANY] * 4 + [WHOLE] + [ANY] * 8,
+        out_shape=[jax.ShapeDtypeStruct(s, BF) for s in shapes]
+        + [jax.ShapeDtypeStruct(vec_shape, F32), jax.ShapeDtypeStruct((2 * seqs, shard_rows, width), BF)]
+        + [jax.ShapeDtypeStruct((rows, 2 * units), BF)] * 2
+        + [jax.ShapeDtypeStruct((rows, 2 * local), BF)] * 3
+        + [jax.ShapeDtypeStruct((rows, width), F32), jax.ShapeDtypeStruct((rows, width), BF)],
         scratch_shapes=[
             pltpu.VMEM((total, 2, half, bt), BF),
             pltpu.VMEM((total, half, bt), BF),
             pltpu.VMEM((total, half, bt), BF),
-            pltpu.VMEM((total, half, bt), BF),
-            pltpu.VMEM((depth, seqs * rows), BF),
-            pltpu.VMEM((seqs, rows, depth), BF),
-            pltpu.VMEM((tiles, seqs, rows, 2 * bt), BF),
+            pltpu.VMEM((2, width, seqs * rows), BF),
+            pltpu.VMEM((seqs, rows, width), BF),
+            pltpu.VMEM((ring, seqs, rows, 2 * bt), BF),
             pltpu.VMEM((mines, 2, half, bt), BF),
             pltpu.VMEM((gives, 2, half, bt), BF),
             pltpu.VMEM((2,) + vec_shape, F32),
             pltpu.VMEM((2,) + vec_shape, F32),
             pltpu.VMEM((chips,) + vec_shape, F32),
-            sem((tiles,)), sem, sem((gives,)), sem((total,)), sem, sem((total,)),
+            pltpu.VMEM((rows, width), BF),
+            pltpu.VMEM((rows, width), BF),
+            pltpu.VMEM((rows, 128), F32),
+            pltpu.VMEM((2, rows, width), BF),
+            pltpu.VMEM((rows, width), F32),
+            pltpu.VMEM((2, 3, width, CW), BF),
+            pltpu.VMEM((2, CW, width), BF),
+            pltpu.VMEM((2, 3, rows, CW), BF),
+            pltpu.VMEM((2, 3, rows, CW), BF),
+            pltpu.VMEM((2, 8, rows), F32),
+            pltpu.VMEM((rows, CW), BF),
+            pltpu.VMEM((rows, rows), F32),
+            pltpu.VMEM((8, width), F32),
+            pltpu.VMEM((2, 2 * units), F32),
+            pltpu.VMEM((2, 2 * local), F32),
+            sem((ring,)), sem((2,)), sem((gives,)), sem((total,)), sem, sem((total,)),
             sem((2,)), sem((2, total)), sem((2,)), sem((2, total)),
-            sem, sem, sem, sem, sem((chips + 1,)), sem((chips + 1,)), sem((seqs,)), sem((seqs,)),
+            sem, sem, sem, sem, sem((chips + 1,)), sem((chips + 1,)), sem((2 * seqs,)), sem((2 * seqs,)),
+            sem((3,)), sem((2, 6)), sem((2, 3)), sem((2,)),
         ],
         compiler_params=pltpu.CompilerParams(
-            collective_id=0, has_side_effects=True, vmem_limit_bytes=VMEM_LIMIT
+            collective_id=0, has_side_effects=True, vmem_limit_bytes=67_000_000
         ),
-        cost_estimate=pl.CostEstimate(flops=flops, bytes_accessed=64 << 20, transcendentals=0),
-        name="weight_grads_reduced",
-    )(*lefts, *rights, sums, *row_grads)
-
-
-def exchange_rows(outputs, grads, turn, earlier, deps):
+        cost_estimate=pl.CostEstimate(flops=flops, bytes_accessed=100 << 20, transcendentals=0),
+        name="backward_and_reduce",
+    )(
+        meta, slopes, vecs, grad, q, k_, v, lse, act, slope, u1, u2, r1, r2, *weights, *lefts, *rights, sums, low_grad, *second
+    )
+
+
+def exchange_rows(outputs, deps):
     seqs = len(outputs)
     rows, width = outputs[0].shape
     shard_rows = rows // 2
-    n_in = seqs + len(grads) + len(earlier) + len(deps)
-    n_out = 2 if grads else 1
+    n_in = seqs + len(deps)
 
     def kernel(*refs):
-        y_refs, grad_refs = refs[:seqs], refs[seqs : seqs + len(grads)]
-        out_ref = refs[n_in]
-        stage, send, recv, l_sem = refs[n_in + n_out :]
+        y_refs, out_ref = refs[:seqs], refs[n_in]
+        stage, send, recv, l_sem = refs[n_in + 1 :]
         t = lax.axis_index("tensor")
         cross = {"tensor": 1 - t}
-
-        def remote(src, dst, index):
-            return pltpu.make_async_remote_copy(
-                src_ref=src, dst_ref=dst, send_sem=send.at[index], recv_sem=recv.at[index],
-                device_id=cross, device_id_type=MESH,
-            )
-
         barrier = pltpu.get_barrier_semaphore()
         pl.semaphore_signal(barrier, inc=1, device_id=cross, device_id_type=MESH)
         pl.semaphore_wait(barrier, 1)
 
-        @pl.when(lax.axis_index("section") == turn)
+        @pl.when(lax.axis_index("section") == 0)
         def _():
-            sent = [remote(y_refs[m].at[block(1 - t, shard_rows)], out_ref.at[t * seqs + m], m) for m in range(seqs)]
-            for m, ref in enumerate(grad_refs):
-                sent.append(remote(ref.at[block(1 - t, shard_rows)], refs[n_in + 1].at[m], seqs + m))
-            for item in sent:
-                item.start()
+            for m in range(seqs):
+                pltpu.make_async_remote_copy(
+                    src_ref=y_refs[m].at[block(1 - t, shard_rows)], dst_ref=out_ref.at[t * seqs + m],
+                    send_sem=send.at[m], recv_sem=recv.at[m], device_id=cross, device_id_type=MESH,
+                ).start()
             for m in range(seqs):
                 copy(y_refs[m].at[block(t, shard_rows)], stage.at[m], l_sem.at[m]).start()
             for m in range(seqs):
@@ -1207,31 +1509,23 @@
             for m in range(seqs):
                 arrived(out_ref.at[(1 - t) * seqs + m], recv.at[m])
                 arrived(stage.at[m], send.at[m])
-            for item in sent[seqs:]:
-                item.wait()
 
     sem = pltpu.SemaphoreType.DMA
-    shapes = [
-        jax.ShapeDtypeStruct((2 * seqs, shard_rows, width), BF),
-        jax.ShapeDtypeStruct((seqs, shard_rows, width), BF),
-    ]
     return pl.pallas_call(
         kernel,
         in_specs=[ANY] * n_in,
-        out_specs=[ANY] * n_out,
-        out_shape=shapes[:n_out],
-        scratch_shapes=[
-            pltpu.VMEM((seqs, shard_rows, width), BF), sem((2 * seqs,)), sem((2 * seqs,)), sem((seqs,)),
-        ],
-        input_output_aliases={seqs + len(grads): 0} if earlier else {},
-        compiler_params=pltpu.CompilerParams(collective_id=2 + turn, has_side_effects=True),
+        out_specs=ANY,
+        out_shape=jax.ShapeDtypeStruct((2 * seqs, shard_rows, width), BF),
+        scratch_shapes=[pltpu.VMEM((seqs, shard_rows, width), BF), sem((seqs,)), sem((seqs,)), sem((seqs,))],
+        compiler_params=pltpu.CompilerParams(collective_id=2, has_side_effects=True),
         cost_estimate=pl.CostEstimate(flops=0, bytes_accessed=0, transcendentals=0),
         name="exchange_rows",
-    )(*outputs, *grads, *earlier, *deps)
-
-
-def widen(reduced, row_grads, gots, sums, units, local):
-    seqs, shard_rows, width = gots[0].shape
+    )(*outputs, *deps)
+
+
+def widen(reduced, row_grads, got, produced, outputs, sums, units, local):
+    shard_rows, width = got.shape[1:]
+    seqs = got.shape[0] // 2
     n = len(reduced)
     jobs = []
     for index, array in enumerate(reduced):
@@ -1242,19 +1536,20 @@
         else:
             jobs += [(index, part, at, step, columns) for part in range(lead) for at in range(0, depth, step)]
     jobs += [(n, m, 0, shard_rows, width) for m in range(seqs)] + [(n + 1, m, 0, shard_rows, width) for m in range(seqs)]
+    jobs += [(n + 2, m, 0, shard_rows, width) for m in range(2 * seqs)]
     ring = 3
-    n_in = n + 2 * seqs + 3
+    n_in = n + 3 * seqs + 3
     parts = units // width
 
     def kernel(*refs):
         ins = refs[:n]
         grad_refs = refs[n : n + 2 * seqs]
-        got_refs = refs[n + 2 * seqs : n + 2 * seqs + 2]
-        sums_ref = refs[n + 2 * seqs + 2]
-        outs = refs[n_in : n_in + n + 1]
-        qv_ref, out_bias_ref, gain_ref, shift_ref, ub_ref, down_bias_ref = refs[n_in + n + 1 : n_in + n + 7]
+        got_ref, produced_ref = refs[n + 2 * seqs : n + 2 * seqs + 2]
+        y_refs, sums_ref = refs[n + 2 * seqs + 2 : n_in - 1], refs[n_in - 1]
+        outs = refs[n_in : n_in + n + 2]
+        qv_ref, out_bias_ref, gain_ref, shift_ref, ub_ref, down_bias_ref = refs[n_in + n + 2 : n_in + n + 8]
         shapes = sorted({(j[3], j[4]) for j in jobs if j[0] != n})
-        buffers = refs[n_in + n + 7 :]
+        buffers = refs[n_in + n + 8 :]
         wide_rows, in_sem, out_sem = buffers[0], buffers[1], buffers[2]
         low = {s: buffers[3 + 2 * i] for i, s in enumerate(shapes)}
         wide = {s: buffers[4 + 2 * i] for i, s in enumerate(shapes)}
@@ -1272,11 +1567,17 @@
                     def _(turn=turn):
                         source = grad_refs[turn * seqs + part].at[block(t, shard_rows)]
                         copy(source, wide_rows.at[part], in_sem.at[s]).start()
+            elif index == n + 1:
+                copy(got_ref.at[part], low[rows, columns].at[s], in_sem.at[s]).start()
             else:
-                for turn in range(2):
-                    @pl.when(section == turn)
-                    def _(turn=turn):
-                        copy(got_refs[turn].at[part], low[rows, columns].at[s], in_sem.at[s]).start()
+                @pl.when(section == 0)
+                def _():
+                    copy(produced_ref.at[part], low[rows, columns].at[s], in_sem.at[s]).start()
+
+                @pl.when(section == 1)
+                def _():
+                    source = y_refs[part].at[block(t, shard_rows)] if part < seqs else got_ref.at[part]
+                    copy(source, low[rows, columns].at[s], in_sem.at[s]).start()
 
         def store(number):
             index, part, at, rows, columns = jobs[number]
@@ -1287,7 +1588,11 @@
                 return copy(wide[rows, columns].at[s], outs[index].at[:, pl.ds(at, rows)], out_sem.at[s])
             if index == n:
                 return copy(wide_rows.at[part], outs[n].at[t * seqs + part], out_sem.at[s])
-            return copy(wide[rows, columns].at[s], outs[n].at[(1 - t) * seqs + part], out_sem.at[s])
+            if index == n + 1:
+                return copy(wide[rows, columns].at[s], outs[n].at[(1 - t) * seqs + part], out_sem.at[s])
+            side, m = divmod(part, seqs)
+            spread = (t + side - 2 * t * side) * seqs + m
+            return copy(low[rows, columns].at[s], outs[n + 1].at[jnp.where(section == 0, part, spread)], out_sem.at[s])
 
         for number in range(ring):
             load(number)
@@ -1313,17 +1618,20 @@
                 arrived(wide_rows.at[part], in_sem.at[s])
             else:
                 arrived(low[rows, columns].at[s], in_sem.at[s])
-            if number >= ring:
+            if number >= ring and jobs[number - ring][0] != n + 2:
                 store(number - ring).wait()
             if index == n - 1:
                 wide[rows, columns][s] = low[rows, columns][s].astype(F32).T
-            elif index != n:
+            elif index not in (n, n + 2):
                 wide[rows, columns][s] = low[rows, columns][s].astype(F32)
             store(number).start()
+            if index == n + 2:
+                store(number).wait()
             if number + ring < len(jobs):
                 load(number + ring)
         for number in range(len(jobs) - ring, len(jobs)):
-            store(number).wait()
+            if jobs[number][0] != n + 2:
+                store(number).wait()
 
     shapes = sorted({(j[3], j[4]) for j in jobs if j[0] != n})
     square = (reduced[-1].shape[1] // 2, reduced[-1].shape[2])
@@ -1334,10 +1642,11 @@
         buffers += [pltpu.VMEM((ring,) + s, BF), pltpu.VMEM((ring,) + ((s[1], s[0]) if s == square else s), F32)]
     return pl.pallas_call(
         kernel,
-        in_specs=[ANY] * (n + 2 * seqs + 2) + [WHOLE],
-        out_specs=[ANY] * (n + 1) + [WHOLE] * 6,
+        in_specs=[ANY] * (n_in - 1) + [WHOLE],
+        out_specs=[ANY] * (n + 2) + [WHOLE] * 6,
         out_shape=[jax.ShapeDtypeStruct(r.shape, F32) for r in reduced[:-1]]
         + [jax.ShapeDtypeStruct((last[2], last[1]), F32), jax.ShapeDtypeStruct((2 * seqs, shard_rows, width), F32)]
+        + [jax.ShapeDtypeStruct((2 * seqs, shard_rows, width), BF)]
         + [
             jax.ShapeDtypeStruct(shape, F32)
             for shape in ((2, local), (1, width), (2, width), (2, width), (2, units), (1, width))
@@ -1346,7 +1655,7 @@
         compiler_params=pltpu.CompilerParams(vmem_limit_bytes=VMEM_LIMIT),
         cost_estimate=pl.CostEstimate(flops=0, bytes_accessed=56 << 20, transcendentals=0),
         name="widen",
-    )(*reduced, *row_grads, *gots, sums)
+    )(*reduced, *row_grads, got, produced, *outputs, sums)
 
 
 MASKED = -1000000000.0
@@ -1829,7 +2138,7 @@
     y_first = [y] + [forward(x_first[m], m, 0) for m in range(1, seqs)]
     x_second = [lax.ppermute(y, "section", [(0, 1)]) for y in y_first]
     y_second = [forward(x_second[0], 0, 1)]
-    (produced,) = exchange_rows(y_first, [], 0, [], deps)
+    produced = exchange_rows(y_first, deps)
     deps = [produced]
     y_second += [forward(x_second[m], m, 1) for m in range(1, seqs)]
 
@@ -1849,17 +2158,11 @@
     grad_middle = [lax.ppermute(gx_second[m][1], "section", [(1, 0)]) for m in range(seqs)]
     x_all = jnp.stack([jnp.where(first, x_first[m], x_second[m]) for m in range(seqs)])
     deps = deps + [x_all]
-    gx_first = [backward(grad_middle[m], m, 0) for m in range(seqs)]
-    produced, got_second = exchange_rows(y_second, [g[1] for g in gx_second], 1, [produced], deps)
-
-    mixed, hidden, normed = kept[3], kept[7], kept[8]
-    gg0, gg1, gl, ga, *gqkv = back
-
-    picked = [
-        sum(jnp.where(first, sums[0][m][index], sums[1][m][index]) for m in range(seqs))
-        for index in range(3)
+    gx_first = [backward(grad_middle[0], 0, 0)]
+
+    norm_sums, up_sums, qv_sums = [
+        jnp.where(first, sums[0][0][index], sum(item[index] for item in sums[1])) for index in range(3)
     ]
-    norm_sums, up_sums, qv_sums = picked
 
     def ordered(values, count):
         return jnp.where(
@@ -1867,12 +2170,15 @@
         ).reshape(-1, width)
 
     packed = jnp.concatenate([norm_sums[:6], ordered(up_sums[:2], units), ordered(qv_sums[:2], local)])
-    *reduced, packed, got_first = weight_grads_reduced(
-        [(gl, [hidden]), (normed, [gg0, gg1]), (x_all, gqkv), (ga, [mixed])], packed, [g[1] for g in gx_first], chips
+    *reduced, packed, got, _, _, _, _, _, gx, _ = backward_and_reduce(
+        grad_middle[1], kept, back, x_all, weights, slopes, vecs, metas[0][1], packed, gx_first[0][1],
+        [g[1] for g in gx_second] + y_second, chips,
     )
-    down_sum, up_sum, qkv_sum, out_sum, grads_in, qv_sum, out_bias_sum, gain_sum, shift_sum, up_bias_sum, down_bias_sum = (
-        widen(reduced, [g[0] for g in gx_first + gx_second], [got_first, got_second], packed, units, local)
-    )
+    gx_all = [gx_first[0][0], gx] + [g[0] for g in gx_second]
+    (
+        down_sum, up_sum, qkv_sum, out_sum, grads_in, produced,
+        qv_sum, out_bias_sum, gain_sum, shift_sum, up_bias_sum, down_bias_sum,
+    ) = widen(reduced, gx_all, got, produced, y_second, packed, units, local)
     return (
         produced[None],
         grads_in[None],

time: 687 us -> 673 us (0.980)
  Pallas kernels: 565 us -> 555 us
    pallas_call x7 -> x6, Pallas kernels: 149 us -> 102 us  [call(): pl.pallas_call(body, in_specs=specs, out_specs=[ANY] * n_out, out_shape=[...]
    pallas_call x4 -> x3, Pallas kernels: 273 us -> 310 us  [the longest x1 262 us: backward_and_reduce(): pl.pallas_call(kernel, in_specs=[SMEM, SMEM, WHOLE] + [ANY] * (32 + 2 * s...]
  transfers between devices with their start and end apart: 4 -> 4, of which waited for: 2 -> 2; matrix products, arithmetic and copies ran while one was open for 1% -> 1% of each run, Pallas kernels for 17% -> 18%
where the time goes in v9:
time: 673 us; the launch traced here: 664 us
  Pallas kernels  555 us (82%)
  waiting for transfers between devices  85.8 us (13%)
  other arithmetic  10.9 us (2%)
    pallas_call x1, Pallas kernels, backward_and_reduce(): pl.pallas_call(kernel, in_specs=[SMEM, SMEM, WHOLE] + [ANY] * (32 + 2 * s...  262 us
    pallas_call x1, Pallas kernels, fetch_and_forward(): pl.pallas_call(kernel, in_specs=[SMEM, SMEM, WHOLE] + [ANY] * 8, out_spec...  144 us
    pallas_call x6, Pallas kernels, call(): pl.pallas_call(body, in_specs=specs, out_specs=[ANY] * n_out, out_shape=[...  102 us
    ppermute x2, waiting for transfers between devices, by_sequence(): lax.ppermute(gx_second[m][1], 'section', [(1, 0)])  85.8 us
    pallas_call x1, Pallas kernels, exchange_rows(): pl.pallas_call(kernel, in_specs=[ANY] * n_in, out_specs=ANY, out_shape=ja...  24.2 us
    pallas_call x1, Pallas kernels, widen(): pl.pallas_call(kernel, in_specs=[ANY] * (n_in - 1) + [WHOLE], out_specs=[...  24.2 us
  transfers between devices with their start and end apart: 4, of which 2 were waited for; matrix products, arithmetic and copies ran while one was open for 1% of the time, Pallas kernels for 18%

profile of v9, /device:TPU:0, one launch (start us, length us, event | category | flops | bytes accessed | tf_op | source)
XLA Modules:
  0.0 663.8 jit_solution(3839150905660612034)
XLA Ops:
  0.7 0.7 dynamic_slice.3
  1.4 0.6 fusion.8
  2.0 0.8 slice_bitcast_fusion
  2.8 0.9 stack.41
  3.6 0.6 convert_element_type.2.refs_2_.refs_12_.refs_21_
  4.2 1.2 broadcast_select_fusion.refs_1_.refs_11_.refs_20_
  5.4 1.2 pad_add_fusion.refs_0_
  6.6 143.6 %fetch_and_forward.1 = (bf16[3,1024,512]{2,1,0:T(8,128)(2,1)}, bf16[512,1024]{1,0:T(8,128)(2,1)}, bf16[2,1024,2048]{2,1,0:T(8,128)(2,1)}, bf16[1024,2048]{1,0:T(...) custom-call(s32[4]{0:T(128)} %pad_add_fusion.refs_0_, ...), custom_call_target="tpu_custom_call" | custom-call | flops 18253611008 | bytes 94371840 | tf_op jit(solution)/shard_map/fetch_and_forward/pallas_call | solution.py:865
  150.2 1.4 collective-permute-start.1
  151.6 1.3 pad_add_fusion.1.refs_0_
  152.9 38.5 %layer_forward.3 = (bf16[2,512,1024]{2,1,0:T(8,128)(2,1)}, bf16[2,512,1024]{2,1,0:T(8,128)(2,1)}, bf16[2,512,1024]{2,1,0:T(8,128)(2,1)}, bf16[2,512,1024]{2,1,0:...) custom-call(s32[4]{0:T(128)} %pad_add_fusion.1.refs_0_, ...), custom_call_target="tpu_custom_call", output_to_operand_aliasing={{0}: (14, {}), {1}: (15, {}), {2}: (16, {}), {3}: (17, {}),... | custom-call | flops 18253611008 | bytes 56623104 | tf_op jit(solution)/shard_map/layer_forward/pallas_call | solution.py:55
  191.4 2.3 collective-permute-start
  193.7 1.9 fusion.2
  195.6 0.0 collective-permute-done.1.refs_1_
  195.6 0.0 copy-start.1
  195.6 1.1 copy-done.1
  196.7 1.3 layer_forward.4
  198.0 24.2 %exchange_rows.1.refs_27_.refs_9_ = bf16[4,256,1024]{2,1,0:T(8,128)(2,1)} custom-call(bf16[512,1024]{1,0:T(8,128)(2,1)} %get-tuple-element.151.refs_27_.refs_0_, bf16[512,1024]{1,0:T(8,128)(2,1)} %get-tuple-element.152.refs_27_.refs_1_, bf16[512,1024]{1,0:T(8,128)(2,1)} %get-tuple-element.179.refs_2_.refs_37_.refs_10_), custom_call_target="tpu_custom_call" | custom-call | tf_op jit(solution)/shard_map/exchange_rows/pallas_call | solution.py:1514
  222.2 0.0 collective-permute-done.refs_1_
  222.2 1.4 layer_forward.5
  223.6 7.1 %layer_backward.3 = (bf16[2,512,4096]{2,1,0:T(8,128)(2,1)}, bf16[2,512,4096]{2,1,0:T(8,128)(2,1)}, bf16[2,512,1024]{2,1,0:T(8,128)(2,1)}, bf16[2,512,1024]{2,1,0...) custom-call(s32[4]{0:T(128)} %get-tuple-element.260.refs_0_, ...), custom_call_target="tpu_custom_call" | custom-call | flops 19864223744 | bytes 73400320 | tf_op jit(solution)/shard_map/layer_backward/pallas_call | solution.py:55
  230.7 1.3 collective-permute-start.3
  232.0 0.0 copy-start
  232.1 5.7 layer_backward.4
  237.8 0.0 copy-start.2
  237.8 0.0 copy-start.3
  237.8 1.4 collective-permute-start.2
  239.2 0.0 copy-done
  239.3 0.1 select_bitcast_fusion
  239.4 0.0 copy-done.2
  239.4 0.0 copy-done.3
  239.4 0.1 select_bitcast_fusion.1
  239.5 1.5 pad_maximum_fusion.refs_30_.refs_24_
  241.1 85.4 %collective-permute-done.3.refs_1_ = bf16[512,1024]{1,0:T(8,128)(2,1)} collective-permute-done((bf16[512,1024]{1,0:T(8,128)(2,1)}, bf16[512,1024]{1,0:T(8,128)(2,1)}, u32[]{:S(2)}, u32[]{:S(2)}) %collective-permute-start.3) | collective-permute-done | bytes 1048608 | tf_op jit(solution)/shard_map/ppermute | solution.py:2158
  326.4 0.0 copy-start.6
  326.4 0.0 copy-start.7
  326.4 0.0 copy-start.8
  326.4 0.0 copy-start.9
  326.4 0.0 copy-start.4
  326.4 0.0 copy-start.5
  326.5 47.4 %layer_backward.5 = (bf16[2,512,4096]{2,1,0:T(8,128)(2,1)}, bf16[2,512,4096]{2,1,0:T(8,128)(2,1)}, bf16[2,512,1024]{2,1,0:T(8,128)(2,1)}, bf16[2,512,1024]{2,1,0...) custom-call(s32[4]{0:T(128)} %pad_add_fusion.refs_0_, ...), custom_call_target="tpu_custom_call", output_to_operand_aliasing={{0}: (22, {}), {1}: (23, {}), {2}: (24, {}), {3}: (25, {}),... | custom-call | flops 19864223744 | bytes 73400320 | tf_op jit(solution)/shard_map/layer_backward/pallas_call | solution.py:55
  373.9 0.0 copy-done.6
  373.9 0.0 copy-done.7
  373.9 0.8 add_select_fusion
  374.8 0.0 copy-done.8
  374.8 0.0 copy-done.9
  374.8 0.7 add_select_fusion.1
  375.5 0.0 copy-done.4
  375.6 0.0 copy-done.5
  375.6 0.8 slice_select_fusion
  376.3 0.6 pad_maximum_fusion.1.refs_33_
  377.0 0.4 collective-permute-done.2.refs_3_
  377.4 261.8 %backward_and_reduce.1 = (bf16[1,1024,2048]{2,1,0:T(8,128)(2,1)}, bf16[2,1024,2048]{2,1,0:T(8,128)(2,1)}, bf16[3,1024,512]{2,1,0:T(8,128)(2,1)}, bf16[1,1024,512...) custom-call(s32[4]{0:T(128)} %pad_add_fusion.1.refs_0_, ...), custom_call_target="tpu_custom_call" | custom-call | flops 34359738368 | bytes 104857600 | tf_op jit(solution)/shard_map/backward_and_reduce/pallas_call | solution.py:1429
  639.1 24.2 %widen.1 = (f32[1,1024,2048]{2,1,0:T(8,128)}, f32[2,1024,2048]{2,1,0:T(8,128)}, f32[3,1024,512]{2,1,0:T(8,128)}, f32[512,1024]{1,0:T(8,128)}, f32[4,256,1024]{2,...) custom-call(bf16[1,1024,2048]{2,1,0:T(8,128)(2,1)} %get-tuple-elemen, ...), custom_call_target="tpu_custom_call" | custom-call | bytes 58720256 | tf_op jit(solution)/shard_map/widen/pallas_call | solution.py:1643
  (5 shorter events, 0.1 us)
Async XLA Ops:
  150.2 45.4 %collective-permute-start.1 = (bf16[512,1024]{1,0:T(8,128)(2,1)}, bf16[512,1024]{1,0:T(8,128)(2,1)S(1)}, u32[]{:S(2)}, u32[]{:S(2)}) collective-permute-start(bf16[512,1024]{1,0:T(8,128)(2,1)} %get-tuple-element.151.refs_27_.refs_0_), channel_id=1, source_target_pairs={{0,16},{1,17},{2,18},{3,19},{4,20},{5,21},{6,22},{7,23},{8,24},{9,... | collective-permute-start | bytes 3145736 | tf_op jit(solution)/shard_map/ppermute | solution.py:2139
  191.4 30.8 %collective-permute-start = (bf16[512,1024]{1,0:T(8,128)(2,1)}, bf16[512,1024]{1,0:T(8,128)(2,1)}, u32[]{:S(2)}, u32[]{:S(2)}) collective-permute-start(bf16[512,1024]{1,0:T(8,128)(2,1)} %get-tuple-element.152.refs_27_.refs_1_), channel_id=1, source_target_pairs={{0,16},{1,17},{2,18},{3,19},{4,20},{5,21},{6,22},{7,23},{8,24},{9,... | collective-permute-start | bytes 3145736 | tf_op jit(solution)/shard_map/ppermute | solution.py:2139
  195.6 1.1 copy-start.1
  230.7 95.7 %collective-permute-start.3 = (bf16[512,1024]{1,0:T(8,128)(2,1)}, bf16[512,1024]{1,0:T(8,128)(2,1)}, u32[]{:S(2)}, u32[]{:S(2)}) collective-permute-start(bf16[512,1024]{1,0:T(8,128)(2,1)} %get-tuple-element.201.refs_35_), channel_id=1, source_target_pairs={{16,0},{17,1},{18,2},{19,3},{20,4},{21,5},{22,6},{23,7},{24,8},{25... | collective-permute-start | bytes 3145736 | tf_op jit(solution)/shard_map/ppermute | solution.py:2158
  232.0 7.2 %copy-start = (bf16[512,1024]{1,0:T(8,128)(2,1)S(1)}, bf16[512,1024]{1,0:T(8,128)(2,1)}, u32[]{:S(2)}) copy-start(bf16[512,1024]{1,0:T(8,128)(2,1)} %get-tuple-element.131.refs_1_) | copy-start | bytes 3145732
  237.8 1.6 copy-start.2
  237.8 1.6 copy-start.3
  237.8 139.6 %collective-permute-start.2 = (bf16[512,1024]{1,0:T(8,128)(2,1)}, bf16[512,1024]{1,0:T(8,128)(2,1)}, u32[]{:S(2)}, u32[]{:S(2)}) collective-permute-start(bf16[512,1024]{1,0:T(8,128)(2,1)} %get-tuple-element.200.refs_36_), channel_id=1, source_target_pairs={{16,0},{17,1},{18,2},{19,3},{20,4},{21,5},{22,6},{23,7},{24,8},{25... | collective-permute-start | bytes 3145736 | tf_op jit(solution)/shard_map/ppermute | solution.py:2158
  326.4 47.5 %copy-start.6 = (f32[2,4096]{1,0:T(2,128)S(1)}, f32[2,4096]{1,0:T(2,128)}, u32[]{:S(2)}) copy-start(f32[2,4096]{1,0:T(2,128)} %get-tuple-element.222) | copy-start | bytes 98308
  326.4 47.5 %copy-start.7 = (f32[2,4096]{1,0:T(2,128)S(1)}, f32[2,4096]{1,0:T(2,128)}, u32[]{:S(2)}) copy-start(f32[2,4096]{1,0:T(2,128)} %get-tuple-element.223) | copy-start | bytes 98308
  326.4 48.4 %copy-start.8 = (f32[2,1024]{1,0:T(2,128)S(1)}, f32[2,1024]{1,0:T(2,128)}, u32[]{:S(2)}) copy-start(f32[2,1024]{1,0:T(2,128)} %get-tuple-element.225) | copy-start | bytes 24580
  326.4 48.4 %copy-start.9 = (f32[2,1024]{1,0:T(2,128)S(1)}, f32[2,1024]{1,0:T(2,128)}, u32[]{:S(2)}) copy-start(f32[2,1024]{1,0:T(2,128)} %get-tuple-element.226) | copy-start | bytes 24580
  326.4 49.1 %copy-start.4 = (f32[8,1024]{1,0:T(8,128)S(1)}, f32[8,1024]{1,0:T(8,128)}, u32[]{:S(2)}) copy-start(f32[8,1024]{1,0:T(8,128)} %get-tuple-element.199.refs_29_) | copy-start | bytes 98308
  326.4 49.1 %copy-start.5 = (f32[8,1024]{1,0:T(8,128)S(1)}, f32[8,1024]{1,0:T(8,128)}, u32[]{:S(2)}) copy-start(f32[8,1024]{1,0:T(8,128)} %get-tuple-element.209.refs_29_) | copy-start | bytes 98308

commit v10 on v9

--- a/solution.py
+++ b/solution.py
@@ -32,7 +32,7 @@
     pltpu.make_async_copy(ref, ref, sem).wait()
 
 
-def call(kernel, inputs, outputs, scratch, meta, chain, deps, name, flops, nbytes):
+def call(kernel, inputs, outputs, scratch, meta, chain, deps, name, flops, nbytes, turn=None):
     pairs = [item if isinstance(item, tuple) else (item, ANY) for item in inputs]
     args = [meta] + [p[0] for p in pairs]
     specs = [SMEM] + [p[1] for p in pairs]
@@ -48,7 +48,7 @@
     n_args, n_out = len(args), len(outputs)
 
     def body(*refs):
-        @pl.when(refs[0][1] == 1)
+        @pl.when(refs[0][1] == 1 if turn is None else lax.axis_index("section") == turn)
         def _():
             kernel(refs[0], refs[1:n_in], refs[n_args : n_args + n_out], refs[n_args + n_out :])
 
@@ -59,7 +59,9 @@
         out_shape=[jax.ShapeDtypeStruct(o[0], o[1]) for o in outputs],
         scratch_shapes=scratch,
         input_output_aliases=aliases,
-        compiler_params=pltpu.CompilerParams(vmem_limit_bytes=VMEM_LIMIT),
+        compiler_params=pltpu.CompilerParams(vmem_limit_bytes=VMEM_LIMIT)
+        if turn is None
+        else pltpu.CompilerParams(vmem_limit_bytes=VMEM_LIMIT, collective_id=3, has_side_effects=True),
         cost_estimate=pl.CostEstimate(flops=flops, bytes_accessed=nbytes, transcendentals=0),
         name=name,
     )(*args)
@@ -333,7 +335,7 @@
     )
 
 
-def layer_backward(grad, kept, weights, slopes, vecs, meta, chain, deps, slots):
+def layer_backward(grad, kept, weights, slopes, vecs, meta, chain, deps, slots, slot=None, turn=None, sent=()):
     qkv_own, qkv_oth, o_own, o_oth, up_own, up_oth, down_own, down_oth = weights
     q, k, v, _, lse, act, slope, _, _, u1, u2, r1, r2 = kept
     rows, width = grad.shape
@@ -343,6 +345,7 @@
     ft = min(512, units)
     tiles = units // ft
     total = 2 * local
+    static_slot = slot
 
     def norm_back(grad_z, u, rstd, gain):
         t = grad_z * gain
@@ -354,12 +357,28 @@
     def kernel(meta_ref, ins, outs, scratch):
         (g_hbm, q_hbm, k_hbm, v_hbm, lse_hbm, a_hbm, b_hbm, u1_hbm, u2_hbm, r1_hbm, r2_hbm,
          qkv_own_ref, qkv_oth_ref, o_own_ref, o_oth_ref, up_own_ref, up_oth_ref, down_own_ref, down_oth_ref,
-         slope_ref, vec_ref) = ins
-        gg0_out, gg1_out, gl_out, ga_out, gq_out, gk_out, gv_out, gx_out, gxl_out, sums_out, ub_out, qv_out = outs
+         slope_ref, vec_ref) = ins[:21]
+        gg0_out, gg1_out, gl_out, ga_out, gq_out, gk_out, gv_out, gx_out, gxl_out, sums_out, ub_out, qv_out = outs[:12]
         (g_ref, u_ref, r_ref, up_ref, down_ref, ab_ref, gg_ref, low_ref, acc_ref, sums_ref, ub_ref, qv_ref,
          w_ref, o_ref, qkv_ref, lse_ref, gm_ref, dist_ref, gqkv_ref,
-         g_sem, f_sem, t_sem, w_sem, q_sem, r_sem) = scratch
-        slot = meta_ref[0]
+         g_sem, f_sem, t_sem, w_sem, q_sem, r_sem, x_send, x_recv) = scratch
+        slot = meta_ref[0] if static_slot is None else static_slot
+        travelling = []
+        if sent:
+            t = lax.axis_index("tensor")
+            cross = {"tensor": 1 - t}
+            barrier = pltpu.get_barrier_semaphore()
+            pl.semaphore_signal(barrier, inc=1, device_id=cross, device_id_type=pl.DeviceIdType.MESH)
+            pl.semaphore_wait(barrier, 1)
+            for index in range(len(sent)):
+                travelling.append(
+                    pltpu.make_async_remote_copy(
+                        src_ref=ins[21 + index].at[block(1 - t, rows // 2)], dst_ref=outs[12].at[index],
+                        send_sem=x_send.at[index], recv_sem=x_recv.at[index],
+                        device_id=cross, device_id_type=pl.DeviceIdType.MESH,
+                    )
+                )
+                travelling[-1].start()
 
         def start_f(i):
             s = lax.rem(i, 2)
@@ -515,11 +534,13 @@
         for i in (2 * heads_steps - 2, 2 * heads_steps - 1):
             for item in write_heads(jnp.int32(i), i % 2):
                 item.wait()
+        for item in travelling:
+            item.wait()
 
     sem = pltpu.SemaphoreType.DMA
     return call(
         kernel,
-        [grad, q, k, v, lse, act, slope, u1, u2, r1, r2, *weights, (slopes, SMEM), (vecs, WHOLE)],
+        [grad, q, k, v, lse, act, slope, u1, u2, r1, r2, *weights, (slopes, SMEM), (vecs, WHOLE), *sent],
         [((slots, rows, 2 * units), BF, True)] * 2
         + [((slots, rows, width), BF, True)] * 2
         + [((slots, rows, total), BF, True)] * 3
@@ -529,7 +550,8 @@
             ((8, width), F32, False),
             ((2, 2 * units), F32, False),
             ((2, total), F32, False),
-        ],
+        ]
+        + ([((len(sent), rows // 2, width), BF, False)] if sent else []),
         [
             pltpu.VMEM((rows, width), BF),
             pltpu.VMEM((2, rows, width), BF),
@@ -550,7 +572,7 @@
             pltpu.VMEM((rows, CW), BF),
             pltpu.VMEM((rows, rows), F32),
             pltpu.VMEM((2, 3, rows, CW), BF),
-            sem((5,)), sem((2, 4)), sem((2, 2)), sem((2, 6)), sem((2, 3)), sem((7,)),
+            sem((5,)), sem((2, 4)), sem((2, 2)), sem((2, 6)), sem((2, 3)), sem((7,)), sem((4,)), sem((4,)),
         ],
         meta,
         chain,
@@ -558,6 +580,7 @@
         "layer_backward",
         2 * rows * width * (4 * total + 6 * units) + 10 * rows * rows * total,
         70 << 20,
+        turn,
     )
 
 
@@ -920,7 +943,7 @@
     shard_rows = rows // 2
     norm_at = 2 * tiles
     head_at = norm_at + 1
-    end_at = head_at + 4 * heads_steps
+    end_at = head_at + 5 * 2 * heads_steps
     x_flip, ga_flip = ffn_blocks - per_pair, ffn_blocks + per_pair
     up_rows = units // width
     assert ahead_of + ffn_blocks - ring > end_at
@@ -930,24 +953,24 @@
         g_hbm, q_hbm, k_hbm, v_hbm, lse_hbm, a_hbm, b_hbm, u1_hbm, u2_hbm, r1_hbm, r2_hbm = refs[3:14]
         (qkv_own_ref, qkv_oth_ref, o_own_ref, o_oth_ref, up_own_ref, up_oth_ref, down_own_ref, down_oth_ref) = refs[14:22]
         left_refs, right_refs = refs[22:26], refs[26:33]
-        sums_ref, low_grad_ref, second_refs = refs[33], refs[34], refs[35 : 35 + 2 * seqs]
-        outs, sums_out, rows_out = refs[39:43], refs[43], refs[44]
-        fresh = refs[45:50]
-        gx_out, gxl_out = refs[50:52]
+        sums_ref, low_grad_ref, second_ref = refs[33:36]
+        outs, sums_out, rows_out = refs[36:40], refs[40], refs[41]
+        fresh = refs[42:47]
+        gx_out, gxl_out = refs[47:49]
         (
             acc, from_x, from_z, flip, stage, tile, mine, give, vec, vec_in, vec_all,
-            g_ref, u_ref, r_ref, low_ref, gacc_ref, w_ref, o_ref, qkv_ref, gqkv_ref, lse_ref, gm_ref, dist_ref,
+            g_ref, u_ref, r_ref, low_ref, gacc_ref, w_ref, o_ref, qkv_ref, gqkv_ref, lse_ref, gm_ref, gs_ref, dist_ref,
             part_sums, ub_sums, qv_sums,
             tile_sem, stage_sem, give_send, core_recv, x_send, x_recv, z_send, z_recv, f_send, f_recv,
             store_sem, out_send, out_recv, v_load, v_send, v_recv, r_send, r_recv,
             g_sem, w_sem, t_sem, e_sem,
-        ) = refs[52:]
+        ) = refs[49:]
         final = from_x
         t, c, z, last, core, cross, above, below = neighbours()
         section = lax.axis_index("section")
         first = section == 0
         greet(c, z, chips, core, cross)
-        fresh_of = {1: fresh[0], 2: fresh[1], 3: fresh[2], 4: fresh[3], 5: fresh[4]}
+        fresh_of = {1: fresh[0].at[0], 2: fresh[1].at[0], 3: fresh[2], 4: fresh[3], 5: fresh[4]}
         vec_w = vec_ref[...]
 
         def remote(src, dst, send, recv, device):
@@ -1030,7 +1053,7 @@
         def write_tile(u):
             at = lax.rem(u, 2)
             side, j = place_of(u)
-            return [copy(gqkv_ref.at[at, n], fresh[n].at[:, block(side * tiles + j, ft)], t_sem.at[at, n]) for n in range(2)]
+            return [copy(gqkv_ref.at[at, n], fresh[n].at[0, :, block(side * tiles + j, ft)], t_sem.at[at, n]) for n in range(2)]
 
         def start_w(i):
             at = lax.rem(i, 2)
@@ -1106,6 +1129,7 @@
                 item.wait()
             for i in range(2):
                 start_w(jnp.int32(i))
+            fill_distance(dist_ref, meta_ref[2])
             for item in norm_load(1, u1_hbm, r1_hbm):
                 item.wait()
             totals = [jnp.zeros((1, width), F32)] * 3
@@ -1121,12 +1145,14 @@
                 part_sums[3 + index : 4 + index, :] = totals[index]
 
         def head_unit(a):
-            i = a // 2
-            pair = lax.rem(a, 2)
+            i = a // 5
+            phase = lax.rem(a, 5)
+            pair = phase // 2
             at = lax.rem(i, 2)
             scale = BF(1.0 / math.sqrt(HD))
-
-            @pl.when(pair == 0)
+            cols = block(lax.rem(pair, 2), 2 * HD)
+
+            @pl.when(phase == 0)
             def _():
                 for index, ref in enumerate(
                     (w_ref.at[at], o_ref.at[at], qkv_ref.at[at, 0], qkv_ref.at[at, 1], qkv_ref.at[at, 2], lse_ref.at[at])
@@ -1140,28 +1166,39 @@
 
                 gm_ref[...] = dot(low_ref[1], o_ref[at], NT).astype(BF)
 
-            cols = block(pair, 2 * HD)
-            query2 = qkv_ref[at, 0, :, cols] * scale
-            key2 = qkv_ref[at, 1, :, cols]
-            value2 = qkv_ref[at, 2, :, cols]
-            gm2 = gm_ref[:, cols]
-            parts = [[], [], []]
-            for head in range(2):
-                here = slice(head * HD, (head + 1) * HD)
-                query, key, gm = query2[:, here], key2[:, here], gm2[:, here]
-                scores = dot(key, query, NT)
-                scores = scores - dist_ref[...] * slope_ref[i * PER + pair * 2 + head]
-                likely = jnp.exp(scores - lse_ref[at, pl.ds(pair * 2 + head, 1), :])
-                parts[2].append(dot(likely.astype(BF), gm).astype(BF))
-                tt = likely * dot(value2[:, here], gm, NT)
-                inner = jnp.sum(tt, axis=0, keepdims=True)
-                gs = (tt - likely * inner).astype(BF)
-                parts[1].append(dot(gs, query).astype(BF))
-                parts[0].append(dot(gs, key * scale, TN).astype(BF))
-            for n in range(3):
-                gqkv_ref[at, n, :, cols] = jnp.concatenate(parts[n], axis=1)
-
-            @pl.when(pair == 1)
+            @pl.when((phase == 0) | (phase == 2))
+            def _():
+                query2 = qkv_ref[at, 0, :, cols] * scale
+                key2 = qkv_ref[at, 1, :, cols]
+                value2 = qkv_ref[at, 2, :, cols]
+                gm2 = gm_ref[:, cols]
+                parts = []
+                for head in range(2):
+                    here = slice(head * HD, (head + 1) * HD)
+                    gm = gm2[:, here]
+                    scores = dot(key2[:, here], query2[:, here], NT)
+                    scores = scores - dist_ref[...] * slope_ref[i * PER + pair * 2 + head]
+                    likely = jnp.exp(scores - lse_ref[at, pl.ds(pair * 2 + head, 1), :])
+                    parts.append(dot(likely.astype(BF), gm).astype(BF))
+                    tt = likely * dot(value2[:, here], gm, NT)
+                    inner = jnp.sum(tt, axis=0, keepdims=True)
+                    gs_ref[head] = (tt - likely * inner).astype(BF)
+                gqkv_ref[at, 2, :, cols] = jnp.concatenate(parts, axis=1)
+
+            @pl.when((phase == 1) | (phase == 3))
+            def _():
+                query2 = qkv_ref[at, 0, :, cols] * scale
+                key2 = qkv_ref[at, 1, :, cols] * scale
+                parts = [[], []]
+                for head in range(2):
+                    here = slice(head * HD, (head + 1) * HD)
+                    gs = gs_ref[head]
+                    parts[1].append(dot(gs, query2[:, here]).astype(BF))
+                    parts[0].append(dot(gs, key2[:, here], TN).astype(BF))
+                for n in range(2):
+                    gqkv_ref[at, n, :, cols] = jnp.concatenate(parts[n], axis=1)
+
+            @pl.when(phase == 4)
             def _():
                 for index, n in enumerate((0, 2)):
                     qv_sums[index : index + 1, block(i, CW)] = row_sum(gqkv_ref[at, n].astype(F32))
@@ -1211,18 +1248,23 @@
         @pl.when(first)
         def _():
             begin()
-            fill_distance(dist_ref, meta_ref[2])
 
         take_left(0, 0, 0)
         vec_load.wait()
         vec_core = remote(vec.at[0], vec_in.at[0], v_send.at[0], v_recv.at[0], core)
         vec_cross = remote(vec.at[1], vec_in.at[1], v_send.at[1], v_recv.at[1], cross)
 
-        row_sources = ((low_grad_ref, gxl_out), second_refs)
-
-        def row_copy(sources, m):
-            source = sources[m].at[block(1 - t, shard_rows)]
-            return remote(source, rows_out.at[m], r_send.at[m], r_recv.at[m], cross)
+        def row_copy(m, source):
+            return remote(
+                source.at[block(1 - t, shard_rows)], rows_out.at[m], r_send.at[m], r_recv.at[m], cross
+            )
+
+        row_plan = [(0, 0, low_grad_ref, True), (0, 1, gxl_out, False), (1, 1, second_ref, True)]
+        for number, m, source, early in row_plan:
+            if early:
+                @pl.when(section == number)
+                def _(m=m, source=source):
+                    row_copy(m, source).start()
 
         up = pl.ds(0, quarter)
         down = pl.ds(quarter, quarter)
@@ -1334,11 +1376,11 @@
             def _():
                 remote(acc.at[k1, 0], from_x.at[k1], x_send, x_recv.at[k1], cross).start()
 
-            for number, sources in enumerate(row_sources):
-                @pl.when((k1 == total - 1) & (section == number))
-                def _(sources=sources):
-                    for m in range(len(sources)):
-                        row_copy(sources, m).start()
+            for number, m, source, early in row_plan:
+                if not early:
+                    @pl.when((k1 == total - 1) & (section == number))
+                    def _(m=m, source=source):
+                        row_copy(m, source).start()
 
             for rows_, way, place, ahead, behind in sides:
                 k3 = k2 - CHAIN_LAG * place
@@ -1390,11 +1432,10 @@
                         vec_all.at[z], vec_all.at[z], v_send.at[1 + shift], v_recv.at[1 + shift], {"dp": to * 2 + c}
                     ).start()
 
-        for number, sources in enumerate(row_sources):
+        for number, m, source, early in row_plan:
             @pl.when(section == number)
-            def _(sources=sources):
-                for m in range(len(sources)):
-                    row_copy(sources, m).wait()
+            def _(m=m, source=source):
+                row_copy(m, source).wait()
 
         vec_core.wait_send()
         vec_cross.wait_send()
@@ -1428,11 +1469,11 @@
     shapes = [(sum(g == index for g in group_of), width, rights[group_of.index(index)].shape[2] // 2) for index in range(4)]
     return pl.pallas_call(
         kernel,
-        in_specs=[SMEM, SMEM, WHOLE] + [ANY] * (32 + 2 * seqs),
+        in_specs=[SMEM, SMEM, WHOLE] + [ANY] * 33,
         out_specs=[ANY] * 4 + [WHOLE] + [ANY] * 8,
         out_shape=[jax.ShapeDtypeStruct(s, BF) for s in shapes]
-        + [jax.ShapeDtypeStruct(vec_shape, F32), jax.ShapeDtypeStruct((2 * seqs, shard_rows, width), BF)]
-        + [jax.ShapeDtypeStruct((rows, 2 * units), BF)] * 2
+        + [jax.ShapeDtypeStruct(vec_shape, F32), jax.ShapeDtypeStruct((seqs, shard_rows, width), BF)]
+        + [jax.ShapeDtypeStruct(act.shape, BF)] * 2
         + [jax.ShapeDtypeStruct((rows, 2 * local), BF)] * 3
         + [jax.ShapeDtypeStruct((rows, width), F32), jax.ShapeDtypeStruct((rows, width), BF)],
         scratch_shapes=[
@@ -1458,22 +1499,24 @@
             pltpu.VMEM((2, 3, rows, CW), BF),
             pltpu.VMEM((2, 8, rows), F32),
             pltpu.VMEM((rows, CW), BF),
+            pltpu.VMEM((2, rows, rows), BF),
             pltpu.VMEM((rows, rows), F32),
             pltpu.VMEM((8, width), F32),
             pltpu.VMEM((2, 2 * units), F32),
             pltpu.VMEM((2, 2 * local), F32),
             sem((ring,)), sem((2,)), sem((gives,)), sem((total,)), sem, sem((total,)),
             sem((2,)), sem((2, total)), sem((2,)), sem((2, total)),
-            sem, sem, sem, sem, sem((chips + 1,)), sem((chips + 1,)), sem((2 * seqs,)), sem((2 * seqs,)),
+            sem, sem, sem, sem, sem((chips + 1,)), sem((chips + 1,)), sem((seqs,)), sem((seqs,)),
             sem((3,)), sem((2, 6)), sem((2, 3)), sem((2,)),
         ],
+        input_output_aliases={8: 6, 9: 7},
         compiler_params=pltpu.CompilerParams(
             collective_id=0, has_side_effects=True, vmem_limit_bytes=67_000_000
         ),
         cost_estimate=pl.CostEstimate(flops=flops, bytes_accessed=100 << 20, transcendentals=0),
         name="backward_and_reduce",
     )(
-        meta, slopes, vecs, grad, q, k_, v, lse, act, slope, u1, u2, r1, r2, *weights, *lefts, *rights, sums, low_grad, *second
+        meta, slopes, vecs, grad, q, k_, v, lse, act, slope, u1, u2, r1, r2, *weights, *lefts, *rights, sums, low_grad, second
     )
 
 
@@ -1523,9 +1566,9 @@
     )(*outputs, *deps)
 
 
-def widen(reduced, row_grads, got, produced, outputs, sums, units, local):
+def widen(reduced, row_grads, got, got_second, produced, outputs, sums, units, local):
     shard_rows, width = got.shape[1:]
-    seqs = got.shape[0] // 2
+    seqs = got.shape[0]
     n = len(reduced)
     jobs = []
     for index, array in enumerate(reduced):
@@ -1538,14 +1581,14 @@
     jobs += [(n, m, 0, shard_rows, width) for m in range(seqs)] + [(n + 1, m, 0, shard_rows, width) for m in range(seqs)]
     jobs += [(n + 2, m, 0, shard_rows, width) for m in range(2 * seqs)]
     ring = 3
-    n_in = n + 3 * seqs + 3
+    n_in = n + 3 * seqs + 4
     parts = units // width
 
     def kernel(*refs):
         ins = refs[:n]
         grad_refs = refs[n : n + 2 * seqs]
-        got_ref, produced_ref = refs[n + 2 * seqs : n + 2 * seqs + 2]
-        y_refs, sums_ref = refs[n + 2 * seqs + 2 : n_in - 1], refs[n_in - 1]
+        got_ref, got_second_ref, produced_ref = refs[n + 2 * seqs : n + 2 * seqs + 3]
+        y_refs, sums_ref = refs[n + 2 * seqs + 3 : n_in - 1], refs[n_in - 1]
         outs = refs[n_in : n_in + n + 2]
         qv_ref, out_bias_ref, gain_ref, shift_ref, ub_ref, down_bias_ref = refs[n_in + n + 2 : n_in + n + 8]
         shapes = sorted({(j[3], j[4]) for j in jobs if j[0] != n})
@@ -1568,7 +1611,11 @@
                         source = grad_refs[turn * seqs + part].at[block(t, shard_rows)]
                         copy(source, wide_rows.at[part], in_sem.at[s]).start()
             elif index == n + 1:
-                copy(got_ref.at[part], low[rows, columns].at[s], in_sem.at[s]).start()
+                for number_ in range(2):
+                    @pl.when(section == number_)
+                    def _(number_=number_):
+                        source = got_second_ref.at[seqs] if number_ == 1 and part == 0 else got_ref.at[part]
+                        copy(source, low[rows, columns].at[s], in_sem.at[s]).start()
             else:
                 @pl.when(section == 0)
                 def _():
@@ -1576,7 +1623,7 @@
 
                 @pl.when(section == 1)
                 def _():
-                    source = y_refs[part].at[block(t, shard_rows)] if part < seqs else got_ref.at[part]
+                    source = y_refs[part].at[block(t, shard_rows)] if part < seqs else got_second_ref.at[part - seqs]
                     copy(source, low[rows, columns].at[s], in_sem.at[s]).start()
 
         def store(number):
@@ -1655,7 +1702,7 @@
         compiler_params=pltpu.CompilerParams(vmem_limit_bytes=VMEM_LIMIT),
         cost_estimate=pl.CostEstimate(flops=0, bytes_accessed=56 << 20, transcendentals=0),
         name="widen",
-    )(*reduced, *row_grads, got, produced, *outputs, sums)
+    )(*reduced, *row_grads, got, got_second, produced, *outputs, sums)
 
 
 MASKED = -1000000000.0
@@ -2145,16 +2192,20 @@
     back = None
     sums = [[None] * seqs, [None] * seqs]
 
-    def backward(grad, m, turn):
-        nonlocal back, deps
-        *back, gx, gx_low, norm_sums, up_sums, qv_sums = layer_backward(
-            grad, kept, weights, slopes, vecs, metas[turn][m], back, deps, seqs
-        )
+    got_second = None
+
+    def backward(grad, m, turn, *extra):
+        nonlocal back, deps, got_second
+        results = layer_backward(grad, kept, weights, slopes, vecs, metas[turn][m], back, deps, seqs, *extra)
+        back, (gx, gx_low, norm_sums, up_sums, qv_sums) = results[:7], results[7:12]
+        if extra:
+            got_second = results[12]
         deps = [norm_sums]
         sums[turn][m] = (norm_sums, up_sums, qv_sums)
         return gx, gx_low
 
-    gx_second = [backward(outer[m], m, 1) for m in range(seqs)]
+    gx_second = [backward(outer[0], 0, 1)]
+    gx_second.append(backward(outer[1], 1, 1, 1, 1, [*y_second, gx_second[0][1]]))
     grad_middle = [lax.ppermute(gx_second[m][1], "section", [(1, 0)]) for m in range(seqs)]
     x_all = jnp.stack([jnp.where(first, x_first[m], x_second[m]) for m in range(seqs)])
     deps = deps + [x_all]
@@ -2172,13 +2223,13 @@
     packed = jnp.concatenate([norm_sums[:6], ordered(up_sums[:2], units), ordered(qv_sums[:2], local)])
     *reduced, packed, got, _, _, _, _, _, gx, _ = backward_and_reduce(
         grad_middle[1], kept, back, x_all, weights, slopes, vecs, metas[0][1], packed, gx_first[0][1],
-        [g[1] for g in gx_second] + y_second, chips,
+        gx_second[1][1], chips,
     )
     gx_all = [gx_first[0][0], gx] + [g[0] for g in gx_second]
     (
         down_sum, up_sum, qkv_sum, out_sum, grads_in, produced,
         qv_sum, out_bias_sum, gain_sum, shift_sum, up_bias_sum, down_bias_sum,
-    ) = widen(reduced, gx_all, got, produced, y_second, packed, units, local)
+    ) = widen(reduced, gx_all, got, got_second, produced, y_second, packed, units, local)
     return (
         produced[None],
         grads_in[None],

time: 673 us -> 663 us (0.985)
  Pallas kernels: 555 us -> 546 us
    pallas_call x1, Pallas kernels: 262 us -> 252 us  [backward_and_reduce(): pl.pallas_call(kernel, in_specs=[SMEM, SMEM, WHOLE] + [ANY] * 33, out_spe...]
  transfers between devices with their start and end apart: 4 -> 4, of which waited for: 2 -> 1; matrix products, arithmetic and copies ran while one was open for 1% -> 1% of each run, Pallas kernels for 18% -> 18%
where the time goes in v10:
time: 663 us; the launch traced here: 654 us
  Pallas kernels  546 us (82%)
  waiting for transfers between devices  85.5 us (13%)
  other arithmetic  10.9 us (2%)
    pallas_call x1, Pallas kernels, backward_and_reduce(): pl.pallas_call(kernel, in_specs=[SMEM, SMEM, WHOLE] + [ANY] * 33, out_spe...  252 us
    pallas_call x1, Pallas kernels, fetch_and_forward(): pl.pallas_call(kernel, in_specs=[SMEM, SMEM, WHOLE] + [ANY] * 8, out_spec...  144 us
    pallas_call x6, Pallas kernels, call(): pl.pallas_call(body, in_specs=specs, out_specs=[ANY] * n_out, out_shape=[...  102 us
    ppermute x2, waiting for transfers between devices, by_sequence(): lax.ppermute(gx_second[m][1], 'section', [(1, 0)])  85.5 us
    pallas_call x1, Pallas kernels, exchange_rows(): pl.pallas_call(kernel, in_specs=[ANY] * n_in, out_specs=ANY, out_shape=ja...  24.2 us
    pallas_call x1, Pallas kernels, widen(): pl.pallas_call(kernel, in_specs=[ANY] * (n_in - 1) + [WHOLE], out_specs=[...  24.2 us
  transfers between devices with their start and end apart: 4, of which 1 were waited for; matrix products, arithmetic and copies ran while one was open for 1% of the time, Pallas kernels for 18%

profile of v10, /device:TPU:0, one launch (start us, length us, event | category | flops | bytes accessed | tf_op | source)
XLA Modules:
  0.0 654.4 jit_solution(12304988209819974297)
XLA Ops:
  0.7 0.7 dynamic_slice.3
  1.4 0.6 fusion.8
  2.0 0.8 slice_bitcast_fusion
  2.8 0.9 stack.41
  3.6 0.6 convert_element_type.2.refs_2_.refs_12_.refs_21_
  4.2 1.2 broadcast_select_fusion.refs_1_.refs_11_.refs_20_
  5.4 1.2 pad_add_fusion.refs_0_
  6.7 143.6 %fetch_and_forward.1 = (bf16[3,1024,512]{2,1,0:T(8,128)(2,1)}, bf16[512,1024]{1,0:T(8,128)(2,1)}, bf16[2,1024,2048]{2,1,0:T(8,128)(2,1)}, bf16[1024,2048]{1,0:T(...) custom-call(s32[4]{0:T(128)} %pad_add_fusion.refs_0_, ...), custom_call_target="tpu_custom_call" | custom-call | flops 18253611008 | bytes 94371840 | tf_op jit(solution)/shard_map/fetch_and_forward/pallas_call | solution.py:888
  150.3 1.4 collective-permute-start.1
  151.7 1.2 pad_add_fusion.1.refs_0_
  152.9 38.5 %layer_forward.3 = (bf16[2,512,1024]{2,1,0:T(8,128)(2,1)}, bf16[2,512,1024]{2,1,0:T(8,128)(2,1)}, bf16[2,512,1024]{2,1,0:T(8,128)(2,1)}, bf16[2,512,1024]{2,1,0:...) custom-call(s32[4]{0:T(128)} %pad_add_fusion.1.refs_0_, ...), custom_call_target="tpu_custom_call", output_to_operand_aliasing={{0}: (14, {}), {1}: (15, {}), {2}: (16, {}), {3}: (17, {}),... | custom-call | flops 18253611008 | bytes 56623104 | tf_op jit(solution)/shard_map/layer_forward/pallas_call | solution.py:55
  191.5 2.2 collective-permute-start
  193.7 1.9 fusion.2
  195.6 0.0 collective-permute-done.1.refs_1_
  195.6 0.0 copy-start.1
  195.6 1.0 copy-done.1
  196.6 1.3 layer_forward.4
  197.9 24.2 %exchange_rows.1.refs_27_.refs_10_ = bf16[4,256,1024]{2,1,0:T(8,128)(2,1)} custom-call(bf16[512,1024]{1,0:T(8,128)(2,1)} %get-tuple-element.152.refs_27_.refs_0_, bf16[512,1024]{1,0:T(8,128)(2,1)} %get-tuple-element.153.refs_27_.refs_1_, bf16[512,1024]{1,0:T(8,128)(2,1)} %get-tuple-element.180.refs_2_.refs_22_.refs_11_), custom_call_target="tpu_custom_call" | custom-call | tf_op jit(solution)/shard_map/exchange_rows/pallas_call | solution.py:1557
  222.1 0.0 collective-permute-done.refs_1_
  222.1 1.4 layer_forward.5
  223.5 7.2 %layer_backward.3 = (bf16[2,512,4096]{2,1,0:T(8,128)(2,1)}, bf16[2,512,4096]{2,1,0:T(8,128)(2,1)}, bf16[2,512,1024]{2,1,0:T(8,128)(2,1)}, bf16[2,512,1024]{2,1,0...) custom-call(s32[4]{0:T(128)} %get-tuple-element.262.refs_0_, ...), custom_call_target="tpu_custom_call" | custom-call | flops 19864223744 | bytes 73400320 | tf_op jit(solution)/shard_map/layer_backward/pallas_call | solution.py:55
  230.7 1.3 collective-permute-start.3
  232.0 0.0 copy-start
  232.1 5.8 layer_backward.4
  237.8 0.0 copy-start.2
  237.8 0.0 copy-start.3
  237.8 1.4 collective-permute-start.2
  239.3 0.0 copy-done
  239.3 0.1 select_bitcast_fusion
  239.4 0.0 copy-done.2
  239.4 0.0 copy-done.3
  239.4 0.1 select_bitcast_fusion.1
  239.5 1.5 pad_maximum_fusion.refs_30_.refs_24_
  241.1 85.5 %collective-permute-done.3.refs_1_ = bf16[512,1024]{1,0:T(8,128)(2,1)} collective-permute-done((bf16[512,1024]{1,0:T(8,128)(2,1)}, bf16[512,1024]{1,0:T(8,128)(2,1)}, u32[]{:S(2)}, u32[]{:S(2)}) %collective-permute-start.3) | collective-permute-done | bytes 1048608 | tf_op jit(solution)/shard_map/ppermute | solution.py:2209
  326.5 0.0 copy-start.6
  326.5 0.0 copy-start.7
  326.5 0.0 copy-start.8
  326.5 0.0 copy-start.9
  326.6 0.0 copy-start.4
  326.6 0.0 copy-start.5
  326.6 47.6 %layer_backward.5 = (bf16[2,512,4096]{2,1,0:T(8,128)(2,1)}, bf16[2,512,4096]{2,1,0:T(8,128)(2,1)}, bf16[2,512,1024]{2,1,0:T(8,128)(2,1)}, bf16[2,512,1024]{2,1,0...) custom-call(s32[4]{0:T(128)} %pad_add_fusion.refs_0_, ...), custom_call_target="tpu_custom_call", output_to_operand_aliasing={{0}: (22, {}), {1}: (23, {}), {2}: (24, {}), {3}: (25, {}),... | custom-call | flops 19864223744 | bytes 73400320 | tf_op jit(solution)/shard_map/layer_backward/pallas_call | solution.py:55
  374.1 0.0 copy-done.6
  374.1 0.0 copy-done.7
  374.2 0.8 add_select_fusion
  375.0 0.0 copy-done.8
  375.0 0.0 copy-done.9
  375.1 0.7 add_select_fusion.1
  375.8 0.0 copy-done.4
  375.8 0.0 copy-done.5
  375.8 0.8 slice_select_fusion
  376.6 0.6 pad_maximum_fusion.1.refs_33_
  377.2 0.0 collective-permute-done.2.refs_3_
  377.2 252.4 %backward_and_reduce.1 = (bf16[1,1024,2048]{2,1,0:T(8,128)(2,1)}, bf16[2,1024,2048]{2,1,0:T(8,128)(2,1)}, bf16[3,1024,512]{2,1,0:T(8,128)(2,1)}, bf16[1,1024,512...) custom-call(s32[4]{0:T(128)} %pad_add_fusion.1.refs_0_, ...), custom_call_target="tpu_custom_call", output_to_operand_aliasing={{6}: (8, {}), {7}: (9, {})} | custom-call | flops 34359738368 | bytes 104857600 | tf_op jit(solution)/shard_map/backward_and_reduce/pallas_call | solution.py:1470
  629.7 24.2 %widen.1 = (f32[1,1024,2048]{2,1,0:T(8,128)}, f32[2,1024,2048]{2,1,0:T(8,128)}, f32[3,1024,512]{2,1,0:T(8,128)}, f32[512,1024]{1,0:T(8,128)}, f32[4,256,1024]{2,...) custom-call(bf16[1,1024,2048]{2,1,0:T(8,128)(2,1)} %get-tuple-elemen, ...), custom_call_target="tpu_custom_call" | custom-call | bytes 58720256 | tf_op jit(solution)/shard_map/widen/pallas_call | solution.py:1690
  (5 shorter events, 0.1 us)
Async XLA Ops:
  150.3 45.3 %collective-permute-start.1 = (bf16[512,1024]{1,0:T(8,128)(2,1)}, bf16[512,1024]{1,0:T(8,128)(2,1)S(1)}, u32[]{:S(2)}, u32[]{:S(2)}) collective-permute-start(bf16[512,1024]{1,0:T(8,128)(2,1)} %get-tuple-element.152.refs_27_.refs_0_), channel_id=1, source_target_pairs={{0,16},{1,17},{2,18},{3,19},{4,20},{5,21},{6,22},{7,23},{8,24},{9,... | collective-permute-start | bytes 3145736 | tf_op jit(solution)/shard_map/ppermute | solution.py:2186
  191.5 30.6 %collective-permute-start = (bf16[512,1024]{1,0:T(8,128)(2,1)}, bf16[512,1024]{1,0:T(8,128)(2,1)}, u32[]{:S(2)}, u32[]{:S(2)}) collective-permute-start(bf16[512,1024]{1,0:T(8,128)(2,1)} %get-tuple-element.153.refs_27_.refs_1_), channel_id=1, source_target_pairs={{0,16},{1,17},{2,18},{3,19},{4,20},{5,21},{6,22},{7,23},{8,24},{9,... | collective-permute-start | bytes 3145736 | tf_op jit(solution)/shard_map/ppermute | solution.py:2186
  195.6 1.0 copy-start.1
  230.7 95.8 %collective-permute-start.3 = (bf16[512,1024]{1,0:T(8,128)(2,1)}, bf16[512,1024]{1,0:T(8,128)(2,1)}, u32[]{:S(2)}, u32[]{:S(2)}) collective-permute-start(bf16[512,1024]{1,0:T(8,128)(2,1)} %get-tuple-element.193.refs_24_), channel_id=1, source_target_pairs={{16,0},{17,1},{18,2},{19,3},{20,4},{21,5},{22,6},{23,7},{24,8},{25... | collective-permute-start | bytes 3145736 | tf_op jit(solution)/shard_map/ppermute | solution.py:2209
  232.0 7.2 %copy-start = (bf16[512,1024]{1,0:T(8,128)(2,1)S(1)}, bf16[512,1024]{1,0:T(8,128)(2,1)}, u32[]{:S(2)}) copy-start(bf16[512,1024]{1,0:T(8,128)(2,1)} %get-tuple-element.132.refs_1_) | copy-start | bytes 3145732
  237.8 1.6 copy-start.2
  237.8 1.6 copy-start.3
  237.8 139.4 %collective-permute-start.2 = (bf16[512,1024]{1,0:T(8,128)(2,1)}, bf16[512,1024]{1,0:T(8,128)(2,1)}, u32[]{:S(2)}, u32[]{:S(2)}) collective-permute-start(bf16[512,1024]{1,0:T(8,128)(2,1)} %get-tuple-element.202.refs_35_), channel_id=1, source_target_pairs={{16,0},{17,1},{18,2},{19,3},{20,4},{21,5},{22,6},{23,7},{24,8},{25... | collective-permute-start | bytes 3145736 | tf_op jit(solution)/shard_map/ppermute | solution.py:2209
  326.5 47.6 %copy-start.6 = (f32[2,4096]{1,0:T(2,128)S(1)}, f32[2,4096]{1,0:T(2,128)}, u32[]{:S(2)}) copy-start(f32[2,4096]{1,0:T(2,128)} %get-tuple-element.223) | copy-start | bytes 98308
  326.5 47.6 %copy-start.7 = (f32[2,4096]{1,0:T(2,128)S(1)}, f32[2,4096]{1,0:T(2,128)}, u32[]{:S(2)}) copy-start(f32[2,4096]{1,0:T(2,128)} %get-tuple-element.224) | copy-start | bytes 98308
  326.5 48.5 %copy-start.8 = (f32[2,1024]{1,0:T(2,128)S(1)}, f32[2,1024]{1,0:T(2,128)}, u32[]{:S(2)}) copy-start(f32[2,1024]{1,0:T(2,128)} %get-tuple-element.226) | copy-start | bytes 24580
  326.5 48.5 %copy-start.9 = (f32[2,1024]{1,0:T(2,128)S(1)}, f32[2,1024]{1,0:T(2,128)}, u32[]{:S(2)}) copy-start(f32[2,1024]{1,0:T(2,128)} %get-tuple-element.227) | copy-start | bytes 24580
  326.6 49.2 %copy-start.4 = (f32[8,1024]{1,0:T(8,128)S(1)}, f32[8,1024]{1,0:T(8,128)}, u32[]{:S(2)}) copy-start(f32[8,1024]{1,0:T(8,128)} %get-tuple-element.201.refs_32_) | copy-start | bytes 98308
  326.6 49.2 %copy-start.5 = (f32[8,1024]{1,0:T(8,128)S(1)}, f32[8,1024]{1,0:T(8,128)}, u32[]{:S(2)}) copy-start(f32[8,1024]{1,0:T(8,128)} %get-tuple-element.210.refs_29_) | copy-start | bytes 98308

commit v11 on v10

--- a/solution.py
+++ b/solution.py
@@ -32,10 +32,10 @@
     pltpu.make_async_copy(ref, ref, sem).wait()
 
 
-def call(kernel, inputs, outputs, scratch, meta, chain, deps, name, flops, nbytes, turn=None):
+def call(kernel, inputs, outputs, scratch, chain, deps, name, flops, nbytes, turn, remote=False):
     pairs = [item if isinstance(item, tuple) else (item, ANY) for item in inputs]
-    args = [meta] + [p[0] for p in pairs]
-    specs = [SMEM] + [p[1] for p in pairs]
+    args = [p[0] for p in pairs]
+    specs = [p[1] for p in pairs]
     n_in = len(args)
     aliases = {}
     if chain is not None:
@@ -46,11 +46,12 @@
     args += deps
     specs += [ANY] * len(deps)
     n_args, n_out = len(args), len(outputs)
+    params = {"collective_id": 3, "has_side_effects": True} if remote else {}
 
     def body(*refs):
-        @pl.when(refs[0][1] == 1 if turn is None else lax.axis_index("section") == turn)
+        @pl.when(lax.axis_index("section") == turn)
         def _():
-            kernel(refs[0], refs[1:n_in], refs[n_args : n_args + n_out], refs[n_args + n_out :])
+            kernel(refs[:n_in], refs[n_args : n_args + n_out], refs[n_args + n_out :])
 
     return pl.pallas_call(
         body,
@@ -59,12 +60,23 @@
         out_shape=[jax.ShapeDtypeStruct(o[0], o[1]) for o in outputs],
         scratch_shapes=scratch,
         input_output_aliases=aliases,
-        compiler_params=pltpu.CompilerParams(vmem_limit_bytes=VMEM_LIMIT)
-        if turn is None
-        else pltpu.CompilerParams(vmem_limit_bytes=VMEM_LIMIT, collective_id=3, has_side_effects=True),
+        compiler_params=pltpu.CompilerParams(vmem_limit_bytes=VMEM_LIMIT, **params),
         cost_estimate=pl.CostEstimate(flops=flops, bytes_accessed=nbytes, transcendentals=0),
         name=name,
     )(*args)
+
+
+NORM_SPECS = [WHOLE] * 4
+
+
+def norm_rows(refs):
+    out_bias, gain, shift, down_bias = refs
+    rows = [out_bias[...], gain[0:1], shift[0:1], down_bias[...], gain[1:2], shift[1:2]]
+    return [row.astype(F32) for row in rows]
+
+
+def slope_of(table_ref, head):
+    return table_ref[lax.axis_index("tensor") * (table_ref.shape[0] // 2) + head]
 
 
 def pick(k, count, own, oth, make):
@@ -143,8 +155,8 @@
             sem, sem((2,)), sem((2,)), sem((2, 2)), sem((2, 4)), sem, sem((2, 3)), sem((6,)),
         ]
 
-    def bind(self, x, weights, bias, slopes, vecs, up_bias, slot, outs, scratch):
-        self.x_hbm, self.weights, self.bias, self.slopes, self.vecs, self.up_bias = x, weights, bias, slopes, vecs, up_bias
+    def bind(self, x, weights, bias, up_bias, slopes, norms, slot, outs, scratch):
+        self.x_hbm, self.weights, self.bias, self.up_bias, self.slopes, self.norms = x, weights, bias, up_bias, slopes, norms
         self.slot, self.outs = slot, outs
         (self.x, self.w, self.o, self.up, self.down, self.qkv, self.lse, self.mixed, self.dist, self.normed, self.acc,
          self.low, self.tile, self.row, self.stat, self.x_sem, self.w_sem, self.o_sem, self.f_sem, self.q_sem, self.m_sem,
@@ -199,7 +211,7 @@
             cols = slice(head * HD, (head + 1) * HD)
             query = qkv[s, 0, :, cols] * BF(1.0 / math.sqrt(HD))
             scores = dot(qkv[s, 1, :, cols], query, NT)
-            scores = scores - self.dist[...] * self.slopes[i * PER + head]
+            scores = scores - self.dist[...] * slope_of(self.slopes, i * PER + head)
             top = jnp.max(scores, axis=0, keepdims=True)
             likely = jnp.exp(scores - top)
             mass = jnp.sum(likely, axis=0, keepdims=True)
@@ -215,11 +227,11 @@
         copy(self.mixed, self.outs[3].at[self.slot], self.m_sem).start()
         for side in range(2):
             arrived(self.o.at[pl.ds(side * self.local, self.local)], self.o_sem.at[side])
-        vec = self.vecs[...]
+        vec = norm_rows(self.norms)
         for rs in halves(rows):
             attended = dot(self.mixed[rs, :], self.o[...])
-            u, rstd = normalize(self.x[rs, :].astype(F32) + attended + vec[0:1])
-            normed = u * vec[1:2] + vec[2:3]
+            u, rstd = normalize(self.x[rs, :].astype(F32) + attended + vec[0])
+            normed = u * vec[1] + vec[2]
             self.normed[rs, :] = normed
             self.low[rs, :] = normed.astype(BF)
             self.row[0, rs, :] = u.astype(BF)
@@ -268,12 +280,12 @@
 
     def finish(self, y_out):
         rows = self.rows
-        vec = self.vecs[...]
+        vec = norm_rows(self.norms)
         for rs in halves(rows):
-            u, rstd = normalize(self.normed[rs, :] + self.acc[rs, :] + vec[3:4])
+            u, rstd = normalize(self.normed[rs, :] + self.acc[rs, :] + vec[3])
             self.row[1, rs, :] = u.astype(BF)
             self.stat[1, rs, :] = jnp.broadcast_to(rstd, (rows // 2, 128))
-            self.row[2, rs, :] = (u * vec[4:5] + vec[5:6]).astype(BF)
+            self.row[2, rs, :] = (u * vec[4] + vec[5]).astype(BF)
         ends = [(self.row.at[1], self.outs[10].at[self.slot]), (self.stat.at[1], self.outs[12].at[self.slot]),
                 (self.row.at[2], y_out)]
         for index, item in enumerate(ends):
@@ -293,12 +305,13 @@
         return 2 * rows * width * (4 * total + 6 * self.units) + 4 * rows * rows * total
 
 
-def layer_forward(x, weights, bias, slopes, vecs, up_bias, meta, chain, deps, slots):
+def layer_forward(x, weights, biases, slopes, norms, lengths, m, turn, chain, deps, slots):
     rows, width = x.shape
     step = Forward(rows, width, weights[0].shape[2], weights[4].shape[2])
 
-    def kernel(meta_ref, ins, outs, scratch):
-        step.bind(ins[0], ins[1:9], *ins[9:13], meta_ref[0], outs[:13], scratch)
+    def kernel(ins, outs, scratch):
+        lengths_ref = ins[0]
+        step.bind(ins[1], ins[2:10], ins[10], ins[11], ins[12], ins[13:17], m, outs[:13], scratch)
         step.start_x()
         for k in range(2):
             step.start_w(jnp.int32(k))
@@ -306,7 +319,7 @@
             step.start_o(side)
         for k in range(2):
             step.start_f(jnp.int32(k))
-        fill_distance(step.dist, meta_ref[2])
+        fill_distance(step.dist, lengths_ref[lax.axis_index("tensor") * slots + m])
         arrived(step.x, step.x_sem)
 
         @pl.loop(0, 2 * step.heads_steps)
@@ -323,19 +336,19 @@
 
     return call(
         kernel,
-        [x, *weights, (bias, WHOLE), (slopes, SMEM), (vecs, WHOLE), (up_bias, WHOLE)],
+        [(lengths, SMEM), x, *weights, *zip(biases, [WHOLE] * 2), (slopes, SMEM), *zip(norms, NORM_SPECS)],
         [shape + (True,) for shape in step.kept(slots)] + [((rows, width), BF, False)],
         step.scratch(),
-        meta,
         chain,
         deps,
         "layer_forward",
         step.flops(),
         54 << 20,
+        turn,
     )
 
 
-def layer_backward(grad, kept, weights, slopes, vecs, meta, chain, deps, slots, slot=None, turn=None, sent=()):
+def layer_backward(grad, kept, weights, slopes, norms, lengths, m, turn, chain, deps, slots, sent=()):
     qkv_own, qkv_oth, o_own, o_oth, up_own, up_oth, down_own, down_oth = weights
     q, k, v, _, lse, act, slope, _, _, u1, u2, r1, r2 = kept
     rows, width = grad.shape
@@ -345,7 +358,6 @@
     ft = min(512, units)
     tiles = units // ft
     total = 2 * local
-    static_slot = slot
 
     def norm_back(grad_z, u, rstd, gain):
         t = grad_z * gain
@@ -354,18 +366,19 @@
     def row_sum(values):
         return jnp.sum(values, axis=0, keepdims=True)
 
-    def kernel(meta_ref, ins, outs, scratch):
-        (g_hbm, q_hbm, k_hbm, v_hbm, lse_hbm, a_hbm, b_hbm, u1_hbm, u2_hbm, r1_hbm, r2_hbm,
+    def kernel(ins, outs, scratch):
+        (lengths_ref, g_hbm, q_hbm, k_hbm, v_hbm, lse_hbm, a_hbm, b_hbm, u1_hbm, u2_hbm, r1_hbm, r2_hbm,
          qkv_own_ref, qkv_oth_ref, o_own_ref, o_oth_ref, up_own_ref, up_oth_ref, down_own_ref, down_oth_ref,
-         slope_ref, vec_ref) = ins[:21]
+         slope_ref) = ins[:21]
         gg0_out, gg1_out, gl_out, ga_out, gq_out, gk_out, gv_out, gx_out, gxl_out, sums_out, ub_out, qv_out = outs[:12]
         (g_ref, u_ref, r_ref, up_ref, down_ref, ab_ref, gg_ref, low_ref, acc_ref, sums_ref, ub_ref, qv_ref,
          w_ref, o_ref, qkv_ref, lse_ref, gm_ref, dist_ref, gqkv_ref,
          g_sem, f_sem, t_sem, w_sem, q_sem, r_sem, x_send, x_recv) = scratch
-        slot = meta_ref[0] if static_slot is None else static_slot
+        slot = m
+        t = lax.axis_index("tensor")
+        length = lengths_ref[t * slots + m]
         travelling = []
         if sent:
-            t = lax.axis_index("tensor")
             cross = {"tensor": 1 - t}
             barrier = pltpu.get_barrier_semaphore()
             pl.semaphore_signal(barrier, inc=1, device_id=cross, device_id_type=pl.DeviceIdType.MESH)
@@ -373,7 +386,7 @@
             for index in range(len(sent)):
                 travelling.append(
                     pltpu.make_async_remote_copy(
-                        src_ref=ins[21 + index].at[block(1 - t, rows // 2)], dst_ref=outs[12].at[index],
+                        src_ref=ins[25 + index].at[block(1 - t, rows // 2)], dst_ref=outs[12].at[index],
                         send_sem=x_send.at[index], recv_sem=x_recv.at[index],
                         device_id=cross, device_id_type=pl.DeviceIdType.MESH,
                     )
@@ -406,16 +419,18 @@
                 start_f(jnp.int32(1))
         start_w(jnp.int32(0))
         start_w(jnp.int32(1))
-        vec = vec_ref[...]
-        fill_distance(dist_ref, meta_ref[2])
+        vec = norm_rows(ins[21:25])
+        fill_distance(dist_ref, length)
         for index, (src, dst) in enumerate(firsts[:3]):
             copy(src, dst, g_sem.at[index]).wait()
         sums = [jnp.zeros((1, width), F32)] * 3
         for rs in halves(rows):
-            places = lax.broadcasted_iota(jnp.int32, (rows // 2, width), 0) + rs.start
-            grad_y = jnp.where(places < meta_ref[3], g_ref[rs, :].astype(F32), 0.0)
+            grad_y = g_ref[rs, :].astype(F32)
+            if turn == 1:
+                places = lax.broadcasted_iota(jnp.int32, (rows // 2, width), 0) + rs.start
+                grad_y = jnp.where(places < length, grad_y, 0.0)
             u = u_ref[1, rs, :].astype(F32)
-            grad_c = norm_back(grad_y, u, r_ref[1, rs, 0:1], vec[4:5])
+            grad_c = norm_back(grad_y, u, r_ref[1, rs, 0:1], vec[4])
             acc_ref[rs, :] = grad_c
             low_ref[0, rs, :] = grad_c.astype(BF)
             for index, values in enumerate((grad_y * u, grad_y, grad_c)):
@@ -463,7 +478,7 @@
         for rs in halves(rows):
             grad_n = acc_ref[rs, :]
             u = u_ref[0, rs, :].astype(F32)
-            grad_a = norm_back(grad_n, u, r_ref[0, rs, 0:1], vec[1:2])
+            grad_a = norm_back(grad_n, u, r_ref[0, rs, 0:1], vec[1])
             low_ref[1, rs, :] = grad_a.astype(BF)
             acc_ref[rs, :] = grad_a
             for index, values in enumerate((grad_n * u, grad_n, grad_a)):
@@ -497,7 +512,7 @@
                 key = qkv_ref[s, 1, :, cols]
                 gm = gm_ref[:, cols]
                 scores = dot(key, query, NT)
-                scores = scores - dist_ref[...] * slope_ref[i * PER + head]
+                scores = scores - dist_ref[...] * slope_of(slope_ref, i * PER + head)
                 likely = jnp.exp(scores - lse_ref[s, head : head + 1, :])
                 parts[2].append(dot(likely.astype(BF), gm).astype(BF))
                 t = likely * dot(qkv_ref[s, 2, :, cols], gm, NT)
@@ -540,7 +555,7 @@
     sem = pltpu.SemaphoreType.DMA
     return call(
         kernel,
-        [grad, q, k, v, lse, act, slope, u1, u2, r1, r2, *weights, (slopes, SMEM), (vecs, WHOLE), *sent],
+        [(lengths, SMEM), grad, q, k, v, lse, act, slope, u1, u2, r1, r2, *weights, (slopes, SMEM), *zip(norms, NORM_SPECS), *sent],
         [((slots, rows, 2 * units), BF, True)] * 2
         + [((slots, rows, width), BF, True)] * 2
         + [((slots, rows, total), BF, True)] * 3
@@ -574,13 +589,13 @@
             pltpu.VMEM((2, 3, rows, CW), BF),
             sem((5,)), sem((2, 4)), sem((2, 2)), sem((2, 6)), sem((2, 3)), sem((7,)), sem((4,)), sem((4,)),
         ],
-        meta,
         chain,
         deps,
         "layer_backward",
         2 * rows * width * (4 * total + 6 * units) + 10 * rows * rows * total,
         70 << 20,
         turn,
+        bool(sent),
     )
 
 
@@ -609,7 +624,7 @@
     pl.semaphore_wait(barrier, 1 + chips)
 
 
-def fetch_and_forward(weights, biases, inputs, cotangent, slopes, vecs, meta, chips, slots):
+def fetch_and_forward(weights, biases, inputs, cotangent, slopes, norms, lengths, chips, slots):
     seqs = inputs.shape[0] // 2
     shard_rows, width = inputs.shape[1:]
     rows = 2 * shard_rows
@@ -622,9 +637,13 @@
     QKV, OUT, UP, DOWN, ROWS, BIAS = range(6)
 
     plan = [(UP, 0, groups), (ROWS, 0, 0), (BIAS, 0, 0), (BIAS, 1, 0)]
-    plan += [(UP, part, groups) for part in range(1, tiles)]
-    plan += [(DOWN, part, groups) for part in range(tiles - 1)]
-    plan += [(QKV, part, 2) for part in range(3)] + [(OUT, 0, 2), (DOWN, tiles - 1, 2)]
+    for part in range(1, tiles):
+        plan.append((UP, part, groups))
+        if part <= 3:
+            plan.append((QKV, part - 1, 2))
+    plan += [(DOWN, 0, groups), (OUT, 0, 2)]
+    plan += [(DOWN, part, groups) for part in range(1, tiles - 1)]
+    plan += [(DOWN, tiles - 1, 2)]
     plan += [(ROWS, part, 0) for part in range(1, seqs)]
     n = len(plan)
     number = {item[:2]: index for index, item in enumerate(plan)}
@@ -650,7 +669,6 @@
 
     needs = [[(ROWS, 0), (BIAS, 0)], []] + [[(QKV, part) for part in range(3)], []] + [[(OUT, 0), (BIAS, 1)]]
     needs += [[] for _ in range(tiles - 1)]
-    fetches = {5 + tiles - 1 + part: tiles + part for part in range(tiles)}
     needs += [[(UP, part), (DOWN, part)] for part in range(tiles)] + [[]]
     assert step.heads_steps == 2
     rounds, taken = [], 0
@@ -667,20 +685,21 @@
     n_kept = len(step.kept(slots))
 
     def kernel(*refs):
-        meta_ref, slope_ref, vec_ref = refs[:3]
-        ins, bias_ins, held_refs = refs[3:7], refs[7:9], refs[9:11]
-        outs, bias_outs, row_refs = refs[11:15], refs[15:17], refs[17 : 17 + seqs]
-        kept_refs = refs[17 + seqs : 17 + seqs + n_kept]
-        y_ref = refs[17 + seqs + n_kept]
+        lengths_ref, slope_ref, norm_refs = refs[0], refs[1], refs[2:6]
+        refs = refs[6:]
+        ins, bias_ins, held_refs = refs[:4], refs[4:6], refs[6:8]
+        outs, bias_outs, row_refs = refs[8:12], refs[12:14], refs[14 : 14 + seqs]
+        kept_refs = refs[14 + seqs : 14 + seqs + n_kept]
+        y_ref = refs[14 + seqs + n_kept]
         stage, qv_bias, ub_bias, x_send, x_recv, c_send, c_recv, u_send, u_recv, d_send, d_recv, l_sem, b_sem = refs[
-            18 + seqs + n_kept : 31 + seqs + n_kept
+            15 + seqs + n_kept : 28 + seqs + n_kept
         ]
         t, c, z, last, core, cross, above, below = neighbours()
         section = lax.axis_index("section")
         greet(c, z, chips, core, cross)
         paired = [item for pair in zip(ins, outs) for item in pair]
         step.bind(
-            row_refs[0], paired, qv_bias, slope_ref, vec_ref, ub_bias, 0, kept_refs, refs[31 + seqs + n_kept :]
+            row_refs[0], paired, qv_bias, ub_bias, slope_ref, norm_refs, 0, kept_refs, refs[28 + seqs + n_kept :]
         )
 
         def span(part):
@@ -749,7 +768,7 @@
             step.start_o(0)
             for k in range(2):
                 step.start_f(jnp.int32(k))
-            fill_distance(step.dist, meta_ref[2])
+            fill_distance(step.dist, lengths_ref[t * seqs])
 
         arrived(stage, l_sem.at[0])
         for m in range(seqs):
@@ -887,7 +906,7 @@
     sem = pltpu.SemaphoreType.DMA
     return pl.pallas_call(
         kernel,
-        in_specs=[SMEM, SMEM, WHOLE] + [ANY] * 8,
+        in_specs=[SMEM, SMEM] + NORM_SPECS + [ANY] * 8,
         out_specs=[ANY] * (7 + seqs + n_kept),
         out_shape=[jax.ShapeDtypeStruct(w.shape, BF) for w in weights]
         + [jax.ShapeDtypeStruct((2, 2 * size_), BF) for size_ in bias_widths]
@@ -903,7 +922,7 @@
         compiler_params=pltpu.CompilerParams(collective_id=1, has_side_effects=True, vmem_limit_bytes=VMEM_LIMIT),
         cost_estimate=pl.CostEstimate(flops=step.flops(), bytes_accessed=90 << 20, transcendentals=0),
         name="fetch_and_forward",
-    )(meta, slopes, vecs, *weights, *biases, inputs, cotangent)
+    )(lengths, slopes, *norms, *weights, *biases, inputs, cotangent)
 
 
 def norm_back(grad_z, u, rstd, gain):
@@ -915,7 +934,7 @@
     return jnp.sum(values, axis=0, keepdims=True)
 
 
-def backward_and_reduce(grad, kept, back, x_all, weights, slopes, vecs, meta, sums, low_grad, second, chips):
+def backward_and_reduce(grad, kept, back, x_all, weights, slopes, norms, lengths, sums, low_grad, second, chips):
     q, k_, v, mixed_all, lse, act, slope, hidden_all, normed_all, u1, u2, r1, r2 = kept
     gg0, gg1, gl, ga, gq, gk, gv = back
     rows, width = grad.shape
@@ -939,39 +958,40 @@
     ring, mines, gives = 4, CORE_LAG + 1, 4
     ahead_of = 4
     drain = CORE_LAG + CROSS_LAG + 2 * (chips - 1) * CHAIN_LAG + 1
-    vec_shape = sums.shape
     shard_rows = rows // 2
     norm_at = 2 * tiles
     head_at = norm_at + 1
     end_at = head_at + 5 * 2 * heads_steps
     x_flip, ga_flip = ffn_blocks - per_pair, ffn_blocks + per_pair
     up_rows = units // width
+    vec_shape = (6 + 4 * up_rows + 2, width)
     assert ahead_of + ffn_blocks - ring > end_at
 
     def kernel(*refs):
-        meta_ref, slope_ref, vec_ref = refs[:3]
+        lengths_ref, slope_ref, norm_refs, sum_refs = refs[0], refs[1], refs[2:6], refs[6:15]
+        refs = refs[12:]
         g_hbm, q_hbm, k_hbm, v_hbm, lse_hbm, a_hbm, b_hbm, u1_hbm, u2_hbm, r1_hbm, r2_hbm = refs[3:14]
         (qkv_own_ref, qkv_oth_ref, o_own_ref, o_oth_ref, up_own_ref, up_oth_ref, down_own_ref, down_oth_ref) = refs[14:22]
         left_refs, right_refs = refs[22:26], refs[26:33]
-        sums_ref, low_grad_ref, second_ref = refs[33:36]
-        outs, sums_out, rows_out = refs[36:40], refs[40], refs[41]
-        fresh = refs[42:47]
-        gx_out, gxl_out = refs[47:49]
+        low_grad_ref, second_ref = refs[33:35]
+        outs, sums_out, rows_out = refs[35:39], refs[39], refs[40]
+        fresh = refs[41:46]
+        gx_out, gxl_out = refs[46:48]
         (
             acc, from_x, from_z, flip, stage, tile, mine, give, vec, vec_in, vec_all,
             g_ref, u_ref, r_ref, low_ref, gacc_ref, w_ref, o_ref, qkv_ref, gqkv_ref, lse_ref, gm_ref, gs_ref, dist_ref,
             part_sums, ub_sums, qv_sums,
             tile_sem, stage_sem, give_send, core_recv, x_send, x_recv, z_send, z_recv, f_send, f_recv,
-            store_sem, out_send, out_recv, v_load, v_send, v_recv, r_send, r_recv,
+            store_sem, out_send, out_recv, v_send, v_recv, r_send, r_recv,
             g_sem, w_sem, t_sem, e_sem,
-        ) = refs[49:]
+        ) = refs[48:]
         final = from_x
         t, c, z, last, core, cross, above, below = neighbours()
         section = lax.axis_index("section")
         first = section == 0
         greet(c, z, chips, core, cross)
         fresh_of = {1: fresh[0].at[0], 2: fresh[1].at[0], 3: fresh[2], 4: fresh[3], 5: fresh[4]}
-        vec_w = vec_ref[...]
+        vec_w = norm_rows(norm_refs)
 
         def remote(src, dst, send, recv, device):
             return pltpu.make_async_remote_copy(
@@ -1084,7 +1104,7 @@
             for rs in halves(rows):
                 grad_y = g_ref[rs, :].astype(F32)
                 u = u_ref[rs, :].astype(F32)
-                grad_c = norm_back(grad_y, u, r_ref[rs, 0:1], vec_w[4:5])
+                grad_c = norm_back(grad_y, u, r_ref[rs, 0:1], vec_w[4])
                 gacc_ref[rs, :] = grad_c
                 low_ref[0, rs, :] = grad_c.astype(BF)
                 for index, values in enumerate((grad_y * u, grad_y, grad_c)):
@@ -1129,14 +1149,14 @@
                 item.wait()
             for i in range(2):
                 start_w(jnp.int32(i))
-            fill_distance(dist_ref, meta_ref[2])
+            fill_distance(dist_ref, lengths_ref[t * seqs + 1])
             for item in norm_load(1, u1_hbm, r1_hbm):
                 item.wait()
             totals = [jnp.zeros((1, width), F32)] * 3
             for rs in halves(rows):
                 grad_n = gacc_ref[rs, :]
                 u = u_ref[rs, :].astype(F32)
-                grad_a = norm_back(grad_n, u, r_ref[rs, 0:1], vec_w[1:2])
+                grad_a = norm_back(grad_n, u, r_ref[rs, 0:1], vec_w[1])
                 low_ref[1, rs, :] = grad_a.astype(BF)
                 gacc_ref[rs, :] = grad_a
                 for index, values in enumerate((grad_n * u, grad_n, grad_a)):
@@ -1177,7 +1197,7 @@
                     here = slice(head * HD, (head + 1) * HD)
                     gm = gm2[:, here]
                     scores = dot(key2[:, here], query2[:, here], NT)
-                    scores = scores - dist_ref[...] * slope_ref[i * PER + pair * 2 + head]
+                    scores = scores - dist_ref[...] * slope_of(slope_ref, i * PER + pair * 2 + head)
                     likely = jnp.exp(scores - lse_ref[at, pl.ds(pair * 2 + head, 1), :])
                     parts.append(dot(likely.astype(BF), gm).astype(BF))
                     tt = likely * dot(value2[:, here], gm, NT)
@@ -1215,16 +1235,8 @@
                 for item in write_heads(i):
                     item.start()
 
-        ends = [(g_ref, gxl_out), (gacc_ref, gx_out)]
-
-        def end_unit():
-            for i in (2 * heads_steps - 2, 2 * heads_steps - 1):
-                for item in write_heads(jnp.int32(i)):
-                    item.wait()
-            g_ref[...] = gacc_ref[...].astype(BF)
-            for index, item in enumerate(ends):
-                copy(*item, e_sem.at[index]).start()
-            vec[0, 0:6] += part_sums[0:6]
+        def add_sums(norm_part, ub_part, qv_part):
+            vec[0, 0:6] += norm_part[0:6]
             for own in range(2):
                 @pl.when(t == own)
                 def _(own=own):
@@ -1234,23 +1246,37 @@
                             for j in range(up_rows):
                                 at = 6 + (2 * n + place) * up_rows + j
                                 start = side * units + j * width
-                                vec[0, at : at + 1] += ub_sums[n : n + 1, start : start + width]
+                                vec[0, at : at + 1] += ub_part[n : n + 1, start : start + width]
                             at = 6 + 4 * up_rows + n
                             cols = slice(place * local, (place + 1) * local)
-                            vec[0, at : at + 1, cols] += qv_sums[n : n + 1, side * local : (side + 1) * local]
-
+                            vec[0, at : at + 1, cols] += qv_part[n : n + 1, side * local : (side + 1) * local]
+
+        ends = [(g_ref, gxl_out), (gacc_ref, gx_out)]
+
+        def end_unit():
+            for i in (2 * heads_steps - 2, 2 * heads_steps - 1):
+                for item in write_heads(jnp.int32(i)):
+                    item.wait()
+            g_ref[...] = gacc_ref[...].astype(BF)
+            for index, item in enumerate(ends):
+                copy(*item, e_sem.at[index]).start()
+            add_sums(part_sums, ub_sums, qv_sums)
             for index, item in enumerate(ends):
                 copy(*item, e_sem.at[index]).wait()
 
-        vec_load = copy(sums_ref, vec.at[0], v_load)
-        vec_load.start()
+        vec[0] = jnp.zeros(vec_shape, F32)
 
         @pl.when(first)
         def _():
             begin()
+            add_sums(*sum_refs[:3])
+
+        @pl.when(section == 1)
+        def _():
+            add_sums(*sum_refs[3:6])
+            add_sums(*sum_refs[6:9])
 
         take_left(0, 0, 0)
-        vec_load.wait()
         vec_core = remote(vec.at[0], vec_in.at[0], v_send.at[0], v_recv.at[0], core)
         vec_cross = remote(vec.at[1], vec_in.at[1], v_send.at[1], v_recv.at[1], cross)
 
@@ -1469,7 +1495,7 @@
     shapes = [(sum(g == index for g in group_of), width, rights[group_of.index(index)].shape[2] // 2) for index in range(4)]
     return pl.pallas_call(
         kernel,
-        in_specs=[SMEM, SMEM, WHOLE] + [ANY] * 33,
+        in_specs=[SMEM, SMEM] + NORM_SPECS + [WHOLE] * 9 + [ANY] * 32,
         out_specs=[ANY] * 4 + [WHOLE] + [ANY] * 8,
         out_shape=[jax.ShapeDtypeStruct(s, BF) for s in shapes]
         + [jax.ShapeDtypeStruct(vec_shape, F32), jax.ShapeDtypeStruct((seqs, shard_rows, width), BF)]
@@ -1506,17 +1532,18 @@
             pltpu.VMEM((2, 2 * local), F32),
             sem((ring,)), sem((2,)), sem((gives,)), sem((total,)), sem, sem((total,)),
             sem((2,)), sem((2, total)), sem((2,)), sem((2, total)),
-            sem, sem, sem, sem, sem((chips + 1,)), sem((chips + 1,)), sem((seqs,)), sem((seqs,)),
+            sem, sem, sem, sem((chips + 1,)), sem((chips + 1,)), sem((seqs,)), sem((seqs,)),
             sem((3,)), sem((2, 6)), sem((2, 3)), sem((2,)),
         ],
-        input_output_aliases={8: 6, 9: 7},
+        input_output_aliases={20: 6, 21: 7},
         compiler_params=pltpu.CompilerParams(
             collective_id=0, has_side_effects=True, vmem_limit_bytes=67_000_000
         ),
         cost_estimate=pl.CostEstimate(flops=flops, bytes_accessed=100 << 20, transcendentals=0),
         name="backward_and_reduce",
     )(
-        meta, slopes, vecs, grad, q, k_, v, lse, act, slope, u1, u2, r1, r2, *weights, *lefts, *rights, sums, low_grad, second
+        lengths, slopes, *norms, *sums, grad, q, k_, v, lse, act, slope, u1, u2, r1, r2, *weights, *lefts, *rights,
+        low_grad, second
     )
 
 
@@ -1580,7 +1607,7 @@
             jobs += [(index, part, at, step, columns) for part in range(lead) for at in range(0, depth, step)]
     jobs += [(n, m, 0, shard_rows, width) for m in range(seqs)] + [(n + 1, m, 0, shard_rows, width) for m in range(seqs)]
     jobs += [(n + 2, m, 0, shard_rows, width) for m in range(2 * seqs)]
-    ring = 3
+    ring = 5
     n_in = n + 3 * seqs + 4
     parts = units // width
 
@@ -1665,20 +1692,17 @@
                 arrived(wide_rows.at[part], in_sem.at[s])
             else:
                 arrived(low[rows, columns].at[s], in_sem.at[s])
-            if number >= ring and jobs[number - ring][0] != n + 2:
+            if number >= ring:
                 store(number - ring).wait()
             if index == n - 1:
                 wide[rows, columns][s] = low[rows, columns][s].astype(F32).T
             elif index not in (n, n + 2):
                 wide[rows, columns][s] = low[rows, columns][s].astype(F32)
             store(number).start()
-            if index == n + 2:
-                store(number).wait()
             if number + ring < len(jobs):
                 load(number + ring)
         for number in range(len(jobs) - ring, len(jobs)):
-            if jobs[number][0] != n + 2:
-                store(number).wait()
+            store(number).wait()
 
     shapes = sorted({(j[3], j[4]) for j in jobs if j[0] != n})
     square = (reduced[-1].shape[1] // 2, reduced[-1].shape[2])
@@ -2148,37 +2172,30 @@
     up_own = w_up[0]
     down_own = w_down[0]
     first = section == 0
-    vecs = jnp.stack(
-        [b_out[0], ln_gain[0, 0], ln_bias[0, 0], b_down[0], ln_gain[0, 1], ln_bias[0, 1], b_out[0], b_out[0]]
-    ).astype(F32)
-    slope_table = np.exp2(-8.0 * (np.arange(2 * heads, dtype=np.float32) + 1.0) / H).astype(np.float32)
-    slopes = jnp.where(place == 0, slope_table, np.roll(slope_table, heads))
-    own_lengths = lax.dynamic_slice_in_dim(lengths, place * seqs, seqs, 0)
-
-    def meta(m, turn):
-        active = section == turn
-        return jnp.stack([jnp.int32(m), active.astype(jnp.int32), own_lengths[m], own_lengths[m] if turn == 1 else jnp.int32(rows)])
-
-    metas = [[meta(m, turn) for m in range(seqs)] for turn in range(2)]
-    qkv_oth, out_oth, up_oth, down_oth, bias, up_bias, *rest = fetch_and_forward(
+    norms = (b_out, ln_gain[0], ln_bias[0], b_down)
+    table = np.exp2(-8.0 * (np.arange(2 * heads, dtype=np.float32) + 1.0) / H).astype(np.float32)
+    slopes = jnp.asarray(np.concatenate([table, np.roll(table, heads)]))
+
+    qkv_oth, out_oth, up_oth, down_oth, *rest = fetch_and_forward(
         (qkv_own, out_own, up_own, down_own),
         (b_qv[0], b_up[0]),
         inputs,
         cotangent,
         slopes,
-        vecs,
-        metas[0][0],
+        norms,
+        lengths,
         chips,
         seqs,
     )
     weights = (qkv_own, qkv_oth, out_own, out_oth, up_own, up_oth, down_own, down_oth)
+    biases, rest = rest[:2], rest[2:]
     x_first = outer = rest[:seqs]
     *kept, y = rest[seqs:]
     deps = [y]
 
     def forward(x, m, turn):
         nonlocal kept, deps
-        *kept, y = layer_forward(x, weights, bias, slopes, vecs, up_bias, metas[turn][m], kept, deps, seqs)
+        *kept, y = layer_forward(x, weights, biases, slopes, norms, lengths, m, turn, kept, deps, seqs)
         deps = [y]
         return y
 
@@ -2196,7 +2213,7 @@
 
     def backward(grad, m, turn, *extra):
         nonlocal back, deps, got_second
-        results = layer_backward(grad, kept, weights, slopes, vecs, metas[turn][m], back, deps, seqs, *extra)
+        results = layer_backward(grad, kept, weights, slopes, norms, lengths, m, turn, back, deps, seqs, *extra)
         back, (gx, gx_low, norm_sums, up_sums, qv_sums) = results[:7], results[7:12]
         if extra:
             got_second = results[12]
@@ -2205,24 +2222,14 @@
         return gx, gx_low
 
     gx_second = [backward(outer[0], 0, 1)]
-    gx_second.append(backward(outer[1], 1, 1, 1, 1, [*y_second, gx_second[0][1]]))
+    gx_second.append(backward(outer[1], 1, 1, [*y_second, gx_second[0][1]]))
     grad_middle = [lax.ppermute(gx_second[m][1], "section", [(1, 0)]) for m in range(seqs)]
     x_all = jnp.stack([jnp.where(first, x_first[m], x_second[m]) for m in range(seqs)])
     deps = deps + [x_all]
     gx_first = [backward(grad_middle[0], 0, 0)]
 
-    norm_sums, up_sums, qv_sums = [
-        jnp.where(first, sums[0][0][index], sum(item[index] for item in sums[1])) for index in range(3)
-    ]
-
-    def ordered(values, count):
-        return jnp.where(
-            place == 0, values, jnp.concatenate([values[:, count:], values[:, :count]], axis=1)
-        ).reshape(-1, width)
-
-    packed = jnp.concatenate([norm_sums[:6], ordered(up_sums[:2], units), ordered(qv_sums[:2], local)])
     *reduced, packed, got, _, _, _, _, _, gx, _ = backward_and_reduce(
-        grad_middle[1], kept, back, x_all, weights, slopes, vecs, metas[0][1], packed, gx_first[0][1],
+        grad_middle[1], kept, back, x_all, weights, slopes, norms, lengths, [*sums[0][0], *sums[1][0], *sums[1][1]], gx_first[0][1],
         gx_second[1][1], chips,
     )
     gx_all = [gx_first[0][0], gx] + [g[0] for g in gx_second]

time: 663 us -> 666 us (level)
  other arithmetic: 10.9 us -> 1.74 us
  waiting for transfers between devices: 85.5 us -> 93.8 us
  Pallas kernels: 546 us -> 553 us
    ppermute x2, waiting for transfers between devices: 85.5 us -> 93.8 us  [by_sequence(): lax.ppermute(gx_second[m][1], 'section', [(1, 0)])]
    pallas_call x2, Pallas kernels: 396 us -> 404 us  [the longest x1 254 us: backward_and_reduce(): pl.pallas_call(kernel, in_specs=[SMEM, SMEM] + NORM_SPECS + [WHOLE] * 9 +...]
  transfers between devices with their start and end apart: 4 -> 4, of which waited for: 1 -> 2; matrix products, arithmetic and copies ran while one was open for 1% -> 0% of each run, Pallas kernels for 18% -> 18%
where the time goes in v11:
time: 666 us; the launch traced here: 658 us
  Pallas kernels  553 us (83%)
  waiting for transfers between devices  93.8 us (14%)
    pallas_call x1, Pallas kernels, backward_and_reduce(): pl.pallas_call(kernel, in_specs=[SMEM, SMEM] + NORM_SPECS + [WHOLE] * 9 +...  254 us
    pallas_call x1, Pallas kernels, fetch_and_forward(): pl.pallas_call(kernel, in_specs=[SMEM, SMEM] + NORM_SPECS + [ANY] * 8, ou...  150 us
    pallas_call x6, Pallas kernels, call(): pl.pallas_call(body, in_specs=specs, out_specs=[ANY] * n_out, out_shape=[...  102 us
    ppermute x2, waiting for transfers between devices, by_sequence(): lax.ppermute(gx_second[m][1], 'section', [(1, 0)])  93.8 us
    pallas_call x1, Pallas kernels, exchange_rows(): pl.pallas_call(kernel, in_specs=[ANY] * n_in, out_specs=ANY, out_shape=ja...  25.8 us
    pallas_call x1, Pallas kernels, widen(): pl.pallas_call(kernel, in_specs=[ANY] * (n_in - 1) + [WHOLE], out_specs=[...  22.1 us
  transfers between devices with their start and end apart: 4, of which 2 were waited for; matrix products, arithmetic and copies ran while one was open for 0% of the time, Pallas kernels for 18%

profile of v11, /device:TPU:0, one launch (start us, length us, event | category | flops | bytes accessed | tf_op | source)
XLA Modules:
  0.0 657.6 jit_solution(5189697904374823601)
XLA Ops:
  0.6 149.6 %fetch_and_forward.1 = (bf16[3,1024,512]{2,1,0:T(8,128)(2,1)}, bf16[512,1024]{1,0:T(8,128)(2,1)}, bf16[2,1024,2048]{2,1,0:T(8,128)(2,1)}, bf16[1024,2048]{1,0:T(...) custom-call(s32[4]{0:T(128)} %refs_0_.15, ...), custom_call_target="tpu_custom_call" | custom-call | flops 18253611008 | bytes 94371840 | tf_op jit(solution)/shard_map/fetch_and_forward/pallas_call | solution.py:907
  150.2 1.4 collective-permute-start.1
  151.6 38.6 %layer_forward.3 = (bf16[2,512,1024]{2,1,0:T(8,128)(2,1)}, bf16[2,512,1024]{2,1,0:T(8,128)(2,1)}, bf16[2,512,1024]{2,1,0:T(8,128)(2,1)}, bf16[2,512,1024]{2,1,0:...) custom-call(s32[4]{0:T(128)} %refs_0_.15, ...), custom_call_target="tpu_custom_call", output_to_operand_aliasing={{0}: (17, {}), {1}: (18, {}), {2}: (19, {}), {3}: (20, {}),... | custom-call | flops 18253611008 | bytes 56623104 | tf_op jit(solution)/shard_map/layer_forward/pallas_call | solution.py:56
  190.1 2.3 collective-permute-start
  192.4 0.0 collective-permute-done.1.refs_1_
  192.4 0.0 copy-start.1
  192.4 1.0 copy-done.1
  193.4 1.3 layer_forward.4
  194.7 25.8 %exchange_rows.1.refs_30_.refs_10_ = bf16[4,256,1024]{2,1,0:T(8,128)(2,1)} custom-call(bf16[512,1024]{1,0:T(8,128)(2,1)} %get-tuple-element.153.refs_30_.refs_0_, bf16[512,1024]{1,0:T(8,128)(2,1)} %get-tuple-element.154.refs_30_.refs_1_, bf16[512,1024]{1,0:T(8,128)(2,1)} %get-tuple-element.181.refs_2_.refs_25_.refs_11_), custom_call_target="tpu_custom_call" | custom-call | tf_op jit(solution)/shard_map/exchange_rows/pallas_call | solution.py:1584
  220.5 0.0 collective-permute-done.refs_1_
  220.5 1.4 layer_forward.5
  222.0 7.2 %layer_backward.3 = (bf16[2,512,4096]{2,1,0:T(8,128)(2,1)}, bf16[2,512,4096]{2,1,0:T(8,128)(2,1)}, bf16[2,512,1024]{2,1,0:T(8,128)(2,1)}, bf16[2,512,1024]{2,1,0...) custom-call(s32[4]{0:T(128)} %refs_0_.15, ...), custom_call_target="tpu_custom_call" | custom-call | flops 19864223744 | bytes 73400320 | tf_op jit(solution)/shard_map/layer_backward/pallas_call | solution.py:56
  229.2 1.3 collective-permute-start.2
  230.5 0.0 copy-start
  230.5 5.7 layer_backward.4
  236.3 0.0 copy-start.2
  236.3 0.0 copy-start.3
  236.3 1.4 collective-permute-start.3
  237.7 0.0 copy-done
  237.8 0.1 select_bitcast_fusion
  237.9 0.0 copy-done.2
  237.9 0.0 copy-done.3
  237.9 0.1 select_bitcast_fusion.1
  238.0 1.5 pad_maximum_fusion.refs_33_.refs_36_
  239.5 89.8 %collective-permute-done.2.refs_1_ = bf16[512,1024]{1,0:T(8,128)(2,1)} collective-permute-done((bf16[512,1024]{1,0:T(8,128)(2,1)}, bf16[512,1024]{1,0:T(8,128)(2,1)}, u32[]{:S(2)}, u32[]{:S(2)}) %collective-permute-start.2) | collective-permute-done | bytes 1048608 | tf_op jit(solution)/shard_map/ppermute | solution.py:2226
  329.4 47.3 %layer_backward.5 = (bf16[2,512,4096]{2,1,0:T(8,128)(2,1)}, bf16[2,512,4096]{2,1,0:T(8,128)(2,1)}, bf16[2,512,1024]{2,1,0:T(8,128)(2,1)}, bf16[2,512,1024]{2,1,0...) custom-call(s32[4]{0:T(128)} %refs_0_.15, ...), custom_call_target="tpu_custom_call", output_to_operand_aliasing={{0}: (25, {}), {1}: (26, {}), {2}: (27, {}), {3}: (28, {}),... | custom-call | flops 19864223744 | bytes 73400320 | tf_op jit(solution)/shard_map/layer_backward/pallas_call | solution.py:56
  376.6 3.9 collective-permute-done.3.refs_15_
  380.5 254.4 %backward_and_reduce.1 = (bf16[1,1024,2048]{2,1,0:T(8,128)(2,1)}, bf16[2,1024,2048]{2,1,0:T(8,128)(2,1)}, bf16[3,1024,512]{2,1,0:T(8,128)(2,1)}, bf16[1,1024,512...) custom-call(s32[4]{0:T(128)} %refs_0_.15, ...), custom_call_target="tpu_custom_call", output_to_operand_aliasing={{6}: (20, {}), {7}: (21, {})} | custom-call | flops 34359738368 | bytes 104857600 | tf_op jit(solution)/shard_map/backward_and_reduce/pallas_call | solution.py:1496
  635.0 22.1 %widen.1 = (f32[1,1024,2048]{2,1,0:T(8,128)}, f32[2,1024,2048]{2,1,0:T(8,128)}, f32[3,1024,512]{2,1,0:T(8,128)}, f32[512,1024]{1,0:T(8,128)}, f32[4,256,1024]{2,...) custom-call(bf16[1,1024,2048]{2,1,0:T(8,128)(2,1)} %get-tuple-elemen, ...), custom_call_target="tpu_custom_call" | custom-call | bytes 58720256 | tf_op jit(solution)/shard_map/widen/pallas_call | solution.py:1714
Async XLA Ops:
  150.2 42.2 %collective-permute-start.1 = (bf16[512,1024]{1,0:T(8,128)(2,1)}, bf16[512,1024]{1,0:T(8,128)(2,1)S(1)}, u32[]{:S(2)}, u32[]{:S(2)}) collective-permute-start(bf16[512,1024]{1,0:T(8,128)(2,1)} %get-tuple-element.153.refs_30_.refs_0_), channel_id=1, source_target_pairs={{0,16},{1,17},{2,18},{3,19},{4,20},{5,21},{6,22},{7,23},{8,24},{9,... | collective-permute-start | bytes 3145736 | tf_op jit(solution)/shard_map/ppermute | solution.py:2203
  190.1 30.4 %collective-permute-start = (bf16[512,1024]{1,0:T(8,128)(2,1)}, bf16[512,1024]{1,0:T(8,128)(2,1)}, u32[]{:S(2)}, u32[]{:S(2)}) collective-permute-start(bf16[512,1024]{1,0:T(8,128)(2,1)} %get-tuple-element.154.refs_30_.refs_1_), channel_id=1, source_target_pairs={{0,16},{1,17},{2,18},{3,19},{4,20},{5,21},{6,22},{7,23},{8,24},{9,... | collective-permute-start | bytes 3145736 | tf_op jit(solution)/shard_map/ppermute | solution.py:2203
  192.4 1.0 copy-start.1
  229.2 100.1 %collective-permute-start.2 = (bf16[512,1024]{1,0:T(8,128)(2,1)}, bf16[512,1024]{1,0:T(8,128)(2,1)}, u32[]{:S(2)}, u32[]{:S(2)}) collective-permute-start(bf16[512,1024]{1,0:T(8,128)(2,1)} %get-tuple-element.193.refs_27_), channel_id=1, source_target_pairs={{16,0},{17,1},{18,2},{19,3},{20,4},{21,5},{22,6},{23,7},{24,8},{25... | collective-permute-start | bytes 3145736 | tf_op jit(solution)/shard_map/ppermute | solution.py:2226
  230.5 7.2 %copy-start = (bf16[512,1024]{1,0:T(8,128)(2,1)S(1)}, bf16[512,1024]{1,0:T(8,128)(2,1)}, u32[]{:S(2)}) copy-start(bf16[512,1024]{1,0:T(8,128)(2,1)} %get-tuple-element.133.refs_1_) | copy-start | bytes 3145732
  236.3 1.6 copy-start.2
  236.3 1.6 copy-start.3
  236.3 144.2 %collective-permute-start.3 = (bf16[512,1024]{1,0:T(8,128)(2,1)}, bf16[512,1024]{1,0:T(8,128)(2,1)}, u32[]{:S(2)}, u32[]{:S(2)}) collective-permute-start(bf16[512,1024]{1,0:T(8,128)(2,1)} %get-tuple-element.217.refs_46_), channel_id=1, source_target_pairs={{16,0},{17,1},{18,2},{19,3},{20,4},{21,5},{22,6},{23,7},{24,8},{25... | collective-permute-start | bytes 3145736 | tf_op jit(solution)/shard_map/ppermute | solution.py:2226

commit v12 on v11

--- a/solution.py
+++ b/solution.py
@@ -637,13 +637,10 @@
     QKV, OUT, UP, DOWN, ROWS, BIAS = range(6)
 
     plan = [(UP, 0, groups), (ROWS, 0, 0), (BIAS, 0, 0), (BIAS, 1, 0)]
-    for part in range(1, tiles):
-        plan.append((UP, part, groups))
-        if part <= 3:
-            plan.append((QKV, part - 1, 2))
-    plan += [(DOWN, 0, groups), (OUT, 0, 2)]
-    plan += [(DOWN, part, groups) for part in range(1, tiles - 1)]
-    plan += [(DOWN, tiles - 1, 2)]
+    plan += [(UP, part, groups) for part in range(1, tiles)]
+    plan += [(DOWN, part, groups) for part in range(tiles - 2)]
+    plan += [(QKV, part, 2) for part in range(3)] + [(OUT, 0, 2)]
+    plan += [(DOWN, part, 2) for part in range(tiles - 2, tiles)]
     plan += [(ROWS, part, 0) for part in range(1, seqs)]
     n = len(plan)
     number = {item[:2]: index for index, item in enumerate(plan)}
@@ -656,11 +653,11 @@
     events, clock, busy = [], 0.0, 0.0
     for index, (kind, part, pieces) in enumerate(plan):
         clock += size(index)
-        events.append((clock, index, 0))
+        events.append((clock + 66000, index, 0))
         if pieces == groups:
             start = max(clock, busy)
-            busy = start + size(index) * (chips - 1)
-            events += [(start + size(index) * hop * 1.001, index, hop) for hop in range(1, chips)]
+            busy = start + size(index) * (chips - 1) * 1.0
+            events += [(start + (size(index) * 1.0 + 66000) * hop, index, hop) for hop in range(1, chips)]
     events.sort()
     when = {event[1:]: event[0] for event in events}
 
@@ -965,7 +962,9 @@
     x_flip, ga_flip = ffn_blocks - per_pair, ffn_blocks + per_pair
     up_rows = units // width
     vec_shape = (6 + 4 * up_rows + 2, width)
-    assert ahead_of + ffn_blocks - ring > end_at
+    spread = 41
+    last_turn = ahead_of - (ahead_of - end_at) * spread // (end_at + 1 - ahead_of) + 1
+    assert spread >= end_at + 1 - ahead_of and last_turn < ahead_of + ffn_blocks - ring
 
     def kernel(*refs):
         lengths_ref, slope_ref, norm_refs, sum_refs = refs[0], refs[1], refs[2:6], refs[6:15]
@@ -1292,6 +1291,10 @@
                 def _(m=m, source=source):
                     row_copy(m, source).start()
 
+        def unit_at(turn):
+            later = ahead_of + (turn - ahead_of) * (end_at + 1 - ahead_of) // spread
+            return jnp.where(turn < ahead_of, turn, later)
+
         up = pl.ds(0, quarter)
         down = pl.ds(quarter, quarter)
         sides = ((up, 0, z, above, below), (down, 1, last - z, below, above))
@@ -1300,21 +1303,23 @@
         def _(turn):
             s = turn - ahead_of
 
-            @pl.when(first)
-            def _():
-                @pl.when(turn < norm_at)
+            unit = unit_at(turn)
+
+            @pl.when(first & (unit != unit_at(turn - 1)))
+            def _():
+                @pl.when(unit < norm_at)
                 def _():
-                    ffn_unit(turn)
-
-                @pl.when(turn == norm_at)
+                    ffn_unit(unit)
+
+                @pl.when(unit == norm_at)
                 def _():
                     norm_unit()
 
-                @pl.when((turn >= head_at) & (turn < end_at))
+                @pl.when((unit >= head_at) & (unit < end_at))
                 def _():
-                    head_unit(turn - head_at)
-
-                @pl.when(turn == end_at)
+                    head_unit(unit - head_at)
+
+                @pl.when(unit == end_at)
                 def _():
                     end_unit()
 
@@ -1366,14 +1371,14 @@
                 arrived(acc.at[k1], core_recv.at[k1])
                 at = lax.rem(k1, mines)
                 for side in range(2):
-                    acc[k1, side] = (acc[k1, side].astype(F32) + mine[at, side].astype(F32)).astype(BF)
+                    acc[k1, side] = acc[k1, side] + mine[at, side]
 
             k2 = k1 - CROSS_LAG
 
             @pl.when(valid(k2))
             def _():
                 arrived(from_x.at[k2], x_recv.at[k2])
-                acc[k2, 1] = (acc[k2, 1].astype(F32) + from_x[k2].astype(F32)).astype(BF)
+                acc[k2, 1] = acc[k2, 1] + from_x[k2]
 
             for rows_, way, place, ahead, behind in sides:
                 k3 = k2 - CHAIN_LAG * place
@@ -1381,7 +1386,7 @@
                 @pl.when(valid(k3) & (place > 0))
                 def _(rows_=rows_, way=way, k3=k3):
                     arrived(from_z.at[k3, rows_], z_recv.at[way, k3])
-                    acc[k3, 1, rows_] = (acc[k3, 1, rows_].astype(F32) + from_z[k3, rows_].astype(F32)).astype(BF)
+                    acc[k3, 1, rows_] = acc[k3, 1, rows_] + from_z[k3, rows_]
 
                 k4 = k2 - CHAIN_LAG * (2 * last - place)
 
@@ -1432,25 +1437,25 @@
 
                 member(k5, visit)
 
-            @pl.when(turn == end_at + 1)
+            @pl.when(turn == last_turn + 1)
             def _():
                 vec_core.start()
 
-            @pl.when(turn == end_at + 6)
+            @pl.when(turn == last_turn + 6)
             def _():
                 vec_core.wait_recv()
                 vec[1] = vec[0] + vec_in[0]
 
-            @pl.when(turn == end_at + 7)
+            @pl.when(turn == last_turn + 7)
             def _():
                 vec_cross.start()
 
-            @pl.when(turn == end_at + 13)
+            @pl.when(turn == last_turn + 13)
             def _():
                 vec_cross.wait_recv()
                 vec_all[z] = vec[1] + vec_in[1]
 
-            @pl.when(turn == end_at + 14)
+            @pl.when(turn == last_turn + 14)
             def _():
                 for shift in range(1, chips):
                     to = lax.rem(z + shift, chips)

time: 666 us -> 650 us (0.976)
  Pallas kernels: 553 us -> 537 us
    pallas_call x1, Pallas kernels: 150 us -> 138 us  [fetch_and_forward(): pl.pallas_call(kernel, in_specs=[SMEM, SMEM] + NORM_SPECS + [ANY] * 8, ou...]
  transfers between devices with their start and end apart: 4 -> 4, of which waited for: 2 -> 2; matrix products, arithmetic and copies ran while one was open for 0% -> 0% of each run, Pallas kernels for 18% -> 19%
where the time goes in v12:
time: 650 us; the launch traced here: 641 us
  Pallas kernels  537 us (83%)
  waiting for transfers between devices  93.7 us (14%)
    pallas_call x1, Pallas kernels, backward_and_reduce(): pl.pallas_call(kernel, in_specs=[SMEM, SMEM] + NORM_SPECS + [WHOLE] * 9 +...  250 us
    pallas_call x1, Pallas kernels, fetch_and_forward(): pl.pallas_call(kernel, in_specs=[SMEM, SMEM] + NORM_SPECS + [ANY] * 8, ou...  138 us
    pallas_call x6, Pallas kernels, call(): pl.pallas_call(body, in_specs=specs, out_specs=[ANY] * n_out, out_shape=[...  102 us
    ppermute x2, waiting for transfers between devices, by_sequence(): lax.ppermute(gx_second[m][1], 'section', [(1, 0)])  93.7 us
    pallas_call x1, Pallas kernels, exchange_rows(): pl.pallas_call(kernel, in_specs=[ANY] * n_in, out_specs=ANY, out_shape=ja...  25.8 us
    pallas_call x1, Pallas kernels, widen(): pl.pallas_call(kernel, in_specs=[ANY] * (n_in - 1) + [WHOLE], out_specs=[...  22.1 us
  transfers between devices with their start and end apart: 4, of which 2 were waited for; matrix products, arithmetic and copies ran while one was open for 0% of the time, Pallas kernels for 19%

profile of v12, /device:TPU:0, one launch (start us, length us, event | category | flops | bytes accessed | tf_op | source)
XLA Modules:
  0.0 641.4 jit_solution(5366524482099427873)
XLA Ops:
  0.6 137.9 %fetch_and_forward.1 = (bf16[3,1024,512]{2,1,0:T(8,128)(2,1)}, bf16[512,1024]{1,0:T(8,128)(2,1)}, bf16[2,1024,2048]{2,1,0:T(8,128)(2,1)}, bf16[1024,2048]{1,0:T(...) custom-call(s32[4]{0:T(128)} %refs_0_.15, ...), custom_call_target="tpu_custom_call" | custom-call | flops 18253611008 | bytes 94371840 | tf_op jit(solution)/shard_map/fetch_and_forward/pallas_call | solution.py:904
  138.5 1.4 collective-permute-start.1
  139.9 38.6 %layer_forward.3 = (bf16[2,512,1024]{2,1,0:T(8,128)(2,1)}, bf16[2,512,1024]{2,1,0:T(8,128)(2,1)}, bf16[2,512,1024]{2,1,0:T(8,128)(2,1)}, bf16[2,512,1024]{2,1,0:...) custom-call(s32[4]{0:T(128)} %refs_0_.15, ...), custom_call_target="tpu_custom_call", output_to_operand_aliasing={{0}: (17, {}), {1}: (18, {}), {2}: (19, {}), {3}: (20, {}),... | custom-call | flops 18253611008 | bytes 56623104 | tf_op jit(solution)/shard_map/layer_forward/pallas_call | solution.py:56
  178.4 2.3 collective-permute-start
  180.7 0.0 collective-permute-done.1.refs_1_
  180.7 0.0 copy-start.1
  180.7 1.0 copy-done.1
  181.7 1.3 layer_forward.4
  183.0 25.8 %exchange_rows.1.refs_30_.refs_10_ = bf16[4,256,1024]{2,1,0:T(8,128)(2,1)} custom-call(bf16[512,1024]{1,0:T(8,128)(2,1)} %get-tuple-element.153.refs_30_.refs_0_, bf16[512,1024]{1,0:T(8,128)(2,1)} %get-tuple-element.154.refs_30_.refs_1_, bf16[512,1024]{1,0:T(8,128)(2,1)} %get-tuple-element.181.refs_2_.refs_25_.refs_11_), custom_call_target="tpu_custom_call" | custom-call | tf_op jit(solution)/shard_map/exchange_rows/pallas_call | solution.py:1589
  208.9 0.0 collective-permute-done.refs_1_
  208.9 1.4 layer_forward.5
  210.3 7.2 %layer_backward.3 = (bf16[2,512,4096]{2,1,0:T(8,128)(2,1)}, bf16[2,512,4096]{2,1,0:T(8,128)(2,1)}, bf16[2,512,1024]{2,1,0:T(8,128)(2,1)}, bf16[2,512,1024]{2,1,0...) custom-call(s32[4]{0:T(128)} %refs_0_.15, ...), custom_call_target="tpu_custom_call" | custom-call | flops 19864223744 | bytes 73400320 | tf_op jit(solution)/shard_map/layer_backward/pallas_call | solution.py:56
  217.6 1.3 collective-permute-start.2
  218.9 0.0 copy-start
  218.9 5.7 layer_backward.4
  224.6 0.0 copy-start.2
  224.6 0.0 copy-start.3
  224.7 1.4 collective-permute-start.3
  226.1 0.0 copy-done
  226.1 0.1 select_bitcast_fusion
  226.2 0.0 copy-done.2
  226.2 0.0 copy-done.3
  226.2 0.1 select_bitcast_fusion.1
  226.4 1.5 pad_maximum_fusion.refs_33_.refs_36_
  227.9 89.8 %collective-permute-done.2.refs_1_ = bf16[512,1024]{1,0:T(8,128)(2,1)} collective-permute-done((bf16[512,1024]{1,0:T(8,128)(2,1)}, bf16[512,1024]{1,0:T(8,128)(2,1)}, u32[]{:S(2)}, u32[]{:S(2)}) %collective-permute-start.2) | collective-permute-done | bytes 1048608 | tf_op jit(solution)/shard_map/ppermute | solution.py:2231
  317.7 47.3 %layer_backward.5 = (bf16[2,512,4096]{2,1,0:T(8,128)(2,1)}, bf16[2,512,4096]{2,1,0:T(8,128)(2,1)}, bf16[2,512,1024]{2,1,0:T(8,128)(2,1)}, bf16[2,512,1024]{2,1,0...) custom-call(s32[4]{0:T(128)} %refs_0_.15, ...), custom_call_target="tpu_custom_call", output_to_operand_aliasing={{0}: (25, {}), {1}: (26, {}), {2}: (27, {}), {3}: (28, {}),... | custom-call | flops 19864223744 | bytes 73400320 | tf_op jit(solution)/shard_map/layer_backward/pallas_call | solution.py:56
  364.9 3.9 collective-permute-done.3.refs_15_
  368.9 250.0 %backward_and_reduce.1 = (bf16[1,1024,2048]{2,1,0:T(8,128)(2,1)}, bf16[2,1024,2048]{2,1,0:T(8,128)(2,1)}, bf16[3,1024,512]{2,1,0:T(8,128)(2,1)}, bf16[1,1024,512...) custom-call(s32[4]{0:T(128)} %refs_0_.15, ...), custom_call_target="tpu_custom_call", output_to_operand_aliasing={{6}: (20, {}), {7}: (21, {})} | custom-call | flops 34359738368 | bytes 104857600 | tf_op jit(solution)/shard_map/backward_and_reduce/pallas_call | solution.py:1501
  618.8 22.1 %widen.1 = (f32[1,1024,2048]{2,1,0:T(8,128)}, f32[2,1024,2048]{2,1,0:T(8,128)}, f32[3,1024,512]{2,1,0:T(8,128)}, f32[512,1024]{1,0:T(8,128)}, f32[4,256,1024]{2,...) custom-call(bf16[1,1024,2048]{2,1,0:T(8,128)(2,1)} %get-tuple-elemen, ...), custom_call_target="tpu_custom_call" | custom-call | bytes 58720256 | tf_op jit(solution)/shard_map/widen/pallas_call | solution.py:1719
Async XLA Ops:
  138.5 42.2 %collective-permute-start.1 = (bf16[512,1024]{1,0:T(8,128)(2,1)}, bf16[512,1024]{1,0:T(8,128)(2,1)S(1)}, u32[]{:S(2)}, u32[]{:S(2)}) collective-permute-start(bf16[512,1024]{1,0:T(8,128)(2,1)} %get-tuple-element.153.refs_30_.refs_0_), channel_id=1, source_target_pairs={{0,16},{1,17},{2,18},{3,19},{4,20},{5,21},{6,22},{7,23},{8,24},{9,... | collective-permute-start | bytes 3145736 | tf_op jit(solution)/shard_map/ppermute | solution.py:2208
  178.4 30.4 %collective-permute-start = (bf16[512,1024]{1,0:T(8,128)(2,1)}, bf16[512,1024]{1,0:T(8,128)(2,1)}, u32[]{:S(2)}, u32[]{:S(2)}) collective-permute-start(bf16[512,1024]{1,0:T(8,128)(2,1)} %get-tuple-element.154.refs_30_.refs_1_), channel_id=1, source_target_pairs={{0,16},{1,17},{2,18},{3,19},{4,20},{5,21},{6,22},{7,23},{8,24},{9,... | collective-permute-start | bytes 3145736 | tf_op jit(solution)/shard_map/ppermute | solution.py:2208
  180.7 1.0 copy-start.1
  217.6 100.1 %collective-permute-start.2 = (bf16[512,1024]{1,0:T(8,128)(2,1)}, bf16[512,1024]{1,0:T(8,128)(2,1)}, u32[]{:S(2)}, u32[]{:S(2)}) collective-permute-start(bf16[512,1024]{1,0:T(8,128)(2,1)} %get-tuple-element.193.refs_27_), channel_id=1, source_target_pairs={{16,0},{17,1},{18,2},{19,3},{20,4},{21,5},{22,6},{23,7},{24,8},{25... | collective-permute-start | bytes 3145736 | tf_op jit(solution)/shard_map/ppermute | solution.py:2231
  218.9 7.2 %copy-start = (bf16[512,1024]{1,0:T(8,128)(2,1)S(1)}, bf16[512,1024]{1,0:T(8,128)(2,1)}, u32[]{:S(2)}) copy-start(bf16[512,1024]{1,0:T(8,128)(2,1)} %get-tuple-element.133.refs_1_) | copy-start | bytes 3145732
  224.6 1.6 copy-start.2
  224.6 1.6 copy-start.3
  224.7 144.2 %collective-permute-start.3 = (bf16[512,1024]{1,0:T(8,128)(2,1)}, bf16[512,1024]{1,0:T(8,128)(2,1)}, u32[]{:S(2)}, u32[]{:S(2)}) collective-permute-start(bf16[512,1024]{1,0:T(8,128)(2,1)} %get-tuple-element.217.refs_46_), channel_id=1, source_target_pairs={{16,0},{17,1},{18,2},{19,3},{20,4},{21,5},{22,6},{23,7},{24,8},{25... | collective-permute-start | bytes 3145736 | tf_op jit(solution)/shard_map/ppermute | solution.py:2231

commit v13 on v12

--- a/solution.py
+++ b/solution.py
@@ -207,17 +207,22 @@
             self.start_w(i + 2)
 
         parts = []
+        scores_of = []
         for head in range(PER):
             cols = slice(head * HD, (head + 1) * HD)
             query = qkv[s, 0, :, cols] * BF(1.0 / math.sqrt(HD))
-            scores = dot(qkv[s, 1, :, cols], query, NT)
-            scores = scores - self.dist[...] * slope_of(self.slopes, i * PER + head)
+            scores_of.append(dot(qkv[s, 1, :, cols], query, NT))
+        lows = []
+        for head in range(PER):
+            scores = scores_of[head] - self.dist[...] * slope_of(self.slopes, i * PER + head)
             top = jnp.max(scores, axis=0, keepdims=True)
             likely = jnp.exp(scores - top)
             mass = jnp.sum(likely, axis=0, keepdims=True)
-            low = (likely * (1.0 / mass)).astype(BF)
-            parts.append(dot(low, qkv[s, 2, :, cols], TN).astype(BF))
+            lows.append((likely * (1.0 / mass)).astype(BF))
             self.lse[s, head : head + 1, :] = top + jnp.log(mass)
+        for head in range(PER):
+            cols = slice(head * HD, (head + 1) * HD)
+            parts.append(dot(lows[head], qkv[s, 2, :, cols], TN).astype(BF))
         self.mixed[:, block(i, CW)] = jnp.concatenate(parts, axis=1)
         for item in self.write_qkv(i, s):
             item.start()
@@ -506,20 +511,25 @@
 
             gm_ref[...] = dot(low_ref[1], o_ref[s], NT).astype(BF)
             parts = [[], [], []]
+            scores_of = []
+            for head in range(PER):
+                cols = slice(head * HD, (head + 1) * HD)
+                query = qkv_ref[s, 0, :, cols] * scale
+                scores_of.append(dot(qkv_ref[s, 1, :, cols], query, NT))
             for head in range(PER):
                 cols = slice(head * HD, (head + 1) * HD)
                 query = qkv_ref[s, 0, :, cols] * scale
                 key = qkv_ref[s, 1, :, cols]
                 gm = gm_ref[:, cols]
-                scores = dot(key, query, NT)
-                scores = scores - dist_ref[...] * slope_of(slope_ref, i * PER + head)
+                gw = dot(qkv_ref[s, 2, :, cols], gm, NT)
+                scores = scores_of[head] - dist_ref[...] * slope_of(slope_ref, i * PER + head)
                 likely = jnp.exp(scores - lse_ref[s, head : head + 1, :])
                 parts[2].append(dot(likely.astype(BF), gm).astype(BF))
-                t = likely * dot(qkv_ref[s, 2, :, cols], gm, NT)
+                t = likely * gw
                 inner = jnp.sum(t, axis=0, keepdims=True)
                 gs = (t - likely * inner).astype(BF)
                 parts[1].append(dot(gs, query).astype(BF))
-                parts[0].append(dot(gs, key * scale, TN).astype(BF))
+                parts[0].append(dot(key * scale, gs, TN).astype(BF).T)
             for c in range(3):
                 gqkv_ref[s, c] = jnp.concatenate(parts[c], axis=1)
             for index, c in enumerate((0, 2)):
@@ -947,13 +957,13 @@
     member_of = [0, 0, 1, 0, 1, 2, 0]
     half = width // 2
     quarter = half // 2
-    per_pair = 2 * ft // bt
-    pairs = tiles // 2
+    per_pair = ft // bt
+    pairs = tiles
     ffn_blocks = 3 * per_pair * pairs
     head_blocks = local // bt
     total = ffn_blocks + 4 * head_blocks
     ring, mines, gives = 4, CORE_LAG + 1, 4
-    ahead_of = 4
+    ahead_of = 2
     drain = CORE_LAG + CROSS_LAG + 2 * (chips - 1) * CHAIN_LAG + 1
     shard_rows = rows // 2
     norm_at = 2 * tiles
@@ -962,7 +972,7 @@
     x_flip, ga_flip = ffn_blocks - per_pair, ffn_blocks + per_pair
     up_rows = units // width
     vec_shape = (6 + 4 * up_rows + 2, width)
-    spread = 41
+    spread = 42
     last_turn = ahead_of - (ahead_of - end_at) * spread // (end_at + 1 - ahead_of) + 1
     assert spread >= end_at + 1 - ahead_of and last_turn < ahead_of + ffn_blocks - ring
 
@@ -1056,9 +1066,7 @@
                 flip[at, :, m * rows : (m + 1) * rows] = stage[m].T
 
         def place_of(u):
-            within = lax.rem(u, 4)
-            side = within // 2
-            return side, u // 4 * 2 + lax.rem(within, 2)
+            return lax.rem(u, 2), u // 2
 
         def start_f(u):
             at = lax.rem(u, 2)
@@ -1192,11 +1200,11 @@
                 value2 = qkv_ref[at, 2, :, cols]
                 gm2 = gm_ref[:, cols]
                 parts = []
-                for head in range(2):
-                    here = slice(head * HD, (head + 1) * HD)
+                pairs_here = [slice(head * HD, (head + 1) * HD) for head in range(2)]
+                scores_of = [dot(key2[:, here], query2[:, here], NT) for here in pairs_here]
+                for head, here in enumerate(pairs_here):
                     gm = gm2[:, here]
-                    scores = dot(key2[:, here], query2[:, here], NT)
-                    scores = scores - dist_ref[...] * slope_of(slope_ref, i * PER + pair * 2 + head)
+                    scores = scores_of[head] - dist_ref[...] * slope_of(slope_ref, i * PER + pair * 2 + head)
                     likely = jnp.exp(scores - lse_ref[at, pl.ds(pair * 2 + head, 1), :])
                     parts.append(dot(likely.astype(BF), gm).astype(BF))
                     tt = likely * dot(value2[:, here], gm, NT)
@@ -1213,7 +1221,7 @@
                     here = slice(head * HD, (head + 1) * HD)
                     gs = gs_ref[head]
                     parts[1].append(dot(gs, query2[:, here]).astype(BF))
-                    parts[0].append(dot(gs, key2[:, here], TN).astype(BF))
+                    parts[0].append(dot(key2[:, here], gs, TN).astype(BF).T)
                 for n in range(2):
                     gqkv_ref[at, n, :, cols] = jnp.concatenate(parts[n], axis=1)
 
@@ -1330,7 +1338,7 @@
 
             @pl.when(valid(s))
             def _():
-                @pl.when(s == per_pair - 2)
+                @pl.when(s == per_pair - 1)
                 def _():
                     take_left(1, 1, None)
 

time: 650 us -> 633 us (0.974)
  Pallas kernels: 537 us -> 525 us
  transfers between devices with their start and end apart: 4 -> 4, of which waited for: 2 -> 2; matrix products, arithmetic and copies ran while one was open for 0% -> 0% of each run, Pallas kernels for 19% -> 18%
where the time goes in v13:
time: 633 us; the launch traced here: 625 us
  Pallas kernels  525 us (83%)
  waiting for transfers between devices  89.5 us (14%)
  starting transfers between devices  6.36 us (1%)
    pallas_call x1, Pallas kernels, backward_and_reduce(): pl.pallas_call(kernel, in_specs=[SMEM, SMEM] + NORM_SPECS + [WHOLE] * 9 +...  245 us
    pallas_call x1, Pallas kernels, fetch_and_forward(): pl.pallas_call(kernel, in_specs=[SMEM, SMEM] + NORM_SPECS + [ANY] * 8, ou...  136 us
    pallas_call x6, Pallas kernels, call(): pl.pallas_call(body, in_specs=specs, out_specs=[ANY] * n_out, out_shape=[...  96 us
    ppermute x2, waiting for transfers between devices, by_sequence(): lax.ppermute(gx_second[m][1], 'section', [(1, 0)])  89.5 us
    pallas_call x1, Pallas kernels, exchange_rows(): pl.pallas_call(kernel, in_specs=[ANY] * n_in, out_specs=ANY, out_shape=ja...  25.9 us
    pallas_call x1, Pallas kernels, widen(): pl.pallas_call(kernel, in_specs=[ANY] * (n_in - 1) + [WHOLE], out_specs=[...  22.1 us
  transfers between devices with their start and end apart: 4, of which 2 were waited for; matrix products, arithmetic and copies ran while one was open for 0% of the time, Pallas kernels for 18%

profile of v13, /device:TPU:0, one launch (start us, length us, event | category | flops | bytes accessed | tf_op | source)
XLA Modules:
  0.0 624.9 jit_solution(12059074509723018156)
XLA Ops:
  0.6 135.8 %fetch_and_forward.1 = (bf16[3,1024,512]{2,1,0:T(8,128)(2,1)}, bf16[512,1024]{1,0:T(8,128)(2,1)}, bf16[2,1024,2048]{2,1,0:T(8,128)(2,1)}, bf16[1024,2048]{1,0:T(...) custom-call(s32[4]{0:T(128)} %refs_0_.15, ...), custom_call_target="tpu_custom_call" | custom-call | flops 18253611008 | bytes 94371840 | tf_op jit(solution)/shard_map/fetch_and_forward/pallas_call | solution.py:914
  136.5 1.4 collective-permute-start.1
  137.8 36.5 %layer_forward.3 = (bf16[2,512,1024]{2,1,0:T(8,128)(2,1)}, bf16[2,512,1024]{2,1,0:T(8,128)(2,1)}, bf16[2,512,1024]{2,1,0:T(8,128)(2,1)}, bf16[2,512,1024]{2,1,0:...) custom-call(s32[4]{0:T(128)} %refs_0_.15, ...), custom_call_target="tpu_custom_call", output_to_operand_aliasing={{0}: (17, {}), {1}: (18, {}), {2}: (19, {}), {3}: (20, {}),... | custom-call | flops 18253611008 | bytes 56623104 | tf_op jit(solution)/shard_map/layer_forward/pallas_call | solution.py:56
  174.3 2.3 collective-permute-start
  176.6 0.0 collective-permute-done.1.refs_1_
  176.6 0.0 copy-start.1
  176.6 1.0 copy-done.1
  177.6 1.3 layer_forward.4
  178.9 25.9 %exchange_rows.1.refs_30_.refs_10_ = bf16[4,256,1024]{2,1,0:T(8,128)(2,1)} custom-call(bf16[512,1024]{1,0:T(8,128)(2,1)} %get-tuple-element.153.refs_30_.refs_0_, bf16[512,1024]{1,0:T(8,128)(2,1)} %get-tuple-element.154.refs_30_.refs_1_, bf16[512,1024]{1,0:T(8,128)(2,1)} %get-tuple-element.181.refs_2_.refs_25_.refs_11_), custom_call_target="tpu_custom_call" | custom-call | tf_op jit(solution)/shard_map/exchange_rows/pallas_call | solution.py:1597
  204.8 0.0 collective-permute-done.refs_1_
  204.8 1.4 layer_forward.5
  206.2 6.9 %layer_backward.3 = (bf16[2,512,4096]{2,1,0:T(8,128)(2,1)}, bf16[2,512,4096]{2,1,0:T(8,128)(2,1)}, bf16[2,512,1024]{2,1,0:T(8,128)(2,1)}, bf16[2,512,1024]{2,1,0...) custom-call(s32[4]{0:T(128)} %refs_0_.15, ...), custom_call_target="tpu_custom_call" | custom-call | flops 19864223744 | bytes 73400320 | tf_op jit(solution)/shard_map/layer_backward/pallas_call | solution.py:56
  213.1 1.3 collective-permute-start.2
  214.4 0.0 copy-start
  214.4 5.4 layer_backward.4
  219.8 0.0 copy-start.2
  219.8 0.0 copy-start.3
  219.9 1.4 collective-permute-start.3
  221.3 0.0 copy-done
  221.3 0.1 select_bitcast_fusion
  221.4 0.0 copy-done.2
  221.4 0.0 copy-done.3
  221.4 0.1 select_bitcast_fusion.1
  221.6 1.5 pad_maximum_fusion.refs_33_.refs_36_
  223.1 85.6 %collective-permute-done.2.refs_1_ = bf16[512,1024]{1,0:T(8,128)(2,1)} collective-permute-done((bf16[512,1024]{1,0:T(8,128)(2,1)}, bf16[512,1024]{1,0:T(8,128)(2,1)}, u32[]{:S(2)}, u32[]{:S(2)}) %collective-permute-start.2) | collective-permute-done | bytes 1048608 | tf_op jit(solution)/shard_map/ppermute | solution.py:2239
  308.6 44.5 %layer_backward.5 = (bf16[2,512,4096]{2,1,0:T(8,128)(2,1)}, bf16[2,512,4096]{2,1,0:T(8,128)(2,1)}, bf16[2,512,1024]{2,1,0:T(8,128)(2,1)}, bf16[2,512,1024]{2,1,0...) custom-call(s32[4]{0:T(128)} %refs_0_.15, ...), custom_call_target="tpu_custom_call", output_to_operand_aliasing={{0}: (25, {}), {1}: (26, {}), {2}: (27, {}), {3}: (28, {}),... | custom-call | flops 19864223744 | bytes 73400320 | tf_op jit(solution)/shard_map/layer_backward/pallas_call | solution.py:56
  353.1 3.9 collective-permute-done.3.refs_15_
  357.0 245.3 %backward_and_reduce.1 = (bf16[1,1024,2048]{2,1,0:T(8,128)(2,1)}, bf16[2,1024,2048]{2,1,0:T(8,128)(2,1)}, bf16[3,1024,512]{2,1,0:T(8,128)(2,1)}, bf16[1,1024,512...) custom-call(s32[4]{0:T(128)} %refs_0_.15, ...), custom_call_target="tpu_custom_call", output_to_operand_aliasing={{6}: (20, {}), {7}: (21, {})} | custom-call | flops 34359738368 | bytes 104857600 | tf_op jit(solution)/shard_map/backward_and_reduce/pallas_call | solution.py:1509
  602.4 22.1 %widen.1 = (f32[1,1024,2048]{2,1,0:T(8,128)}, f32[2,1024,2048]{2,1,0:T(8,128)}, f32[3,1024,512]{2,1,0:T(8,128)}, f32[512,1024]{1,0:T(8,128)}, f32[4,256,1024]{2,...) custom-call(bf16[1,1024,2048]{2,1,0:T(8,128)(2,1)} %get-tuple-elemen, ...), custom_call_target="tpu_custom_call" | custom-call | bytes 58720256 | tf_op jit(solution)/shard_map/widen/pallas_call | solution.py:1727
Async XLA Ops:
  136.5 40.1 %collective-permute-start.1 = (bf16[512,1024]{1,0:T(8,128)(2,1)}, bf16[512,1024]{1,0:T(8,128)(2,1)S(1)}, u32[]{:S(2)}, u32[]{:S(2)}) collective-permute-start(bf16[512,1024]{1,0:T(8,128)(2,1)} %get-tuple-element.153.refs_30_.refs_0_), channel_id=1, source_target_pairs={{0,16},{1,17},{2,18},{3,19},{4,20},{5,21},{6,22},{7,23},{8,24},{9,... | collective-permute-start | bytes 3145736 | tf_op jit(solution)/shard_map/ppermute | solution.py:2216
  174.3 30.4 %collective-permute-start = (bf16[512,1024]{1,0:T(8,128)(2,1)}, bf16[512,1024]{1,0:T(8,128)(2,1)}, u32[]{:S(2)}, u32[]{:S(2)}) collective-permute-start(bf16[512,1024]{1,0:T(8,128)(2,1)} %get-tuple-element.154.refs_30_.refs_1_), channel_id=1, source_target_pairs={{0,16},{1,17},{2,18},{3,19},{4,20},{5,21},{6,22},{7,23},{8,24},{9,... | collective-permute-start | bytes 3145736 | tf_op jit(solution)/shard_map/ppermute | solution.py:2216
  176.6 1.0 copy-start.1
  213.1 95.5 %collective-permute-start.2 = (bf16[512,1024]{1,0:T(8,128)(2,1)}, bf16[512,1024]{1,0:T(8,128)(2,1)}, u32[]{:S(2)}, u32[]{:S(2)}) collective-permute-start(bf16[512,1024]{1,0:T(8,128)(2,1)} %get-tuple-element.193.refs_27_), channel_id=1, source_target_pairs={{16,0},{17,1},{18,2},{19,3},{20,4},{21,5},{22,6},{23,7},{24,8},{25... | collective-permute-start | bytes 3145736 | tf_op jit(solution)/shard_map/ppermute | solution.py:2239
  214.4 6.9 %copy-start = (bf16[512,1024]{1,0:T(8,128)(2,1)S(1)}, bf16[512,1024]{1,0:T(8,128)(2,1)}, u32[]{:S(2)}) copy-start(bf16[512,1024]{1,0:T(8,128)(2,1)} %get-tuple-element.133.refs_1_) | copy-start | bytes 3145732
  219.8 1.6 copy-start.2
  219.8 1.6 copy-start.3
  219.9 137.2 %collective-permute-start.3 = (bf16[512,1024]{1,0:T(8,128)(2,1)}, bf16[512,1024]{1,0:T(8,128)(2,1)}, u32[]{:S(2)}, u32[]{:S(2)}) collective-permute-start(bf16[512,1024]{1,0:T(8,128)(2,1)} %get-tuple-element.217.refs_46_), channel_id=1, source_target_pairs={{16,0},{17,1},{18,2},{19,3},{20,4},{21,5},{22,6},{23,7},{24,8},{25... | collective-permute-start | bytes 3145736 | tf_op jit(solution)/shard_map/ppermute | solution.py:2239

commit v14 on v13

--- a/solution.py
+++ b/solution.py
@@ -610,8 +610,8 @@
 
 
 MESH = pl.DeviceIdType.MESH
-CORE_LAG = 3
-CROSS_LAG = 3
+CORE_LAG = 2
+CROSS_LAG = 2
 CHAIN_LAG = 2
 
 
@@ -663,11 +663,11 @@
     events, clock, busy = [], 0.0, 0.0
     for index, (kind, part, pieces) in enumerate(plan):
         clock += size(index)
-        events.append((clock + 66000, index, 0))
+        events.append((clock + 132000, index, 0))
         if pieces == groups:
             start = max(clock, busy)
             busy = start + size(index) * (chips - 1) * 1.0
-            events += [(start + (size(index) * 1.0 + 66000) * hop, index, hop) for hop in range(1, chips)]
+            events += [(start + (size(index) * 1.0 + 132000) * hop, index, hop) for hop in range(1, chips)]
     events.sort()
     when = {event[1:]: event[0] for event in events}
 
@@ -1292,7 +1292,7 @@
                 source.at[block(1 - t, shard_rows)], rows_out.at[m], r_send.at[m], r_recv.at[m], cross
             )
 
-        row_plan = [(0, 0, low_grad_ref, True), (0, 1, gxl_out, False), (1, 1, second_ref, True)]
+        row_plan = [(0, 0, low_grad_ref, True), (0, 1, gxl_out, False), (1, 1, second_ref, False)]
         for number, m, source, early in row_plan:
             if early:
                 @pl.when(section == number)
@@ -1620,7 +1620,7 @@
             jobs += [(index, part, at, step, columns) for part in range(lead) for at in range(0, depth, step)]
     jobs += [(n, m, 0, shard_rows, width) for m in range(seqs)] + [(n + 1, m, 0, shard_rows, width) for m in range(seqs)]
     jobs += [(n + 2, m, 0, shard_rows, width) for m in range(2 * seqs)]
-    ring = 5
+    ring = 6
     n_in = n + 3 * seqs + 4
     parts = units // width
 

time: 633 us -> 626 us (0.989)
  no operation moved by 1% of the time
where the time goes in v14:
time: 626 us; the launch traced here: 618 us
  Pallas kernels  519 us (83%)
  waiting for transfers between devices  88.1 us (14%)
  starting transfers between devices  6.36 us (1%)
    pallas_call x1, Pallas kernels, backward_and_reduce(): pl.pallas_call(kernel, in_specs=[SMEM, SMEM] + NORM_SPECS + [WHOLE] * 9 +...  244 us
    pallas_call x1, Pallas kernels, fetch_and_forward(): pl.pallas_call(kernel, in_specs=[SMEM, SMEM] + NORM_SPECS + [ANY] * 8, ou...  133 us
    pallas_call x6, Pallas kernels, call(): pl.pallas_call(body, in_specs=specs, out_specs=[ANY] * n_out, out_shape=[...  96 us
    ppermute x2, waiting for transfers between devices, by_sequence(): lax.ppermute(gx_second[m][1], 'section', [(1, 0)])  88.1 us
    pallas_call x1, Pallas kernels, exchange_rows(): pl.pallas_call(kernel, in_specs=[ANY] * n_in, out_specs=ANY, out_shape=ja...  24.8 us
    pallas_call x1, Pallas kernels, widen(): pl.pallas_call(kernel, in_specs=[ANY] * (n_in - 1) + [WHOLE], out_specs=[...  21.7 us
  transfers between devices with their start and end apart: 4, of which 2 were waited for; matrix products, arithmetic and copies ran while one was open for 0% of the time, Pallas kernels for 18%

profile of v14, /device:TPU:0, one launch (start us, length us, event | category | flops | bytes accessed | tf_op | source)
XLA Modules:
  0.0 617.9 jit_solution(6051153459757791798)
XLA Ops:
  0.6 133.3 %fetch_and_forward.1 = (bf16[3,1024,512]{2,1,0:T(8,128)(2,1)}, bf16[512,1024]{1,0:T(8,128)(2,1)}, bf16[2,1024,2048]{2,1,0:T(8,128)(2,1)}, bf16[1024,2048]{1,0:T(...) custom-call(s32[4]{0:T(128)} %refs_0_.15, ...), custom_call_target="tpu_custom_call" | custom-call | flops 18253611008 | bytes 94371840 | tf_op jit(solution)/shard_map/fetch_and_forward/pallas_call | solution.py:914
  133.9 1.4 collective-permute-start.1
  135.3 36.5 %layer_forward.3 = (bf16[2,512,1024]{2,1,0:T(8,128)(2,1)}, bf16[2,512,1024]{2,1,0:T(8,128)(2,1)}, bf16[2,512,1024]{2,1,0:T(8,128)(2,1)}, bf16[2,512,1024]{2,1,0:...) custom-call(s32[4]{0:T(128)} %refs_0_.15, ...), custom_call_target="tpu_custom_call", output_to_operand_aliasing={{0}: (17, {}), {1}: (18, {}), {2}: (19, {}), {3}: (20, {}),... | custom-call | flops 18253611008 | bytes 56623104 | tf_op jit(solution)/shard_map/layer_forward/pallas_call | solution.py:56
  171.8 2.3 collective-permute-start
  174.1 0.0 collective-permute-done.1.refs_1_
  174.1 0.0 copy-start.1
  174.1 1.0 copy-done.1
  175.0 1.3 layer_forward.4
  176.4 24.8 %exchange_rows.1.refs_30_.refs_10_ = bf16[4,256,1024]{2,1,0:T(8,128)(2,1)} custom-call(bf16[512,1024]{1,0:T(8,128)(2,1)} %get-tuple-element.153.refs_30_.refs_0_, bf16[512,1024]{1,0:T(8,128)(2,1)} %get-tuple-element.154.refs_30_.refs_1_, bf16[512,1024]{1,0:T(8,128)(2,1)} %get-tuple-element.181.refs_2_.refs_25_.refs_11_), custom_call_target="tpu_custom_call" | custom-call | tf_op jit(solution)/shard_map/exchange_rows/pallas_call | solution.py:1597
  201.2 0.0 collective-permute-done.refs_1_
  201.2 1.4 layer_forward.5
  202.6 6.9 %layer_backward.3 = (bf16[2,512,4096]{2,1,0:T(8,128)(2,1)}, bf16[2,512,4096]{2,1,0:T(8,128)(2,1)}, bf16[2,512,1024]{2,1,0:T(8,128)(2,1)}, bf16[2,512,1024]{2,1,0...) custom-call(s32[4]{0:T(128)} %refs_0_.15, ...), custom_call_target="tpu_custom_call" | custom-call | flops 19864223744 | bytes 73400320 | tf_op jit(solution)/shard_map/layer_backward/pallas_call | solution.py:56
  209.6 1.3 collective-permute-start.2
  210.9 0.0 copy-start
  210.9 5.4 layer_backward.4
  216.3 0.0 copy-start.2
  216.3 0.0 copy-start.3
  216.3 1.4 collective-permute-start.3
  217.7 0.0 copy-done
  217.7 0.1 select_bitcast_fusion
  217.9 0.0 copy-done.2
  217.9 0.0 copy-done.3
  217.9 0.1 select_bitcast_fusion.1
  218.0 1.5 pad_maximum_fusion.refs_33_.refs_36_
  219.5 84.2 %collective-permute-done.2.refs_1_ = bf16[512,1024]{1,0:T(8,128)(2,1)} collective-permute-done((bf16[512,1024]{1,0:T(8,128)(2,1)}, bf16[512,1024]{1,0:T(8,128)(2,1)}, u32[]{:S(2)}, u32[]{:S(2)}) %collective-permute-start.2) | collective-permute-done | bytes 1048608 | tf_op jit(solution)/shard_map/ppermute | solution.py:2239
  303.7 44.5 %layer_backward.5 = (bf16[2,512,4096]{2,1,0:T(8,128)(2,1)}, bf16[2,512,4096]{2,1,0:T(8,128)(2,1)}, bf16[2,512,1024]{2,1,0:T(8,128)(2,1)}, bf16[2,512,1024]{2,1,0...) custom-call(s32[4]{0:T(128)} %refs_0_.15, ...), custom_call_target="tpu_custom_call", output_to_operand_aliasing={{0}: (25, {}), {1}: (26, {}), {2}: (27, {}), {3}: (28, {}),... | custom-call | flops 19864223744 | bytes 73400320 | tf_op jit(solution)/shard_map/layer_backward/pallas_call | solution.py:56
  348.2 3.9 collective-permute-done.3.refs_15_
  352.1 243.6 %backward_and_reduce.1 = (bf16[1,1024,2048]{2,1,0:T(8,128)(2,1)}, bf16[2,1024,2048]{2,1,0:T(8,128)(2,1)}, bf16[3,1024,512]{2,1,0:T(8,128)(2,1)}, bf16[1,1024,512...) custom-call(s32[4]{0:T(128)} %refs_0_.15, ...), custom_call_target="tpu_custom_call", output_to_operand_aliasing={{6}: (20, {}), {7}: (21, {})} | custom-call | flops 34359738368 | bytes 104857600 | tf_op jit(solution)/shard_map/backward_and_reduce/pallas_call | solution.py:1509
  595.6 21.7 %widen.1 = (f32[1,1024,2048]{2,1,0:T(8,128)}, f32[2,1024,2048]{2,1,0:T(8,128)}, f32[3,1024,512]{2,1,0:T(8,128)}, f32[512,1024]{1,0:T(8,128)}, f32[4,256,1024]{2,...) custom-call(bf16[1,1024,2048]{2,1,0:T(8,128)(2,1)} %get-tuple-elemen, ...), custom_call_target="tpu_custom_call" | custom-call | bytes 58720256 | tf_op jit(solution)/shard_map/widen/pallas_call | solution.py:1727
Async XLA Ops:
  133.9 40.1 %collective-permute-start.1 = (bf16[512,1024]{1,0:T(8,128)(2,1)}, bf16[512,1024]{1,0:T(8,128)(2,1)S(1)}, u32[]{:S(2)}, u32[]{:S(2)}) collective-permute-start(bf16[512,1024]{1,0:T(8,128)(2,1)} %get-tuple-element.153.refs_30_.refs_0_), channel_id=1, source_target_pairs={{0,16},{1,17},{2,18},{3,19},{4,20},{5,21},{6,22},{7,23},{8,24},{9,... | collective-permute-start | bytes 3145736 | tf_op jit(solution)/shard_map/ppermute | solution.py:2216
  171.8 29.4 %collective-permute-start = (bf16[512,1024]{1,0:T(8,128)(2,1)}, bf16[512,1024]{1,0:T(8,128)(2,1)}, u32[]{:S(2)}, u32[]{:S(2)}) collective-permute-start(bf16[512,1024]{1,0:T(8,128)(2,1)} %get-tuple-element.154.refs_30_.refs_1_), channel_id=1, source_target_pairs={{0,16},{1,17},{2,18},{3,19},{4,20},{5,21},{6,22},{7,23},{8,24},{9,... | collective-permute-start | bytes 3145736 | tf_op jit(solution)/shard_map/ppermute | solution.py:2216
  174.1 1.0 copy-start.1
  209.6 94.1 %collective-permute-start.2 = (bf16[512,1024]{1,0:T(8,128)(2,1)}, bf16[512,1024]{1,0:T(8,128)(2,1)}, u32[]{:S(2)}, u32[]{:S(2)}) collective-permute-start(bf16[512,1024]{1,0:T(8,128)(2,1)} %get-tuple-element.193.refs_27_), channel_id=1, source_target_pairs={{16,0},{17,1},{18,2},{19,3},{20,4},{21,5},{22,6},{23,7},{24,8},{25... | collective-permute-start | bytes 3145736 | tf_op jit(solution)/shard_map/ppermute | solution.py:2239
  210.9 6.9 %copy-start = (bf16[512,1024]{1,0:T(8,128)(2,1)S(1)}, bf16[512,1024]{1,0:T(8,128)(2,1)}, u32[]{:S(2)}) copy-start(bf16[512,1024]{1,0:T(8,128)(2,1)} %get-tuple-element.133.refs_1_) | copy-start | bytes 3145732
  216.3 1.6 copy-start.2
  216.3 1.6 copy-start.3
  216.3 135.8 %collective-permute-start.3 = (bf16[512,1024]{1,0:T(8,128)(2,1)}, bf16[512,1024]{1,0:T(8,128)(2,1)}, u32[]{:S(2)}, u32[]{:S(2)}) collective-permute-start(bf16[512,1024]{1,0:T(8,128)(2,1)} %get-tuple-element.217.refs_46_), channel_id=1, source_target_pairs={{16,0},{17,1},{18,2},{19,3},{20,4},{21,5},{22,6},{23,7},{24,8},{25... | collective-permute-start | bytes 3145736 | tf_op jit(solution)/shard_map/ppermute | solution.py:2239

commit v15 on v14

--- a/solution.py
+++ b/solution.py
@@ -612,7 +612,7 @@
 MESH = pl.DeviceIdType.MESH
 CORE_LAG = 2
 CROSS_LAG = 2
-CHAIN_LAG = 2
+CHAIN_LAG = 1
 
 
 def neighbours():

time: 626 us -> 710 us (1.13)
  Pallas kernels: 519 us -> 602 us
    pallas_call x1, Pallas kernels: 244 us -> 326 us  [backward_and_reduce(): pl.pallas_call(kernel, in_specs=[SMEM, SMEM] + NORM_SPECS + [WHOLE] * 9 +...]
  transfers between devices with their start and end apart: 4 -> 4, of which waited for: 2 -> 2; matrix products, arithmetic and copies ran while one was open for 0% -> 0% of each run, Pallas kernels for 18% -> 16%
where the time goes in v15:
time: 710 us; the launch traced here: 701 us
  Pallas kernels  602 us (85%)
  waiting for transfers between devices  88.1 us (12%)
    pallas_call x1, Pallas kernels, backward_and_reduce(): pl.pallas_call(kernel, in_specs=[SMEM, SMEM] + NORM_SPECS + [WHOLE] * 9 +...  326 us
    pallas_call x1, Pallas kernels, fetch_and_forward(): pl.pallas_call(kernel, in_specs=[SMEM, SMEM] + NORM_SPECS + [ANY] * 8, ou...  133 us
    pallas_call x6, Pallas kernels, call(): pl.pallas_call(body, in_specs=specs, out_specs=[ANY] * n_out, out_shape=[...  96 us
    ppermute x2, waiting for transfers between devices, by_sequence(): lax.ppermute(gx_second[m][1], 'section', [(1, 0)])  88.1 us
    pallas_call x1, Pallas kernels, exchange_rows(): pl.pallas_call(kernel, in_specs=[ANY] * n_in, out_specs=ANY, out_shape=ja...  24.8 us
    pallas_call x1, Pallas kernels, widen(): pl.pallas_call(kernel, in_specs=[ANY] * (n_in - 1) + [WHOLE], out_specs=[...  21.7 us
  transfers between devices with their start and end apart: 4, of which 2 were waited for; matrix products, arithmetic and copies ran while one was open for 0% of the time, Pallas kernels for 16%

profile of v15, /device:TPU:0, one launch (start us, length us, event | category | flops | bytes accessed | tf_op | source)
XLA Modules:
  0.0 700.7 jit_solution(4475798170200266028)
XLA Ops:
  0.6 133.3 %fetch_and_forward.1 = (bf16[3,1024,512]{2,1,0:T(8,128)(2,1)}, bf16[512,1024]{1,0:T(8,128)(2,1)}, bf16[2,1024,2048]{2,1,0:T(8,128)(2,1)}, bf16[1024,2048]{1,0:T(...) custom-call(s32[4]{0:T(128)} %refs_0_.15, ...), custom_call_target="tpu_custom_call" | custom-call | flops 18253611008 | bytes 94371840 | tf_op jit(solution)/shard_map/fetch_and_forward/pallas_call | solution.py:914
  133.9 1.4 collective-permute-start.1
  135.3 36.5 %layer_forward.3 = (bf16[2,512,1024]{2,1,0:T(8,128)(2,1)}, bf16[2,512,1024]{2,1,0:T(8,128)(2,1)}, bf16[2,512,1024]{2,1,0:T(8,128)(2,1)}, bf16[2,512,1024]{2,1,0:...) custom-call(s32[4]{0:T(128)} %refs_0_.15, ...), custom_call_target="tpu_custom_call", output_to_operand_aliasing={{0}: (17, {}), {1}: (18, {}), {2}: (19, {}), {3}: (20, {}),... | custom-call | flops 18253611008 | bytes 56623104 | tf_op jit(solution)/shard_map/layer_forward/pallas_call | solution.py:56
  171.8 2.3 collective-permute-start
  174.1 0.0 collective-permute-done.1.refs_1_
  174.1 0.0 copy-start.1
  174.1 1.0 copy-done.1
  175.0 1.3 layer_forward.4
  176.4 24.8 %exchange_rows.1.refs_30_.refs_10_ = bf16[4,256,1024]{2,1,0:T(8,128)(2,1)} custom-call(bf16[512,1024]{1,0:T(8,128)(2,1)} %get-tuple-element.153.refs_30_.refs_0_, bf16[512,1024]{1,0:T(8,128)(2,1)} %get-tuple-element.154.refs_30_.refs_1_, bf16[512,1024]{1,0:T(8,128)(2,1)} %get-tuple-element.181.refs_2_.refs_25_.refs_11_), custom_call_target="tpu_custom_call" | custom-call | tf_op jit(solution)/shard_map/exchange_rows/pallas_call | solution.py:1597
  201.2 0.0 collective-permute-done.refs_1_
  201.2 1.4 layer_forward.5
  202.6 6.9 layer_backward.3
  209.6 1.3 collective-permute-start.2
  210.9 0.0 copy-start
  210.9 5.4 layer_backward.4
  216.3 0.0 copy-start.2
  216.3 0.0 copy-start.3
  216.3 1.4 collective-permute-start.3
  217.7 0.0 copy-done
  217.7 0.1 select_bitcast_fusion
  217.9 0.0 copy-done.2
  217.9 0.0 copy-done.3
  217.9 0.1 select_bitcast_fusion.1
  218.0 1.5 pad_maximum_fusion.refs_33_.refs_36_
  219.5 84.2 %collective-permute-done.2.refs_1_ = bf16[512,1024]{1,0:T(8,128)(2,1)} collective-permute-done((bf16[512,1024]{1,0:T(8,128)(2,1)}, bf16[512,1024]{1,0:T(8,128)(2,1)}, u32[]{:S(2)}, u32[]{:S(2)}) %collective-permute-start.2) | collective-permute-done | bytes 1048608 | tf_op jit(solution)/shard_map/ppermute | solution.py:2239
  303.7 44.5 %layer_backward.5 = (bf16[2,512,4096]{2,1,0:T(8,128)(2,1)}, bf16[2,512,4096]{2,1,0:T(8,128)(2,1)}, bf16[2,512,1024]{2,1,0:T(8,128)(2,1)}, bf16[2,512,1024]{2,1,0...) custom-call(s32[4]{0:T(128)} %refs_0_.15, ...), custom_call_target="tpu_custom_call", output_to_operand_aliasing={{0}: (25, {}), {1}: (26, {}), {2}: (27, {}), {3}: (28, {}),... | custom-call | flops 19864223744 | bytes 73400320 | tf_op jit(solution)/shard_map/layer_backward/pallas_call | solution.py:56
  348.2 3.9 collective-permute-done.3.refs_15_
  352.1 326.3 %backward_and_reduce.1 = (bf16[1,1024,2048]{2,1,0:T(8,128)(2,1)}, bf16[2,1024,2048]{2,1,0:T(8,128)(2,1)}, bf16[3,1024,512]{2,1,0:T(8,128)(2,1)}, bf16[1,1024,512...) custom-call(s32[4]{0:T(128)} %refs_0_.15, ...), custom_call_target="tpu_custom_call", output_to_operand_aliasing={{6}: (20, {}), {7}: (21, {})} | custom-call | flops 34359738368 | bytes 104857600 | tf_op jit(solution)/shard_map/backward_and_reduce/pallas_call | solution.py:1509
  678.4 21.7 %widen.1 = (f32[1,1024,2048]{2,1,0:T(8,128)}, f32[2,1024,2048]{2,1,0:T(8,128)}, f32[3,1024,512]{2,1,0:T(8,128)}, f32[512,1024]{1,0:T(8,128)}, f32[4,256,1024]{2,...) custom-call(bf16[1,1024,2048]{2,1,0:T(8,128)(2,1)} %get-tuple-elemen, ...), custom_call_target="tpu_custom_call" | custom-call | bytes 58720256 | tf_op jit(solution)/shard_map/widen/pallas_call | solution.py:1727
Async XLA Ops:
  133.9 40.1 %collective-permute-start.1 = (bf16[512,1024]{1,0:T(8,128)(2,1)}, bf16[512,1024]{1,0:T(8,128)(2,1)S(1)}, u32[]{:S(2)}, u32[]{:S(2)}) collective-permute-start(bf16[512,1024]{1,0:T(8,128)(2,1)} %get-tuple-element.153.refs_30_.refs_0_), channel_id=1, source_target_pairs={{0,16},{1,17},{2,18},{3,19},{4,20},{5,21},{6,22},{7,23},{8,24},{9,... | collective-permute-start | bytes 3145736 | tf_op jit(solution)/shard_map/ppermute | solution.py:2216
  171.8 29.4 %collective-permute-start = (bf16[512,1024]{1,0:T(8,128)(2,1)}, bf16[512,1024]{1,0:T(8,128)(2,1)}, u32[]{:S(2)}, u32[]{:S(2)}) collective-permute-start(bf16[512,1024]{1,0:T(8,128)(2,1)} %get-tuple-element.154.refs_30_.refs_1_), channel_id=1, source_target_pairs={{0,16},{1,17},{2,18},{3,19},{4,20},{5,21},{6,22},{7,23},{8,24},{9,... | collective-permute-start | bytes 3145736 | tf_op jit(solution)/shard_map/ppermute | solution.py:2216
  174.1 1.0 copy-start.1
  209.6 94.1 %collective-permute-start.2 = (bf16[512,1024]{1,0:T(8,128)(2,1)}, bf16[512,1024]{1,0:T(8,128)(2,1)}, u32[]{:S(2)}, u32[]{:S(2)}) collective-permute-start(bf16[512,1024]{1,0:T(8,128)(2,1)} %get-tuple-element.193.refs_27_), channel_id=1, source_target_pairs={{16,0},{17,1},{18,2},{19,3},{20,4},{21,5},{22,6},{23,7},{24,8},{25... | collective-permute-start | bytes 3145736 | tf_op jit(solution)/shard_map/ppermute | solution.py:2239
  210.9 6.9 copy-start
  216.3 1.6 copy-start.2
  216.3 1.6 copy-start.3
  216.3 135.8 %collective-permute-start.3 = (bf16[512,1024]{1,0:T(8,128)(2,1)}, bf16[512,1024]{1,0:T(8,128)(2,1)}, u32[]{:S(2)}, u32[]{:S(2)}) collective-permute-start(bf16[512,1024]{1,0:T(8,128)(2,1)} %get-tuple-element.217.refs_46_), channel_id=1, source_target_pairs={{16,0},{17,1},{18,2},{19,3},{20,4},{21,5},{22,6},{23,7},{24,8},{25... | collective-permute-start | bytes 3145736 | tf_op jit(solution)/shard_map/ppermute | solution.py:2239
